TPU v7x, 32 devices: a whole 2x2x4 slice. The times are simulated.
32 devices in a mesh: ctx: 8 (over z, x), fsdp: 4 (over y, core).
Axes of the slice: x: 2, y: 2, z: 4, core: 2. Of those that a mesh axis runs over, the one named last changes fastest.
Arguments:
- tokens: bfloat16 [4, 8192, 512], P('fsdp', 'ctx'), may hold values from -6 to 6
- ln1_gain: bfloat16 [512], P('fsdp'), may hold values from 0.5 to 1.5
- ln1_shift: bfloat16 [512], P('fsdp'), may hold values from -1.1953125 to 1.1953125
- qkv_weight: bfloat16 [512, 1536], P('fsdp'), may hold values from -0.25 to 0.25
- qkv_bias: bfloat16 [1536], P('fsdp'), may hold values from -0.59765625 to 0.59765625
- out_weight: bfloat16 [512, 512], P('fsdp'), may hold values from -3 to 3
- out_bias: bfloat16 [512], P('fsdp'), may hold values from -1.1953125 to 1.1953125
- ln2_gain: bfloat16 [512], P('fsdp'), may hold values from 0.5 to 1.5
- ln2_shift: bfloat16 [512], P('fsdp'), may hold values from -1.1953125 to 1.1953125
- up_weight: bfloat16 [512, 2048], P('fsdp'), may hold values from -0.25 to 0.25
- up_bias: bfloat16 [2048], P('fsdp'), may hold values from -1.1953125 to 1.1953125
- down_weight: bfloat16 [2048, 512], P('fsdp'), may hold values from -0.125 to 0.125
- down_bias: bfloat16 [512], P('fsdp'), may hold values from -4 to 4
- seq_lengths: int32 [4, 9], P('fsdp'), may hold values from 128 to 4096, as said below
- span_order: int32 [4, 64], P('fsdp'), may hold values from 0 to 63, each once within a row
- cotangent: bfloat16 [4, 8192, 512], P('fsdp', 'ctx'), may hold values from -6 to 6
Outputs:
- mixed: bfloat16 [4, 8192, 512], P('fsdp', 'ctx')
- tokens_grad: float32 [4, 8192, 512], P('fsdp', 'ctx')
- ln1_gain_grad: float32 [512], P('fsdp')
- ln1_shift_grad: float32 [512], P('fsdp')
- qkv_weight_grad: float32 [512, 1536], P('fsdp')
- qkv_bias_grad: float32 [1536], P('fsdp')
- out_weight_grad: float32 [512, 512], P('fsdp')
- out_bias_grad: float32 [512], P('fsdp')
- ln2_gain_grad: float32 [512], P('fsdp')
- ln2_shift_grad: float32 [512], P('fsdp')
- up_weight_grad: float32 [512, 2048], P('fsdp')
- up_bias_grad: float32 [2048], P('fsdp')
- down_weight_grad: float32 [2048, 512], P('fsdp')
- down_bias_grad: float32 [512], P('fsdp')
Inputs may be any that keep to these rules, and one draw needn't show every extreme that they name: `seq_lengths`: row g holds the lengths of group g's prompt and then of its 8 continuations, which follow one another in that order from the group's first position; each is a multiple of 128, and together they fill 8192 positions. The prompt holds 4096 positions; the continuations hold the other half, each between 128 and 896 positions. `span_order`: row g gives, for each slot of 128 rows of tokens[g] in row order, the span of the group that it holds (span b covers positions b * 128 to (b + 1) * 128 - 1); each span once.
All inputs are finite; a program needn't handle non-finite values.
Results may differ from a plain program's by a relative error of at most 0.013.
Values may be sent and summed in bfloat16 or wider, within the bound.
No kernel may reach another device: no remote copies, remote signals or barrier semaphores. Data moves between devices by JAX's collectives and lax.ppermute only.
A program may use at most 128 MiB of HBM per device.

v0:
```python
import jax
import jax.numpy as jnp
from jax import lax
from jax.sharding import PartitionSpec as P

D = 512
HEADS = 8
HEAD = 64
SPAN = 128


EPSILON = 1e-05
MASKED = -1e30


def cut_along(array, dim, length):
    before, after = (array.shape[:dim], array.shape[dim + 1 :])
    return jnp.moveaxis(array.reshape(*before, length, -1, *after), dim, 0)


def summed_on_arrival(array, axis, dim):
    pieces = cut_along(array, dim, lax.axis_size(axis))
    arrived = lax.all_to_all(pieces, axis, split_axis=0, concat_axis=0, tiled=True)
    return arrived.astype(jnp.float32).sum(axis=0)


def sent_together(arrays, axis, dim, along):
    both = jnp.concatenate(arrays, axis=along)
    filled, at, done = (summed_on_arrival(both, axis, dim), 0, [])
    for a in arrays:
        done.append(lax.slice_in_dim(filled, at, at + a.shape[along], axis=along))
        at += a.shape[along]
    return tuple(done)


def layer_norm(values, gain, shift):
    centre = values - jnp.mean(values, axis=-1, keepdims=True)
    spread = jnp.mean(centre * centre, axis=-1, keepdims=True)
    return centre * lax.rsqrt(spread + EPSILON) * gain + shift


def gelu_tanh(values):
    return jax.nn.gelu(values, approximate=True)


def span_begins(lengths_row, span_ids):
    seq_ends = jnp.cumsum(lengths_row) // SPAN
    seq_starts = seq_ends - lengths_row // SPAN
    started = seq_starts[None, :] <= span_ids[:, None]
    return jnp.max(jnp.where(started, seq_starts[None, :], 0), axis=1)


def score_masks(row_spans, row_begins, all_spans, prompt_spans):
    offset = jnp.arange(SPAN)
    causal = offset[None, :] <= offset[:, None]
    query_span = jnp.repeat(row_spans, SPAN)
    query_begin = jnp.repeat(row_begins, SPAN)
    allowed = (all_spans[None, :] < query_span[:, None]) & (
        (all_spans[None, :] >= query_begin[:, None]) | (all_spans[None, :] < prompt_spans)
    )
    return (causal, allowed)


def split_packed(packed_rows, span_count):
    shaped = packed_rows.reshape(span_count, SPAN, 3, HEADS, HEAD)
    return (shaped[:, :, 0], shaped[:, :, 1], shaped[:, :, 2])


def block_scores(queries, key_rows, key_table, causal, allowed):
    span_count = queries.shape[0]
    row_count = span_count * SPAN
    score_scale = HEAD ** (-0.5)
    nearby = (
        jnp.einsum("sqhd,skhd->hsqk", queries, key_rows, preferred_element_type=jnp.float32)
        * score_scale
    )
    nearby = jnp.where(causal, nearby, MASKED).reshape(HEADS, row_count, SPAN)
    distant = (
        jnp.einsum(
            "rhd,jhd->hrj",
            queries.reshape(row_count, HEADS, HEAD),
            key_table,
            preferred_element_type=jnp.float32,
        )
        * score_scale
    )
    distant = jnp.where(allowed[None], distant, MASKED)
    return (nearby, distant)


def attend_forward(members, key_table, value_table, all_spans, prompt_spans):
    packed_rows, row_spans, row_begins = members
    span_count = row_spans.shape[0]
    row_count = span_count * SPAN
    queries, key_rows, value_rows = split_packed(packed_rows, span_count)
    causal, allowed = score_masks(row_spans, row_begins, all_spans, prompt_spans)
    nearby, distant = block_scores(queries, key_rows, key_table, causal, allowed)
    row_peak = jnp.maximum(jnp.max(nearby, axis=-1), jnp.max(distant, axis=-1))
    nearby_exp = jnp.exp(nearby - row_peak[..., None])
    distant_exp = jnp.exp(distant - row_peak[..., None])
    row_total = jnp.sum(nearby_exp, axis=-1) + jnp.sum(distant_exp, axis=-1)
    near_weights = (
        (nearby_exp / row_total[..., None])
        .astype(jnp.bfloat16)
        .reshape(HEADS, span_count, SPAN, SPAN)
    )
    far_weights = (distant_exp / row_total[..., None]).astype(jnp.bfloat16)
    mixed_near = jnp.einsum(
        "hsqk,skhd->sqhd", near_weights, value_rows, preferred_element_type=jnp.float32
    ).reshape(row_count, D)
    mixed_far = jnp.einsum(
        "hrj,jhd->rhd", far_weights, value_table, preferred_element_type=jnp.float32
    ).reshape(row_count, D)
    log_total = row_peak + jnp.log(row_total)
    return ((mixed_near + mixed_far).astype(jnp.bfloat16), log_total)


def attend_backward(carry, members, key_table, value_table, all_spans, prompt_spans):
    grad_keys, grad_values = carry
    packed_rows, row_spans, row_begins, log_total, grad_out = members
    span_count = row_spans.shape[0]
    row_count = span_count * SPAN
    score_scale = HEAD ** (-0.5)
    queries, key_rows, value_rows = split_packed(packed_rows, span_count)
    causal, allowed = score_masks(row_spans, row_begins, all_spans, prompt_spans)
    nearby, distant = block_scores(queries, key_rows, key_table, causal, allowed)
    near_prob = jnp.exp(nearby - log_total[..., None])
    far_prob = jnp.exp(distant - log_total[..., None])
    grad_rows = grad_out.reshape(span_count, SPAN, HEADS, HEAD)
    flat_grads = grad_out.reshape(row_count, HEADS, HEAD)
    flat_queries = queries.reshape(row_count, HEADS, HEAD)
    near_dp = jnp.einsum(
        "sqhd,skhd->hsqk", grad_rows, value_rows, preferred_element_type=jnp.float32
    ).reshape(HEADS, row_count, SPAN)
    far_dp = jnp.einsum("rhd,jhd->hrj", flat_grads, value_table, preferred_element_type=jnp.float32)
    row_delta = jnp.sum(near_prob * near_dp, axis=-1) + jnp.sum(far_prob * far_dp, axis=-1)
    near_ds = (
        (near_prob * (near_dp - row_delta[..., None]))
        .astype(jnp.bfloat16)
        .reshape(HEADS, span_count, SPAN, SPAN)
    )
    far_ds = (far_prob * (far_dp - row_delta[..., None])).astype(jnp.bfloat16)
    grad_query = (
        jnp.einsum(
            "hsqk,skhd->sqhd", near_ds, key_rows, preferred_element_type=jnp.float32
        ).reshape(row_count, D)
        + jnp.einsum("hrj,jhd->rhd", far_ds, key_table, preferred_element_type=jnp.float32).reshape(
            row_count, D
        )
    ) * score_scale
    grad_key = (
        jnp.einsum("hsqk,sqhd->skhd", near_ds, queries, preferred_element_type=jnp.float32).reshape(
            row_count, D
        )
        * score_scale
    )
    near_low = near_prob.astype(jnp.bfloat16).reshape(HEADS, span_count, SPAN, SPAN)
    grad_value = jnp.einsum(
        "hsqk,sqhd->skhd", near_low, grad_rows, preferred_element_type=jnp.float32
    ).reshape(row_count, D)
    grad_keys = (
        grad_keys
        + jnp.einsum("hrj,rhd->jhd", far_ds, flat_queries, preferred_element_type=jnp.float32)
        * score_scale
    )
    grad_values = grad_values + jnp.einsum(
        "hrj,rhd->jhd",
        far_prob.astype(jnp.bfloat16),
        flat_grads,
        preferred_element_type=jnp.float32,
    )
    return ((grad_keys, grad_values), jnp.concatenate([grad_query, grad_key, grad_value], axis=1))


def local(
    tokens,
    ln1_gain,
    ln1_shift,
    qkv_weight,
    qkv_bias,
    out_weight,
    out_bias,
    ln2_gain,
    ln2_shift,
    up_weight,
    up_bias,
    down_weight,
    down_bias,
    seq_lengths,
    span_order,
    cotangent,
):
    gain_one, shift_one, weight_qkv, bias_qkv, weight_out, bias_out = (
        lax.all_gather(ln1_gain, "fsdp", axis=0, tiled=True),
        lax.all_gather(ln1_shift, "fsdp", axis=0, tiled=True),
        lax.all_gather(qkv_weight, "fsdp", axis=0, tiled=True),
        lax.all_gather(qkv_bias, "fsdp", axis=0, tiled=True),
        lax.all_gather(out_weight, "fsdp", axis=0, tiled=True),
        lax.all_gather(out_bias, "fsdp", axis=0, tiled=True),
    )
    inputs = tokens[0].astype(jnp.float32)
    local_rows = inputs.shape[0]
    local_spans = local_rows // SPAN
    all_spans = span_order[0]
    lengths_row = seq_lengths[0]
    own_spans = lax.dynamic_slice_in_dim(
        all_spans, lax.axis_index("ctx") * local_spans, local_spans
    )
    begins = span_begins(lengths_row, own_spans)
    prompt_spans = lengths_row[0] // SPAN
    normed_one, pull_one = jax.vjp(
        layer_norm, inputs, gain_one.astype(jnp.float32), shift_one.astype(jnp.float32)
    )
    normed_low = normed_one.astype(jnp.bfloat16)
    packed = (
        jnp.dot(normed_low, weight_qkv, preferred_element_type=jnp.float32)
        + bias_qkv.astype(jnp.float32)
    ).astype(jnp.bfloat16)
    inv_root = SPAN ** (-0.5)
    summed = (
        jnp.sum(packed[:, D:].reshape(local_spans, SPAN, 2 * D), axis=1, dtype=jnp.float32)
        * inv_root
    )
    own_keys = summed[:, :D].astype(jnp.bfloat16)
    own_values = summed[:, D:].astype(jnp.bfloat16)
    span_keys, span_values = (
        lax.all_gather(own_keys, "ctx", axis=0, tiled=True),
        lax.all_gather(own_values, "ctx", axis=0, tiled=True),
    )
    key_table = span_keys.reshape(-1, HEADS, HEAD)
    value_table = span_values.reshape(-1, HEADS, HEAD)
    row_block = min(512, local_rows)
    block_count = local_rows // row_block
    spans_per_block = row_block // SPAN
    packed_blocks = packed.reshape(block_count, row_block, 3 * D)
    span_blocks = own_spans.reshape(block_count, spans_per_block)
    begin_blocks = begins.reshape(block_count, spans_per_block)

    def forward_block(members):
        return attend_forward(members, key_table, value_table, all_spans, prompt_spans)

    attended, log_totals = lax.map(forward_block, (packed_blocks, span_blocks, begin_blocks))
    heads_out = attended.reshape(local_rows, D)
    gain_two, shift_two, weight_up, bias_up, weight_down, bias_down = (
        lax.all_gather(ln2_gain, "fsdp", axis=0, tiled=True),
        lax.all_gather(ln2_shift, "fsdp", axis=0, tiled=True),
        lax.all_gather(up_weight, "fsdp", axis=0, tiled=True),
        lax.all_gather(up_bias, "fsdp", axis=0, tiled=True),
        lax.all_gather(down_weight, "fsdp", axis=0, tiled=True),
        lax.all_gather(down_bias, "fsdp", axis=0, tiled=True),
    )
    residual = inputs + (
        jnp.dot(heads_out, weight_out, preferred_element_type=jnp.float32)
        + bias_out.astype(jnp.float32)
    )
    normed_two, pull_two = jax.vjp(
        layer_norm, residual, gain_two.astype(jnp.float32), shift_two.astype(jnp.float32)
    )
    normed_low_two = normed_two.astype(jnp.bfloat16)
    hidden = jnp.dot(
        normed_low_two, weight_up, preferred_element_type=jnp.float32
    ) + bias_up.astype(jnp.float32)
    activated, pull_gelu = jax.vjp(gelu_tanh, hidden)
    activated_low = activated.astype(jnp.bfloat16)
    mixed = (
        residual
        + jnp.dot(activated_low, weight_down, preferred_element_type=jnp.float32)
        + bias_down.astype(jnp.float32)
    ).astype(jnp.bfloat16)
    upstream = cotangent[0]
    grad_down_bias = jnp.sum(upstream, axis=0, dtype=jnp.float32)
    grad_down = jnp.einsum("rf,rd->fd", activated_low, upstream, preferred_element_type=jnp.float32)
    grad_active = jnp.einsum("rd,fd->rf", upstream, weight_down, preferred_element_type=jnp.float32)
    (grad_hidden,) = pull_gelu(grad_active)
    grad_hidden_low = grad_hidden.astype(jnp.bfloat16)
    grad_up_bias = jnp.sum(grad_hidden_low, axis=0, dtype=jnp.float32)
    grad_up = jnp.einsum(
        "rd,rf->df", normed_low_two, grad_hidden_low, preferred_element_type=jnp.float32
    )
    grad_normed_two = jnp.einsum(
        "rf,df->rd", grad_hidden_low, weight_up, preferred_element_type=jnp.float32
    )
    grad_norm_input, grad_gain_two, grad_shift_two = pull_two(grad_normed_two)
    grad_residual = upstream.astype(jnp.float32) + grad_norm_input
    grad_residual_low = grad_residual.astype(jnp.bfloat16)
    grad_out_bias = jnp.sum(grad_residual_low, axis=0, dtype=jnp.float32)
    grad_out = jnp.einsum(
        "rd,re->de", heads_out, grad_residual_low, preferred_element_type=jnp.float32
    )
    grad_heads = jnp.einsum(
        "re,de->rd", grad_residual_low, weight_out, preferred_element_type=jnp.float32
    ).astype(jnp.bfloat16)

    def backward_step(carry, members):
        return attend_backward(carry, members, key_table, value_table, all_spans, prompt_spans)

    zero_table = jnp.zeros(key_table.shape, jnp.float32)
    (grad_key_table, grad_value_table), grad_blocks = lax.scan(
        backward_step,
        (zero_table, zero_table),
        (
            packed_blocks,
            span_blocks,
            begin_blocks,
            log_totals,
            grad_heads.reshape(block_count, row_block, D),
        ),
    )
    grad_packed = grad_blocks.reshape(local_rows, 3 * D)
    own_key_grad, own_value_grad = sent_together(
        (
            grad_key_table.reshape(-1, D).astype(jnp.bfloat16),
            grad_value_table.reshape(-1, D).astype(jnp.bfloat16),
        ),
        "ctx",
        0,
        1,
    )
    spread_back = jnp.concatenate([own_key_grad, own_value_grad], axis=1) * inv_root
    grad_pairs = grad_packed[:, D:].reshape(local_spans, SPAN, 2 * D) + spread_back[:, None, :]
    grad_packed_low = jnp.concatenate(
        [grad_packed[:, :D], grad_pairs.reshape(local_rows, 2 * D)], axis=1
    ).astype(jnp.bfloat16)
    grad_qkv_bias = jnp.sum(grad_packed_low, axis=0, dtype=jnp.float32)
    grad_qkv = jnp.einsum(
        "rd,re->de", normed_low, grad_packed_low, preferred_element_type=jnp.float32
    )
    grad_normed_one = jnp.einsum(
        "re,de->rd", grad_packed_low, weight_qkv, preferred_element_type=jnp.float32
    )
    grad_first_input, grad_gain_one, grad_shift_one = pull_one(grad_normed_one)
    tokens_grad = (grad_residual + grad_first_input)[None]
    (
        sum_gain_one,
        sum_shift_one,
        sum_qkv,
        sum_qkv_bias,
        sum_out,
        sum_out_bias,
        sum_gain_two,
        sum_shift_two,
        sum_up,
        sum_up_bias,
        sum_down,
        sum_down_bias,
    ) = lax.psum(
        (
            grad_gain_one,
            grad_shift_one,
            grad_qkv,
            grad_qkv_bias,
            grad_out,
            grad_out_bias,
            grad_gain_two,
            grad_shift_two,
            grad_up,
            grad_up_bias,
            grad_down,
            grad_down_bias,
        ),
        "ctx",
    )
    (
        part_gain_one,
        part_shift_one,
        part_qkv,
        part_qkv_bias,
        part_out,
        part_out_bias,
        part_gain_two,
        part_shift_two,
        part_up,
        part_up_bias,
        part_down,
        part_down_bias,
    ) = (
        lax.psum_scatter(
            sum_gain_one.astype(jnp.bfloat16), "fsdp", scatter_dimension=0, tiled=True
        ).astype(jnp.float32),
        lax.psum_scatter(
            sum_shift_one.astype(jnp.bfloat16), "fsdp", scatter_dimension=0, tiled=True
        ).astype(jnp.float32),
        lax.psum_scatter(
            sum_qkv.astype(jnp.bfloat16), "fsdp", scatter_dimension=0, tiled=True
        ).astype(jnp.float32),
        lax.psum_scatter(
            sum_qkv_bias.astype(jnp.bfloat16), "fsdp", scatter_dimension=0, tiled=True
        ).astype(jnp.float32),
        lax.psum_scatter(
            sum_out.astype(jnp.bfloat16), "fsdp", scatter_dimension=0, tiled=True
        ).astype(jnp.float32),
        lax.psum_scatter(
            sum_out_bias.astype(jnp.bfloat16), "fsdp", scatter_dimension=0, tiled=True
        ).astype(jnp.float32),
        lax.psum_scatter(
            sum_gain_two.astype(jnp.bfloat16), "fsdp", scatter_dimension=0, tiled=True
        ).astype(jnp.float32),
        lax.psum_scatter(
            sum_shift_two.astype(jnp.bfloat16), "fsdp", scatter_dimension=0, tiled=True
        ).astype(jnp.float32),
        lax.psum_scatter(
            sum_up.astype(jnp.bfloat16), "fsdp", scatter_dimension=0, tiled=True
        ).astype(jnp.float32),
        lax.psum_scatter(
            sum_up_bias.astype(jnp.bfloat16), "fsdp", scatter_dimension=0, tiled=True
        ).astype(jnp.float32),
        lax.psum_scatter(
            sum_down.astype(jnp.bfloat16), "fsdp", scatter_dimension=0, tiled=True
        ).astype(jnp.float32),
        lax.psum_scatter(
            sum_down_bias.astype(jnp.bfloat16), "fsdp", scatter_dimension=0, tiled=True
        ).astype(jnp.float32),
    )
    return (
        mixed[None],
        tokens_grad,
        part_gain_one,
        part_shift_one,
        part_qkv,
        part_qkv_bias,
        part_out,
        part_out_bias,
        part_gain_two,
        part_shift_two,
        part_up,
        part_up_bias,
        part_down,
        part_down_bias,
    )


def solution(mesh):
    placed = (
        P("fsdp", "ctx", None),
        P("fsdp"),
        P("fsdp"),
        P("fsdp", None),
        P("fsdp"),
        P("fsdp", None),
        P("fsdp"),
        P("fsdp"),
        P("fsdp"),
        P("fsdp", None),
        P("fsdp"),
        P("fsdp", None),
        P("fsdp"),
        P("fsdp", None),
        P("fsdp", None),
        P("fsdp", "ctx", None),
    )
    return jax.shard_map(
        local,
        mesh=mesh,
        in_specs=placed,
        out_specs=(
            P("fsdp", "ctx", None),
            P("fsdp", "ctx", None),
            P("fsdp"),
            P("fsdp"),
            P("fsdp", None),
            P("fsdp"),
            P("fsdp", None),
            P("fsdp"),
            P("fsdp"),
            P("fsdp"),
            P("fsdp", None),
            P("fsdp"),
            P("fsdp", None),
            P("fsdp"),
        ),
        check_vma=False,
    )
```

profile of v0, /device:TPU:0, one launch (start us, length us, event | category | flops | bytes accessed | tf_op | source)
XLA Modules:
  0.0 931.8 jit_solution(6520395576070504783)
XLA Ops:
  15.3 6.2 all-gather
  21.5 5.4 all-gather.1
  26.9 5.2 all-gather.3
  32.6 5.2 all-gather.4
  38.3 5.2 all-gather.5
  44.7 5.1 all-gather.2
  49.9 5.2 all-gather.6
  55.7 9.4 %all_gather.48 = bf16[512,512]{1,0:T(8,128)(2,1)} all-gather(bf16[128,512]{1,0:T(8,128)(2,1)} %param.25), channel_id=1, replica_groups=mesh['ctx'=8,'fsdp'=4] {'fsdp'}, dimensions={0}, use_global_device_ids=true | all-gather | bytes 655360 | tf_op jit(solution)/shard_map/all_gather | solution.py:198
  73.5 30.8 %all_gather.47 = bf16[64,512]{1,0:T(8,128)(2,1)S(1)} all-gather(bf16[8,512]{1,0:T(8,128)(2,1)S(1)} %get-tuple-element.427), channel_id=1, replica_groups=mesh['ctx'=8,'fsdp'=4] {'ctx'}, dimensions={0}, use_global_device_ids=true | all-gather | bytes 73728 | tf_op jit(solution)/shard_map/all_gather | solution.py:228
  104.4 31.0 %all_gather.46 = bf16[64,512]{1,0:T(8,128)(2,1)S(1)} all-gather(bf16[8,512]{1,0:T(8,128)(2,1)S(1)} %get-tuple-element.428), channel_id=1, replica_groups=mesh['ctx'=8,'fsdp'=4] {'ctx'}, dimensions={0}, use_global_device_ids=true | all-gather | bytes 73728 | tf_op jit(solution)/shard_map/all_gather | solution.py:227
  137.1 4.7 copy.170
  141.9 44.0 %while.27 = (s32[]{:T(128)}, bf16[2,512,512]{2,1,0:T(8,128)(2,1)}, f32[2,8,512]{2,1,0:T(8,128)}, bf16[2,512,1536]{1,2,0:T(8,128)(2,1)}, s32[1,64]{1,0:T(1,128)},...) while((s32[]{:T(128)}, bf16[2,512,512]{2,1,0:T(8,128)(2,1)}, ...), condition=%wide.region_10.11_spmd, body=%wide.region_5.10_spmd.sunk | while | flops 210399296 | bytes 41084656 | solution.py:242
  190.6 4.3 fusion.72
  198.2 5.2 fusion.57
  203.5 10.7 %convert_reduce_fusion = (f32[2048]{0:T(1024)}, bf16[1024,2048]{1,0:T(8,128)(2,1)S(1)}) fusion(f32[1024,2048]{1,0:T(8,128)} %copy-done.68, f32[2048]{0:T(1024)} %bitcast.396, bf16[2048,512]{1,0:T(8,128)(2,1)} %all-gather.16.cloned.1.call-done, bf16[1,1024,512]{2,1,0:T(8,128)(2,1)S(1)} %copy-done.32), kind=kOutput, calls=%fused_computation.100 | convolution fusion | flops 2195716096 | bytes 15745024 | tf_op jit(solution)/shard_map/rd,fd->rf/dot_general | solution.py:273
  214.2 4.5 fusion.71
  218.8 4.3 fusion.81
  232.9 67.2 %while.28 = (s32[]{:T(128)}, f32[64,8,64]{0,2,1:T(8,128)}, f32[64,8,64]{0,2,1:T(8,128)S(1)}, f32[2,512,1536]{2,1,0:T(8,128)}, bf16[2,512,1536]{1,2,0:T(8,128)(2,...) while((s32[]{:T(128)}, f32[64,8,64]{0,2,1:T(8,128)}, ...), condition=%wide.region_18.19_spmd.clone, body=%wide.region_15.18_spmd.clone.sunk | while | flops 513065024 | bytes 94643328 | solution.py:298
  241.5 3.5 reshape.579
  262.7 3.9 constant_dynamic-update-slice_fusion.5
  274.9 3.5 reshape.579
  296.1 3.9 constant_dynamic-update-slice_fusion.5
  302.4 5.5 all-to-all-start
  311.7 3.6 all-to-all-done
  319.4 3.6 fusion.60
  333.1 470.7 %all-reduce.11 = (bf16[512]{0:T(512)(128)(2,1)S(1)}, bf16[512]{0:T(512)(128)(2,1)S(1)}, bf16[512,1536]{1,0:T(8,128)(2,1)}, bf16[1536]{0:T(1024)(128)(2,1)S(1)}, ...) all-reduce(f32[512]{0:T(512)S(1)} %get-tuple-element.333, ...), channel_id=1, replica_groups=mesh['ctx'=8,'fsdp'=4] {'ctx'}, use_global_device_ids=true, to_apply=%region_23.24 | all-reduce | flops 3152384 | bytes 18914304 | tf_op jit(solution)/shard_map/psum | solution.py:346
  808.3 5.3 all-gather.7
  813.7 7.7 fusion.55
  825.2 10.6 %all-reduce.9 = (bf16[512]{0:T(512)(128)(2,1)S(1)}, bf16[512]{0:T(512)(128)(2,1)S(1)}, bf16[1536]{0:T(1024)(128)(2,1)S(1)}, bf16[512]{0:T(512)(128)(2,1)S(1)}, b...) all-reduce(bf16[512]{0:T(512)(128)(2,1)S(1)} %get-tuple-element.381, ...), channel_id=2, replica_groups=mesh['ctx'=8,'fsdp'=4] {'fsdp'}, use_global_device_ids=true, to_apply=%region_24.25.clone | all-reduce | flops 6656 | bytes 26624
  840.5 13.9 %reduce-scatter.5.cloned.1.call-done = bf16[128,1536]{1,0:T(8,128)(2,1)} async-done(((bf16[512,1536]{1,0:T(8,128)(2,1)}), bf16[128,1536]{1,0:T(8,128)(2,1)}) %reduce-scatter.5.cloned.1.call-update) | async-done | bytes 393232 | tf_op jit(solution)/shard_map/reduce_scatter | solution.py:383
  856.3 31.9 %reduce-scatter.11.cloned.1.call-done = bf16[512,512]{1,0:T(8,128)(2,1)} async-done(((bf16[2048,512]{1,0:T(8,128)(2,1)}), bf16[512,512]{1,0:T(8,128)(2,1)}) %reduce-scatter.11.cloned.1.call-update) | async-done | bytes 524304 | tf_op jit(solution)/shard_map/reduce_scatter | solution.py:407
  890.3 32.0 %reduce-scatter.9.cloned.1.call-done = bf16[128,2048]{1,0:T(8,128)(2,1)} async-done(((bf16[512,2048]{1,0:T(8,128)(2,1)}), bf16[128,2048]{1,0:T(8,128)(2,1)}) %reduce-scatter.9.cloned.1.call-update) | async-done | bytes 524304 | tf_op jit(solution)/shard_map/reduce_scatter | solution.py:401
  (410 shorter events, 169.0 us)
Async XLA Ops:
  7.2 57.9 %copy-start.30 = (bf16[1,1024,512]{2,1,0:T(8,128)(2,1)S(1)}, bf16[1,1024,512]{2,1,0:T(8,128)(2,1)}, u32[]{:S(2)}) copy-start(bf16[1,1024,512]{2,1,0:T(8,128)(2,1)} %param.20) | copy-start | bytes 3145732
  7.2 60.8 %all-gather.12.cloned.1.call-start = ((), (), s32[]{:S(2)}) async-start(), calls=%async_computation.5 | async-start | bytes 1966080 | tf_op jit(solution)/shard_map/all_gather | solution.py:196
  7.9 182.4 %all-gather.14.cloned.1.call-start = ((), (), s32[]{:S(2)}) async-start(), calls=%async_computation.6 | async-start | bytes 2621440 | tf_op jit(solution)/shard_map/all_gather | solution.py:247
  8.7 194.8 %all-gather.16.cloned.1.call-start = ((), (), s32[]{:S(2)}) async-start(), calls=%async_computation.7 | async-start | bytes 2621440 | tf_op jit(solution)/shard_map/all_gather | solution.py:249
  21.5 46.5 %copy-start.45 = (f32[4,1,128]{2,1,0:T(1,128)}, f32[4,1,128]{2,1,0:T(1,128)S(1)}, u32[]{:S(2)}) copy-start(f32[4,1,128]{2,1,0:T(1,128)S(1)} %convert_element_type.250) | copy-start | bytes 6148
  26.9 41.1 %copy-start.60 = (f32[4,1,128]{2,1,0:T(1,128)}, f32[4,1,128]{2,1,0:T(1,128)S(1)}, u32[]{:S(2)}) copy-start(f32[4,1,128]{2,1,0:T(1,128)S(1)} %convert_element_type.251) | copy-start | bytes 6148
  65.9 5.6 copy-start.37
  66.2 5.3 copy-start.43
  66.7 4.8 copy-start.39
  104.4 37.5 %copy-start.27 = (bf16[64,8,64]{2,1,0:T(8,128)(2,1)}, bf16[64,8,64]{2,1,0:T(8,128)(2,1)S(1)}, u32[]{:S(2)}) copy-start(bf16[64,8,64]{2,1,0:T(8,128)(2,1)S(1)} %reshape.522) | copy-start | bytes 196612
  141.9 4.7 copy-start.47
  141.9 4.7 copy-start.50
  163.9 4.7 copy-start.47
  163.9 4.7 copy-start.50
  185.9 4.1 copy-start.49
  185.9 4.1 copy-start.52
  190.0 38.9 %copy-start.8 = (f32[1024,512]{0,1:T(8,128)}, f32[1024,512]{0,1:T(8,128)S(1)}, u32[]{:S(2)}) copy-start(f32[1024,512]{0,1:T(8,128)S(1)} %get-tuple-element.432) | copy-start | bytes 6291460
  190.6 7.6 copy-start.32
  190.6 7.6 copy-start.57
  203.5 10.7 %copy-start.62 = (f32[4,1,128]{2,1,0:T(1,128)S(1)}, f32[4,1,128]{2,1,0:T(1,128)}, u32[]{:S(2)}) copy-start(f32[4,1,128]{2,1,0:T(1,128)} %convert_element_type.255) | copy-start | bytes 6148
  214.2 4.5 copy-start.64
  233.1 4.4 copy-start.19
  266.6 4.4 copy-start.19
  300.0 8.2 copy-start.29
  300.0 8.2 copy-start.66
  302.4 12.8 %all-to-all-start = ((bf16[8,8,1024]{2,1,0:T(8,128)(2,1)}), bf16[8,8,1024]{2,1,0:T(8,128)(2,1)S(1)}, u32[]{:S(2)}, u32[]{:S(2)}) async-start(bf16[8,8,1024]{2,1,0:T(8,128)(2,1)} %pad_maximum_fusion.3), calls=%async_computation | async-start | bytes 262144 | tf_op jit(solution)/shard_map/all_to_all | solution.py:23
  307.9 530.9 %reduce-scatter.7.cloned.1.call-start = ((), (), s32[]{:S(2)}) async-start(), calls=%async_computation.9 | async-start | bytes 655360 | tf_op jit(solution)/shard_map/reduce_scatter | solution.py:389
  803.9 50.5 %reduce-scatter.5.cloned.1.call-start = ((), (), s32[]{:S(2)}) async-start(), calls=%async_computation.8 | async-start | bytes 1966080 | tf_op jit(solution)/shard_map/reduce_scatter | solution.py:383
  804.4 83.7 %reduce-scatter.11.cloned.1.call-start = ((), (), s32[]{:S(2)}) async-start(), calls=%async_computation.11 | async-start | bytes 2621440 | tf_op jit(solution)/shard_map/reduce_scatter | solution.py:407
  804.5 9.2 copy-start.9
  804.5 9.1 copy-start.58
  805.0 117.3 %reduce-scatter.9.cloned.1.call-start = ((), (), s32[]{:S(2)}) async-start(), calls=%async_computation.10 | async-start | bytes 2621440 | tf_op jit(solution)/shard_map/reduce_scatter | solution.py:401
  (67 other events, 111.9 us)
Sparse Core Ops, SparseCore 0:
  9.6 22.3 all-gather.11
  33.5 22.6 all-gather.13
  57.8 22.5 all-gather.15
  804.0 19.5 reduce-scatter.6
  826.1 28.1 reduce-scatter.4
  856.7 31.4 reduce-scatter.10
  890.9 31.4 reduce-scatter.8
where the time goes:
time: 938 us; the launch traced here: 932 us
  blocking collectives  595 us (63%)
  local copies, waits for them, and re-layouts  95.4 us (10%)
  waiting for transfers between devices  85.1 us (9%)
  matrix products  76.5 us (8%)
  other arithmetic  52.7 us (6%)
  between operations  19.8 us (2%)
    psum x1, blocking collectives, local(): lax.psum((grad_gain_one, grad_shift_one, grad_qkv, grad_qkv_bias, grad_ou...  471 us
    reduce_scatter x1, waiting for transfers between devices, local(): lax.psum_scatter(sum_up.astype(jnp.bfloat16), 'fsdp', scatter_dimension=0...  32 us
    reduce_scatter x1, waiting for transfers between devices, local(): lax.psum_scatter(sum_down.astype(jnp.bfloat16), 'fsdp', scatter_dimension...  31.9 us
    all_gather x1, blocking collectives, local(): lax.all_gather(own_keys, 'ctx', axis=0, tiled=True)  31 us
    all_gather x1, blocking collectives, local(): lax.all_gather(own_values, 'ctx', axis=0, tiled=True)  30.8 us
  transfers between devices with their start and end apart: 8, of which 4 were waited for; matrix products, arithmetic and copies ran while one was open for 11% of the time, Pallas kernels for 0%

commit v1 on v0

v1 whole, which is shorter than its diff:
```python
import functools

import jax
import jax.numpy as jnp
from jax import lax
from jax.experimental import pallas as pl
from jax.experimental.pallas import tpu as pltpu
from jax.sharding import PartitionSpec as P

D = 512
HEADS = 8
HEAD = 64
SPAN = 128
LANE = 128
PAIRS = D // LANE
ROWS = 256
EPSILON = 1e-05
MASKED = -1e30
SCALE = HEAD**-0.5
INV_ROOT = SPAN**-0.5
F32 = jnp.float32
BF16 = jnp.bfloat16
VMEM_LIMIT = 56 * 1024 * 1024

G1, S1, OB, G2, S2, DB, QB, UB = range(8)
SC_F, SC_SLOT, SC_LEN = 0, 1, 2


def dot(a, b):
    return lax.dot_general(a, b, (((1,), (0,)), ((), ())), preferred_element_type=F32)


def dot_bt(a, b):
    return lax.dot_general(a, b, (((1,), (1,)), ((), ())), preferred_element_type=F32)


def dot_at(a, b):
    return lax.dot_general(a, b, (((0,), (0,)), ((), ())), preferred_element_type=F32)


def normalize(values):
    centre = values - jnp.mean(values, axis=-1, keepdims=True)
    spread = jnp.mean(centre * centre, axis=-1, keepdims=True)
    rstd = lax.rsqrt(spread + EPSILON)
    return centre * rstd, rstd


def norm_back(e, n, rstd):
    return rstd * (
        e - jnp.mean(e, axis=-1, keepdims=True) - n * jnp.mean(e * n, axis=-1, keepdims=True)
    )


def params(steps, semantics=True):
    return pltpu.CompilerParams(
        dimension_semantics=("arbitrary",), vmem_limit_bytes=VMEM_LIMIT
    )


def full(shape):
    return pl.BlockSpec(shape, lambda i, *_: (0,) * len(shape))


def rows_of(shape):
    return pl.BlockSpec(shape, lambda i, *_: (i,) + (0,) * (len(shape) - 1))


def sums_kernel(x_ref, o_ref):
    spans = x_ref.shape[0] // SPAN
    sums = []
    for s in range(spans):
        n, _ = normalize(x_ref[s * SPAN : (s + 1) * SPAN, :].astype(F32))
        sums.append(jnp.sum(n, axis=0, keepdims=True))
    table = jnp.concatenate(sums, axis=0)
    for k in range(o_ref.shape[0]):
        o_ref[k] = table


def span_sums(x, copies):
    spans = x.shape[0] // SPAN
    return pl.pallas_call(
        sums_kernel,
        out_shape=jax.ShapeDtypeStruct((copies, spans, D), F32),
        compiler_params=pltpu.CompilerParams(vmem_limit_bytes=VMEM_LIMIT),
        name="span_sums",
    )(x)


def attend_kernel(
    sc, x_ref, order_ref, nsum_ref, *refs, nf, seqs
):
    qkv_refs, out_refs, small_refs = refs[:nf], refs[nf : 2 * nf], refs[2 * nf : 3 * nf]
    (packed_ref, p_ref, att_ref, r1_ref, h1_ref, h2_ref, wqkv, wout, vec, tabs) = refs[3 * nf :]
    i = pl.program_id(0)
    nspan = nsum_ref.shape[0]
    block = D // nf

    @pl.when(i == 0)
    def _():
        vec[...] = jnp.zeros_like(vec)
        for q in range(nf):
            fq = sc[SC_F] ^ q
            at = pl.ds(pl.multiple_of(fq * block, block), block)
            wqkv[at, :] = qkv_refs[q][...]
            wout[at, :] = out_refs[q][...]
            sm = small_refs[q][...].astype(F32)
            for row, src in ((G1, 0), (S1, 1), (OB, 5), (G2, 6), (S2, 7), (DB, 12)):
                vec[row : row + 1, at] = sm[src : src + 1]
            for t in range(3):
                at3 = pl.ds(pl.multiple_of(fq * 3 * block + t * block, block), block)
                vec[QB : QB + 1, at3] = sm[2 + t : 3 + t]
            for t in range(4):
                at4 = pl.ds(pl.multiple_of(fq * 4 * block + t * block, block), block)
                vec[UB : UB + 1, at4] = sm[8 + t : 9 + t]
        hs = nsum_ref[...] * vec[G1 : G1 + 1, :D] + SPAN * vec[S1 : S1 + 1, :D]
        hi = hs.astype(BF16)
        lo = (hs - hi.astype(F32)).astype(BF16)
        wkv = wqkv[:, D:]
        t = dot(hi, wkv) + dot(lo, wkv) + SPAN * vec[QB : QB + 1, D : 3 * D]
        tabs[...] = (t * INV_ROOT).astype(BF16)

    x = x_ref[...].astype(F32)
    n1, _ = normalize(x)
    h1 = (n1 * vec[G1 : G1 + 1, :D] + vec[S1 : S1 + 1, :D]).astype(BF16)
    h1_ref[...] = h1
    packed_ref[...] = (dot(h1, wqkv[...]) + vec[QB : QB + 1, : 3 * D]).astype(BF16)

    lane = lax.broadcasted_iota(jnp.int32, (SPAN, LANE), 1)
    low = lane < HEAD
    causal = jnp.where(
        lane <= lax.broadcasted_iota(jnp.int32, (SPAN, LANE), 0), 0.0, MASKED
    ).astype(F32)
    order = order_ref[...]
    prompt = lax.div(sc[SC_LEN], SPAN)
    spans = ROWS // SPAN
    for s in range(spans):
        a = sc[SC_LEN + seqs + sc[SC_SLOT] + i * spans + s]
        start, begin = 0, 0
        for k in range(seqs):
            begin = jnp.where(start <= a, start, begin)
            start = start + lax.div(sc[SC_LEN + k], SPAN)
        seen = (order < a) & ((order >= begin) | (order < prompt))
        far = jnp.where(seen, 0.0, MASKED).astype(F32)
        bias = jnp.concatenate([causal, jnp.broadcast_to(far, (SPAN, nspan))], axis=1)
        bias = jnp.concatenate([bias, bias], axis=0)
        at = slice(s * SPAN, (s + 1) * SPAN)
        for p in range(PAIRS):
            cols = slice(p * LANE, (p + 1) * LANE)
            q = packed_ref[at, cols] * SCALE
            k = packed_ref[at, D + p * LANE : D + (p + 1) * LANE]
            v = packed_ref[at, 2 * D + p * LANE : 2 * D + (p + 1) * LANE]
            zero = jnp.zeros_like(q)
            q2 = jnp.concatenate([jnp.where(low, q, zero), jnp.where(low, zero, q)], axis=0)
            kc = jnp.concatenate([k, tabs[:, cols]], axis=0)
            vc = jnp.concatenate([v, tabs[:, D + p * LANE : D + (p + 1) * LANE]], axis=0)
            scores = dot_bt(q2, kc) + bias
            peak = jnp.max(scores, axis=1, keepdims=True)
            e = jnp.exp(scores - peak)
            w = (e * (1.0 / jnp.sum(e, axis=1, keepdims=True))).astype(BF16)
            p_ref[s * PAIRS + p] = w
            o2 = dot(w, vc)
            att_ref[at, cols] = jnp.where(low, o2[:SPAN], o2[SPAN:]).astype(BF16)

    r1 = x + (dot(att_ref[...], wout[...]) + vec[OB : OB + 1, :D])
    r1_ref[...] = r1
    n2, _ = normalize(r1)
    h2_ref[...] = (n2 * vec[G2 : G2 + 1, :D] + vec[S2 : S2 + 1, :D]).astype(BF16)


def attend(sc, x, order, nsum, qkv, out, small, seqs):
    nf = len(qkv)
    rows = x.shape[0]
    nspan = nsum.shape[0]
    keys = SPAN + nspan
    per = ROWS // SPAN * PAIRS
    return pl.pallas_call(
        functools.partial(attend_kernel, nf=nf, seqs=seqs),
        grid_spec=pltpu.PrefetchScalarGridSpec(
            num_scalar_prefetch=1,
            grid=(rows // ROWS,),
            in_specs=[rows_of((ROWS, D)), full((1, nspan)), full((nspan, D))]
            + [full(a.shape) for a in (*qkv, *out, *small)],
            out_specs=[
                rows_of((ROWS, 3 * D)),
                rows_of((per, 2 * SPAN, keys)),
                rows_of((ROWS, D)),
                rows_of((ROWS, D)),
                rows_of((ROWS, D)),
                rows_of((ROWS, D)),
                full((D, 3 * D)),
                full((D, D)),
                full((8, 4 * D)),
                full((nspan, 2 * D)),
            ],
        ),
        out_shape=[
            jax.ShapeDtypeStruct((rows, 3 * D), BF16),
            jax.ShapeDtypeStruct((rows // SPAN * PAIRS, 2 * SPAN, keys), BF16),
            jax.ShapeDtypeStruct((rows, D), BF16),
            jax.ShapeDtypeStruct((rows, D), F32),
            jax.ShapeDtypeStruct((rows, D), BF16),
            jax.ShapeDtypeStruct((rows, D), BF16),
            jax.ShapeDtypeStruct((D, 3 * D), BF16),
            jax.ShapeDtypeStruct((D, D), BF16),
            jax.ShapeDtypeStruct((8, 4 * D), F32),
            jax.ShapeDtypeStruct((nspan, 2 * D), BF16),
        ],
        compiler_params=params(1),
        name="attend",
    )(sc, x, order, nsum, *qkv, *out, *small)


def relative(step, nf):
    half = nf // 2
    return jnp.where(step < half, 2 * step + 1, 2 * (step - half))


def up_kernel(sc, h2_ref, c_ref, vec_ref, *refs, nf):
    up_refs = refs[:nf]
    g_ref, gp_ref, w_ref, send_ref, keep_ref = refs[nf:]
    s = pl.program_id(0)
    f = sc[SC_F] ^ relative(s, nf)
    block = D // nf
    for q in range(nf):
        at = pl.ds(pl.multiple_of((sc[SC_F] ^ q) * block, block), block)
        w_ref[at, :] = up_refs[q][...]
    width = w_ref.shape[1]
    bias = vec_ref[UB : UB + 1, pl.ds(pl.multiple_of(f * width, width), width)]
    w = w_ref[...]
    k0 = 0.7978845608028654
    for r in range(0, h2_ref.shape[0], ROWS):
        u = dot(h2_ref[r : r + ROWS, :], w) + bias
        u2 = u * u
        t = jnp.tanh(u * (k0 + (k0 * 0.044715) * u2))
        half = 0.5 + 0.5 * t
        g_ref[r : r + ROWS, :] = (u * half).astype(BF16)
        slope = u * (k0 + (3 * k0 * 0.044715) * u2)
        gp_ref[r : r + ROWS, :] = (half + (0.5 - 0.5 * t * t) * slope).astype(BF16)
    grad = dot_at(g_ref[...], c_ref[...]).astype(BF16)

    def store(ref):
        for j in range(D // LANE):
            ref[0, j * width : (j + 1) * width, :] = grad[:, j * LANE : (j + 1) * LANE]

    @pl.when(s < nf // 2)
    def _():
        store(send_ref)

    @pl.when(s >= nf // 2)
    def _():
        store(keep_ref)


def ffn_up(sc, h2, c, vec, up):
    nf = len(up)
    rows = h2.shape[0]
    ff = up[0].shape[1]
    width = ff // nf
    half = nf // 2
    at = lambda s, sc: (0, sc[SC_F] ^ relative(s, nf))
    piece = width * D // LANE
    return pl.pallas_call(
        functools.partial(up_kernel, nf=nf),
        grid_spec=pltpu.PrefetchScalarGridSpec(
            num_scalar_prefetch=1,
            grid=(nf,),
            in_specs=[full((rows, D)), full((rows, D)), full(vec.shape)]
            + [pl.BlockSpec((D // nf, width), at) for _ in up],
            out_specs=[
                pl.BlockSpec((rows, width), at),
                pl.BlockSpec((rows, width), at),
                pl.BlockSpec((D, width), at),
                pl.BlockSpec((1, piece, LANE), lambda s, sc: (jnp.minimum(s, half - 1), 0, 0)),
                pl.BlockSpec((1, piece, LANE), lambda s, sc: (jnp.maximum(s - half, 0), 0, 0)),
            ],
        ),
        out_shape=[
            jax.ShapeDtypeStruct((rows, ff), BF16),
            jax.ShapeDtypeStruct((rows, ff), BF16),
            jax.ShapeDtypeStruct((D, ff), BF16),
            jax.ShapeDtypeStruct((half, piece, LANE), BF16),
            jax.ShapeDtypeStruct((half, piece, LANE), BF16),
        ],
        compiler_params=params(1),
        name="ffn_up",
    )(sc, h2, c, vec, *up)


def down_kernel(sc, h2_ref, c_ref, gp_ref, w_ref, *refs, nf):
    down_refs = refs[:nf]
    dh2_ref, dub_ref, wd_ref, send_ref, keep_ref, du_ref, grad_ref = refs[nf:]
    s = pl.program_id(0)
    for q in range(nf):

        @pl.when(s == q)
        def _():
            wd_ref[...] = down_refs[q][...]

    @pl.when(s == 0)
    def _():
        dh2_ref[...] = jnp.zeros_like(dh2_ref)

    wd = wd_ref[...]
    w = w_ref[...]
    total = jnp.zeros((1, w.shape[1]), F32)
    for r in range(0, h2_ref.shape[0], ROWS):
        at = slice(r, r + ROWS)
        dg = dot_bt(c_ref[at, :], wd)
        du = (dg * gp_ref[at, :].astype(F32)).astype(BF16)
        du_ref[at, :] = du
        total = total + jnp.sum(du.astype(F32), axis=0, keepdims=True)
        dh2_ref[at, :] += dot_bt(du, w)
    dub_ref[...] = total
    grad_ref[...] = dot_at(h2_ref[...], du_ref[...])
    block = D // nf
    for q in range(nf):
        ref = send_ref if q % 2 else keep_ref
        piece = grad_ref[pl.ds(pl.multiple_of((sc[SC_F] ^ q) * block, block), block), :]
        piece = piece.astype(BF16)
        for j in range(w.shape[1] // LANE):
            ref[q // 2, j * block : (j + 1) * block, :] = piece[:, j * LANE : (j + 1) * LANE]


def ffn_down(sc, h2, c, gp, w, down):
    nf = len(down)
    rows = h2.shape[0]
    ff = w.shape[1]
    width = ff // nf
    half = nf // 2
    block = D // nf
    part = width // LANE * block
    cols = lambda s, sc: (0, sc[SC_F] ^ s)
    return pl.pallas_call(
        functools.partial(down_kernel, nf=nf),
        grid_spec=pltpu.PrefetchScalarGridSpec(
            num_scalar_prefetch=1,
            grid=(nf,),
            in_specs=[
                full((rows, D)),
                full((rows, D)),
                pl.BlockSpec((rows, width), cols),
                pl.BlockSpec((D, width), cols),
            ]
            + [full(a.shape) for a in down],
            out_specs=[
                full((rows, D)),
                pl.BlockSpec((1, width), cols),
                pl.BlockSpec((width, D), lambda s, sc: (sc[SC_F] ^ s, 0)),
                pl.BlockSpec((half, part, LANE), lambda s, sc: (0, sc[SC_F] ^ s, 0)),
                pl.BlockSpec((half, part, LANE), lambda s, sc: (0, sc[SC_F] ^ s, 0)),
            ],
            scratch_shapes=[pltpu.VMEM((rows, width), BF16), pltpu.VMEM((D, width), F32)],
        ),
        out_shape=[
            jax.ShapeDtypeStruct((rows, D), F32),
            jax.ShapeDtypeStruct((1, ff), F32),
            jax.ShapeDtypeStruct((ff, D), BF16),
            jax.ShapeDtypeStruct((half, part * nf, LANE), BF16),
            jax.ShapeDtypeStruct((half, part * nf, LANE), BF16),
        ],
        compiler_params=params(1),
        name="ffn_down",
    )(sc, h2, c, gp, w, *down)


def back_kernel(
    sc, x_ref, c_ref, dh2_ref, r1_ref, att_ref, h1_ref, packed_ref, p_ref,
    tabs, wqkv, wout, vec, nsum_ref, dub_ref,
    dr1_ref, dh1_ref, dspan_ref, send_ref, keep_ref,
    acc_qkv, acc_out, acc_span, accv, dp_ref, *, nf
):
    i = pl.program_id(0)
    last = pl.num_programs(0) - 1

    @pl.when(i == 0)
    def _():
        for ref in (acc_qkv, acc_out, acc_span, accv):
            ref[...] = jnp.zeros_like(ref)

    def add(row, values):
        accv[row : row + 1, : values.shape[1]] += jnp.sum(values, axis=0, keepdims=True)

    c = c_ref[...].astype(F32)
    dh2 = dh2_ref[...]
    n2, rstd2 = normalize(r1_ref[...])
    add(G2, dh2 * n2)
    add(S2, dh2)
    add(DB, c)
    dr1 = c + norm_back(dh2 * vec[G2 : G2 + 1, :D], n2, rstd2)
    dr1_ref[...] = dr1
    dy = dr1.astype(BF16)
    add(OB, dy.astype(F32))
    att = att_ref[...]
    acc_out[...] += dot_at(att, dy)
    da = dot_bt(dy, wout[...]).astype(BF16)

    low = lax.broadcasted_iota(jnp.int32, (SPAN, LANE), 1) < HEAD
    for s in range(ROWS // SPAN):
        at = slice(s * SPAN, (s + 1) * SPAN)
        for p in range(PAIRS):
            cq, ck, cv = (slice(t * D + p * LANE, t * D + (p + 1) * LANE) for t in range(3))
            cp = slice(D + p * LANE, D + (p + 1) * LANE)
            q = packed_ref[at, cq] * SCALE
            do = da[at, cq]
            zero = jnp.zeros_like(q)
            q2 = jnp.concatenate([jnp.where(low, q, zero), jnp.where(low, zero, q)], axis=0)
            do2 = jnp.concatenate([jnp.where(low, do, zero), jnp.where(low, zero, do)], axis=0)
            kc = jnp.concatenate([packed_ref[at, ck], tabs[:, cq]], axis=0)
            vc = jnp.concatenate([packed_ref[at, cv], tabs[:, cp]], axis=0)
            w = p_ref[s * PAIRS + p]
            wf = w.astype(F32)
            dp = dot_bt(do2, vc)
            delta = jnp.sum(wf * dp, axis=1, keepdims=True)
            ds = (wf * (dp - delta)).astype(BF16)
            dq2 = dot(ds, kc)
            dq = jnp.where(low, dq2[:SPAN], dq2[SPAN:]) * SCALE
            dk = dot_at(ds, q2)
            dv = dot_at(w, do2)
            acc_span[:, cq] += dk[SPAN:]
            acc_span[:, cp] += dv[SPAN:]
            dp_ref[at, cq] = dq.astype(BF16)
            dp_ref[at, ck] = dk[:SPAN].astype(BF16)
            dp_ref[at, cv] = dv[:SPAN].astype(BF16)
    dpk = dp_ref[...]
    add(QB, dpk.astype(F32))
    acc_qkv[...] += dot_at(h1_ref[...], dpk)
    dh1 = dot_bt(dpk, wqkv[...])
    dh1_ref[...] = dh1
    n1, _ = normalize(x_ref[...].astype(F32))
    add(G1, dh1 * n1)
    add(S1, dh1)

    @pl.when(i == last)
    def _():
        span = acc_span[...]
        copies, own = dspan_ref.shape[0], dspan_ref.shape[1]
        for k in range(copies):
            dspan_ref[k] = span[k * own : (k + 1) * own].astype(BF16)
        span = span * INV_ROOT
        low_span = span.astype(BF16)
        nsum = nsum_ref[...]
        hs = (nsum * vec[G1 : G1 + 1, :D] + SPAN * vec[S1 : S1 + 1, :D]).astype(BF16)
        acc_qkv[:, D:] += dot_at(hs, low_span)
        accv[QB : QB + 1, D : 3 * D] += SPAN * jnp.sum(span, axis=0, keepdims=True)
        de = dot_bt(low_span, wqkv[:, D:])
        add(G1, de * nsum)
        accv[S1 : S1 + 1, :D] += SPAN * jnp.sum(de, axis=0, keepdims=True)
        block = D // nf
        for q in range(nf):
            ref = send_ref if q % 2 else keep_ref
            fq = sc[SC_F] ^ q
            at = pl.ds(pl.multiple_of(fq * block, block), block)
            piece = acc_qkv[at, :].astype(BF16)
            for j in range(3 * D // LANE):
                ref[q // 2, j * block : (j + 1) * block, :] = piece[:, j * LANE : (j + 1) * LANE]
            base = 3 * D // LANE * block
            piece = acc_out[at, :].astype(BF16)
            for j in range(D // LANE):
                ref[q // 2, base + j * block : base + (j + 1) * block, :] = piece[
                    :, j * LANE : (j + 1) * LANE
                ]
            base += D // LANE * block
            three = [
                accv[QB : QB + 1, pl.ds(pl.multiple_of(fq * 3 * block + t * block, block), block)]
                for t in range(3)
            ]
            four = [
                dub_ref[0:1, pl.ds(pl.multiple_of(fq * 4 * block + t * block, block), block)]
                for t in range(4)
            ]
            small = jnp.concatenate(
                [accv[G1 : G1 + 1, at], accv[S1 : S1 + 1, at]]
                + three
                + [accv[OB : OB + 1, at], accv[G2 : G2 + 1, at], accv[S2 : S2 + 1, at]]
                + four
                + [accv[DB : DB + 1, at], jnp.zeros((3, LANE), F32)],
                axis=0,
            ).astype(BF16)
            ref[q // 2, base : base + 16, :] = small
            ref[q // 2, base + 16 : base + block, :] = jnp.zeros((block - 16, LANE), BF16)


def back(sc, x, c, dh2, r1, att, h1, packed, p, tabs, wqkv, wout, vec, nsum, dub, nf, copies):
    rows = x.shape[0]
    nspan = nsum.shape[0]
    per = ROWS // SPAN * PAIRS
    half = nf // 2
    piece = (4 * D // LANE + 1) * (D // nf)
    return pl.pallas_call(
        functools.partial(back_kernel, nf=nf),
        grid_spec=pltpu.PrefetchScalarGridSpec(
            num_scalar_prefetch=1,
            grid=(rows // ROWS,),
            in_specs=[rows_of((ROWS, D))] * 6
            + [rows_of((ROWS, 3 * D)), rows_of((per,) + p.shape[1:])]
            + [full(a.shape) for a in (tabs, wqkv, wout, vec, nsum, dub)],
            out_specs=[
                rows_of((ROWS, D)),
                rows_of((ROWS, D)),
                full((copies, nspan // copies, 2 * D)),
                full((half, piece, LANE)),
                full((half, piece, LANE)),
            ],
            scratch_shapes=[
                pltpu.VMEM((D, 3 * D), F32),
                pltpu.VMEM((D, D), F32),
                pltpu.VMEM((nspan, 2 * D), F32),
                pltpu.VMEM((8, 3 * D), F32),
                pltpu.VMEM((ROWS, 3 * D), BF16),
            ],
        ),
        out_shape=[
            jax.ShapeDtypeStruct((rows, D), F32),
            jax.ShapeDtypeStruct((rows, D), F32),
            jax.ShapeDtypeStruct((copies, nspan // copies, 2 * D), BF16),
            jax.ShapeDtypeStruct((half, piece, LANE), BF16),
            jax.ShapeDtypeStruct((half, piece, LANE), BF16),
        ],
        compiler_params=params(1),
        name="back",
    )(sc, x, c, dh2, r1, att, h1, packed, p, tabs, wqkv, wout, vec, nsum, dub)


def first_kernel(x_ref, dr1_ref, dh1_ref, got_ref, wqkv, vec, o_ref, e_ref):
    i = pl.program_id(0)

    @pl.when(i == 0)
    def _():
        total = jnp.sum(got_ref[...].astype(F32), axis=0) * INV_ROOT
        e_ref[...] = dot_bt(total.astype(BF16), wqkv[:, D:])

    n1, rstd1 = normalize(x_ref[...].astype(F32))
    spans = ROWS // SPAN
    extra = jnp.concatenate(
        [
            jnp.broadcast_to(e_ref[pl.ds(i * spans + s, 1), :], (SPAN, D))
            for s in range(spans)
        ],
        axis=0,
    )
    dh1 = dh1_ref[...] + extra
    o_ref[...] = dr1_ref[...] + norm_back(dh1 * vec[G1 : G1 + 1, :D], n1, rstd1)


def first_back(x, dr1, dh1, got, wqkv, vec):
    rows = x.shape[0]
    return pl.pallas_call(
        first_kernel,
        grid=(rows // ROWS,),
        in_specs=[rows_of((ROWS, D))] * 3 + [full(a.shape) for a in (got, wqkv, vec)],
        out_specs=rows_of((ROWS, D)),
        out_shape=jax.ShapeDtypeStruct((rows, D), F32),
        scratch_shapes=[pltpu.VMEM((rows // SPAN, D), F32)],
        compiler_params=params(1),
        name="first_back",
    )(x, dr1, dh1, got, wqkv, vec)


def mixed_kernel(r1_ref, g_ref, w_ref, vec, o_ref):
    o_ref[...] = (r1_ref[...] + dot(g_ref[...], w_ref[...]) + vec[DB : DB + 1, :D]).astype(BF16)


def block_output(r1, g, w, vec):
    rows = r1.shape[0]
    return pl.pallas_call(
        mixed_kernel,
        grid=(rows // ROWS,),
        in_specs=[rows_of((ROWS, D)), rows_of((ROWS, g.shape[1])), full(w.shape), full(vec.shape)],
        out_specs=rows_of((ROWS, D)),
        out_shape=jax.ShapeDtypeStruct((rows, D), BF16),
        compiler_params=params(1),
        name="block_output",
    )(r1, g, w, vec)


def swap(array, axis, bit):
    n = lax.axis_size(axis)
    return lax.ppermute(array, axis, [(k, k ^ bit) for k in range(n)])


def gathered(array, axis):
    n = lax.axis_size(axis)
    held = {0: array}
    bit = n // 2
    while bit:
        for r in sorted(held):
            held[r ^ bit] = swap(held[r], axis, bit)
        bit //= 2
    return [held[r] for r in range(n)]


def add_low(a, b):
    return (a.astype(F32) + b.astype(F32)).astype(BF16)


def to_owner(keep, send, axis):
    n = lax.axis_size(axis)
    bit = 1
    while True:
        keep = add_low(keep, swap(send, axis, bit))
        bit *= 2
        if bit == n:
            return keep[0]
        keep, send = keep[0::2], keep[1::2]


def over_all(piece, axis):
    n = lax.axis_size(axis)
    split = piece.reshape(n, piece.shape[0] // n, LANE)
    got = lax.all_to_all(split, axis, 0, 0, tiled=True)
    own = got.astype(F32).sum(axis=0).astype(BF16)
    wide = jnp.broadcast_to(own[None], (n,) + own.shape)
    return lax.all_to_all(wide, axis, 0, 0, tiled=True).reshape(piece.shape).astype(F32)


def unblocked(rows, height):
    blocks = rows.reshape(-1, height, LANE)
    return jnp.swapaxes(blocks, 0, 1).reshape(height, -1)


def local(
    tokens, ln1_gain, ln1_shift, qkv_weight, qkv_bias, out_weight, out_bias, ln2_gain, ln2_shift,
    up_weight, up_bias, down_weight, down_bias, seq_lengths, span_order, cotangent,
):
    nf = lax.axis_size("fsdp")
    nc = lax.axis_size("ctx")
    x, c = tokens[0], cotangent[0]
    spans = x.shape[0] // SPAN
    seqs = seq_lengths.shape[1]
    small = jnp.concatenate(
        [ln1_gain, ln1_shift, qkv_bias, out_bias, ln2_gain, ln2_shift, up_bias, down_bias]
    )
    small = jnp.pad(small, (0, 16 * LANE - small.shape[0])).reshape(16, LANE)
    scalars = jnp.concatenate(
        [
            lax.axis_index("fsdp").reshape(1),
            (lax.axis_index("ctx") * spans).reshape(1),
            seq_lengths[0],
            span_order[0],
        ]
    ).astype(jnp.int32)
    qkv = gathered(qkv_weight, "fsdp")
    smalls = gathered(small, "fsdp")
    out = gathered(out_weight, "fsdp")
    up = gathered(up_weight, "fsdp")
    down = gathered(down_weight, "fsdp")
    nsum = lax.all_to_all(span_sums(x, nc), "ctx", 0, 0, tiled=True).reshape(nc * spans, D)

    packed, p, att, r1, h1, h2, wqkv, wout, vec, tabs = attend(
        scalars, x, span_order, nsum, qkv, out, smalls, seqs
    )
    g, gp, wup, dsend, dkeep = ffn_up(scalars, h2, c, vec, up)
    dh2, dub, wdown, usend, ukeep = ffn_down(scalars, h2, c, gp, wup, down)
    dr1, dh1, dspan, bsend, bkeep = back(
        scalars, x, c, dh2, r1, att, h1, packed, p, tabs, wqkv, wout, vec, nsum, dub, nf, nc
    )
    got = lax.all_to_all(dspan, "ctx", 0, 0, tiled=True)
    tokens_grad = first_back(x, dr1, dh1, got, wqkv, vec)
    mixed = block_output(r1, g, wdown, vec)

    grad_down = unblocked(over_all(to_owner(dkeep, dsend, "fsdp"), "ctx"), down_weight.shape[0])
    grad_up = unblocked(over_all(to_owner(ukeep, usend, "fsdp"), "ctx"), D // nf)
    rest = over_all(to_owner(bkeep, bsend, "fsdp"), "ctx")
    block = D // nf
    at_out = 3 * D // LANE * block
    at_small = 4 * D // LANE * block
    grad_qkv = unblocked(rest[:at_out], block)
    grad_out = unblocked(rest[at_out:at_small], block)
    tail = rest[at_small : at_small + 16].reshape(-1)
    pieces, at = [], 0
    for width in (block, block, 3 * block, block, block, block, 4 * block, block):
        pieces.append(tail[at : at + width])
        at += width
    g1, s1, qb, ob, g2, s2, ub, db = pieces
    return (
        mixed[None], tokens_grad[None], g1, s1, grad_qkv, qb, grad_out, ob, g2, s2,
        grad_up, ub, grad_down, db,
    )


def solution(mesh):
    rows, one, two = P("fsdp", "ctx", None), P("fsdp"), P("fsdp", None)
    return jax.shard_map(
        local,
        mesh=mesh,
        in_specs=(
            rows, one, one, two, one, two, one, one, one, two, one, two, one, two, two, rows,
        ),
        out_specs=(rows, rows, one, one, two, one, two, one, one, one, two, one, two, one),
        check_vma=False,
    )
```

time: 938 us -> 264 us (0.28)
  blocking collectives: 595 us -> 0 us
  Pallas kernels: 0 us -> 84.1 us
  matrix products: 76.5 us -> 0 us
  local copies, waits for them, and re-layouts: 95.4 us -> 21.2 us
  other arithmetic: 52.7 us -> 8.04 us
  starting transfers between devices: 6.02 us -> 45 us
  waiting for transfers between devices: 85.1 us -> 104 us
  between operations: 19.8 us -> 0.94 us
    psum x1 -> x0, blocking collectives: 471 us -> none  [local(): lax.psum((grad_gain_one, grad_shift_one, grad_qkv, grad_qkv_bias, grad_ou...]
    all_gather x11 -> x0, blocking collectives: 114 us -> none  [the longest x1 31 us: local(): lax.all_gather(own_keys, 'ctx', axis=0, tiled=True)]
    pallas_call x0 -> x7, Pallas kernels: none -> 84.1 us  [the longest x1 26.7 us: back(): pl.pallas_call(functools.partial(back_kernel, nf=nf), grid_spec=pltpu.Pre...]
    reduce_scatter x4 -> x0, waiting for transfers between devices: 77.8 us -> none  [the longest x1 32 us: local(): lax.psum_scatter(sum_up.astype(jnp.bfloat16), 'fsdp', scatter_dimension=0...]
    dot_general x40 -> x0, matrix products: 76.5 us -> none  [the longest x1 10.7 us: local(): jnp.einsum('rd,fd->rf', upstream, weight_down, preferred_element_type=jnp...]
    all_to_all x1 -> x8, waiting for transfers between devices: 3.57 us -> 71.2 us  [the longest x3 36 us: over_all(): got = lax.all_to_all(split, axis, 0, 0, tiled=True)]
    ppermute x0 -> x21, waiting for transfers between devices: none -> 32.4 us  [swap(): return lax.ppermute(array, axis, [(k, k ^ bit) for k in range(n)])]
    all_to_all x1 -> x8, starting transfers between devices: 5.49 us -> 32.9 us  [the longest x3 12.8 us: over_all(): got = lax.all_to_all(split, axis, 0, 0, tiled=True)]
  transfers between devices with their start and end apart: 8 -> 29, of which waited for: 4 -> 13; matrix products, arithmetic and copies ran while one was open for 11% -> 7% of each run, Pallas kernels for 0% -> 32%
where the time goes in v1:
time: 264 us; the launch traced here: 263 us
  waiting for transfers between devices  104 us (39%)
  Pallas kernels  84.1 us (32%)
  starting transfers between devices  45 us (17%)
  local copies, waits for them, and re-layouts  21.2 us (8%)
  other arithmetic  8.04 us (3%)
    all_to_all x3, waiting for transfers between devices, over_all(): got = lax.all_to_all(split, axis, 0, 0, tiled=True)  36 us
    ppermute x21, waiting for transfers between devices, swap(): return lax.ppermute(array, axis, [(k, k ^ bit) for k in range(n)])  32.4 us
    all_to_all x3, waiting for transfers between devices, over_all(): lax.all_to_all(wide, axis, 0, 0, tiled=True).reshape(piece.shape)  29.2 us
    pallas_call x1, Pallas kernels, back(): pl.pallas_call(functools.partial(back_kernel, nf=nf), grid_spec=pltpu.Pre...  26.7 us
    pallas_call x1, Pallas kernels, attend(): pl.pallas_call(functools.partial(attend_kernel, nf=nf, seqs=seqs), grid_s...  14.9 us
    pallas_call x1, Pallas kernels, ffn_down(): pl.pallas_call(functools.partial(down_kernel, nf=nf), grid_spec=pltpu.Pre...  13.9 us
    pallas_call x1, Pallas kernels, ffn_up(): pl.pallas_call(functools.partial(up_kernel, nf=nf), grid_spec=pltpu.Prefe...  13.3 us
    all_to_all x3, starting transfers between devices, over_all(): got = lax.all_to_all(split, axis, 0, 0, tiled=True)  12.8 us
  transfers between devices with their start and end apart: 29, of which 13 were waited for; matrix products, arithmetic and copies ran while one was open for 7% of the time, Pallas kernels for 32%

profile of v1, /device:TPU:0, one launch (start us, length us, event | category | flops | bytes accessed | tf_op | source)
XLA Modules:
  0.0 262.8 jit_solution(12049831949799618161)
XLA Ops:
  0.6 3.0 %collective-permute-start.10 = (bf16[128,2048]{1,0:T(8,128)(2,1)}, bf16[128,2048]{1,0:T(8,128)(2,1)S(1)}, u32[]{:S(2)}, u32[]{:S(2)}) collective-permute-start(bf16[128,2048]{1,0:T(8,128)(2,1)} %refs_0_.4), channel_id=1, source_target_pairs={{0,2},{1,3},{2,0},{3,1},{4,6},{5,7},{6,4},{7,5},{8,10},{9,11},{10,... | collective-permute-start | bytes 1572872 | tf_op jit(solution)/shard_map/ppermute | solution.py:578
  3.8 1.9 collective-permute-start.4
  12.6 14.6 %collective-permute-done.7.refs_10_ = bf16[16,128]{1,0:T(8,128)(2,1)S(1)} collective-permute-done((bf16[16,128]{1,0:T(8,128)(2,1)S(1)}, bf16[16,128]{1,0:T(8,128)(2,1)S(1)}, u32[]{:S(2)}, u32[]{:S(2)}) %collective-permute-start.7) | collective-permute-done | bytes 4128 | tf_op jit(solution)/shard_map/ppermute | solution.py:578
  30.0 1.7 collective-permute-start.13
  32.3 2.6 span_sums.1
  34.9 5.8 %all-to-all-start = ((f32[8,8,512]{2,1,0:T(8,128)}), f32[8,8,512]{2,1,0:T(8,128)S(1)}, u32[]{:S(2)}, u32[]{:S(2)}) async-start(f32[8,8,512]{2,1,0:T(8,128)} %span_sums.1), calls=%async_computation | async-start | bytes 262144 | tf_op jit(solution)/shard_map/all_to_all | solution.py:647
  40.7 1.3 pad_add_fusion.sc
  41.9 6.1 %all-to-all-done = f32[8,8,512]{2,1,0:T(8,128)S(1)} async-done(((f32[8,8,512]{2,1,0:T(8,128)}), f32[8,8,512]{2,1,0:T(8,128)S(1)}, u32[]{:S(2)}, u32[]{:S(2)}) %all-to-all-start) | async-done | bytes 131104 | tf_op jit(solution)/shard_map/all_to_all | solution.py:647
  49.0 14.9 %attend.1 = (bf16[1024,1536]{1,0:T(8,128)(2,1)}, bf16[32,256,192]{2,1,0:T(8,128)(2,1)}, bf16[1024,512]{1,0:T(8,128)(2,1)}, f32[1024,512]{1,0:T(8,128)}, bf16[102...) custom-call(s32[75]{0:T(128)} %pad_add_fusion.sc, ...), custom_call_target="tpu_custom_call" | custom-call | tf_op jit(solution)/shard_map/attend/pallas_call | solution.py:176
  64.9 13.3 %ffn_up.1 = (bf16[1024,2048]{1,0:T(8,128)(2,1)}, bf16[1024,2048]{1,0:T(8,128)(2,1)}, bf16[512,2048]{1,0:T(8,128)(2,1)}, bf16[2,2048,128]{2,1,0:T(8,128)(2,1)}, bf16[2,2048,128]{2,1,0:T(8,128)(2,1)}) custom-call(s32[75]{0:T(128)} %pad_add_fusion.sc, bf16[1024,512]{1,0:T(8,128)(2,1)} %get-tuple-element.40.h2_ref, bf16[1024,512]{1,0:T(8,128)(2,1)} %bitcast.60, ...), custom_call_target="tpu_custom_call" | custom-call | tf_op jit(solution)/shard_map/ffn_up/pallas_call | solution.py:262
  78.8 2.8 %collective-permute-done.12.refs_1_ = bf16[512,512]{1,0:T(8,128)(2,1)S(1)} collective-permute-done((bf16[512,512]{1,0:T(8,128)(2,1)S(1)}, bf16[512,512]{1,0:T(8,128)(2,1)S(1)}, u32[]{:S(2)}, u32[]{:S(2)}) %collective-permute-start.12) | collective-permute-done | bytes 524320 | tf_op jit(solution)/shard_map/ppermute | solution.py:578
  83.2 13.9 %ffn_down.1 = (f32[1024,512]{1,0:T(8,128)}, f32[1,2048]{1,0:T(1,128)}, bf16[2048,512]{1,0:T(8,128)(2,1)}, bf16[2,2048,128]{2,1,0:T(8,128)(2,1)}, bf16[2,2048,128]{2,1,0:T(8,128)(2,1)}) custom-call(s32[75]{0:T(128)} %pad_add_fusion.sc, bf16[1024,512]{1,0:T(8,128)(2,1)} %get-tuple-element.40.h2_ref, bf16[1024,512]{1,0:T(8,128)(2,1)} %bitcast.61, ...), custom_call_target="tpu_custom_call" | custom-call | tf_op jit(solution)/shard_map/ffn_down/pallas_call | solution.py:333
  97.3 26.7 %back.1 = (f32[1024,512]{1,0:T(8,128)}, f32[1024,512]{1,0:T(8,128)}, bf16[8,8,1024]{2,1,0:T(8,128)(2,1)}, bf16[2,2176,128]{2,1,0:T(8,128)(2,1)}, bf16[2,2176,128]{2,1,0:T(8,128)(2,1)}) custom-call(s32[75]{0:T(128)} %pad_add_fusion.sc, bf16[1024,512]{1,0:T(8,128)(2,1)} %bitcast.58, bf16[1024,512]{1,0:T(8,128)(2,1)} %bitcast.62, ...), custom_call_target="tpu_custom_call" | custom-call | tf_op jit(solution)/shard_map/back/pallas_call | solution.py:489
  124.0 3.4 %all-to-all-start.1 = ((bf16[8,8,1024]{2,1,0:T(8,128)(2,1)}), bf16[8,8,1024]{2,1,0:T(8,128)(2,1)S(1)}, u32[]{:S(2)}, u32[]{:S(2)}) async-start(bf16[8,8,1024]{2,1,0:T(8,128)(2,1)} %get-tuple-element.57), calls=%async_computation.1 | async-start | bytes 262144 | tf_op jit(solution)/shard_map/all_to_all | solution.py:657
  131.4 11.6 %collective-permute-done.20 = bf16[1,2048,128]{2,1,0:T(8,128)(2,1)S(1)} collective-permute-done((bf16[1,2048,128]{2,1,0:T(8,128)(2,1)S(1)}, bf16[1,2048,128]{2,1,0:T(8,128)(2,1)S(1)}, u32[]{:S(2)}, u32[]{:S(2)}) %collective-permute-start.20) | collective-permute-done | bytes 524320 | tf_op jit(solution)/shard_map/ppermute | solution.py:578
  144.0 5.6 %all-to-all-start.6 = ((bf16[8,256,128]{2,1,0:T(8,128)(2,1)}), bf16[8,256,128]{2,1,0:T(8,128)(2,1)S(1)}, u32[]{:S(2)}, u32[]{:S(2)}) async-start(bf16[8,256,128]{2,1,0:T(8,128)(2,1)} %bitcast.29), calls=%async_computation.6 | async-start | bytes 1048576 | tf_op jit(solution)/shard_map/all_to_all | solution.py:610
  149.5 1.9 add_convert_fusion
  153.6 2.0 add_convert_fusion.5
  155.5 7.9 %all-to-all-done.6 = bf16[8,256,128]{2,1,0:T(8,128)(2,1)S(1)} async-done(((bf16[8,256,128]{2,1,0:T(8,128)(2,1)}), bf16[8,256,128]{2,1,0:T(8,128)(2,1)S(1)}, u32[]{:S(2)}, u32[]{:S(2)}) %all-to-all-start.6) | async-done | bytes 524320 | tf_op jit(solution)/shard_map/all_to_all | solution.py:610
  163.4 3.6 %all-to-all-start.4 = ((bf16[8,256,128]{2,1,0:T(8,128)(2,1)}), bf16[8,256,128]{2,1,0:T(8,128)(2,1)S(1)}, u32[]{:S(2)}, u32[]{:S(2)}) async-start(bf16[8,256,128]{2,1,0:T(8,128)(2,1)} %bitcast.24), calls=%async_computation.4 | async-start | bytes 1048576 | tf_op jit(solution)/shard_map/all_to_all | solution.py:610
  168.0 13.2 %all-to-all-done.4 = bf16[8,256,128]{2,1,0:T(8,128)(2,1)S(1)} async-done(((bf16[8,256,128]{2,1,0:T(8,128)(2,1)}), bf16[8,256,128]{2,1,0:T(8,128)(2,1)S(1)}, u32[]{:S(2)}, u32[]{:S(2)}) %all-to-all-start.4) | async-done | bytes 524320 | tf_op jit(solution)/shard_map/all_to_all | solution.py:610
  181.2 3.6 %all-to-all-start.2 = ((bf16[8,272,128]{2,1,0:T(8,128)(2,1)}), bf16[8,272,128]{2,1,0:T(8,128)(2,1)S(1)}, u32[]{:S(2)}, u32[]{:S(2)}) async-start(bf16[8,272,128]{2,1,0:T(8,128)(2,1)} %bitcast.10), calls=%async_computation.2 | async-start | bytes 1114112 | tf_op jit(solution)/shard_map/all_to_all | solution.py:610
  184.9 14.9 %all-to-all-done.2 = bf16[8,272,128]{2,1,0:T(8,128)(2,1)S(1)} async-done(((bf16[8,272,128]{2,1,0:T(8,128)(2,1)}), bf16[8,272,128]{2,1,0:T(8,128)(2,1)S(1)}, u32[]{:S(2)}, u32[]{:S(2)}) %all-to-all-start.2) | async-done | bytes 557088 | tf_op jit(solution)/shard_map/all_to_all | solution.py:610
  200.7 3.6 %all-to-all-start.7 = ((bf16[8,256,128]{2,1,0:T(8,128)(2,1)}), bf16[8,256,128]{2,1,0:T(8,128)(2,1)S(1)}, u32[]{:S(2)}, u32[]{:S(2)}) async-start(bf16[8,256,128]{2,1,0:T(8,128)(2,1)} %broadcast_in_dim.28), calls=%async_computation.7 | async-start | bytes 1048576 | tf_op jit(solution)/shard_map/all_to_all | solution.py:613
  204.4 14.6 %all-to-all-done.7 = bf16[8,256,128]{2,1,0:T(8,128)(2,1)S(1)} async-done(((bf16[8,256,128]{2,1,0:T(8,128)(2,1)}), bf16[8,256,128]{2,1,0:T(8,128)(2,1)S(1)}, u32[]{:S(2)}, u32[]{:S(2)}) %all-to-all-start.7) | async-done | bytes 524320 | tf_op jit(solution)/shard_map/all_to_all | solution.py:613
  219.8 3.6 %all-to-all-start.5 = ((bf16[8,256,128]{2,1,0:T(8,128)(2,1)}), bf16[8,256,128]{2,1,0:T(8,128)(2,1)S(1)}, u32[]{:S(2)}, u32[]{:S(2)}) async-start(bf16[8,256,128]{2,1,0:T(8,128)(2,1)} %broadcast_in_dim.13), calls=%async_computation.5 | async-start | bytes 1048576 | tf_op jit(solution)/shard_map/all_to_all | solution.py:613
  223.6 14.6 %all-to-all-done.5 = bf16[8,256,128]{2,1,0:T(8,128)(2,1)S(1)} async-done(((bf16[8,256,128]{2,1,0:T(8,128)(2,1)}), bf16[8,256,128]{2,1,0:T(8,128)(2,1)S(1)}, u32[]{:S(2)}, u32[]{:S(2)}) %all-to-all-start.5) | async-done | bytes 524320 | tf_op jit(solution)/shard_map/all_to_all | solution.py:613
  239.0 3.6 %all-to-all-start.3 = ((bf16[8,272,128]{2,1,0:T(8,128)(2,1)}), bf16[8,272,128]{2,1,0:T(8,128)(2,1)S(1)}, u32[]{:S(2)}, u32[]{:S(2)}) async-start(bf16[8,272,128]{2,1,0:T(8,128)(2,1)} %broadcast_in_dim.12), calls=%async_computation.3 | async-start | bytes 1114112 | tf_op jit(solution)/shard_map/all_to_all | solution.py:613
  242.7 6.6 %block_output.1 = bf16[1024,512]{1,0:T(8,128)(2,1)} custom-call(f32[1024,512]{1,0:T(8,128)} %get-tuple-element.39.r1_ref, bf16[1024,2048]{1,0:T(8,128)(2,1)} %get-tuple-element.42.g_ref, bf16[2048,512]{1,0:T(8,128)(2,1)} %get-tuple-element.45.w_ref, f32[8,2048]{1,0:T(8,128)} %get-tuple-element.41.vec_ref.vec), custom_call_target="tpu_custom_call" | custom-call | tf_op jit(solution)/shard_map/block_output/pallas_call | solution.py:565
  249.2 6.0 %first_back.1 = f32[1024,512]{1,0:T(8,128)} custom-call(bf16[1024,512]{1,0:T(8,128)(2,1)} %bitcast.59, f32[1024,512]{1,0:T(8,128)} %get-tuple-element.55.dr1_ref, f32[1024,512]{1,0:T(8,128)} %get-tuple-element.56.dh1_ref, bf16[8,8,1024]{2,1,0:T(8,128)(2,1)} %copy-done.3, bf16[512,1536]{1,0:T(8,128)(2,1)} %get-tuple-element.52.wqkv, ...), custom_call_target="tpu_custom_call" | custom-call | tf_op jit(solution)/shard_map/first_back/pallas_call | solution.py:547
  255.7 1.3 copy.40
  257.4 1.3 copy.39
  (114 shorter events, 30.2 us)
Async XLA Ops:
  0.6 29.0 %collective-permute-start.10 = (bf16[128,2048]{1,0:T(8,128)(2,1)}, bf16[128,2048]{1,0:T(8,128)(2,1)S(1)}, u32[]{:S(2)}, u32[]{:S(2)}) collective-permute-start(bf16[128,2048]{1,0:T(8,128)(2,1)} %refs_0_.4), channel_id=1, source_target_pairs={{0,2},{1,3},{2,0},{3,1},{4,6},{5,7},{6,4},{7,5},{8,10},{9,11},{10,... | collective-permute-start | bytes 1572872 | tf_op jit(solution)/shard_map/ppermute | solution.py:578
  3.7 28.1 %collective-permute-start.1 = (bf16[128,1536]{1,0:T(8,128)(2,1)}, bf16[128,1536]{1,0:T(8,128)(2,1)S(1)}, u32[]{:S(2)}, u32[]{:S(2)}) collective-permute-start(bf16[128,1536]{1,0:T(8,128)(2,1)} %refs_0_.3), channel_id=1, source_target_pairs={{0,2},{1,3},{2,0},{3,1},{4,6},{5,7},{6,4},{7,5},{8,10},{9,11},{10,... | collective-permute-start | bytes 1179656 | tf_op jit(solution)/shard_map/ppermute | solution.py:578
  3.8 24.7 %collective-permute-start.4 = (bf16[128,512]{1,0:T(8,128)(2,1)}, bf16[128,512]{1,0:T(8,128)(2,1)S(1)}, u32[]{:S(2)}, u32[]{:S(2)}) collective-permute-start(bf16[128,512]{1,0:T(8,128)(2,1)} %refs_4_.1), channel_id=1, source_target_pairs={{0,2},{1,3},{2,0},{3,1},{4,6},{5,7},{6,4},{7,5},{8,10},{9,11},{10,... | collective-permute-start | bytes 393224 | tf_op jit(solution)/shard_map/ppermute | solution.py:578
  5.7 24.3 %collective-permute-start.3 = (bf16[128,512]{1,0:T(8,128)(2,1)}, bf16[128,512]{1,0:T(8,128)(2,1)S(1)}, u32[]{:S(2)}, u32[]{:S(2)}) collective-permute-start(bf16[128,512]{1,0:T(8,128)(2,1)} %refs_4_.1), channel_id=1, source_target_pairs={{0,1},{1,0},{2,3},{3,2},{4,5},{5,4},{6,7},{7,6},{8,9},{9,8},{10,11... | collective-permute-start | bytes 393224 | tf_op jit(solution)/shard_map/ppermute | solution.py:578
  12.4 35.6 %copy-start.16 = (bf16[16,128]{1,0:T(8,128)(2,1)}, bf16[16,128]{1,0:T(8,128)(2,1)S(1)}, u32[]{:S(2)}) copy-start(bf16[16,128]{1,0:T(8,128)(2,1)S(1)} %pad_bitcast_fusion.refs_8_) | copy-start | bytes 12292
  12.4 14.7 %collective-permute-start.7 = (bf16[16,128]{1,0:T(8,128)(2,1)S(1)}, bf16[16,128]{1,0:T(8,128)(2,1)S(1)}, u32[]{:S(2)}, u32[]{:S(2)}) collective-permute-start(bf16[16,128]{1,0:T(8,128)(2,1)S(1)} %pad_bitcast_fusion.refs_8_), channel_id=1, source_target_pairs={{0,2},{1,3},{2,0},{3,1},{4,6},{5,7},{6,4},{7,5},{8,10},{9,11},{10,... | collective-permute-start | bytes 12296 | tf_op jit(solution)/shard_map/ppermute | solution.py:578
  27.1 1.2 collective-permute-start.6
  28.3 1.2 collective-permute-start.8
  28.5 3.3 %collective-permute-start.5 = (bf16[128,512]{1,0:T(8,128)(2,1)S(1)}, bf16[128,512]{1,0:T(8,128)(2,1)}, u32[]{:S(2)}, u32[]{:S(2)}) collective-permute-start(bf16[128,512]{1,0:T(8,128)(2,1)S(1)} %collective-permute-done.4.refs_6_), channel_id=1, source_target_pairs={{0,1},{1,0},{2,3},{3,2},{4,5},{5,4},{6,7},{7,6},{8,9},{9,8},{10,11... | collective-permute-start | bytes 393224 | tf_op jit(solution)/shard_map/ppermute | solution.py:578
  29.5 34.4 %collective-permute-start.9 = (bf16[128,2048]{1,0:T(8,128)(2,1)}, bf16[128,2048]{1,0:T(8,128)(2,1)S(1)}, u32[]{:S(2)}, u32[]{:S(2)}) collective-permute-start(bf16[128,2048]{1,0:T(8,128)(2,1)} %refs_0_.4), channel_id=1, source_target_pairs={{0,1},{1,0},{2,3},{3,2},{4,5},{5,4},{6,7},{7,6},{8,9},{9,8},{10,11... | collective-permute-start | bytes 1572872 | tf_op jit(solution)/shard_map/ppermute | solution.py:578
  29.6 34.2 %copy-start.4 = (bf16[128,2048]{1,0:T(8,128)(2,1)}, bf16[128,2048]{1,0:T(8,128)(2,1)S(1)}, u32[]{:S(2)}) copy-start(bf16[128,2048]{1,0:T(8,128)(2,1)S(1)} %collective-permute-done.10.refs_2_) | copy-start | bytes 1572868
  29.6 34.2 %collective-permute-start.11 = (bf16[128,2048]{1,0:T(8,128)(2,1)S(1)}, bf16[128,2048]{1,0:T(8,128)(2,1)S(1)}, u32[]{:S(2)}, u32[]{:S(2)}) collective-permute-start(bf16[128,2048]{1,0:T(8,128)(2,1)S(1)} %collective-permute-done.10.refs_2_), channel_id=1, source_target_pairs={{0,1},{1,0},{2,3},{3,2},{4,5},{5,4},{6,7},{7,6},{8,9},{9,8},{10,11... | collective-permute-start | bytes 1572872 | tf_op jit(solution)/shard_map/ppermute | solution.py:578
  30.0 48.7 %collective-permute-start.13 = (bf16[512,512]{1,0:T(8,128)(2,1)}, bf16[512,512]{1,0:T(8,128)(2,1)S(1)}, u32[]{:S(2)}, u32[]{:S(2)}) collective-permute-start(bf16[512,512]{1,0:T(8,128)(2,1)} %refs_0_.5), channel_id=1, source_target_pairs={{0,2},{1,3},{2,0},{3,1},{4,6},{5,7},{6,4},{7,5},{8,10},{9,11},{10,... | collective-permute-start | bytes 1572872 | tf_op jit(solution)/shard_map/ppermute | solution.py:578
  31.7 16.3 %collective-permute-start = (bf16[128,1536]{1,0:T(8,128)(2,1)}, bf16[128,1536]{1,0:T(8,128)(2,1)S(1)}, u32[]{:S(2)}, u32[]{:S(2)}) collective-permute-start(bf16[128,1536]{1,0:T(8,128)(2,1)} %refs_0_.3), channel_id=1, source_target_pairs={{0,1},{1,0},{2,3},{3,2},{4,5},{5,4},{6,7},{7,6},{8,9},{9,8},{10,11... | collective-permute-start | bytes 1179656 | tf_op jit(solution)/shard_map/ppermute | solution.py:578
  31.8 16.3 %collective-permute-start.2 = (bf16[128,1536]{1,0:T(8,128)(2,1)S(1)}, bf16[128,1536]{1,0:T(8,128)(2,1)S(1)}, u32[]{:S(2)}, u32[]{:S(2)}) collective-permute-start(bf16[128,1536]{1,0:T(8,128)(2,1)S(1)} %collective-permute-done.1.refs_2_), channel_id=1, source_target_pairs={{0,1},{1,0},{2,3},{3,2},{4,5},{5,4},{6,7},{7,6},{8,9},{9,8},{10,11... | collective-permute-start | bytes 1179656 | tf_op jit(solution)/shard_map/ppermute | solution.py:578
  34.9 13.2 %all-to-all-start = ((f32[8,8,512]{2,1,0:T(8,128)}), f32[8,8,512]{2,1,0:T(8,128)S(1)}, u32[]{:S(2)}, u32[]{:S(2)}) async-start(f32[8,8,512]{2,1,0:T(8,128)} %span_sums.1), calls=%async_computation | async-start | bytes 262144 | tf_op jit(solution)/shard_map/all_to_all | solution.py:647
  78.2 49.6 %collective-permute-start.19 = (bf16[2,2048,128]{2,1,0:T(8,128)(2,1)}, bf16[2,2048,128]{2,1,0:T(8,128)(2,1)S(1)}, u32[]{:S(2)}, u32[]{:S(2)}) collective-permute-start(bf16[2,2048,128]{2,1,0:T(8,128)(2,1)} %get-tuple-element.63), channel_id=1, source_target_pairs={{0,1},{1,0},{2,3},{3,2},{4,5},{5,4},{6,7},{7,6},{8,9},{9,8},{10,11... | collective-permute-start | bytes 3145736 | tf_op jit(solution)/shard_map/ppermute | solution.py:578
  78.2 3.4 %collective-permute-start.12 = (bf16[512,512]{1,0:T(8,128)(2,1)S(1)}, bf16[512,512]{1,0:T(8,128)(2,1)S(1)}, u32[]{:S(2)}, u32[]{:S(2)}) collective-permute-start(bf16[512,512]{1,0:T(8,128)(2,1)S(1)} %copy-done.7), channel_id=1, source_target_pairs={{0,1},{1,0},{2,3},{3,2},{4,5},{5,4},{6,7},{7,6},{8,9},{9,8},{10,11... | collective-permute-start | bytes 1572872 | tf_op jit(solution)/shard_map/ppermute | solution.py:578
  78.7 3.6 %collective-permute-start.14 = (bf16[512,512]{1,0:T(8,128)(2,1)S(1)}, bf16[512,512]{1,0:T(8,128)(2,1)S(1)}, u32[]{:S(2)}, u32[]{:S(2)}) collective-permute-start(bf16[512,512]{1,0:T(8,128)(2,1)S(1)} %collective-permute-done.13.refs_2_), channel_id=1, source_target_pairs={{0,1},{1,0},{2,3},{3,2},{4,5},{5,4},{6,7},{7,6},{8,9},{9,8},{10,11... | collective-permute-start | bytes 1572872 | tf_op jit(solution)/shard_map/ppermute | solution.py:578
  97.1 31.7 %collective-permute-start.17 = (bf16[2,2048,128]{2,1,0:T(8,128)(2,1)}, bf16[2,2048,128]{2,1,0:T(8,128)(2,1)S(1)}, u32[]{:S(2)}, u32[]{:S(2)}) collective-permute-start(bf16[2,2048,128]{2,1,0:T(8,128)(2,1)} %get-tuple-element.61), channel_id=1, source_target_pairs={{0,1},{1,0},{2,3},{3,2},{4,5},{5,4},{6,7},{7,6},{8,9},{9,8},{10,11... | collective-permute-start | bytes 3145736 | tf_op jit(solution)/shard_map/ppermute | solution.py:578
  97.3 30.6 %copy-start.1 = (bf16[2,2048,128]{2,1,0:T(8,128)(2,1)S(1)}, bf16[2,2048,128]{2,1,0:T(8,128)(2,1)}, u32[]{:S(2)}) copy-start(bf16[2,2048,128]{2,1,0:T(8,128)(2,1)} %get-tuple-element.62) | copy-start | bytes 3145732
  124.0 19.9 %all-to-all-start.1 = ((bf16[8,8,1024]{2,1,0:T(8,128)(2,1)}), bf16[8,8,1024]{2,1,0:T(8,128)(2,1)S(1)}, u32[]{:S(2)}, u32[]{:S(2)}) async-start(bf16[8,8,1024]{2,1,0:T(8,128)(2,1)} %get-tuple-element.57), calls=%async_computation.1 | async-start | bytes 262144 | tf_op jit(solution)/shard_map/all_to_all | solution.py:657
  127.4 22.1 %collective-permute-start.15 = (bf16[2,2176,128]{2,1,0:T(8,128)(2,1)}, bf16[2,2176,128]{2,1,0:T(8,128)(2,1)}, u32[]{:S(2)}, u32[]{:S(2)}) collective-permute-start(bf16[2,2176,128]{2,1,0:T(8,128)(2,1)} %get-tuple-element.59), channel_id=1, source_target_pairs={{0,1},{1,0},{2,3},{3,2},{4,5},{5,4},{6,7},{7,6},{8,9},{9,8},{10,11... | collective-permute-start | bytes 3342344 | tf_op jit(solution)/shard_map/ppermute | solution.py:578
  128.2 14.8 %collective-permute-start.20 = (bf16[1,2048,128]{2,1,0:T(8,128)(2,1)S(1)}, bf16[1,2048,128]{2,1,0:T(8,128)(2,1)S(1)}, u32[]{:S(2)}, u32[]{:S(2)}) collective-permute-start(bf16[1,2048,128]{2,1,0:T(8,128)(2,1)S(1)} %slice.125), channel_id=1, source_target_pairs={{0,2},{1,3},{2,0},{3,1},{4,6},{5,7},{6,4},{7,5},{8,10},{9,11},{10,... | collective-permute-start | bytes 1572872 | tf_op jit(solution)/shard_map/ppermute | solution.py:578
  130.2 23.4 %collective-permute-start.18 = (bf16[1,2048,128]{2,1,0:T(8,128)(2,1)}, bf16[1,2048,128]{2,1,0:T(8,128)(2,1)}, u32[]{:S(2)}, u32[]{:S(2)}) collective-permute-start(bf16[1,2048,128]{2,1,0:T(8,128)(2,1)} %slice.122), channel_id=1, source_target_pairs={{0,2},{1,3},{2,0},{3,1},{4,6},{5,7},{6,4},{7,5},{8,10},{9,11},{10,... | collective-permute-start | bytes 1572872 | tf_op jit(solution)/shard_map/ppermute | solution.py:578
  144.0 19.4 %all-to-all-start.6 = ((bf16[8,256,128]{2,1,0:T(8,128)(2,1)}), bf16[8,256,128]{2,1,0:T(8,128)(2,1)S(1)}, u32[]{:S(2)}, u32[]{:S(2)}) async-start(bf16[8,256,128]{2,1,0:T(8,128)(2,1)} %bitcast.29), calls=%async_computation.6 | async-start | bytes 1048576 | tf_op jit(solution)/shard_map/all_to_all | solution.py:610
  152.2 14.8 %collective-permute-start.16 = (bf16[1,2176,128]{2,1,0:T(8,128)(2,1)}, bf16[1,2176,128]{2,1,0:T(8,128)(2,1)S(1)}, u32[]{:S(2)}, u32[]{:S(2)}) collective-permute-start(bf16[1,2176,128]{2,1,0:T(8,128)(2,1)} %slice.112), channel_id=1, source_target_pairs={{0,2},{1,3},{2,0},{3,1},{4,6},{5,7},{6,4},{7,5},{8,10},{9,11},{10,... | collective-permute-start | bytes 1671176 | tf_op jit(solution)/shard_map/ppermute | solution.py:578
  163.4 17.8 %all-to-all-start.4 = ((bf16[8,256,128]{2,1,0:T(8,128)(2,1)}), bf16[8,256,128]{2,1,0:T(8,128)(2,1)S(1)}, u32[]{:S(2)}, u32[]{:S(2)}) async-start(bf16[8,256,128]{2,1,0:T(8,128)(2,1)} %bitcast.24), calls=%async_computation.4 | async-start | bytes 1048576 | tf_op jit(solution)/shard_map/all_to_all | solution.py:610
  181.2 18.7 %all-to-all-start.2 = ((bf16[8,272,128]{2,1,0:T(8,128)(2,1)}), bf16[8,272,128]{2,1,0:T(8,128)(2,1)S(1)}, u32[]{:S(2)}, u32[]{:S(2)}) async-start(bf16[8,272,128]{2,1,0:T(8,128)(2,1)} %bitcast.10), calls=%async_computation.2 | async-start | bytes 1114112 | tf_op jit(solution)/shard_map/all_to_all | solution.py:610
  200.7 18.3 %all-to-all-start.7 = ((bf16[8,256,128]{2,1,0:T(8,128)(2,1)}), bf16[8,256,128]{2,1,0:T(8,128)(2,1)S(1)}, u32[]{:S(2)}, u32[]{:S(2)}) async-start(bf16[8,256,128]{2,1,0:T(8,128)(2,1)} %broadcast_in_dim.28), calls=%async_computation.7 | async-start | bytes 1048576 | tf_op jit(solution)/shard_map/all_to_all | solution.py:613
  219.8 18.3 %all-to-all-start.5 = ((bf16[8,256,128]{2,1,0:T(8,128)(2,1)}), bf16[8,256,128]{2,1,0:T(8,128)(2,1)S(1)}, u32[]{:S(2)}, u32[]{:S(2)}) async-start(bf16[8,256,128]{2,1,0:T(8,128)(2,1)} %broadcast_in_dim.13), calls=%async_computation.5 | async-start | bytes 1048576 | tf_op jit(solution)/shard_map/all_to_all | solution.py:613
  239.0 19.7 %all-to-all-start.3 = ((bf16[8,272,128]{2,1,0:T(8,128)(2,1)}), bf16[8,272,128]{2,1,0:T(8,128)(2,1)S(1)}, u32[]{:S(2)}, u32[]{:S(2)}) async-start(bf16[8,272,128]{2,1,0:T(8,128)(2,1)} %broadcast_in_dim.12), calls=%async_computation.3 | async-start | bytes 1114112 | tf_op jit(solution)/shard_map/all_to_all | solution.py:613
  (17 other events, 131.7 us)

commit v2 on v1

v2 whole, which is shorter than its diff:
```python
import functools

import jax
import jax.numpy as jnp
from jax import lax
from jax.experimental import pallas as pl
from jax.experimental.pallas import tpu as pltpu
from jax.sharding import PartitionSpec as P

D = 512
HEADS = 8
HEAD = 64
SPAN = 128
LANE = 128
PAIRS = D // LANE
ROWS = 256
EPSILON = 1e-05
MASKED = -1e30
SCALE = HEAD**-0.5
INV_ROOT = SPAN**-0.5
F32 = jnp.float32
BF16 = jnp.bfloat16

G1, S1, OB, G2, S2, DB, QB, UB = range(8)
SC_F, SC_C, SC_SLOT, SC_LEN = range(4)


def dot(a, b):
    return lax.dot_general(a, b, (((1,), (0,)), ((), ())), preferred_element_type=F32)


def dot_bt(a, b):
    return lax.dot_general(a, b, (((1,), (1,)), ((), ())), preferred_element_type=F32)


def dot_at(a, b):
    return lax.dot_general(a, b, (((0,), (0,)), ((), ())), preferred_element_type=F32)


def normalize(values):
    centre = values - jnp.mean(values, axis=-1, keepdims=True)
    spread = jnp.mean(centre * centre, axis=-1, keepdims=True)
    rstd = lax.rsqrt(spread + EPSILON)
    return centre * rstd, rstd


def norm_back(e, n, rstd):
    return rstd * (
        e - jnp.mean(e, axis=-1, keepdims=True) - n * jnp.mean(e * n, axis=-1, keepdims=True)
    )


def params(mib):
    return pltpu.CompilerParams(vmem_limit_bytes=mib * 1024 * 1024)


def in_vmem(count):
    return [pl.BlockSpec(memory_space=pltpu.VMEM) for _ in range(count)]


def cost(micros):
    return pl.CostEstimate(
        flops=int(micros * 1e9), transcendentals=0, bytes_accessed=int(micros * 1e6)
    )


def resident(kernel, name, micros, mib, scalars, arrays, outs, scratch=()):
    return pl.pallas_call(
        kernel,
        in_specs=[pl.BlockSpec(memory_space=pltpu.SMEM)] * len(scalars) + in_vmem(len(arrays)),
        out_specs=in_vmem(len(outs)),
        out_shape=[jax.ShapeDtypeStruct(shape, dtype) for shape, dtype in outs],
        scratch_shapes=list(scratch),
        compiler_params=params(mib),
        name=name,
        cost_estimate=cost(micros),
    )(*scalars, *arrays)


def block_rows(i, size=ROWS):
    return pl.ds(pl.multiple_of(i * size, size), size)


def each_block(rows, body):
    def step(i, carry):
        body(i)
        return carry

    lax.fori_loop(0, rows // ROWS, step, 0)


def sums_kernel(x_ref, o_ref):
    spans = x_ref.shape[0] // SPAN
    sums = []
    for s in range(spans):
        n, _ = normalize(x_ref[s * SPAN : (s + 1) * SPAN, :].astype(F32))
        sums.append(jnp.sum(n, axis=0, keepdims=True))
    table = jnp.concatenate(sums, axis=0)
    for k in range(o_ref.shape[0]):
        o_ref[k] = table


def span_sums(x, copies):
    spans = x.shape[0] // SPAN
    return resident(sums_kernel, "span_sums", 3, 16, (), (x,), [((copies, spans, D), F32)])[0]


def pack_kernel(qkv_ref, out_ref, *refs):
    o_ref = refs[-1]
    rows, width = qkv_ref.shape
    o_ref[:rows, :width] = qkv_ref[...]
    o_ref[:rows, width:] = out_ref[...]
    parts = [ref[...].astype(F32) for ref in refs[:-1]]
    used = sum(part.shape[0] for part in parts)
    parts.append(jnp.zeros((16 - used, LANE), F32))
    o_ref[rows:, :LANE] = jnp.concatenate(parts, axis=0).astype(BF16)
    o_ref[rows:, LANE:] = jnp.zeros((16, o_ref.shape[1] - LANE), BF16)


def packed_params(qkv, out, vectors):
    shape = (qkv.shape[0] + 16, qkv.shape[1] + out.shape[1])
    vectors = [v.reshape(-1, LANE) for v in vectors]
    arrays = [qkv, out] + vectors
    return pl.pallas_call(
        pack_kernel,
        out_shape=jax.ShapeDtypeStruct(shape, BF16),
        compiler_params=params(58),
        name="pack",
        cost_estimate=cost(1),
    )(*arrays)


def attend_kernel(sc, x_ref, order_ref, nsum_ref, *refs, nf, seqs):
    param_refs = refs[:nf]
    (packed_ref, p_ref, att_ref, h1_ref, wqkv, wout, vec, tabs) = refs[nf:]
    nspan = nsum_ref.shape[0]
    block = D // nf

    vec[...] = jnp.zeros_like(vec)
    for q in range(nf):
        fq = sc[SC_F] ^ q
        at = pl.ds(pl.multiple_of(fq * block, block), block)
        wqkv[at, :] = param_refs[q][:block, : 3 * D]
        wout[at, :] = param_refs[q][:block, 3 * D :]
        sm = param_refs[q][block:, :LANE].astype(F32)
        for row, src in ((G1, 0), (S1, 1), (OB, 5), (G2, 6), (S2, 7), (DB, 12)):
            vec[row : row + 1, at] = sm[src : src + 1]
        for t in range(3):
            at3 = pl.ds(pl.multiple_of(fq * 3 * block + t * block, block), block)
            vec[QB : QB + 1, at3] = sm[2 + t : 3 + t]
        for t in range(4):
            at4 = pl.ds(pl.multiple_of(fq * 4 * block + t * block, block), block)
            vec[UB : UB + 1, at4] = sm[8 + t : 9 + t]
    hs = nsum_ref[...] * vec[G1 : G1 + 1, :D] + SPAN * vec[S1 : S1 + 1, :D]
    hi = hs.astype(BF16)
    lo = (hs - hi.astype(F32)).astype(BF16)
    t = dot(hi, wqkv[:, D:]) + dot(lo, wqkv[:, D:]) + SPAN * vec[QB : QB + 1, D : 3 * D]
    tabs[...] = (t * INV_ROOT).astype(BF16)
    prompt = lax.div(sc[SC_LEN], SPAN)
    spans = ROWS // SPAN

    def body(i):
        rows = block_rows(i)
        n1, _ = normalize(x_ref[rows, :].astype(F32))
        h1 = (n1 * vec[G1 : G1 + 1, :D] + vec[S1 : S1 + 1, :D]).astype(BF16)
        h1_ref[rows, :] = h1
        packed_ref[rows, :] = (dot(h1, wqkv[...]) + vec[QB : QB + 1, : 3 * D]).astype(BF16)

        lane = lax.broadcasted_iota(jnp.int32, (SPAN, LANE), 1)
        low = lane < HEAD
        causal = jnp.where(
            lane <= lax.broadcasted_iota(jnp.int32, (SPAN, LANE), 0), 0.0, MASKED
        ).astype(F32)
        order = order_ref[...]
        for s in range(spans):
            a = sc[SC_LEN + seqs + sc[SC_SLOT] + i * spans + s]
            start, begin = 0, 0
            for k in range(seqs):
                begin = jnp.where(start <= a, start, begin)
                start = start + lax.div(sc[SC_LEN + k], SPAN)
            seen = (order < a) & ((order >= begin) | (order < prompt))
            far = jnp.where(seen, 0.0, MASKED).astype(F32)
            bias = jnp.concatenate([causal, jnp.broadcast_to(far, (SPAN, nspan))], axis=1)
            bias = jnp.concatenate([bias, bias], axis=0)
            at = block_rows(i * spans + s, SPAN)
            for p in range(PAIRS):
                cq, ck, cv = (slice(t * D + p * LANE, t * D + (p + 1) * LANE) for t in range(3))
                q = packed_ref[at, cq] * SCALE
                zero = jnp.zeros_like(q)
                q2 = jnp.concatenate([jnp.where(low, q, zero), jnp.where(low, zero, q)], axis=0)
                kc = jnp.concatenate([packed_ref[at, ck], tabs[:, cq]], axis=0)
                vc = jnp.concatenate([packed_ref[at, cv], tabs[:, ck]], axis=0)
                scores = dot_bt(q2, kc) + bias
                peak = jnp.max(scores, axis=1, keepdims=True)
                e = jnp.exp(scores - peak)
                w = (e * (1.0 / jnp.sum(e, axis=1, keepdims=True))).astype(BF16)
                p_ref[(i * spans + s) * PAIRS + p] = w
                o2 = dot(w, vc)
                att_ref[at, cq] = jnp.where(low, o2[:SPAN], o2[SPAN:]).astype(BF16)

    each_block(x_ref.shape[0], body)


def proj_kernel(x_ref, att_ref, wout, vec, r1_ref, h2_ref):
    def body(i):
        at = block_rows(i)
        r1 = x_ref[at, :].astype(F32) + (dot(att_ref[at, :], wout[...]) + vec[OB : OB + 1, :D])
        r1_ref[at, :] = r1
        n2, _ = normalize(r1)
        h2_ref[at, :] = (n2 * vec[G2 : G2 + 1, :D] + vec[S2 : S2 + 1, :D]).astype(BF16)

    each_block(x_ref.shape[0], body)


def proj(x, att, wout, vec):
    outs = [(x.shape, F32), (x.shape, BF16)]
    return resident(proj_kernel, "proj", 3, 8, (), (x, att, wout, vec), outs)


def attend(sc, x, order, nsum, weights, seqs):
    rows = x.shape[0]
    nspan = nsum.shape[0]
    outs = [
        ((rows, 3 * D), BF16),
        ((rows // SPAN * PAIRS, 2 * SPAN, SPAN + nspan), BF16),
        ((rows, D), BF16),
        ((rows, D), BF16),
        ((D, 3 * D), BF16),
        ((D, D), BF16),
        ((8, 4 * D), F32),
        ((nspan, 2 * D), BF16),
    ]
    kernel = functools.partial(attend_kernel, nf=len(weights), seqs=seqs)
    arrays = (x, order, nsum, *weights)
    return resident(kernel, "attend", 12, 12, (sc,), arrays, outs)


def relative(step, nf):
    half = nf // 2
    return jnp.where(step < half, 2 * step + 1, 2 * (step - half))


def up_kernel(sc, h2_ref, vec_ref, *refs, nf):
    up_refs = refs[:nf]
    g_ref, gp_ref, w_ref = refs[nf:]
    block = D // nf
    width = w_ref.shape[1] // nf
    k0 = 0.7978845608028654
    for q in range(nf):
        at = pl.ds(pl.multiple_of((sc[SC_F] ^ q) * block, block), block)
        w_ref[at, :] = up_refs[q][...]
    for j in range(nf):
        cols = slice(j * width, (j + 1) * width)

        def body(i):
            at = block_rows(i)
            u = dot(h2_ref[at, :], w_ref[:, cols]) + vec_ref[UB : UB + 1, cols]
            u2 = u * u
            t = jnp.tanh(u * (k0 + (k0 * 0.044715) * u2))
            half = 0.5 + 0.5 * t
            g_ref[at, cols] = (u * half).astype(BF16)
            slope = u * (k0 + (3 * k0 * 0.044715) * u2)
            gp_ref[at, cols] = (half + (0.5 - 0.5 * t * t) * slope).astype(BF16)

        each_block(h2_ref.shape[0], body)


def ffn_up(sc, h2, vec, up):
    rows, ff = h2.shape[0], up[0].shape[1]
    outs = [((rows, ff), BF16), ((rows, ff), BF16), ((D, ff), BF16)]
    kernel = functools.partial(up_kernel, nf=len(up))
    return resident(kernel, "ffn_up", 8, 12, (sc,), (h2, vec, *up), outs)


def down_grad_kernel(sc, g_ref, c_ref, send_ref, keep_ref, *, nf):
    width = g_ref.shape[1] // nf
    for q in range(nf):
        at = pl.ds(pl.multiple_of((sc[SC_F] ^ q) * width, width), width)
        grad = dot_at(g_ref[:, at], c_ref[...]).astype(BF16)
        ref = send_ref if q % 2 else keep_ref
        for j in range(D // LANE):
            ref[q // 2, j * width : (j + 1) * width, :] = grad[:, j * LANE : (j + 1) * LANE]


def down_gradient(sc, g, c, nf):
    piece = g.shape[1] // nf * D // LANE
    outs = [((nf // 2, piece, LANE), BF16)] * 2
    kernel = functools.partial(down_grad_kernel, nf=nf)
    return resident(kernel, "down_grad", 4, 12, (sc,), (g, c), outs)


def down_kernel(sc, h2_ref, c_ref, gp_ref, w_ref, *refs, nf):
    down_refs = refs[:nf]
    dh2_ref, dub_ref, send_ref, keep_ref, du_ref, grad_ref = refs[nf:]
    width = w_ref.shape[1] // nf
    block = D // nf
    rows = h2_ref.shape[0]
    for s in range(nf):
        f = sc[SC_F] ^ s
        cols = pl.ds(pl.multiple_of(f * width, width), width)
        dub_ref[:, cols] = jnp.zeros((1, width), F32)

        def body(i):
            at = block_rows(i)
            dg = dot_bt(c_ref[at, :], down_refs[s][...])
            du = (dg * gp_ref[at, cols].astype(F32)).astype(BF16)
            du_ref[at, :] = du
            dub_ref[:, cols] += jnp.sum(du.astype(F32), axis=0, keepdims=True)
            dh2 = dot_bt(du, w_ref[:, cols])
            if s == 0:
                dh2_ref[at, :] = dh2
            else:
                dh2_ref[at, :] += dh2

        each_block(rows, body)
        grad_ref[...] = dot_at(h2_ref[...], du_ref[...])
        for q in range(nf):
            ref = send_ref if q % 2 else keep_ref
            piece = grad_ref[pl.ds(pl.multiple_of((sc[SC_F] ^ q) * block, block), block), :]
            piece = piece.astype(BF16)
            for j in range(width // LANE):
                to = pl.multiple_of((f * (width // LANE) + j) * block, block)
                ref[q // 2, pl.ds(to, block), :] = piece[:, j * LANE : (j + 1) * LANE]


def ffn_down(sc, h2, c, gp, w, down):
    nf = len(down)
    rows = h2.shape[0]
    ff = w.shape[1]
    piece = ff // LANE * (D // nf)
    outs = [((rows, D), F32), ((1, ff), F32)] + [((nf // 2, piece, LANE), BF16)] * 2
    scratch = [pltpu.VMEM((rows, ff // nf), BF16), pltpu.VMEM((D, ff // nf), F32)]
    kernel = functools.partial(down_kernel, nf=nf)
    arrays = (h2, c, gp, w, *down)
    return resident(kernel, "ffn_down", 8, 14, (sc,), arrays, outs, scratch)


def mid_kernel(c_ref, dh2_ref, r1_ref, att_ref, wout, vec, dr1_ref, da_ref, gout_ref, gvec_ref):
    gout_ref[...] = jnp.zeros_like(gout_ref)
    gvec_ref[...] = jnp.zeros_like(gvec_ref)

    def add(row, values):
        gvec_ref[row : row + 1, :] += jnp.sum(values, axis=0, keepdims=True)

    def body(i):
        at = block_rows(i)
        c = c_ref[at, :].astype(F32)
        dh2 = dh2_ref[at, :]
        n2, rstd2 = normalize(r1_ref[at, :])
        add(G2, dh2 * n2)
        add(S2, dh2)
        add(DB, c)
        dr1 = c + norm_back(dh2 * vec[G2 : G2 + 1, :D], n2, rstd2)
        dr1_ref[at, :] = dr1
        dy = dr1.astype(BF16)
        add(OB, dy.astype(F32))
        gout_ref[...] += dot_at(att_ref[at, :], dy)
        da_ref[at, :] = dot_bt(dy, wout[...]).astype(BF16)

    each_block(c_ref.shape[0], body)


def mid(c, dh2, r1, att, wout, vec):
    rows = c.shape[0]
    outs = [((rows, D), F32), ((rows, D), BF16), ((D, D), F32), ((8, D), F32)]
    return resident(mid_kernel, "mid", 5, 12, (), (c, dh2, r1, att, wout, vec), outs)


def piece_rows(used, parts):
    return -(-used // (16 * parts)) * 16 * parts


def columns_of(half):
    wide = PAIRS // 2 * LANE
    return [slice(t * D + half * wide, t * D + (half + 1) * wide) for t in range(3)]


def back_kernel(sc, x_ref, da_ref, h1_ref, packed_ref, p_ref, tabs, wqkv, vec, nsum_ref, *refs, nf, copies, half):
    if half:
        (dub_ref, gvec_ref, before_ref, sums_ref), refs = refs[:4], refs[4:]
    else:
        (gout_ref,), refs = refs[:1], refs[1:]
    dh1_ref, sum_ref, far_send, far_keep, send_ref, keep_ref, acc, acc_span, accv, dp_ref = refs
    wide = PAIRS // 2 * LANE
    columns = columns_of(half)
    for ref in (acc, acc_span, accv):
        ref[...] = jnp.zeros_like(ref)

    def add(row, values):
        accv[row : row + 1, : values.shape[1]] += jnp.sum(values, axis=0, keepdims=True)

    def body(i):
        rows = block_rows(i)
        low = lax.broadcasted_iota(jnp.int32, (SPAN, LANE), 1) < HEAD
        for s in range(ROWS // SPAN):
            at = block_rows(i * (ROWS // SPAN) + s, SPAN)
            to = slice(s * SPAN, (s + 1) * SPAN)
            for k in range(PAIRS // 2):
                p = half * (PAIRS // 2) + k
                cq, ck, cv = (slice(t * D + p * LANE, t * D + (p + 1) * LANE) for t in range(3))
                oq, ok, ov = (slice(t * wide + k * LANE, t * wide + (k + 1) * LANE) for t in range(3))
                q = packed_ref[at, cq] * SCALE
                do = da_ref[at, cq]
                zero = jnp.zeros_like(q)
                q2 = jnp.concatenate([jnp.where(low, q, zero), jnp.where(low, zero, q)], axis=0)
                do2 = jnp.concatenate([jnp.where(low, do, zero), jnp.where(low, zero, do)], axis=0)
                kc = jnp.concatenate([packed_ref[at, ck], tabs[:, cq]], axis=0)
                vc = jnp.concatenate([packed_ref[at, cv], tabs[:, ck]], axis=0)
                w = p_ref[(i * (ROWS // SPAN) + s) * PAIRS + p]
                wf = w.astype(F32)
                dp = dot_bt(do2, vc)
                delta = jnp.sum(wf * dp, axis=1, keepdims=True)
                ds = (wf * (dp - delta)).astype(BF16)
                dq2 = dot(ds, kc)
                dq = jnp.where(low, dq2[:SPAN], dq2[SPAN:]) * SCALE
                dk = dot_at(ds, q2)
                dv = dot_at(w, do2)
                acc_span[:, oq] += dk[SPAN:]
                acc_span[:, ok] += dv[SPAN:]
                dp_ref[to, oq] = dq.astype(BF16)
                dp_ref[to, ok] = dk[:SPAN].astype(BF16)
                dp_ref[to, ov] = dv[:SPAN].astype(BF16)
        dpk = dp_ref[...]
        add(QB, dpk.astype(F32))
        acc[...] += dot_at(h1_ref[rows, :], dpk)
        dh1 = dot_bt(dpk[:, :wide], wqkv[:, columns[0]])
        for t in (1, 2):
            dh1 = dh1 + dot_bt(dpk[:, t * wide : (t + 1) * wide], wqkv[:, columns[t]])
        if half:
            dh1 = dh1 + before_ref[rows, :]
            n1, _ = normalize(x_ref[rows, :].astype(F32))
            add(G1, dh1 * n1)
            add(S1, dh1)
        dh1_ref[rows, :] = dh1

    each_block(x_ref.shape[0], body)

    span = acc_span[...]
    bit = sc[SC_C] & 1
    each = span.shape[0] // copies
    for k in range(copies):
        code = code_of(k, copies)
        part = span[k * each : (k + 1) * each]
        hold = jnp.concatenate(
            [part[:, t * LANE : (t + 1) * LANE] for t in range(2 * wide // LANE)], axis=0
        ).astype(BF16)
        to = slice(code % (copies // 2) * hold.shape[0], (code % (copies // 2) + 1) * hold.shape[0])
        mine = bit == code // (copies // 2)

        @pl.when(mine)
        def _():
            far_keep[to, :] = hold

        @pl.when(jnp.logical_not(mine))
        def _():
            far_send[to, :] = hold

    span = span * INV_ROOT
    low_span = span.astype(BF16)
    nsum = nsum_ref[...]
    hs = (nsum * vec[G1 : G1 + 1, :D] + SPAN * vec[S1 : S1 + 1, :D]).astype(BF16)
    acc[:, wide:] += dot_at(hs, low_span)
    accv[QB : QB + 1, wide : 3 * wide] += SPAN * jnp.sum(span, axis=0, keepdims=True)
    de = dot_bt(low_span[:, :wide], wqkv[:, columns[1]])
    de = de + dot_bt(low_span[:, wide:], wqkv[:, columns[2]])
    block = D // nf
    if half:
        de = de + sums_ref[: de.shape[0], :]
        add(G1, de * nsum)
        accv[S1 : S1 + 1, :D] += SPAN * jnp.sum(de, axis=0, keepdims=True)
        bias = sums_ref[de.shape[0] : de.shape[0] + 8, :]
    else:
        sum_ref[: de.shape[0], :] = de
        tail = [accv[QB : QB + 1, t * wide : (t + 1) * wide] for t in range(3)]
        bias = jnp.concatenate(tail + [jnp.zeros((5, wide), F32)], axis=0)
        sum_ref[de.shape[0] : de.shape[0] + 8, :] = jnp.concatenate([bias, bias], axis=1)

    for q in range(nf):
        ref = send_ref if q % 2 else keep_ref
        fq = sc[SC_F] ^ q
        at = pl.ds(pl.multiple_of(fq * block, block), block)
        base = 0
        pieces = [acc[at, :].astype(BF16)]
        if not half:
            pieces.append(gout_ref[at, :].astype(BF16))
        for piece in pieces:
            for j in range(piece.shape[1] // LANE):
                ref[q // 2, base : base + block, :] = piece[:, j * LANE : (j + 1) * LANE]
                base += block
        if half:
            whole = jnp.concatenate(
                [
                    part
                    for t in range(3)
                    for part in (bias[t : t + 1, :wide], accv[QB : QB + 1, t * wide : (t + 1) * wide])
                ],
                axis=1,
            )
            accv[QB + 1 : QB + 2, : 3 * D] = whole
            three = [
                accv[QB + 1 : QB + 2, pl.ds(pl.multiple_of((fq * 3 + t) * block, block), block)]
                for t in range(3)
            ]
            four = [
                dub_ref[0:1, pl.ds(pl.multiple_of((fq * 4 + t) * block, block), block)]
                for t in range(4)
            ]
            small = jnp.concatenate(
                [accv[G1 : G1 + 1, at], accv[S1 : S1 + 1, at]]
                + three
                + [gvec_ref[OB : OB + 1, at], gvec_ref[G2 : G2 + 1, at], gvec_ref[S2 : S2 + 1, at]]
                + four
                + [gvec_ref[DB : DB + 1, at], jnp.zeros((3, LANE), F32)],
                axis=0,
            ).astype(BF16)
            ref[q // 2, base : base + 16, :] = small
            base += 16
        left = ref.shape[1] - base
        if left:
            ref[q // 2, base:, :] = jnp.zeros((left, LANE), BF16)


def back(sc, x, da, h1, packed, p, tabs, wqkv, vec, nsum, more, half, nf, copies):
    rows = x.shape[0]
    nspan = nsum.shape[0]
    wide = PAIRS // 2 * LANE
    block = D // nf
    used = 3 * wide // LANE * block + (16 if half else D // LANE * block)
    piece = piece_rows(used, copies)
    far = nspan // 2 * 2 * wide // LANE
    outs = [((rows, D), F32), ((nspan + 8, D), F32)]
    outs += [((far, LANE), BF16)] * 2 + [((nf // 2, piece, LANE), BF16)] * 2
    scratch = [
        pltpu.VMEM((D, 3 * wide), F32),
        pltpu.VMEM((nspan, 2 * wide), F32),
        pltpu.VMEM((16, 3 * D), F32),
        pltpu.VMEM((ROWS, 3 * wide), BF16),
    ]
    kernel = functools.partial(back_kernel, nf=nf, copies=copies, half=half)
    arrays = (x, da, h1, packed, p, tabs, wqkv, vec, nsum, *more)
    return resident(kernel, f"back_{half}", 9, 18, (sc,), arrays, outs, scratch)


def first_kernel(x_ref, dr1_ref, dh1_ref, own_ref, wqkv, vec, o_ref, e_ref):
    i = pl.program_id(0)
    spans = ROWS // SPAN

    @pl.when(i == 0)
    def _():
        each = e_ref.shape[0]
        wide = PAIRS // 2 * LANE
        total = jnp.zeros((each, D), F32)
        for half in range(2):
            for k, columns in enumerate(columns_of(half)[1:]):
                for t in range(wide // LANE):
                    row = ((half * 2 + k) * (wide // LANE) + t) * each
                    own = own_ref[row : row + each, :].astype(F32) * INV_ROOT
                    cols = slice(columns.start + t * LANE, columns.start + (t + 1) * LANE)
                    total = total + dot_bt(own.astype(BF16), wqkv[:, cols])
        e_ref[...] = total

    at = block_rows(i)
    n1, rstd1 = normalize(x_ref[at, :].astype(F32))
    extra = jnp.concatenate(
        [jnp.broadcast_to(e_ref[pl.ds(i * spans + s, 1), :], (SPAN, D)) for s in range(spans)],
        axis=0,
    )
    dh1 = dh1_ref[at, :] + extra
    o_ref[...] = dr1_ref[at, :] + norm_back(dh1 * vec[G1 : G1 + 1, :D], n1, rstd1)


def first_back(x, dr1, dh1, own, wqkv, vec):
    rows = x.shape[0]
    return pl.pallas_call(
        first_kernel,
        grid=(rows // ROWS,),
        in_specs=in_vmem(6),
        out_specs=pl.BlockSpec((ROWS, D), lambda i: (i, 0)),
        out_shape=jax.ShapeDtypeStruct((rows, D), F32),
        scratch_shapes=[pltpu.VMEM((rows // SPAN, D), F32)],
        compiler_params=params(8),
        name="first_back",
        cost_estimate=cost(3),
    )(x, dr1, dh1, own, wqkv, vec)


def mixed_kernel(sc, r1_ref, g_ref, vec, *refs):
    w_refs, o_ref = refs[:-1], refs[-1]
    at = block_rows(pl.program_id(0))
    total = r1_ref[at, :] + vec[DB : DB + 1, :D]
    width = w_refs[0].shape[0]
    for q, w_ref in enumerate(w_refs):
        cols = pl.ds(pl.multiple_of((sc[SC_F] ^ q) * width, width), width)
        total = total + dot(g_ref[at, cols], w_ref[...])
    o_ref[...] = total.astype(BF16)


def block_output(sc, r1, g, vec, down):
    rows = r1.shape[0]
    return pl.pallas_call(
        mixed_kernel,
        grid=(rows // ROWS,),
        in_specs=[pl.BlockSpec(memory_space=pltpu.SMEM)] + in_vmem(3 + len(down)),
        out_specs=pl.BlockSpec((ROWS, D), lambda i: (i, 0)),
        out_shape=jax.ShapeDtypeStruct((rows, D), BF16),
        compiler_params=params(8),
        name="block_output",
        cost_estimate=cost(4),
    )(sc, r1, g, vec, *down)


def swap(array, axis, bit):
    n = lax.axis_size(axis)
    return lax.ppermute(array, axis, [(k, k ^ bit) for k in range(n)])


def after(array, *others):
    return lax.optimization_barrier((array, others))[0]


def first_gather(array, axis):
    return swap(array, axis, lax.axis_size(axis) // 2)


def gathered(array, far, axis):
    n = lax.axis_size(axis)
    bit = n // 2
    held = {0: array, bit: far}
    bit //= 2
    while bit:
        for r in sorted(held):
            held[r ^ bit] = swap(held[r], axis, bit)
        bit //= 2
    return [held[r] for r in range(n)]


def fold_kernel(sc, *refs, bit):
    own = lax.div(sc[SC_C], bit) & 1 if bit else 0
    arrays, (send_ref, own_ref) = refs[:-2], refs[-2:]
    at = 0
    for keep_ref, got_ref in zip(arrays[0::2], arrays[1::2]):
        a, _, h, _ = keep_ref.shape
        for ref, half in ((send_ref, 1 - own), (own_ref, own)):
            for k in range(a):
                total = keep_ref[k, half].astype(F32) + got_ref[k, half].astype(F32)
                ref[k, at : at + h, :] = total.astype(BF16)
        at += h


def fold(sc, bit, *pairs):
    a = pairs[0][0].shape[0]
    h = sum(keep.shape[2] for keep, _ in pairs)
    arrays = [array for pair in pairs for array in pair]
    kernel = functools.partial(fold_kernel, bit=bit)
    return resident(kernel, "fold", 1, 8, (sc,), arrays, [((a, h, LANE), BF16)] * 2)


def refold_kernel(sc, keep_ref, got_ref, send_ref, own_ref, *, bit, sizes):
    own = lax.div(sc[SC_C], bit) & 1
    at = 0
    for h in sizes:
        for ref, half in ((send_ref, 1 - own), (own_ref, own)):
            rows = pl.ds(pl.multiple_of(2 * at + half * h, 16), h)
            total = keep_ref[rows, :].astype(F32) + got_ref[rows, :].astype(F32)
            ref[at : at + h, :] = total.astype(BF16)
        at += h


def refold(sc, bit, keep, got, sizes):
    outs = [((sum(sizes), LANE), BF16)] * 2
    kernel = functools.partial(refold_kernel, bit=bit, sizes=sizes)
    return resident(kernel, "fold", 1, 8, (sc,), (keep, got), outs)


def last_kernel(keep_ref, got_ref, o_ref, *rest):
    used = o_ref.shape[0]
    total = keep_ref[:used, :].astype(F32) + got_ref[:used, :].astype(F32)
    o_ref[...] = total.astype(BF16)
    for ref in rest:
        total = keep_ref[used:, :].astype(F32) + got_ref[used:, :].astype(F32)
        ref[...] = total.astype(BF16)


def last_sum(keep, got, used):
    outs = [((used, LANE), BF16)]
    if used < keep.shape[0]:
        outs.append(((keep.shape[0] - used, LANE), BF16))
    return resident(last_kernel, "last", 1, 8, (), (keep, got), outs)


class Part:
    def __init__(self, sc, keep, send):
        self.sc, self.keep, self.send = sc, keep, send
        self.count, self.rows = keep.shape[0], keep.shape[1]
        self.total = self.rows
        self.move("fsdp", 1)

    def move(self, axis, bit):
        self.got = swap(self.send, axis, bit)

    def view(self, axis):
        if axis == "fsdp":
            self.count //= 2
            return 1, 2, self.count * self.rows, LANE
        self.rows //= 2
        return self.count, 2, self.rows, LANE

    def pair(self, axis):
        view = self.view(axis)
        return self.keep.reshape(view), self.got.reshape(view)

    def step(self, axis, bit):
        pair = self.pair(axis)
        self.send, self.keep = fold(self.sc, bit if axis == "ctx" else 0, pair)
        self.move(axis, bit)

    def wait(self, *arrays):
        self.keep = after(self.keep, *arrays)


def ctx_bits():
    n = lax.axis_size("ctx")
    return [1 << k for k in range(n.bit_length() - 1)]


def ctx_sum(sc, parts, extra=()):
    bits = ctx_bits()
    pairs = [part.pair("ctx") for part in parts]
    for keep, got in extra:
        view = (1, 2, keep.shape[0] // 2, LANE)
        pairs.append((keep.reshape(view), got.reshape(view)))
    sizes = [keep.shape[2] for keep, _ in pairs]
    used = sum(sizes[: len(parts)]) * 2 // bits[-1]
    send, keep = (a[0] for a in fold(sc, bits[1], *pairs))
    got = swap(send, "ctx", bits[1])
    for bit in bits[2:]:
        sizes = [size // 2 for size in sizes]
        send, keep = refold(sc, bit, keep, got, sizes)
        got = swap(send, "ctx", bit)
    return last_sum(keep, got, used)


def over_ctx(own):
    for bit in reversed(ctx_bits()):
        own = jnp.concatenate([own, swap(own, "ctx", bit)], axis=0)
    return own.reshape(lax.axis_size("ctx"), -1, LANE)


def code_of(index, n):
    code = 0
    for k in range(n.bit_length() - 1):
        bit = index >> k if isinstance(index, int) else lax.div(index, 1 << k)
        code = 2 * code + (bit & 1)
    return code


def finish_kernel(sc, got_ref, *refs, heights, plan):
    outs, rows = refs[:-1], refs[-1]
    n = got_ref.shape[0]
    code = code_of(sc[SC_C], n)
    for k in range(n):
        at, base = 0, 0
        for height in heights:
            h = height // n
            to = pl.multiple_of(base + (code ^ k) * h, 16)
            rows[pl.ds(to, h), :] = got_ref[k, at : at + h, :].astype(F32)
            at, base = at + h, base + height
    for ref, places in zip(outs, plan):
        height = ref.shape[0]
        for j, place in enumerate(places):
            ref[:, j * LANE : (j + 1) * LANE] = rows[place : place + height, :]


def finish(sc, got, heights, shapes, plan):
    return pl.pallas_call(
        functools.partial(finish_kernel, heights=heights, plan=plan),
        in_specs=[pl.BlockSpec(memory_space=pltpu.SMEM)] + in_vmem(1),
        out_shape=[jax.ShapeDtypeStruct(shape, F32) for shape in shapes],
        scratch_shapes=[pltpu.VMEM((sum(heights), LANE), F32)],
        compiler_params=params(16),
        name="finish",
        cost_estimate=cost(2),
    )(sc, got)


def local(
    tokens, ln1_gain, ln1_shift, qkv_weight, qkv_bias, out_weight, out_bias, ln2_gain, ln2_shift,
    up_weight, up_bias, down_weight, down_bias, seq_lengths, span_order, cotangent,
):
    nf = lax.axis_size("fsdp")
    nc = lax.axis_size("ctx")
    x, c = tokens[0], cotangent[0]
    spans = x.shape[0] // SPAN
    seqs = seq_lengths.shape[1]
    weights = packed_params(
        qkv_weight, out_weight,
        (ln1_gain, ln1_shift, qkv_bias, out_bias, ln2_gain, ln2_shift, up_bias, down_bias),
    )
    scalars = jnp.concatenate(
        [
            lax.axis_index("fsdp").reshape(1),
            lax.axis_index("ctx").reshape(1),
            (lax.axis_index("ctx") * spans).reshape(1),
            seq_lengths[0],
            span_order[0],
        ]
    ).astype(jnp.int32)
    far_weights = first_gather(weights, "fsdp")
    sums = span_sums(x, nc)
    nsum = lax.all_to_all(sums, "ctx", 0, 0, tiled=True).reshape(nc * spans, D)
    far_weights = after(far_weights, nsum)
    weights = gathered(weights, far_weights, "fsdp")
    up_weight = after(up_weight, far_weights)
    far_up = first_gather(up_weight, "fsdp")
    down_weight = after(down_weight, far_weights)
    far_down = first_gather(down_weight, "fsdp")

    packed, p, att, h1, wqkv, wout, vec, tabs = attend(
        scalars, x, span_order, nsum, weights, seqs
    )
    up = gathered(up_weight, after(far_up, att), "fsdp")
    r1, h2 = proj(x, att, wout, vec)
    g, gp, wup = ffn_up(scalars, h2, vec, up)
    down = gathered(down_weight, after(far_down, g), "fsdp")
    dsend, dkeep = down_gradient(scalars, g, c, nf)
    gp = after(gp, dkeep)
    dh2, dub, usend, ukeep = ffn_down(scalars, h2, c, gp, wup, down)
    bits = ctx_bits()
    near = [("fsdp", 1 << k) for k in range(1, nf.bit_length() - 1)]

    from_down = Part(scalars, dkeep, dsend)
    from_down.step(*near[0])
    dh2 = after(dh2, from_down.keep)
    dr1, da, gout, gvec = mid(c, dh2, r1, att, wout, vec)
    from_up = Part(scalars, ukeep, usend)
    from_up.step("ctx", bits[0])
    da = after(da, from_up.keep)
    fixed = (x, da, h1, packed, p, tabs, wqkv, vec, nsum)
    dh1, sums, fsend0, fkeep0, send, keep = back(scalars, *fixed, (gout,), 0, nf, nc)
    first = Part(scalars, keep, send)
    from_down.step("ctx", bits[0])
    from_up.step(*near[0])
    dh1 = after(dh1, from_down.keep, from_up.keep)
    dh1, _, fsend1, fkeep1, send, keep = back(
        scalars, *fixed, (dub, gvec, dh1, sums), 1, nf, nc
    )
    second = Part(scalars, keep, send)
    first.step(*near[0])
    second.step("ctx", bits[0])
    first.step("ctx", bits[0])
    second.step(*near[0])
    far = [(k, swap(t, "ctx", bits[0])) for k, t in ((fkeep0, fsend0), (fkeep1, fsend1))]

    block = D // nf
    height, width = down_weight.shape[0], up_weight.shape[1]
    feed = (from_down.total, from_up.total)
    (own,) = ctx_sum(scalars, [from_down, from_up])
    grad_down, grad_up = finish(
        scalars,
        over_ctx(own),
        feed,
        [(height, D), (block, width)],
        [
            [height * j for j in range(D // LANE)],
            [feed[0] + block * j for j in range(width // LANE)],
        ],
    )

    own, own_span = ctx_sum(scalars, [first, second], far)
    tokens_grad = first_back(x, dr1, dh1, own_span, wqkv, vec)
    mixed = block_output(scalars, r1, after(g, first.keep), vec, down)
    half = PAIRS // 2
    plan = [
        [
            p // half * first.total + block * (t * half + p % half)
            for t in range(3)
            for p in range(PAIRS)
        ],
        [block * (3 * half + j) for j in range(D // LANE)],
    ]
    shapes = [(block, 3 * D), (block, D)]
    at = first.total + 3 * half * block
    for wide in (block, block, 3 * block, block, block, block, 4 * block, block):
        shapes.append((1, wide))
        plan.append([at + j for j in range(wide // LANE)])
        at += wide // LANE
    grad_qkv, grad_out, *vectors = finish(
        scalars, over_ctx(own), (first.total, second.total), shapes, plan
    )
    g1, s1, qb, ob, g2, s2, ub, db = (v.reshape(-1) for v in vectors)
    return (
        mixed[None], tokens_grad[None], g1, s1, grad_qkv, qb, grad_out, ob, g2, s2,
        grad_up, ub, grad_down, db,
    )


def solution(mesh):
    rows, one, two = P("fsdp", "ctx", None), P("fsdp"), P("fsdp", None)
    return jax.shard_map(
        local,
        mesh=mesh,
        in_specs=(
            rows, one, one, two, one, two, one, one, one, two, one, two, one, two, two, rows,
        ),
        out_specs=(rows, rows, one, one, two, one, two, one, one, one, two, one, two, one),
        check_vma=False,
    )
```

time: 264 us -> 169 us (0.64)
  waiting for transfers between devices: 104 us -> 46.1 us
  local copies, waits for them, and re-layouts: 21.2 us -> 0.1 us
  starting transfers between devices: 45 us -> 37 us
  other arithmetic: 8.04 us -> 0.78 us
    all_to_all x8 -> x1, waiting for transfers between devices: 71.2 us -> 7.26 us  [local(): nsum = lax.all_to_all(sums, 'ctx', 0, 0, tiled=True).reshape(nc * spans, D)]
    all_to_all x8 -> x1, starting transfers between devices: 32.9 us -> 5.81 us  [local(): nsum = lax.all_to_all(sums, 'ctx', 0, 0, tiled=True).reshape(nc * spans, D)]
    ppermute x21 -> x33, starting transfers between devices: 12.1 us -> 31.2 us  [swap(): return lax.ppermute(array, axis, [(k, k ^ bit) for k in range(n)])]
    unnamed x50 -> x14, local copies, waits for them, and re-layouts: 12.6 us -> 0.03 us
    ppermute x21 -> x33, waiting for transfers between devices: 32.4 us -> 38.9 us  [swap(): return lax.ppermute(array, axis, [(k, k ^ bit) for k in range(n)])]
    convert_element_type x7 -> x0, other arithmetic: 6.39 us -> none  [the longest x6 6.28 us: add_low(): return (a.astype(F32) + b.astype(F32)).astype(BF16)]
    slice x8 -> x0, local copies, waits for them, and re-layouts: 3.47 us -> none  [the longest x3 1.7 us: to_owner(): keep, send = (keep[0::2], keep[1::2])]
    pallas_call x7 -> x28, Pallas kernels: 84.1 us -> 83.3 us  [the longest x23 70.2 us: resident(): pl.pallas_call(kernel, in_specs=[pl.BlockSpec(memory_space=pltpu.SMEM)] *...]
  transfers between devices with their start and end apart: 29 -> 34, of which waited for: 13 -> 15; matrix products, arithmetic and copies ran while one was open for 7% -> 0% of each run, Pallas kernels for 32% -> 47%
where the time goes in v2:
time: 169 us; the launch traced here: 168 us
  Pallas kernels  83.3 us (49%)
  waiting for transfers between devices  46.1 us (27%)
  starting transfers between devices  37 us (22%)
    pallas_call x23, Pallas kernels, resident(): pl.pallas_call(kernel, in_specs=[pl.BlockSpec(memory_space=pltpu.SMEM)] *...  70.2 us
    ppermute x33, waiting for transfers between devices, swap(): return lax.ppermute(array, axis, [(k, k ^ bit) for k in range(n)])  38.9 us
    ppermute x33, starting transfers between devices, swap(): return lax.ppermute(array, axis, [(k, k ^ bit) for k in range(n)])  31.2 us
    all_to_all x1, waiting for transfers between devices, local(): nsum = lax.all_to_all(sums, 'ctx', 0, 0, tiled=True).reshape(nc * spans, D)  7.26 us
    all_to_all x1, starting transfers between devices, local(): nsum = lax.all_to_all(sums, 'ctx', 0, 0, tiled=True).reshape(nc * spans, D)  5.81 us
    pallas_call x1, Pallas kernels, block_output(): pl.pallas_call(mixed_kernel, grid=(rows // ROWS,), in_specs=[pl.BlockSpec...  4.13 us
    pallas_call x2, Pallas kernels, finish(): pl.pallas_call(functools.partial(finish_kernel, heights=heights, plan=pla...  3.78 us
  transfers between devices with their start and end apart: 34, of which 15 were waited for; matrix products, arithmetic and copies ran while one was open for 0% of the time, Pallas kernels for 47%

profile of v2, /device:TPU:0, one launch (start us, length us, event | category | flops | bytes accessed | tf_op | source)
XLA Modules:
  0.0 168.3 jit_solution(6832548915362517247)
XLA Ops:
  0.7 2.1 %pack.1.refs_0_ = bf16[144,2048]{1,0:T(8,128)(2,1)} custom-call(bf16[128,1536]{1,0:T(8,128)(2,1)} %qkv_ref.1, bf16[128,512]{1,0:T(8,128)(2,1)} %out_ref.1, bf16[1,128]{1,0:T(2,128)(2,1)} %bitcast.109, bf16[1,128]{1,0:T(2,128)(2,1)} %bitcast.110, bf16[3,128]{1,0:T(4,128)(2,1)} %bitcast.107, bf16[1,128]{1,0:T(2,128)(2,1)} %bitcast.111, ...), custom_call_target="tpu_custom_call" | custom-call | flops 1000000000 | bytes 1000000 | tf_op jit(solution)/shard_map/pack/pallas_call | solution.py:124
  2.7 3.0 %collective-permute-start.1 = (bf16[144,2048]{1,0:T(8,128)(2,1)}, bf16[144,2048]{1,0:T(8,128)(2,1)S(1)}, u32[]{:S(2)}, u32[]{:S(2)}) collective-permute-start(bf16[144,2048]{1,0:T(8,128)(2,1)} %pack.1.refs_0_), channel_id=1, source_target_pairs={{0,2},{1,3},{2,0},{3,1},{4,6},{5,7},{6,4},{7,5},{8,10},{9,11},{10,... | collective-permute-start | bytes 1769480 | tf_op jit(solution)/shard_map/ppermute | solution.py:614
  7.1 5.8 %all-to-all-start = ((f32[8,8,512]{2,1,0:T(8,128)}), f32[8,8,512]{2,1,0:T(8,128)S(1)}, u32[]{:S(2)}, u32[]{:S(2)}) async-start(f32[8,8,512]{2,1,0:T(8,128)} %span_sums.1), calls=%async_computation | async-start | bytes 262144 | tf_op jit(solution)/shard_map/all_to_all | solution.py:810
  13.0 7.3 %all-to-all-done = f32[8,8,512]{2,1,0:T(8,128)S(1)} async-done(((f32[8,8,512]{2,1,0:T(8,128)}), f32[8,8,512]{2,1,0:T(8,128)S(1)}, u32[]{:S(2)}, u32[]{:S(2)}) %all-to-all-start) | async-done | bytes 131104 | tf_op jit(solution)/shard_map/all_to_all | solution.py:810
  22.3 9.5 %attend.1 = (bf16[1024,1536]{1,0:T(8,128)(2,1)S(1)}, bf16[32,256,192]{2,1,0:T(8,128)(2,1)S(1)}, bf16[1024,512]{1,0:T(8,128)(2,1)S(1)}, bf16[1024,512]{1,0:T(8,12...) custom-call(s32[76]{0:T(128)S(1)} %concatenate.25.sc, ...), custom_call_target="tpu_custom_call" | custom-call | flops 12000000000 | bytes 12000000 | tf_op jit(solution)/shard_map/attend/pallas_call | solution.py:68
  31.7 3.2 %collective-permute-done.4.refs_2_ = bf16[128,2048]{1,0:T(8,128)(2,1)S(1)} collective-permute-done((bf16[128,2048]{1,0:T(8,128)(2,1)}, bf16[128,2048]{1,0:T(8,128)(2,1)S(1)}, u32[]{:S(2)}, u32[]{:S(2)}) %collective-permute-start.4) | collective-permute-done | bytes 524320 | tf_op jit(solution)/shard_map/ppermute | solution.py:614
  35.9 1.9 %proj.1 = (f32[1024,512]{1,0:T(8,128)S(1)}, bf16[1024,512]{1,0:T(8,128)(2,1)S(1)}) custom-call(bf16[1024,512]{1,0:T(8,128)(2,1)S(1)} %bitcast.70, bf16[1024,512]{1,0:T(8,128)(2,1)S(1)} %get-tuple-element.97.att_ref, bf16[512,512]{1,0:T(8,128)(2,1)S(1)} %get-tuple-element.98.wout, f32[8,2048]{1,0:T(8,128)S(1)} %get-tuple-element.99.vec.vec_ref), custom_call_target="tpu_custom_call" | custom-call | flops 3000000000 | bytes 3000000 | tf_op jit(solution)/shard_map/proj/pallas_call | solution.py:68
  37.8 9.2 %ffn_up.1 = (bf16[1024,2048]{1,0:T(8,128)(2,1)S(1)}, bf16[1024,2048]{1,0:T(8,128)(2,1)S(1)}, bf16[512,2048]{1,0:T(8,128)(2,1)S(1)}) custom-call(s32[76]{0:T(128)S(1)} %concatenate.25.sc, bf16[1024,512]{1,0:T(8,128)(2,1)S(1)} %get-tuple-element.101.h2_ref, f32[8,2048]{1,0:T(8,128)S(1)} %get-tuple-element.99.vec.vec_ref, bf16[128,2048]{1,0:T(8,128)(2,1)S(1)} %copy-done.4, ...), custom_call_target="tpu_custom_call" | custom-call | flops 8000000000 | bytes 8000000 | tf_op jit(solution)/shard_map/ffn_up/pallas_call | solution.py:68
  47.1 2.2 %collective-permute-done.7.refs_2_ = bf16[512,512]{1,0:T(8,128)(2,1)S(1)} collective-permute-done((bf16[512,512]{1,0:T(8,128)(2,1)S(1)}, bf16[512,512]{1,0:T(8,128)(2,1)S(1)}, u32[]{:S(2)}, u32[]{:S(2)}) %collective-permute-start.7) | collective-permute-done | bytes 524320 | tf_op jit(solution)/shard_map/ppermute | solution.py:614
  49.3 2.9 %down_grad.1 = (bf16[2,2048,128]{2,1,0:T(8,128)(2,1)S(1)}, bf16[2,2048,128]{2,1,0:T(8,128)(2,1)S(1)}) custom-call(s32[76]{0:T(128)S(1)} %concatenate.25.sc, bf16[1024,2048]{1,0:T(8,128)(2,1)S(1)} %get-tuple-element.131.g_ref, bf16[1024,512]{1,0:T(8,128)(2,1)S(1)} %bitcast.65), custom_call_target="tpu_custom_call" | custom-call | flops 4000000000 | bytes 4000000 | tf_op jit(solution)/shard_map/down_grad/pallas_call | solution.py:68
  52.8 12.9 %ffn_down.1 = (f32[1024,512]{1,0:T(8,128)S(1)}, f32[1,2048]{1,0:T(1,128)S(1)}, bf16[2,2048,128]{2,1,0:T(8,128)(2,1)S(1)}, bf16[2,2048,128]{2,1,0:T(8,128)(2,1)S(1)}) custom-call(s32[76]{0:T(128)S(1)} %concatenate.25.sc, bf16[1024,512]{1,0:T(8,128)(2,1)S(1)} %get-tuple-element.101.h2_ref, bf16[1024,512]{1,0:T(8,128)(2,1)S(1)} %bitcast.66, ...), custom_call_target="tpu_custom_call" | custom-call | flops 8000000000 | bytes 8000000 | tf_op jit(solution)/shard_map/ffn_down/pallas_call | solution.py:68
  67.4 3.7 %mid.1 = (f32[1024,512]{1,0:T(8,128)S(1)}, bf16[1024,512]{1,0:T(8,128)(2,1)S(1)}, f32[512,512]{1,0:T(8,128)S(1)}, f32[8,512]{1,0:T(8,128)S(1)}) custom-call(bf16[1024,512]{1,0:T(8,128)(2,1)S(1)} %bitcast.67, f32[1024,512]{1,0:T(8,128)S(1)} %get-tuple-element.114.dh2_ref, f32[1024,512]{1,0:T(8,128)S(1)} %get-tuple-element.100.r1_ref, ...), custom_call_target="tpu_custom_call" | custom-call | flops 5000000000 | bytes 5000000 | tf_op jit(solution)/shard_map/mid/pallas_call | solution.py:68
  73.4 10.1 %back_0.1 = (f32[1024,512]{1,0:T(8,128)S(1)}, f32[72,512]{1,0:T(8,128)S(1)}, bf16[128,128]{1,0:T(8,128)(2,1)S(1)}, bf16[128,128]{1,0:T(8,128)(2,1)S(1)}, bf16[2,...) custom-call(s32[76]{0:T(128)S(1)} %concatenate.25.sc, bf16[1024,512]{1,0:T(8,128)(2,1)S(1)} %bitcast.71, ...), custom_call_target="tpu_custom_call" | custom-call | flops 8999999488 | bytes 9000000 | tf_op jit(solution)/shard_map/back_0/pallas_call | solution.py:68
  84.2 1.7 %collective-permute-done.14 = bf16[2,1024,128]{2,1,0:T(8,128)(2,1)S(1)} collective-permute-done((bf16[2,1024,128]{2,1,0:T(8,128)(2,1)S(1)}, bf16[2,1024,128]{2,1,0:T(8,128)(2,1)S(1)}, u32[]{:S(2)}, u32[]{:S(2)}) %collective-permute-start.14) | collective-permute-done | bytes 524320 | tf_op jit(solution)/shard_map/ppermute | solution.py:614
  86.6 10.6 %back_1.1 = (f32[1024,512]{1,0:T(8,128)S(1)}, f32[72,512]{1,0:T(8,128)}, bf16[128,128]{1,0:T(8,128)(2,1)S(1)}, bf16[128,128]{1,0:T(8,128)(2,1)S(1)}, bf16[2,896,...) custom-call(s32[76]{0:T(128)S(1)} %concatenate.25.sc, bf16[1024,512]{1,0:T(8,128)(2,1)S(1)} %bitcast.72, ...), custom_call_target="tpu_custom_call" | custom-call | flops 8999999488 | bytes 9000000 | tf_op jit(solution)/shard_map/back_1/pallas_call | solution.py:68
  102.8 3.6 %collective-permute-done.26 = bf16[1,1024,128]{2,1,0:T(8,128)(2,1)S(1)} collective-permute-done((bf16[1,1024,128]{2,1,0:T(8,128)(2,1)S(1)}, bf16[1,1024,128]{2,1,0:T(8,128)(2,1)S(1)}, u32[]{:S(2)}, u32[]{:S(2)}) %collective-permute-start.26) | collective-permute-done | bytes 262176 | tf_op jit(solution)/shard_map/ppermute | solution.py:614
  108.5 1.6 collective-permute-start.28
  110.2 4.0 %collective-permute-done.12 = bf16[1,1280,128]{2,1,0:T(8,128)(2,1)S(1)} collective-permute-done((bf16[1,1280,128]{2,1,0:T(8,128)(2,1)S(1)}, bf16[1,1280,128]{2,1,0:T(8,128)(2,1)S(1)}, u32[]{:S(2)}, u32[]{:S(2)}) %collective-permute-start.12) | collective-permute-done | bytes 327712 | tf_op jit(solution)/shard_map/ppermute | solution.py:614
  120.0 1.8 %collective-permute-start.29 = (bf16[512,128]{1,0:T(8,128)(2,1)S(1)}, bf16[512,128]{1,0:T(8,128)(2,1)S(1)}, u32[]{:S(2)}, u32[]{:S(2)}) collective-permute-start(bf16[512,128]{1,0:T(8,128)(2,1)S(1)} %get-tuple-element.173), channel_id=1, source_target_pairs={{0,16},{4,20},{8,24},{12,28},{16,0},{20,4},{24,8},{28,12},{1,17},{... | collective-permute-start | bytes 393224 | tf_op jit(solution)/shard_map/ppermute | solution.py:614
  122.6 1.6 collective-permute-start.21
  124.3 3.3 %collective-permute-done.29.got_ref = bf16[512,128]{1,0:T(8,128)(2,1)S(1)} collective-permute-done((bf16[512,128]{1,0:T(8,128)(2,1)S(1)}, bf16[512,128]{1,0:T(8,128)(2,1)S(1)}, u32[]{:S(2)}, u32[]{:S(2)}) %collective-permute-start.29) | collective-permute-done | bytes 131104 | tf_op jit(solution)/shard_map/ppermute | solution.py:614
  129.3 1.9 %collective-permute-done.21.got_ref = bf16[672,128]{1,0:T(8,128)(2,1)S(1)} collective-permute-done((bf16[672,128]{1,0:T(8,128)(2,1)S(1)}, bf16[672,128]{1,0:T(8,128)(2,1)S(1)}, u32[]{:S(2)}, u32[]{:S(2)}) %collective-permute-start.21) | collective-permute-done | bytes 172064 | tf_op jit(solution)/shard_map/ppermute | solution.py:614
  132.7 4.0 %collective-permute-done.30 = bf16[512,128]{1,0:T(8,128)(2,1)S(1)} collective-permute-done((bf16[512,128]{1,0:T(8,128)(2,1)S(1)}, bf16[512,128]{1,0:T(8,128)(2,1)S(1)}, u32[]{:S(2)}, u32[]{:S(2)}) %collective-permute-start.30) | collective-permute-done | bytes 131104 | tf_op jit(solution)/shard_map/ppermute | solution.py:614
  138.4 2.2 %collective-permute-start.23 = (bf16[272,128]{1,0:T(8,128)(2,1)S(1)}, bf16[272,128]{1,0:T(8,128)(2,1)S(1)}, u32[]{:S(2)}, u32[]{:S(2)}) collective-permute-start(bf16[272,128]{1,0:T(8,128)(2,1)S(1)} %get-tuple-element.159), channel_id=1, source_target_pairs={{0,16},{4,20},{8,24},{12,28},{16,0},{20,4},{24,8},{28,12},{1,17},{... | collective-permute-start | bytes 208904 | tf_op jit(solution)/shard_map/ppermute | solution.py:614
  140.7 4.1 %block_output.1 = bf16[1024,512]{1,0:T(8,128)(2,1)} custom-call(s32[76]{0:T(128)S(1)} %concatenate.25.sc, f32[1024,512]{1,0:T(8,128)S(1)} %get-tuple-element.100.r1_ref, bf16[1024,2048]{1,0:T(8,128)(2,1)S(1)} %get-tuple-element.131.g_ref, f32[8,2048]{1,0:T(8,128)S(1)} %get-tuple-element.99.vec.vec_ref, bf16[512,512]{1,0:T(8,128)(2,1)S(1)} %copy-done.5, ...), custom_call_target="tpu_custom_call" | custom-call | flops 4000000000 | bytes 4000000 | tf_op jit(solution)/shard_map/block_output/pallas_call | solution.py:600
  145.9 2.0 %collective-permute-start.32 = (bf16[2048,128]{1,0:T(8,128)(2,1)S(1)}, bf16[2048,128]{1,0:T(8,128)(2,1)S(1)}, u32[]{:S(2)}, u32[]{:S(2)}) collective-permute-start(bf16[2048,128]{1,0:T(8,128)(2,1)S(1)} %pad_maximum_fusion.2), channel_id=1, source_target_pairs={{0,4},{4,0},{8,12},{12,8},{16,20},{20,16},{24,28},{28,24},{1,5},{5... | collective-permute-start | bytes 1572872 | tf_op jit(solution)/shard_map/ppermute | solution.py:614
  147.9 2.0 %collective-permute-done.24 = bf16[544,128]{1,0:T(8,128)(2,1)S(1)} collective-permute-done((bf16[544,128]{1,0:T(8,128)(2,1)S(1)}, bf16[544,128]{1,0:T(8,128)(2,1)S(1)}, u32[]{:S(2)}, u32[]{:S(2)}) %collective-permute-start.24) | collective-permute-done | bytes 139296 | tf_op jit(solution)/shard_map/ppermute | solution.py:614
  150.0 1.8 %collective-permute-start.25 = (bf16[1088,128]{1,0:T(8,128)(2,1)S(1)}, bf16[1088,128]{1,0:T(8,128)(2,1)S(1)}, u32[]{:S(2)}, u32[]{:S(2)}) collective-permute-start(bf16[1088,128]{1,0:T(8,128)(2,1)S(1)} %pad_maximum_fusion.3), channel_id=1, source_target_pairs={{0,4},{4,0},{8,12},{12,8},{16,20},{20,16},{24,28},{28,24},{1,5},{5... | collective-permute-start | bytes 835592 | tf_op jit(solution)/shard_map/ppermute | solution.py:614
  151.8 3.1 %first_back.1 = f32[1024,512]{1,0:T(8,128)} custom-call(bf16[1024,512]{1,0:T(8,128)(2,1)S(1)} %bitcast.73, f32[1024,512]{1,0:T(8,128)S(1)} %get-tuple-element.132.dr1_ref, f32[1024,512]{1,0:T(8,128)S(1)} %get-tuple-element.142.dh1_ref, bf16[64,128]{1,0:T(8,128)(2,1)S(1)} %get-tuple-element.158.own_ref, bf16[512,1536]{1,0:T(8,128)(2,1)S(1)} %get-tuple-element.124.wqkv, ...), custom_call_target="tpu_custom_call" | custom-call | flops 3000000000 | bytes 3000000 | tf_op jit(solution)/shard_map/first_back/pallas_call | solution.py:574
  154.9 8.9 %collective-permute-done.25 = bf16[1088,128]{1,0:T(8,128)(2,1)S(1)} collective-permute-done((bf16[1088,128]{1,0:T(8,128)(2,1)S(1)}, bf16[1088,128]{1,0:T(8,128)(2,1)S(1)}, u32[]{:S(2)}, u32[]{:S(2)}) %collective-permute-start.25) | collective-permute-done | bytes 278560 | tf_op jit(solution)/shard_map/ppermute | solution.py:614
  163.8 1.6 finish.2
  166.2 2.1 %finish.3 = (f32[512,512]{1,0:T(8,128)}, f32[128,2048]{1,0:T(8,128)}) custom-call(s32[76]{0:T(128)S(1)} %concatenate.25.sc, bf16[8,512,128]{2,1,0:T(8,128)(2,1)S(1)} %bitcast.59), custom_call_target="tpu_custom_call" | custom-call | flops 2000000000 | bytes 2000000 | tf_op jit(solution)/shard_map/finish/pallas_call | solution.py:775
  (86 shorter events, 31.3 us)
Async XLA Ops:
  2.7 17.5 %collective-permute-start.1 = (bf16[144,2048]{1,0:T(8,128)(2,1)}, bf16[144,2048]{1,0:T(8,128)(2,1)S(1)}, u32[]{:S(2)}, u32[]{:S(2)}) collective-permute-start(bf16[144,2048]{1,0:T(8,128)(2,1)} %pack.1.refs_0_), channel_id=1, source_target_pairs={{0,2},{1,3},{2,0},{3,1},{4,6},{5,7},{6,4},{7,5},{8,10},{9,11},{10,... | collective-permute-start | bytes 1769480 | tf_op jit(solution)/shard_map/ppermute | solution.py:614
  7.1 13.1 %all-to-all-start = ((f32[8,8,512]{2,1,0:T(8,128)}), f32[8,8,512]{2,1,0:T(8,128)S(1)}, u32[]{:S(2)}, u32[]{:S(2)}) async-start(f32[8,8,512]{2,1,0:T(8,128)} %span_sums.1), calls=%async_computation | async-start | bytes 262144 | tf_op jit(solution)/shard_map/all_to_all | solution.py:810
  12.9 8.4 %collective-permute-start = (bf16[144,2048]{1,0:T(8,128)(2,1)S(1)}, bf16[144,2048]{1,0:T(8,128)(2,1)S(1)}, u32[]{:S(2)}, u32[]{:S(2)}) collective-permute-start(bf16[144,2048]{1,0:T(8,128)(2,1)S(1)} %copy-done.3), channel_id=1, source_target_pairs={{0,1},{1,0},{2,3},{3,2},{4,5},{5,4},{6,7},{7,6},{8,9},{9,8},{10,11... | collective-permute-start | bytes 1769480 | tf_op jit(solution)/shard_map/ppermute | solution.py:614
  20.4 14.6 %collective-permute-start.4 = (bf16[128,2048]{1,0:T(8,128)(2,1)}, bf16[128,2048]{1,0:T(8,128)(2,1)S(1)}, u32[]{:S(2)}, u32[]{:S(2)}) collective-permute-start(bf16[128,2048]{1,0:T(8,128)(2,1)} %refs_0_), channel_id=1, source_target_pairs={{0,2},{1,3},{2,0},{3,1},{4,6},{5,7},{6,4},{7,5},{8,10},{9,11},{10,... | collective-permute-start | bytes 1572872 | tf_op jit(solution)/shard_map/ppermute | solution.py:614
  21.1 16.7 %collective-permute-start.3 = (bf16[128,2048]{1,0:T(8,128)(2,1)}, bf16[128,2048]{1,0:T(8,128)(2,1)S(1)}, u32[]{:S(2)}, u32[]{:S(2)}) collective-permute-start(bf16[128,2048]{1,0:T(8,128)(2,1)} %refs_0_), channel_id=1, source_target_pairs={{0,1},{1,0},{2,3},{3,2},{4,5},{5,4},{6,7},{7,6},{8,9},{9,8},{10,11... | collective-permute-start | bytes 1572872 | tf_op jit(solution)/shard_map/ppermute | solution.py:614
  34.9 14.3 %collective-permute-start.7 = (bf16[512,512]{1,0:T(8,128)(2,1)S(1)}, bf16[512,512]{1,0:T(8,128)(2,1)S(1)}, u32[]{:S(2)}, u32[]{:S(2)}) collective-permute-start(bf16[512,512]{1,0:T(8,128)(2,1)S(1)} %copy-done.5), channel_id=1, source_target_pairs={{0,2},{1,3},{2,0},{3,1},{4,6},{5,7},{6,4},{7,5},{8,10},{9,11},{10,... | collective-permute-start | bytes 1572872 | tf_op jit(solution)/shard_map/ppermute | solution.py:614
  35.6 17.1 %collective-permute-start.6 = (bf16[512,512]{1,0:T(8,128)(2,1)S(1)}, bf16[512,512]{1,0:T(8,128)(2,1)S(1)}, u32[]{:S(2)}, u32[]{:S(2)}) collective-permute-start(bf16[512,512]{1,0:T(8,128)(2,1)S(1)} %copy-done.5), channel_id=1, source_target_pairs={{0,1},{1,0},{2,3},{3,2},{4,5},{5,4},{6,7},{7,6},{8,9},{9,8},{10,11... | collective-permute-start | bytes 1572872 | tf_op jit(solution)/shard_map/ppermute | solution.py:614
  49.2 3.5 %collective-permute-start.8 = (bf16[512,512]{1,0:T(8,128)(2,1)S(1)}, bf16[512,512]{1,0:T(8,128)(2,1)S(1)}, u32[]{:S(2)}, u32[]{:S(2)}) collective-permute-start(bf16[512,512]{1,0:T(8,128)(2,1)S(1)} %collective-permute-done.7.refs_2_), channel_id=1, source_target_pairs={{0,1},{1,0},{2,3},{3,2},{4,5},{5,4},{6,7},{7,6},{8,9},{9,8},{10,11... | collective-permute-start | bytes 1572872 | tf_op jit(solution)/shard_map/ppermute | solution.py:614
  52.2 13.6 %collective-permute-start.9 = (bf16[2,2048,128]{2,1,0:T(8,128)(2,1)S(1)}, bf16[2,2048,128]{2,1,0:T(8,128)(2,1)S(1)}, u32[]{:S(2)}, u32[]{:S(2)}) collective-permute-start(bf16[2,2048,128]{2,1,0:T(8,128)(2,1)S(1)} %get-tuple-element.112), channel_id=1, source_target_pairs={{0,1},{1,0},{2,3},{3,2},{4,5},{5,4},{6,7},{7,6},{8,9},{9,8},{10,11... | collective-permute-start | bytes 3145736 | tf_op jit(solution)/shard_map/ppermute | solution.py:614
  65.7 5.4 %collective-permute-start.10 = (bf16[2,2048,128]{2,1,0:T(8,128)(2,1)S(1)}, bf16[2,2048,128]{2,1,0:T(8,128)(2,1)S(1)}, u32[]{:S(2)}, u32[]{:S(2)}) collective-permute-start(bf16[2,2048,128]{2,1,0:T(8,128)(2,1)S(1)} %get-tuple-element.117), channel_id=1, source_target_pairs={{0,1},{1,0},{2,3},{3,2},{4,5},{5,4},{6,7},{7,6},{8,9},{9,8},{10,11... | collective-permute-start | bytes 3145736 | tf_op jit(solution)/shard_map/ppermute | solution.py:614
  66.6 17.0 %collective-permute-start.13 = (bf16[1,2048,128]{2,1,0:T(8,128)(2,1)S(1)}, bf16[1,2048,128]{2,1,0:T(8,128)(2,1)S(1)}, u32[]{:S(2)}, u32[]{:S(2)}) collective-permute-start(bf16[1,2048,128]{2,1,0:T(8,128)(2,1)S(1)} %get-tuple-element.136), channel_id=1, source_target_pairs={{0,2},{1,3},{2,0},{3,1},{4,6},{5,7},{6,4},{7,5},{8,10},{9,11},{10,... | collective-permute-start | bytes 1572872 | tf_op jit(solution)/shard_map/ppermute | solution.py:614
  71.9 14.1 %collective-permute-start.14 = (bf16[2,1024,128]{2,1,0:T(8,128)(2,1)S(1)}, bf16[2,1024,128]{2,1,0:T(8,128)(2,1)S(1)}, u32[]{:S(2)}, u32[]{:S(2)}) collective-permute-start(bf16[2,1024,128]{2,1,0:T(8,128)(2,1)S(1)} %get-tuple-element.138), channel_id=1, source_target_pairs={{0,4},{4,0},{8,12},{12,8},{16,20},{20,16},{24,28},{28,24},{1,5},{5... | collective-permute-start | bytes 1572872 | tf_op jit(solution)/shard_map/ppermute | solution.py:614
  83.4 15.8 %collective-permute-start.11 = (bf16[2,1280,128]{2,1,0:T(8,128)(2,1)S(1)}, bf16[2,1280,128]{2,1,0:T(8,128)(2,1)S(1)}, u32[]{:S(2)}, u32[]{:S(2)}) collective-permute-start(bf16[2,1280,128]{2,1,0:T(8,128)(2,1)S(1)} %get-tuple-element.127), channel_id=1, source_target_pairs={{0,1},{1,0},{2,3},{3,2},{4,5},{5,4},{6,7},{7,6},{8,9},{9,8},{10,11... | collective-permute-start | bytes 1966088 | tf_op jit(solution)/shard_map/ppermute | solution.py:614
  97.2 4.3 %collective-permute-start.16 = (bf16[2,896,128]{2,1,0:T(8,128)(2,1)S(1)}, bf16[2,896,128]{2,1,0:T(8,128)(2,1)S(1)}, u32[]{:S(2)}, u32[]{:S(2)}) collective-permute-start(bf16[2,896,128]{2,1,0:T(8,128)(2,1)S(1)} %get-tuple-element.145), channel_id=1, source_target_pairs={{0,1},{1,0},{2,3},{3,2},{4,5},{5,4},{6,7},{7,6},{8,9},{9,8},{10,11... | collective-permute-start | bytes 1376264 | tf_op jit(solution)/shard_map/ppermute | solution.py:614
  97.2 9.1 %collective-permute-start.26 = (bf16[1,1024,128]{2,1,0:T(8,128)(2,1)S(1)}, bf16[1,1024,128]{2,1,0:T(8,128)(2,1)S(1)}, u32[]{:S(2)}, u32[]{:S(2)}) collective-permute-start(bf16[1,1024,128]{2,1,0:T(8,128)(2,1)S(1)} %get-tuple-element.168), channel_id=1, source_target_pairs={{0,4},{4,0},{8,12},{12,8},{16,20},{20,16},{24,28},{28,24},{1,5},{5... | collective-permute-start | bytes 786440 | tf_op jit(solution)/shard_map/ppermute | solution.py:614
  98.7 9.1 %collective-permute-start.27 = (bf16[1,1024,128]{2,1,0:T(8,128)(2,1)S(1)}, bf16[1,1024,128]{2,1,0:T(8,128)(2,1)S(1)}, u32[]{:S(2)}, u32[]{:S(2)}) collective-permute-start(bf16[1,1024,128]{2,1,0:T(8,128)(2,1)S(1)} %get-tuple-element.169), channel_id=1, source_target_pairs={{0,2},{1,3},{2,0},{3,1},{4,6},{5,7},{6,4},{7,5},{8,10},{9,11},{10,... | collective-permute-start | bytes 786440 | tf_op jit(solution)/shard_map/ppermute | solution.py:614
  99.9 14.3 %collective-permute-start.12 = (bf16[1,1280,128]{2,1,0:T(8,128)(2,1)S(1)}, bf16[1,1280,128]{2,1,0:T(8,128)(2,1)S(1)}, u32[]{:S(2)}, u32[]{:S(2)}) collective-permute-start(bf16[1,1280,128]{2,1,0:T(8,128)(2,1)S(1)} %get-tuple-element.129), channel_id=1, source_target_pairs={{0,2},{1,3},{2,0},{3,1},{4,6},{5,7},{6,4},{7,5},{8,10},{9,11},{10,... | collective-permute-start | bytes 983048 | tf_op jit(solution)/shard_map/ppermute | solution.py:614
  102.2 13.2 %collective-permute-start.17 = (bf16[2,448,128]{2,1,0:T(8,128)(2,1)S(1)}, bf16[2,448,128]{2,1,0:T(8,128)(2,1)S(1)}, u32[]{:S(2)}, u32[]{:S(2)}) collective-permute-start(bf16[2,448,128]{2,1,0:T(8,128)(2,1)S(1)} %get-tuple-element.147), channel_id=1, source_target_pairs={{0,4},{4,0},{8,12},{12,8},{16,20},{20,16},{24,28},{28,24},{1,5},{5... | collective-permute-start | bytes 688136 | tf_op jit(solution)/shard_map/ppermute | solution.py:614
  108.5 10.9 %collective-permute-start.28 = (bf16[1024,128]{1,0:T(8,128)(2,1)S(1)}, bf16[1024,128]{1,0:T(8,128)(2,1)S(1)}, u32[]{:S(2)}, u32[]{:S(2)}) collective-permute-start(bf16[1024,128]{1,0:T(8,128)(2,1)S(1)} %bitcast.81), channel_id=1, source_target_pairs={{0,8},{4,12},{8,0},{12,4},{16,24},{20,28},{24,16},{28,20},{1,9},{5... | collective-permute-start | bytes 786440 | tf_op jit(solution)/shard_map/ppermute | solution.py:614
  114.8 7.2 %collective-permute-start.15 = (bf16[1,640,128]{2,1,0:T(8,128)(2,1)S(1)}, bf16[1,640,128]{2,1,0:T(8,128)(2,1)S(1)}, u32[]{:S(2)}, u32[]{:S(2)}) collective-permute-start(bf16[1,640,128]{2,1,0:T(8,128)(2,1)S(1)} %get-tuple-element.143), channel_id=1, source_target_pairs={{0,4},{4,0},{8,12},{12,8},{16,20},{20,16},{24,28},{28,24},{1,5},{5... | collective-permute-start | bytes 491528 | tf_op jit(solution)/shard_map/ppermute | solution.py:614
  116.0 6.0 %collective-permute-start.18 = (bf16[1,448,128]{2,1,0:T(8,128)(2,1)S(1)}, bf16[1,448,128]{2,1,0:T(8,128)(2,1)S(1)}, u32[]{:S(2)}, u32[]{:S(2)}) collective-permute-start(bf16[1,448,128]{2,1,0:T(8,128)(2,1)S(1)} %get-tuple-element.149), channel_id=1, source_target_pairs={{0,2},{1,3},{2,0},{3,1},{4,6},{5,7},{6,4},{7,5},{8,10},{9,11},{10,... | collective-permute-start | bytes 344072 | tf_op jit(solution)/shard_map/ppermute | solution.py:614
  117.4 4.5 %collective-permute-start.19 = (bf16[128,128]{1,0:T(8,128)(2,1)S(1)}, bf16[128,128]{1,0:T(8,128)(2,1)S(1)}, u32[]{:S(2)}, u32[]{:S(2)}) collective-permute-start(bf16[128,128]{1,0:T(8,128)(2,1)S(1)} %get-tuple-element.151), channel_id=1, source_target_pairs={{0,4},{4,0},{8,12},{12,8},{16,20},{20,16},{24,28},{28,24},{1,5},{5... | collective-permute-start | bytes 98312 | tf_op jit(solution)/shard_map/ppermute | solution.py:614
  118.1 3.9 %collective-permute-start.20 = (bf16[128,128]{1,0:T(8,128)(2,1)S(1)}, bf16[128,128]{1,0:T(8,128)(2,1)S(1)}, u32[]{:S(2)}, u32[]{:S(2)}) collective-permute-start(bf16[128,128]{1,0:T(8,128)(2,1)S(1)} %get-tuple-element.153), channel_id=1, source_target_pairs={{0,4},{4,0},{8,12},{12,8},{16,20},{20,16},{24,28},{28,24},{1,5},{5... | collective-permute-start | bytes 98312 | tf_op jit(solution)/shard_map/ppermute | solution.py:614
  120.0 7.6 %collective-permute-start.29 = (bf16[512,128]{1,0:T(8,128)(2,1)S(1)}, bf16[512,128]{1,0:T(8,128)(2,1)S(1)}, u32[]{:S(2)}, u32[]{:S(2)}) collective-permute-start(bf16[512,128]{1,0:T(8,128)(2,1)S(1)} %get-tuple-element.173), channel_id=1, source_target_pairs={{0,16},{4,20},{8,24},{12,28},{16,0},{20,4},{24,8},{28,12},{1,17},{... | collective-permute-start | bytes 393224 | tf_op jit(solution)/shard_map/ppermute | solution.py:614
  122.6 8.6 %collective-permute-start.21 = (bf16[672,128]{1,0:T(8,128)(2,1)S(1)}, bf16[672,128]{1,0:T(8,128)(2,1)S(1)}, u32[]{:S(2)}, u32[]{:S(2)}) collective-permute-start(bf16[672,128]{1,0:T(8,128)(2,1)S(1)} %bitcast.85), channel_id=1, source_target_pairs={{0,8},{4,12},{8,0},{12,4},{16,24},{20,28},{24,16},{28,20},{1,9},{5... | collective-permute-start | bytes 516104 | tf_op jit(solution)/shard_map/ppermute | solution.py:614
  127.6 9.2 %collective-permute-start.30 = (bf16[512,128]{1,0:T(8,128)(2,1)S(1)}, bf16[512,128]{1,0:T(8,128)(2,1)S(1)}, u32[]{:S(2)}, u32[]{:S(2)}) collective-permute-start(bf16[512,128]{1,0:T(8,128)(2,1)S(1)} %last.3), channel_id=1, source_target_pairs={{0,16},{4,20},{8,24},{12,28},{16,0},{20,4},{24,8},{28,12},{1,17},{... | collective-permute-start | bytes 393224 | tf_op jit(solution)/shard_map/ppermute | solution.py:614
  131.8 6.6 %collective-permute-start.22 = (bf16[336,128]{1,0:T(8,128)(2,1)S(1)}, bf16[336,128]{1,0:T(8,128)(2,1)S(1)}, u32[]{:S(2)}, u32[]{:S(2)}) collective-permute-start(bf16[336,128]{1,0:T(8,128)(2,1)S(1)} %get-tuple-element.157), channel_id=1, source_target_pairs={{0,16},{4,20},{8,24},{12,28},{16,0},{20,4},{24,8},{28,12},{1,17},{... | collective-permute-start | bytes 258056 | tf_op jit(solution)/shard_map/ppermute | solution.py:614
  136.8 9.0 %collective-permute-start.31 = (bf16[1024,128]{1,0:T(8,128)(2,1)S(1)}, bf16[1024,128]{1,0:T(8,128)(2,1)S(1)}, u32[]{:S(2)}, u32[]{:S(2)}) collective-permute-start(bf16[1024,128]{1,0:T(8,128)(2,1)S(1)} %pad_maximum_fusion.4), channel_id=1, source_target_pairs={{0,8},{4,12},{8,0},{12,4},{16,24},{20,28},{24,16},{28,20},{1,9},{5... | collective-permute-start | bytes 786440 | tf_op jit(solution)/shard_map/ppermute | solution.py:614
  138.4 6.4 %collective-permute-start.23 = (bf16[272,128]{1,0:T(8,128)(2,1)S(1)}, bf16[272,128]{1,0:T(8,128)(2,1)S(1)}, u32[]{:S(2)}, u32[]{:S(2)}) collective-permute-start(bf16[272,128]{1,0:T(8,128)(2,1)S(1)} %get-tuple-element.159), channel_id=1, source_target_pairs={{0,16},{4,20},{8,24},{12,28},{16,0},{20,4},{24,8},{28,12},{1,17},{... | collective-permute-start | bytes 208904 | tf_op jit(solution)/shard_map/ppermute | solution.py:614
  144.8 5.1 %collective-permute-start.24 = (bf16[544,128]{1,0:T(8,128)(2,1)S(1)}, bf16[544,128]{1,0:T(8,128)(2,1)S(1)}, u32[]{:S(2)}, u32[]{:S(2)}) collective-permute-start(bf16[544,128]{1,0:T(8,128)(2,1)S(1)} %pad_maximum_fusion.5), channel_id=1, source_target_pairs={{0,8},{4,12},{8,0},{12,4},{16,24},{20,28},{24,16},{28,20},{1,9},{5... | collective-permute-start | bytes 417800 | tf_op jit(solution)/shard_map/ppermute | solution.py:614
  145.9 20.2 %collective-permute-start.32 = (bf16[2048,128]{1,0:T(8,128)(2,1)S(1)}, bf16[2048,128]{1,0:T(8,128)(2,1)S(1)}, u32[]{:S(2)}, u32[]{:S(2)}) collective-permute-start(bf16[2048,128]{1,0:T(8,128)(2,1)S(1)} %pad_maximum_fusion.2), channel_id=1, source_target_pairs={{0,4},{4,0},{8,12},{12,8},{16,20},{20,16},{24,28},{28,24},{1,5},{5... | collective-permute-start | bytes 1572872 | tf_op jit(solution)/shard_map/ppermute | solution.py:614
  150.0 13.9 %collective-permute-start.25 = (bf16[1088,128]{1,0:T(8,128)(2,1)S(1)}, bf16[1088,128]{1,0:T(8,128)(2,1)S(1)}, u32[]{:S(2)}, u32[]{:S(2)}) collective-permute-start(bf16[1088,128]{1,0:T(8,128)(2,1)S(1)} %pad_maximum_fusion.3), channel_id=1, source_target_pairs={{0,4},{4,0},{8,12},{12,8},{16,20},{20,16},{24,28},{28,24},{1,5},{5... | collective-permute-start | bytes 835592 | tf_op jit(solution)/shard_map/ppermute | solution.py:614
  (9 other events, 74.3 us)

commit v3 on v2

--- a/solution.py
+++ b/solution.py
@@ -17,6 +17,7 @@
 EPSILON = 1e-05
 MASKED = -1e30
 SCALE = HEAD**-0.5
+FILL = 4
 INV_ROOT = SPAN**-0.5
 F32 = jnp.float32
 BF16 = jnp.bfloat16
@@ -375,16 +376,20 @@
     return [slice(t * D + half * wide, t * D + (half + 1) * wide) for t in range(3)]
 
 
-def back_kernel(sc, x_ref, da_ref, h1_ref, packed_ref, p_ref, tabs, wqkv, vec, nsum_ref, *refs, nf, copies, half):
+def back_kernel(sc, x_ref, da_ref, h1_ref, packed_ref, p_ref, tabs, wqkv, vec, nsum_ref, *refs, nf, copies, half, first, last):
     if half:
         (dub_ref, gvec_ref, before_ref, sums_ref), refs = refs[:4], refs[4:]
     else:
         (gout_ref,), refs = refs[:1], refs[1:]
-    dh1_ref, sum_ref, far_send, far_keep, send_ref, keep_ref, acc, acc_span, accv, dp_ref = refs
+    olds, refs = ((), refs) if first else (refs[:3], refs[3:])
+    (dh1_ref, acc, acc_span, accv), refs = refs[:4], refs[4:]
+    if last:
+        (sum_ref, far_send, far_keep, send_ref, keep_ref), refs = refs[:5], refs[5:]
+    (dp_ref,) = refs
     wide = PAIRS // 2 * LANE
     columns = columns_of(half)
-    for ref in (acc, acc_span, accv):
-        ref[...] = jnp.zeros_like(ref)
+    for k, ref in enumerate((acc, acc_span, accv)):
+        ref[...] = jnp.zeros_like(ref) if first else olds[k][...]
 
     def add(row, values):
         accv[row : row + 1, : values.shape[1]] += jnp.sum(values, axis=0, keepdims=True)
@@ -431,9 +436,13 @@
             n1, _ = normalize(x_ref[rows, :].astype(F32))
             add(G1, dh1 * n1)
             add(S1, dh1)
-        dh1_ref[rows, :] = dh1
-
-    each_block(x_ref.shape[0], body)
+        dh1_ref[block_rows(i - start), :] = dh1
+
+    blocks = dh1_ref.shape[0] // ROWS
+    start = 0 if first else x_ref.shape[0] // ROWS - blocks
+    each_block(blocks * ROWS, lambda i: body(i + start))
+    if not last:
+        return
 
     span = acc_span[...]
     bit = sc[SC_C] & 1
@@ -520,28 +529,41 @@
             ref[q // 2, base:, :] = jnp.zeros((left, LANE), BF16)
 
 
-def back(sc, x, da, h1, packed, p, tabs, wqkv, vec, nsum, more, half, nf, copies):
-    rows = x.shape[0]
+def back(sc, fixed, more, half, nf, copies, old=None, last=True):
+    x, nsum = fixed[0], fixed[-1]
+    rows = x.shape[0] if last and old is None else x.shape[0] // 2
     nspan = nsum.shape[0]
     wide = PAIRS // 2 * LANE
     block = D // nf
     used = 3 * wide // LANE * block + (16 if half else D // LANE * block)
     piece = piece_rows(used, copies)
     far = nspan // 2 * 2 * wide // LANE
-    outs = [((rows, D), F32), ((nspan + 8, D), F32)]
-    outs += [((far, LANE), BF16)] * 2 + [((nf // 2, piece, LANE), BF16)] * 2
-    scratch = [
-        pltpu.VMEM((D, 3 * wide), F32),
-        pltpu.VMEM((nspan, 2 * wide), F32),
-        pltpu.VMEM((16, 3 * D), F32),
-        pltpu.VMEM((ROWS, 3 * wide), BF16),
-    ]
-    kernel = functools.partial(back_kernel, nf=nf, copies=copies, half=half)
-    arrays = (x, da, h1, packed, p, tabs, wqkv, vec, nsum, *more)
-    return resident(kernel, f"back_{half}", 9, 18, (sc,), arrays, outs, scratch)
-
-
-def first_kernel(x_ref, dr1_ref, dh1_ref, own_ref, wqkv, vec, o_ref, e_ref):
+    sums = [((D, 3 * wide), F32), ((nspan, 2 * wide), F32), ((16, 3 * D), F32)]
+    outs = [((rows, D), F32)]
+    scratch = [pltpu.VMEM((ROWS, 3 * wide), BF16)]
+    if last:
+        scratch = [pltpu.VMEM(*a) for a in sums] + scratch
+        outs += [((nspan + 8, D), F32)]
+        outs += [((far, LANE), BF16)] * 2 + [((nf // 2, piece, LANE), BF16)] * 2
+    else:
+        outs += sums
+    kernel = functools.partial(
+        back_kernel, nf=nf, copies=copies, half=half, first=old is None, last=last
+    )
+
+    def ordered(*refs):
+        if not last:
+            return kernel(*refs)
+        at = len(refs) - len(scratch)
+        return kernel(
+            *refs[: at - len(outs) + 1], *refs[at:-1], *refs[at - len(outs) + 1 : at], refs[-1]
+        )
+
+    arrays = (*fixed, *more, *(old or ()))
+    return resident(ordered, f"back_{half}", 9, 18, (sc,), arrays, outs, scratch)
+
+
+def first_kernel(x_ref, dr1_ref, upper_ref, lower_ref, own_ref, wqkv, vec, o_ref, e_ref):
     i = pl.program_id(0)
     spans = ROWS // SPAN
 
@@ -565,23 +587,34 @@
         [jnp.broadcast_to(e_ref[pl.ds(i * spans + s, 1), :], (SPAN, D)) for s in range(spans)],
         axis=0,
     )
-    dh1 = dh1_ref[at, :] + extra
-    o_ref[...] = dr1_ref[at, :] + norm_back(dh1 * vec[G1 : G1 + 1, :D], n1, rstd1)
-
-
-def first_back(x, dr1, dh1, own, wqkv, vec):
+    half = pl.num_programs(0) // 2
+
+    def write(ref, k):
+        dh1 = ref[block_rows(k), :] + extra
+        o_ref[...] = dr1_ref[at, :] + norm_back(dh1 * vec[G1 : G1 + 1, :D], n1, rstd1)
+
+    @pl.when(i < half)
+    def _():
+        write(upper_ref, i)
+
+    @pl.when(i >= half)
+    def _():
+        write(lower_ref, i - half)
+
+
+def first_back(x, dr1, upper, lower, own, wqkv, vec):
     rows = x.shape[0]
     return pl.pallas_call(
         first_kernel,
         grid=(rows // ROWS,),
-        in_specs=in_vmem(6),
+        in_specs=in_vmem(7),
         out_specs=pl.BlockSpec((ROWS, D), lambda i: (i, 0)),
         out_shape=jax.ShapeDtypeStruct((rows, D), F32),
         scratch_shapes=[pltpu.VMEM((rows // SPAN, D), F32)],
         compiler_params=params(8),
         name="first_back",
         cost_estimate=cost(3),
-    )(x, dr1, dh1, own, wqkv, vec)
+    )(x, dr1, upper, lower, own, wqkv, vec)
 
 
 def mixed_kernel(sc, r1_ref, g_ref, vec, *refs):
@@ -647,12 +680,12 @@
         at += h
 
 
-def fold(sc, bit, *pairs):
+def fold(sc, bit, *pairs, micros=1):
     a = pairs[0][0].shape[0]
     h = sum(keep.shape[2] for keep, _ in pairs)
     arrays = [array for pair in pairs for array in pair]
     kernel = functools.partial(fold_kernel, bit=bit)
-    return resident(kernel, "fold", 1, 8, (sc,), arrays, [((a, h, LANE), BF16)] * 2)
+    return resident(kernel, "fold", micros, 8, (sc,), arrays, [((a, h, LANE), BF16)] * 2)
 
 
 def refold_kernel(sc, keep_ref, got_ref, send_ref, own_ref, *, bit, sizes):
@@ -666,10 +699,10 @@
         at += h
 
 
-def refold(sc, bit, keep, got, sizes):
+def refold(sc, bit, keep, got, sizes, micros=1):
     outs = [((sum(sizes), LANE), BF16)] * 2
     kernel = functools.partial(refold_kernel, bit=bit, sizes=sizes)
-    return resident(kernel, "fold", 1, 8, (sc,), (keep, got), outs)
+    return resident(kernel, "fold", micros, 8, (sc,), (keep, got), outs)
 
 
 def last_kernel(keep_ref, got_ref, o_ref, *rest):
@@ -688,9 +721,20 @@
     return resident(last_kernel, "last", 1, 8, (), (keep, got), outs)
 
 
+class Sequence:
+    def __init__(self):
+        self.last = ()
+
+    def next(self, array):
+        return after(array, *self.last) if self.last else array
+
+    def made(self, *arrays):
+        self.last = arrays
+
+
 class Part:
-    def __init__(self, sc, keep, send):
-        self.sc, self.keep, self.send = sc, keep, send
+    def __init__(self, sc, seq, keep, send):
+        self.sc, self.seq, self.keep, self.send = sc, seq, keep, send
         self.count, self.rows = keep.shape[0], keep.shape[1]
         self.total = self.rows
         self.move("fsdp", 1)
@@ -709,13 +753,12 @@
         view = self.view(axis)
         return self.keep.reshape(view), self.got.reshape(view)
 
-    def step(self, axis, bit):
-        pair = self.pair(axis)
-        self.send, self.keep = fold(self.sc, bit if axis == "ctx" else 0, pair)
+    def step(self, axis, bit, micros=1):
+        keep, got = self.pair(axis)
+        pair = (self.seq.next(keep), got)
+        self.send, self.keep = fold(self.sc, bit if axis == "ctx" else 0, pair, micros=micros)
+        self.seq.made(self.keep, self.send)
         self.move(axis, bit)
-
-    def wait(self, *arrays):
-        self.keep = after(self.keep, *arrays)
 
 
 def ctx_bits():
@@ -723,27 +766,52 @@
     return [1 << k for k in range(n.bit_length() - 1)]
 
 
-def ctx_sum(sc, parts, extra=()):
-    bits = ctx_bits()
-    pairs = [part.pair("ctx") for part in parts]
-    for keep, got in extra:
-        view = (1, 2, keep.shape[0] // 2, LANE)
-        pairs.append((keep.reshape(view), got.reshape(view)))
-    sizes = [keep.shape[2] for keep, _ in pairs]
-    used = sum(sizes[: len(parts)]) * 2 // bits[-1]
-    send, keep = (a[0] for a in fold(sc, bits[1], *pairs))
-    got = swap(send, "ctx", bits[1])
-    for bit in bits[2:]:
-        sizes = [size // 2 for size in sizes]
-        send, keep = refold(sc, bit, keep, got, sizes)
-        got = swap(send, "ctx", bit)
-    return last_sum(keep, got, used)
-
-
-def over_ctx(own):
-    for bit in reversed(ctx_bits()):
-        own = jnp.concatenate([own, swap(own, "ctx", bit)], axis=0)
-    return own.reshape(lax.axis_size("ctx"), -1, LANE)
+class Union:
+    def __init__(self, sc, seq, parts, extra=()):
+        self.sc, self.seq = sc, seq
+        self.bits = ctx_bits()
+        pairs = [part.pair("ctx") for part in parts]
+        for keep, got in extra:
+            view = (1, 2, keep.shape[0] // 2, LANE)
+            pairs.append((keep.reshape(view), got.reshape(view)))
+        self.sizes = [keep.shape[2] for keep, _ in pairs]
+        self.used = sum(self.sizes[: len(parts)]) * 2 // self.bits[-1]
+        pairs[0] = (self.seq.next(pairs[0][0]), pairs[0][1])
+        self.received(self.bits[1], *(a[0] for a in fold(sc, self.bits[1], *pairs)))
+        self.at = 2
+
+    def received(self, bit, send, keep):
+        self.keep = keep
+        self.seq.made(keep, send)
+        self.got = swap(send, "ctx", bit)
+
+    def more(self):
+        return self.at < len(self.bits)
+
+    def step(self, micros=1):
+        bit = self.bits[self.at]
+        self.at += 1
+        self.sizes = [size // 2 for size in self.sizes]
+        keep = self.seq.next(self.keep)
+        self.received(bit, *refold(self.sc, bit, keep, self.got, self.sizes, micros))
+
+    def end(self):
+        own, *rest = last_sum(self.seq.next(self.keep), self.got, self.used)
+        self.received(self.bits[-1], own, own)
+        self.at = len(self.bits) - 1
+        return rest[0] if rest else None
+
+    def gathering(self):
+        return self.at > 0
+
+    def join(self):
+        both = jnp.concatenate([self.seq.next(self.keep), self.got], axis=0)
+        self.at -= 1
+        self.received(self.bits[self.at], both, both)
+
+    def rows(self):
+        both = jnp.concatenate([self.seq.next(self.keep), self.got], axis=0)
+        return both.reshape(lax.axis_size("ctx"), -1, LANE)
 
 
 def code_of(index, n):
@@ -828,47 +896,66 @@
     bits = ctx_bits()
     near = [("fsdp", 1 << k) for k in range(1, nf.bit_length() - 1)]
 
-    from_down = Part(scalars, dkeep, dsend)
+    seq = Sequence()
+    from_down = Part(scalars, seq, dkeep, dsend)
     from_down.step(*near[0])
-    dh2 = after(dh2, from_down.keep)
-    dr1, da, gout, gvec = mid(c, dh2, r1, att, wout, vec)
-    from_up = Part(scalars, ukeep, usend)
+    dr1, da, gout, gvec = mid(c, seq.next(dh2), r1, att, wout, vec)
+    seq.made(da)
+    from_up = Part(scalars, seq, ukeep, usend)
     from_up.step("ctx", bits[0])
-    da = after(da, from_up.keep)
+    da = seq.next(da)
     fixed = (x, da, h1, packed, p, tabs, wqkv, vec, nsum)
-    dh1, sums, fsend0, fkeep0, send, keep = back(scalars, *fixed, (gout,), 0, nf, nc)
-    first = Part(scalars, keep, send)
+    dh1, sums, fsend0, fkeep0, send, keep = back(scalars, fixed, (gout,), 0, nf, nc)
+    seq.made(dh1)
+    first = Part(scalars, seq, keep, send)
     from_down.step("ctx", bits[0])
     from_up.step(*near[0])
-    dh1 = after(dh1, from_down.keep, from_up.keep)
-    dh1, _, fsend1, fkeep1, send, keep = back(
-        scalars, *fixed, (dub, gvec, dh1, sums), 1, nf, nc
-    )
-    second = Part(scalars, keep, send)
+    dh1 = seq.next(dh1)
+    upper, *old = back(scalars, fixed, (dub, gvec, dh1, sums), 1, nf, nc, last=False)
+    seq.made(old[0])
     first.step(*near[0])
+    feed = Union(scalars, seq, [from_down, from_up])
+    old[0] = seq.next(old[0])
+    lower, _, fsend1, fkeep1, send, keep = back(
+        scalars, fixed, (dub, gvec, dh1, sums), 1, nf, nc, old=old
+    )
+    seq.made(lower)
+    second = Part(scalars, seq, keep, send)
+    far = [(k, swap(t, "ctx", bits[0])) for k, t in ((fkeep0, fsend0), (fkeep1, fsend1))]
+    while feed.more():
+        feed.step(FILL)
+    first.step("ctx", bits[0], FILL)
+    second.step(*near[0])
+    mixed = block_output(scalars, seq.next(r1), g, vec, down)
+    seq.made(mixed, *(got for _, got in far))
     second.step("ctx", bits[0])
-    first.step("ctx", bits[0])
-    second.step(*near[0])
-    far = [(k, swap(t, "ctx", bits[0])) for k, t in ((fkeep0, fsend0), (fkeep1, fsend1))]
-
+    feed.end()
+    rest = Union(scalars, seq, [first, second], far)
+    feed.join()
+    while rest.more():
+        rest.step()
+    while feed.at > 1:
+        feed.join()
+    own_span = rest.end()
+    feed.join()
+    tokens_grad = first_back(seq.next(x), dr1, upper, lower, own_span, wqkv, vec)
+    seq.made(tokens_grad)
+    while rest.gathering():
+        rest.join()
     block = D // nf
     height, width = down_weight.shape[0], up_weight.shape[1]
-    feed = (from_down.total, from_up.total)
-    (own,) = ctx_sum(scalars, [from_down, from_up])
+    heights = (from_down.total, from_up.total)
     grad_down, grad_up = finish(
         scalars,
-        over_ctx(own),
-        feed,
+        feed.rows(),
+        heights,
         [(height, D), (block, width)],
         [
             [height * j for j in range(D // LANE)],
-            [feed[0] + block * j for j in range(width // LANE)],
+            [heights[0] + block * j for j in range(width // LANE)],
         ],
     )
-
-    own, own_span = ctx_sum(scalars, [first, second], far)
-    tokens_grad = first_back(x, dr1, dh1, own_span, wqkv, vec)
-    mixed = block_output(scalars, r1, after(g, first.keep), vec, down)
+    seq.made(grad_down)
     half = PAIRS // 2
     plan = [
         [
@@ -885,7 +972,7 @@
         plan.append([at + j for j in range(wide // LANE)])
         at += wide // LANE
     grad_qkv, grad_out, *vectors = finish(
-        scalars, over_ctx(own), (first.total, second.total), shapes, plan
+        scalars, rest.rows(), (first.total, second.total), shapes, plan
     )
     g1, s1, qb, ob, g2, s2, ub, db = (v.reshape(-1) for v in vectors)
     return (

time: 169 us -> 160 us (0.947)
  starting transfers between devices: 37 us -> 30 us
  waiting for transfers between devices: 46.1 us -> 42.3 us
    ppermute x33, starting transfers between devices: 31.2 us -> 24.2 us  [swap(): return lax.ppermute(array, axis, [(k, k ^ bit) for k in range(n)])]
    ppermute x33, waiting for transfers between devices: 38.9 us -> 35.1 us  [swap(): return lax.ppermute(array, axis, [(k, k ^ bit) for k in range(n)])]
    pallas_call x23 -> x24, Pallas kernels: 70.2 us -> 70.9 us  [resident(): pl.pallas_call(kernel, in_specs=[pl.BlockSpec(memory_space=pltpu.SMEM)] *...]
  transfers between devices with their start and end apart: 34 -> 34, of which waited for: 15 -> 14; matrix products, arithmetic and copies ran while one was open for 0% -> 0% of each run, Pallas kernels for 47% -> 50%
where the time goes in v3:
time: 160 us
  Pallas kernels  84.3 us (53%)
  waiting for transfers between devices  42.3 us (26%)
  starting transfers between devices  30 us (19%)
    pallas_call x24, Pallas kernels, resident(): pl.pallas_call(kernel, in_specs=[pl.BlockSpec(memory_space=pltpu.SMEM)] *...  70.9 us
    ppermute x33, waiting for transfers between devices, swap(): return lax.ppermute(array, axis, [(k, k ^ bit) for k in range(n)])  35.1 us
    ppermute x33, starting transfers between devices, swap(): return lax.ppermute(array, axis, [(k, k ^ bit) for k in range(n)])  24.2 us
    all_to_all x1, waiting for transfers between devices, local(): nsum = lax.all_to_all(sums, 'ctx', 0, 0, tiled=True).reshape(nc * spans, D)  7.26 us
    all_to_all x1, starting transfers between devices, local(): nsum = lax.all_to_all(sums, 'ctx', 0, 0, tiled=True).reshape(nc * spans, D)  5.81 us
    pallas_call x1, Pallas kernels, block_output(): pl.pallas_call(mixed_kernel, grid=(rows // ROWS,), in_specs=[pl.BlockSpec...  4.13 us
    pallas_call x2, Pallas kernels, finish(): pl.pallas_call(functools.partial(finish_kernel, heights=heights, plan=pla...  3.78 us
    pallas_call x1, Pallas kernels, first_back(): pl.pallas_call(first_kernel, grid=(rows // ROWS,), in_specs=in_vmem(7), o...  3.44 us
  transfers between devices with their start and end apart: 34, of which 14 were waited for; matrix products, arithmetic and copies ran while one was open for 0% of the time, Pallas kernels for 50%

profile of v3, /device:TPU:0, one launch (start us, length us, event | category | flops | bytes accessed | tf_op | source)
XLA Modules:
  0.0 159.6 jit_solution(10722674598491207933)
XLA Ops:
  0.7 2.1 %pack.1.refs_0_ = bf16[144,2048]{1,0:T(8,128)(2,1)} custom-call(bf16[128,1536]{1,0:T(8,128)(2,1)} %qkv_ref.1, bf16[128,512]{1,0:T(8,128)(2,1)} %out_ref.1, bf16[1,128]{1,0:T(2,128)(2,1)} %bitcast.111, bf16[1,128]{1,0:T(2,128)(2,1)} %bitcast.112, bf16[3,128]{1,0:T(4,128)(2,1)} %bitcast.109, bf16[1,128]{1,0:T(2,128)(2,1)} %bitcast.113, ...), custom_call_target="tpu_custom_call" | custom-call | flops 1000000000 | bytes 1000000 | tf_op jit(solution)/shard_map/pack/pallas_call | solution.py:125
  2.7 3.0 %collective-permute-start.1 = (bf16[144,2048]{1,0:T(8,128)(2,1)}, bf16[144,2048]{1,0:T(8,128)(2,1)S(1)}, u32[]{:S(2)}, u32[]{:S(2)}) collective-permute-start(bf16[144,2048]{1,0:T(8,128)(2,1)} %pack.1.refs_0_), channel_id=1, source_target_pairs={{0,2},{1,3},{2,0},{3,1},{4,6},{5,7},{6,4},{7,5},{8,10},{9,11},{10,... | collective-permute-start | bytes 1769480 | tf_op jit(solution)/shard_map/ppermute | solution.py:647
  7.1 5.8 %all-to-all-start = ((f32[8,8,512]{2,1,0:T(8,128)}), f32[8,8,512]{2,1,0:T(8,128)S(1)}, u32[]{:S(2)}, u32[]{:S(2)}) async-start(f32[8,8,512]{2,1,0:T(8,128)} %span_sums.1), calls=%async_computation | async-start | bytes 262144 | tf_op jit(solution)/shard_map/all_to_all | solution.py:878
  13.0 7.3 %all-to-all-done = f32[8,8,512]{2,1,0:T(8,128)S(1)} async-done(((f32[8,8,512]{2,1,0:T(8,128)}), f32[8,8,512]{2,1,0:T(8,128)S(1)}, u32[]{:S(2)}, u32[]{:S(2)}) %all-to-all-start) | async-done | bytes 131104 | tf_op jit(solution)/shard_map/all_to_all | solution.py:878
  22.3 9.5 %attend.1 = (bf16[1024,1536]{1,0:T(8,128)(2,1)S(1)}, bf16[32,256,192]{2,1,0:T(8,128)(2,1)S(1)}, bf16[1024,512]{1,0:T(8,128)(2,1)S(1)}, bf16[1024,512]{1,0:T(8,12...) custom-call(s32[76]{0:T(128)S(1)} %concatenate.21.sc.refs_0_, ...), custom_call_target="tpu_custom_call" | custom-call | flops 12000000000 | bytes 12000000 | tf_op jit(solution)/shard_map/attend/pallas_call | solution.py:69
  32.7 2.2 %collective-permute-done.4.refs_2_ = bf16[128,2048]{1,0:T(8,128)(2,1)S(1)} collective-permute-done((bf16[128,2048]{1,0:T(8,128)(2,1)}, bf16[128,2048]{1,0:T(8,128)(2,1)S(1)}, u32[]{:S(2)}, u32[]{:S(2)}) %collective-permute-start.4) | collective-permute-done | bytes 524320 | tf_op jit(solution)/shard_map/ppermute | solution.py:647
  35.9 1.9 %proj.1 = (f32[1024,512]{1,0:T(8,128)S(1)}, bf16[1024,512]{1,0:T(8,128)(2,1)S(1)}) custom-call(bf16[1024,512]{1,0:T(8,128)(2,1)S(1)} %bitcast.71, bf16[1024,512]{1,0:T(8,128)(2,1)S(1)} %get-tuple-element.122.att_ref, bf16[512,512]{1,0:T(8,128)(2,1)S(1)} %get-tuple-element.123.wout, f32[8,2048]{1,0:T(8,128)S(1)} %get-tuple-element.124.vec.vec_ref.refs_8_), custom_call_target="tpu_custom_call" | custom-call | flops 3000000000 | bytes 3000000 | tf_op jit(solution)/shard_map/proj/pallas_call | solution.py:69
  37.8 9.2 %ffn_up.1 = (bf16[1024,2048]{1,0:T(8,128)(2,1)S(1)}, bf16[1024,2048]{1,0:T(8,128)(2,1)S(1)}, bf16[512,2048]{1,0:T(8,128)(2,1)S(1)}) custom-call(s32[76]{0:T(128)S(1)} %concatenate.21.sc.refs_0_, bf16[1024,512]{1,0:T(8,128)(2,1)S(1)} %get-tuple-element.126.h2_ref, f32[8,2048]{1,0:T(8,128)S(1)} %get-tuple-element.124.vec.vec_ref.refs_8_, ...), custom_call_target="tpu_custom_call" | custom-call | flops 8000000000 | bytes 8000000 | tf_op jit(solution)/shard_map/ffn_up/pallas_call | solution.py:69
  47.1 2.2 %collective-permute-done.7.refs_2_ = bf16[512,512]{1,0:T(8,128)(2,1)S(1)} collective-permute-done((bf16[512,512]{1,0:T(8,128)(2,1)S(1)}, bf16[512,512]{1,0:T(8,128)(2,1)S(1)}, u32[]{:S(2)}, u32[]{:S(2)}) %collective-permute-start.7) | collective-permute-done | bytes 524320 | tf_op jit(solution)/shard_map/ppermute | solution.py:647
  49.3 2.9 %down_grad.1 = (bf16[2,2048,128]{2,1,0:T(8,128)(2,1)S(1)}, bf16[2,2048,128]{2,1,0:T(8,128)(2,1)S(1)}) custom-call(s32[76]{0:T(128)S(1)} %concatenate.21.sc.refs_0_, bf16[1024,2048]{1,0:T(8,128)(2,1)S(1)} %get-tuple-element.130.g_ref, bf16[1024,512]{1,0:T(8,128)(2,1)S(1)} %bitcast.66), custom_call_target="tpu_custom_call" | custom-call | flops 4000000000 | bytes 4000000 | tf_op jit(solution)/shard_map/down_grad/pallas_call | solution.py:69
  52.8 12.9 %ffn_down.1 = (f32[1024,512]{1,0:T(8,128)S(1)}, f32[1,2048]{1,0:T(1,128)S(1)}, bf16[2,2048,128]{2,1,0:T(8,128)(2,1)S(1)}, bf16[2,2048,128]{2,1,0:T(8,128)(2,1)S(1)}) custom-call(s32[76]{0:T(128)S(1)} %concatenate.21.sc.refs_0_, bf16[1024,512]{1,0:T(8,128)(2,1)S(1)} %get-tuple-element.126.h2_ref, bf16[1024,512]{1,0:T(8,128)(2,1)S(1)} %bitcast.67, ...), custom_call_target="tpu_custom_call" | custom-call | flops 8000000000 | bytes 8000000 | tf_op jit(solution)/shard_map/ffn_down/pallas_call | solution.py:69
  67.4 3.7 %mid.1 = (f32[1024,512]{1,0:T(8,128)S(1)}, bf16[1024,512]{1,0:T(8,128)(2,1)S(1)}, f32[512,512]{1,0:T(8,128)S(1)}, f32[8,512]{1,0:T(8,128)S(1)}) custom-call(bf16[1024,512]{1,0:T(8,128)(2,1)S(1)} %bitcast.68, f32[1024,512]{1,0:T(8,128)S(1)} %get-tuple-element.140.dh2_ref, f32[1024,512]{1,0:T(8,128)S(1)} %get-tuple-element.189.r1_ref, ...), custom_call_target="tpu_custom_call" | custom-call | flops 5000000000 | bytes 5000000 | tf_op jit(solution)/shard_map/mid/pallas_call | solution.py:69
  71.9 1.5 collective-permute-start.12
  73.4 10.1 %back_0.1 = (f32[1024,512]{1,0:T(8,128)S(1)}, f32[72,512]{1,0:T(8,128)S(1)}, bf16[128,128]{1,0:T(8,128)(2,1)S(1)}, bf16[128,128]{1,0:T(8,128)(2,1)S(1)}, bf16[2,...) custom-call(s32[76]{0:T(128)S(1)} %concatenate.21.sc.refs_0_, bf16[1024,512]{1,0:T(8,128)(2,1)S(1)} %bitcast.72, ...), custom_call_target="tpu_custom_call" | custom-call | flops 8999999488 | bytes 9000000 | tf_op jit(solution)/shard_map/back_0/pallas_call | solution.py:69
  88.0 5.1 %back_1.2 = (f32[512,512]{1,0:T(8,128)S(1)}, f32[512,768]{1,0:T(8,128)S(1)}, f32[64,512]{1,0:T(8,128)S(1)}, f32[16,1536]{1,0:T(8,128)S(1)}) custom-call(s32[76]{0:T(128)S(1)} %concatenate.21.sc.refs_0_, bf16[1024,512]{1,0:T(8,128)(2,1)S(1)} %bitcast.73, bf16[1024,512]{1,0:T(8,128)(2,1)S(1)} %get-tuple-element.147.refs_2_, bf16[1024,512]{1,0:T(8,128)(2,1)S(1)} %copy-done.7, ...), custom_call_target="tpu_custom_call" | custom-call | flops 8999999488 | bytes 9000000 | tf_op jit(solution)/shard_map/back_1/pallas_call | solution.py:69
  96.1 1.7 %collective-permute-start.16 = (bf16[1024,128]{1,0:T(8,128)(2,1)S(1)}, bf16[1024,128]{1,0:T(8,128)(2,1)S(1)}, u32[]{:S(2)}, u32[]{:S(2)}) collective-permute-start(bf16[1024,128]{1,0:T(8,128)(2,1)S(1)} %bitcast.84), channel_id=1, source_target_pairs={{0,8},{4,12},{8,0},{12,4},{16,24},{20,28},{24,16},{28,20},{1,9},{5... | collective-permute-start | bytes 786440 | tf_op jit(solution)/shard_map/ppermute | solution.py:647
  97.8 6.2 %back_1.3 = (f32[512,512]{1,0:T(8,128)S(1)}, f32[72,512]{1,0:T(8,128)}, bf16[128,128]{1,0:T(8,128)(2,1)S(1)}, bf16[128,128]{1,0:T(8,128)(2,1)S(1)}, bf16[2,896,1...) custom-call(s32[76]{0:T(128)S(1)} %concatenate.21.sc.refs_0_, bf16[1024,512]{1,0:T(8,128)(2,1)S(1)} %bitcast.74, ...), custom_call_target="tpu_custom_call" | custom-call | flops 8999999488 | bytes 9000000 | tf_op jit(solution)/shard_map/back_1/pallas_call | solution.py:69
  105.3 2.6 %collective-permute-start.22 = (bf16[512,128]{1,0:T(8,128)(2,1)S(1)}, bf16[512,128]{1,0:T(8,128)(2,1)S(1)}, u32[]{:S(2)}, u32[]{:S(2)}) collective-permute-start(bf16[512,128]{1,0:T(8,128)(2,1)S(1)} %get-tuple-element.181), channel_id=1, source_target_pairs={{0,16},{4,20},{8,24},{12,28},{16,0},{20,4},{24,8},{28,12},{1,17},{... | collective-permute-start | bytes 393224 | tf_op jit(solution)/shard_map/ppermute | solution.py:647
  111.2 4.1 %block_output.1 = bf16[1024,512]{1,0:T(8,128)(2,1)} custom-call(s32[76]{0:T(128)S(1)} %concatenate.21.sc.refs_0_, f32[1024,512]{1,0:T(8,128)S(1)} %get-tuple-element.189.r1_ref, bf16[1024,2048]{1,0:T(8,128)(2,1)S(1)} %get-tuple-element.130.g_ref, f32[8,2048]{1,0:T(8,128)S(1)} %get-tuple-element.124.vec.vec_ref.refs_8_, bf16[512,512]{1,0:T(8,128)(2,1)S(1)} %copy-done.5, ...), custom_call_target="tpu_custom_call" | custom-call | flops 4000000000 | bytes 4000000 | tf_op jit(solution)/shard_map/block_output/pallas_call | solution.py:633
  115.4 2.5 %collective-permute-done.21 = bf16[1,896,128]{2,1,0:T(8,128)(2,1)S(1)} collective-permute-done((bf16[1,896,128]{2,1,0:T(8,128)(2,1)S(1)}, bf16[1,896,128]{2,1,0:T(8,128)(2,1)S(1)}, u32[]{:S(2)}, u32[]{:S(2)}) %collective-permute-start.21) | collective-permute-done | bytes 229408 | tf_op jit(solution)/shard_map/ppermute | solution.py:647
  119.7 3.7 %collective-permute-done.24 = bf16[1,448,128]{2,1,0:T(8,128)(2,1)S(1)} collective-permute-done((bf16[1,448,128]{2,1,0:T(8,128)(2,1)S(1)}, bf16[1,448,128]{2,1,0:T(8,128)(2,1)S(1)}, u32[]{:S(2)}, u32[]{:S(2)}) %collective-permute-start.24) | collective-permute-done | bytes 114720 | tf_op jit(solution)/shard_map/ppermute | solution.py:647
  124.5 2.1 %collective-permute-done.25 = bf16[512,128]{1,0:T(8,128)(2,1)S(1)} collective-permute-done((bf16[512,128]{1,0:T(8,128)(2,1)S(1)}, bf16[512,128]{1,0:T(8,128)(2,1)S(1)}, u32[]{:S(2)}, u32[]{:S(2)}) %collective-permute-start.25) | collective-permute-done | bytes 131104 | tf_op jit(solution)/shard_map/ppermute | solution.py:647
  126.6 2.8 %collective-permute-done.26.got_ref = bf16[672,128]{1,0:T(8,128)(2,1)S(1)} collective-permute-done((bf16[672,128]{1,0:T(8,128)(2,1)S(1)}, bf16[672,128]{1,0:T(8,128)(2,1)S(1)}, u32[]{:S(2)}, u32[]{:S(2)}) %collective-permute-start.26) | collective-permute-done | bytes 172064 | tf_op jit(solution)/shard_map/ppermute | solution.py:647
  130.9 6.1 %collective-permute-done.27.got_ref = bf16[336,128]{1,0:T(8,128)(2,1)S(1)} collective-permute-done((bf16[336,128]{1,0:T(8,128)(2,1)S(1)}, bf16[336,128]{1,0:T(8,128)(2,1)S(1)}, u32[]{:S(2)}, u32[]{:S(2)}) %collective-permute-start.27) | collective-permute-done | bytes 86048 | tf_op jit(solution)/shard_map/ppermute | solution.py:647
  137.1 1.6 %collective-permute-done.28 = bf16[1024,128]{1,0:T(8,128)(2,1)S(1)} collective-permute-done((bf16[1024,128]{1,0:T(8,128)(2,1)S(1)}, bf16[1024,128]{1,0:T(8,128)(2,1)S(1)}, u32[]{:S(2)}, u32[]{:S(2)}) %collective-permute-start.28) | collective-permute-done | bytes 262176 | tf_op jit(solution)/shard_map/ppermute | solution.py:647
  138.8 1.9 %collective-permute-start.31 = (bf16[2048,128]{1,0:T(8,128)(2,1)S(1)}, bf16[2048,128]{1,0:T(8,128)(2,1)S(1)}, u32[]{:S(2)}, u32[]{:S(2)}) collective-permute-start(bf16[2048,128]{1,0:T(8,128)(2,1)S(1)} %constant_dynamic-update-slice_fusion.2), channel_id=1, source_target_pairs={{0,4},{4,0},{8,12},{12,8},{16,20},{20,16},{24,28},{28,24},{1,5},{5... | collective-permute-start | bytes 1572872 | tf_op jit(solution)/shard_map/ppermute | solution.py:647
  140.7 3.4 %first_back.1 = f32[1024,512]{1,0:T(8,128)} custom-call(bf16[1024,512]{1,0:T(8,128)(2,1)S(1)} %bitcast.75, f32[1024,512]{1,0:T(8,128)S(1)} %get-tuple-element.209.dr1_ref, f32[512,512]{1,0:T(8,128)S(1)} %get-tuple-element.210.upper_ref, f32[512,512]{1,0:T(8,128)S(1)} %get-tuple-element.178.lower_ref, bf16[64,128]{1,0:T(8,128)(2,1)S(1)} %get-tuple-element.211.own_ref, ...), custom_call_target="tpu_custom_call" | custom-call | flops 3000000000 | bytes 3000000 | tf_op jit(solution)/shard_map/first_back/pallas_call | solution.py:607
  144.5 4.8 %collective-permute-done.30 = bf16[544,128]{1,0:T(8,128)(2,1)S(1)} collective-permute-done((bf16[544,128]{1,0:T(8,128)(2,1)S(1)}, bf16[544,128]{1,0:T(8,128)(2,1)S(1)}, u32[]{:S(2)}, u32[]{:S(2)}) %collective-permute-start.30) | collective-permute-done | bytes 139296 | tf_op jit(solution)/shard_map/ppermute | solution.py:647
  149.6 3.7 %collective-permute-done.31 = bf16[2048,128]{1,0:T(8,128)(2,1)S(1)} collective-permute-done((bf16[2048,128]{1,0:T(8,128)(2,1)S(1)}, bf16[2048,128]{1,0:T(8,128)(2,1)S(1)}, u32[]{:S(2)}, u32[]{:S(2)}) %collective-permute-start.31) | collective-permute-done | bytes 524320 | tf_op jit(solution)/shard_map/ppermute | solution.py:647
  153.3 2.1 %finish.2 = (f32[512,512]{1,0:T(8,128)}, f32[128,2048]{1,0:T(8,128)}) custom-call(s32[76]{0:T(128)S(1)} %concatenate.21.sc.refs_0_, bf16[8,512,128]{2,1,0:T(8,128)(2,1)S(1)} %bitcast.59), custom_call_target="tpu_custom_call" | custom-call | flops 2000000000 | bytes 2000000 | tf_op jit(solution)/shard_map/finish/pallas_call | solution.py:843
  155.5 1.9 %collective-permute-done.32 = bf16[1088,128]{1,0:T(8,128)(2,1)S(1)} collective-permute-done((bf16[1088,128]{1,0:T(8,128)(2,1)S(1)}, bf16[1088,128]{1,0:T(8,128)(2,1)S(1)}, u32[]{:S(2)}, u32[]{:S(2)}) %collective-permute-start.32) | collective-permute-done | bytes 278560 | tf_op jit(solution)/shard_map/ppermute | solution.py:647
  157.4 1.6 %finish.3 = (f32[128,1536]{1,0:T(8,128)}, f32[128,512]{1,0:T(8,128)}, f32[1,128]{1,0:T(1,128)}, f32[1,128]{1,0:T(1,128)}, f32[1,384]{1,0:T(1,128)S(1)}, /*index=...) custom-call(s32[76]{0:T(128)S(1)} %concatenate.21.sc.refs_0_, ...), custom_call_target="tpu_custom_call" | custom-call | flops 2000000000 | bytes 2000000 | tf_op jit(solution)/shard_map/finish/pallas_call | solution.py:843
  (95 shorter events, 26.4 us)
Async XLA Ops:
  2.7 17.5 %collective-permute-start.1 = (bf16[144,2048]{1,0:T(8,128)(2,1)}, bf16[144,2048]{1,0:T(8,128)(2,1)S(1)}, u32[]{:S(2)}, u32[]{:S(2)}) collective-permute-start(bf16[144,2048]{1,0:T(8,128)(2,1)} %pack.1.refs_0_), channel_id=1, source_target_pairs={{0,2},{1,3},{2,0},{3,1},{4,6},{5,7},{6,4},{7,5},{8,10},{9,11},{10,... | collective-permute-start | bytes 1769480 | tf_op jit(solution)/shard_map/ppermute | solution.py:647
  7.1 13.1 %all-to-all-start = ((f32[8,8,512]{2,1,0:T(8,128)}), f32[8,8,512]{2,1,0:T(8,128)S(1)}, u32[]{:S(2)}, u32[]{:S(2)}) async-start(f32[8,8,512]{2,1,0:T(8,128)} %span_sums.1), calls=%async_computation | async-start | bytes 262144 | tf_op jit(solution)/shard_map/all_to_all | solution.py:878
  12.9 8.4 %collective-permute-start = (bf16[144,2048]{1,0:T(8,128)(2,1)S(1)}, bf16[144,2048]{1,0:T(8,128)(2,1)S(1)}, u32[]{:S(2)}, u32[]{:S(2)}) collective-permute-start(bf16[144,2048]{1,0:T(8,128)(2,1)S(1)} %copy-done.3), channel_id=1, source_target_pairs={{0,1},{1,0},{2,3},{3,2},{4,5},{5,4},{6,7},{7,6},{8,9},{9,8},{10,11... | collective-permute-start | bytes 1769480 | tf_op jit(solution)/shard_map/ppermute | solution.py:647
  20.4 14.6 %collective-permute-start.4 = (bf16[128,2048]{1,0:T(8,128)(2,1)}, bf16[128,2048]{1,0:T(8,128)(2,1)S(1)}, u32[]{:S(2)}, u32[]{:S(2)}) collective-permute-start(bf16[128,2048]{1,0:T(8,128)(2,1)} %refs_0_), channel_id=1, source_target_pairs={{0,2},{1,3},{2,0},{3,1},{4,6},{5,7},{6,4},{7,5},{8,10},{9,11},{10,... | collective-permute-start | bytes 1572872 | tf_op jit(solution)/shard_map/ppermute | solution.py:647
  21.1 16.7 %collective-permute-start.3 = (bf16[128,2048]{1,0:T(8,128)(2,1)}, bf16[128,2048]{1,0:T(8,128)(2,1)S(1)}, u32[]{:S(2)}, u32[]{:S(2)}) collective-permute-start(bf16[128,2048]{1,0:T(8,128)(2,1)} %refs_0_), channel_id=1, source_target_pairs={{0,1},{1,0},{2,3},{3,2},{4,5},{5,4},{6,7},{7,6},{8,9},{9,8},{10,11... | collective-permute-start | bytes 1572872 | tf_op jit(solution)/shard_map/ppermute | solution.py:647
  34.9 14.3 %collective-permute-start.7 = (bf16[512,512]{1,0:T(8,128)(2,1)S(1)}, bf16[512,512]{1,0:T(8,128)(2,1)S(1)}, u32[]{:S(2)}, u32[]{:S(2)}) collective-permute-start(bf16[512,512]{1,0:T(8,128)(2,1)S(1)} %copy-done.5), channel_id=1, source_target_pairs={{0,2},{1,3},{2,0},{3,1},{4,6},{5,7},{6,4},{7,5},{8,10},{9,11},{10,... | collective-permute-start | bytes 1572872 | tf_op jit(solution)/shard_map/ppermute | solution.py:647
  35.6 17.1 %collective-permute-start.6 = (bf16[512,512]{1,0:T(8,128)(2,1)S(1)}, bf16[512,512]{1,0:T(8,128)(2,1)S(1)}, u32[]{:S(2)}, u32[]{:S(2)}) collective-permute-start(bf16[512,512]{1,0:T(8,128)(2,1)S(1)} %copy-done.5), channel_id=1, source_target_pairs={{0,1},{1,0},{2,3},{3,2},{4,5},{5,4},{6,7},{7,6},{8,9},{9,8},{10,11... | collective-permute-start | bytes 1572872 | tf_op jit(solution)/shard_map/ppermute | solution.py:647
  49.2 3.5 %collective-permute-start.8 = (bf16[512,512]{1,0:T(8,128)(2,1)S(1)}, bf16[512,512]{1,0:T(8,128)(2,1)S(1)}, u32[]{:S(2)}, u32[]{:S(2)}) collective-permute-start(bf16[512,512]{1,0:T(8,128)(2,1)S(1)} %collective-permute-done.7.refs_2_), channel_id=1, source_target_pairs={{0,1},{1,0},{2,3},{3,2},{4,5},{5,4},{6,7},{7,6},{8,9},{9,8},{10,11... | collective-permute-start | bytes 1572872 | tf_op jit(solution)/shard_map/ppermute | solution.py:647
  52.2 13.6 %collective-permute-start.9 = (bf16[2,2048,128]{2,1,0:T(8,128)(2,1)S(1)}, bf16[2,2048,128]{2,1,0:T(8,128)(2,1)S(1)}, u32[]{:S(2)}, u32[]{:S(2)}) collective-permute-start(bf16[2,2048,128]{2,1,0:T(8,128)(2,1)S(1)} %get-tuple-element.137), channel_id=1, source_target_pairs={{0,1},{1,0},{2,3},{3,2},{4,5},{5,4},{6,7},{7,6},{8,9},{9,8},{10,11... | collective-permute-start | bytes 3145736 | tf_op jit(solution)/shard_map/ppermute | solution.py:647
  65.7 5.4 %collective-permute-start.10 = (bf16[2,2048,128]{2,1,0:T(8,128)(2,1)S(1)}, bf16[2,2048,128]{2,1,0:T(8,128)(2,1)S(1)}, u32[]{:S(2)}, u32[]{:S(2)}) collective-permute-start(bf16[2,2048,128]{2,1,0:T(8,128)(2,1)S(1)} %get-tuple-element.144), channel_id=1, source_target_pairs={{0,1},{1,0},{2,3},{3,2},{4,5},{5,4},{6,7},{7,6},{8,9},{9,8},{10,11... | collective-permute-start | bytes 3145736 | tf_op jit(solution)/shard_map/ppermute | solution.py:647
  66.6 16.9 %collective-permute-start.11 = (bf16[1,2048,128]{2,1,0:T(8,128)(2,1)S(1)}, bf16[1,2048,128]{2,1,0:T(8,128)(2,1)S(1)}, u32[]{:S(2)}, u32[]{:S(2)}) collective-permute-start(bf16[1,2048,128]{2,1,0:T(8,128)(2,1)S(1)} %get-tuple-element.139), channel_id=1, source_target_pairs={{0,2},{1,3},{2,0},{3,1},{4,6},{5,7},{6,4},{7,5},{8,10},{9,11},{10,... | collective-permute-start | bytes 1572872 | tf_op jit(solution)/shard_map/ppermute | solution.py:647
  71.9 14.4 %collective-permute-start.12 = (bf16[2,1024,128]{2,1,0:T(8,128)(2,1)S(1)}, bf16[2,1024,128]{2,1,0:T(8,128)(2,1)S(1)}, u32[]{:S(2)}, u32[]{:S(2)}) collective-permute-start(bf16[2,1024,128]{2,1,0:T(8,128)(2,1)S(1)} %get-tuple-element.146), channel_id=1, source_target_pairs={{0,4},{4,0},{8,12},{12,8},{16,20},{20,16},{24,28},{28,24},{1,5},{5... | collective-permute-start | bytes 1572872 | tf_op jit(solution)/shard_map/ppermute | solution.py:647
  84.2 10.8 %collective-permute-start.14 = (bf16[1,1024,128]{2,1,0:T(8,128)(2,1)S(1)}, bf16[1,1024,128]{2,1,0:T(8,128)(2,1)S(1)}, u32[]{:S(2)}, u32[]{:S(2)}) collective-permute-start(bf16[1,1024,128]{2,1,0:T(8,128)(2,1)S(1)} %get-tuple-element.159), channel_id=1, source_target_pairs={{0,4},{4,0},{8,12},{12,8},{16,20},{20,16},{24,28},{28,24},{1,5},{5... | collective-permute-start | bytes 786440 | tf_op jit(solution)/shard_map/ppermute | solution.py:647
  84.8 8.3 %collective-permute-start.13 = (bf16[2,1280,128]{2,1,0:T(8,128)(2,1)S(1)}, bf16[2,1280,128]{2,1,0:T(8,128)(2,1)S(1)}, u32[]{:S(2)}, u32[]{:S(2)}) collective-permute-start(bf16[2,1280,128]{2,1,0:T(8,128)(2,1)S(1)} %get-tuple-element.168), channel_id=1, source_target_pairs={{0,1},{1,0},{2,3},{3,2},{4,5},{5,4},{6,7},{7,6},{8,9},{9,8},{10,11... | collective-permute-start | bytes 1966088 | tf_op jit(solution)/shard_map/ppermute | solution.py:647
  84.8 30.6 %collective-permute-start.19 = (bf16[128,128]{1,0:T(8,128)(2,1)S(1)}, bf16[128,128]{1,0:T(8,128)(2,1)S(1)}, u32[]{:S(2)}, u32[]{:S(2)}) collective-permute-start(bf16[128,128]{1,0:T(8,128)(2,1)S(1)} %get-tuple-element.190), channel_id=1, source_target_pairs={{0,4},{4,0},{8,12},{12,8},{16,20},{20,16},{24,28},{28,24},{1,5},{5... | collective-permute-start | bytes 98312 | tf_op jit(solution)/shard_map/ppermute | solution.py:647
  86.9 8.5 %collective-permute-start.15 = (bf16[1,1024,128]{2,1,0:T(8,128)(2,1)S(1)}, bf16[1,1024,128]{2,1,0:T(8,128)(2,1)S(1)}, u32[]{:S(2)}, u32[]{:S(2)}) collective-permute-start(bf16[1,1024,128]{2,1,0:T(8,128)(2,1)S(1)} %get-tuple-element.162), channel_id=1, source_target_pairs={{0,2},{1,3},{2,0},{3,1},{4,6},{5,7},{6,4},{7,5},{8,10},{9,11},{10,... | collective-permute-start | bytes 786440 | tf_op jit(solution)/shard_map/ppermute | solution.py:647
  93.8 14.1 %collective-permute-start.17 = (bf16[1,1280,128]{2,1,0:T(8,128)(2,1)S(1)}, bf16[1,1280,128]{2,1,0:T(8,128)(2,1)S(1)}, u32[]{:S(2)}, u32[]{:S(2)}) collective-permute-start(bf16[1,1280,128]{2,1,0:T(8,128)(2,1)S(1)} %get-tuple-element.170), channel_id=1, source_target_pairs={{0,2},{1,3},{2,0},{3,1},{4,6},{5,7},{6,4},{7,5},{8,10},{9,11},{10,... | collective-permute-start | bytes 983048 | tf_op jit(solution)/shard_map/ppermute | solution.py:647
  96.1 8.5 %collective-permute-start.16 = (bf16[1024,128]{1,0:T(8,128)(2,1)S(1)}, bf16[1024,128]{1,0:T(8,128)(2,1)S(1)}, u32[]{:S(2)}, u32[]{:S(2)}) collective-permute-start(bf16[1024,128]{1,0:T(8,128)(2,1)S(1)} %bitcast.84), channel_id=1, source_target_pairs={{0,8},{4,12},{8,0},{12,4},{16,24},{20,28},{24,16},{28,20},{1,9},{5... | collective-permute-start | bytes 786440 | tf_op jit(solution)/shard_map/ppermute | solution.py:647
  104.0 6.0 %collective-permute-start.18 = (bf16[2,896,128]{2,1,0:T(8,128)(2,1)S(1)}, bf16[2,896,128]{2,1,0:T(8,128)(2,1)S(1)}, u32[]{:S(2)}, u32[]{:S(2)}) collective-permute-start(bf16[2,896,128]{2,1,0:T(8,128)(2,1)S(1)} %get-tuple-element.186), channel_id=1, source_target_pairs={{0,1},{1,0},{2,3},{3,2},{4,5},{5,4},{6,7},{7,6},{8,9},{9,8},{10,11... | collective-permute-start | bytes 1376264 | tf_op jit(solution)/shard_map/ppermute | solution.py:647
  104.0 11.4 %collective-permute-start.20 = (bf16[128,128]{1,0:T(8,128)(2,1)S(1)}, bf16[128,128]{1,0:T(8,128)(2,1)S(1)}, u32[]{:S(2)}, u32[]{:S(2)}) collective-permute-start(bf16[128,128]{1,0:T(8,128)(2,1)S(1)} %get-tuple-element.191), channel_id=1, source_target_pairs={{0,4},{4,0},{8,12},{12,8},{16,20},{20,16},{24,28},{28,24},{1,5},{5... | collective-permute-start | bytes 98312 | tf_op jit(solution)/shard_map/ppermute | solution.py:647
  105.3 13.9 %collective-permute-start.22 = (bf16[512,128]{1,0:T(8,128)(2,1)S(1)}, bf16[512,128]{1,0:T(8,128)(2,1)S(1)}, u32[]{:S(2)}, u32[]{:S(2)}) collective-permute-start(bf16[512,128]{1,0:T(8,128)(2,1)S(1)} %get-tuple-element.181), channel_id=1, source_target_pairs={{0,16},{4,20},{8,24},{12,28},{16,0},{20,4},{24,8},{28,12},{1,17},{... | collective-permute-start | bytes 393224 | tf_op jit(solution)/shard_map/ppermute | solution.py:647
  108.5 11.1 %collective-permute-start.23 = (bf16[1,640,128]{2,1,0:T(8,128)(2,1)S(1)}, bf16[1,640,128]{2,1,0:T(8,128)(2,1)S(1)}, u32[]{:S(2)}, u32[]{:S(2)}) collective-permute-start(bf16[1,640,128]{2,1,0:T(8,128)(2,1)S(1)} %get-tuple-element.184), channel_id=1, source_target_pairs={{0,4},{4,0},{8,12},{12,8},{16,20},{20,16},{24,28},{28,24},{1,5},{5... | collective-permute-start | bytes 491528 | tf_op jit(solution)/shard_map/ppermute | solution.py:647
  110.6 7.2 %collective-permute-start.21 = (bf16[1,896,128]{2,1,0:T(8,128)(2,1)S(1)}, bf16[1,896,128]{2,1,0:T(8,128)(2,1)S(1)}, u32[]{:S(2)}, u32[]{:S(2)}) collective-permute-start(bf16[1,896,128]{2,1,0:T(8,128)(2,1)S(1)} %get-tuple-element.188), channel_id=1, source_target_pairs={{0,2},{1,3},{2,0},{3,1},{4,6},{5,7},{6,4},{7,5},{8,10},{9,11},{10,... | collective-permute-start | bytes 688136 | tf_op jit(solution)/shard_map/ppermute | solution.py:647
  118.5 4.9 %collective-permute-start.24 = (bf16[1,448,128]{2,1,0:T(8,128)(2,1)S(1)}, bf16[1,448,128]{2,1,0:T(8,128)(2,1)S(1)}, u32[]{:S(2)}, u32[]{:S(2)}) collective-permute-start(bf16[1,448,128]{2,1,0:T(8,128)(2,1)S(1)} %get-tuple-element.194), channel_id=1, source_target_pairs={{0,4},{4,0},{8,12},{12,8},{16,20},{20,16},{24,28},{28,24},{1,5},{5... | collective-permute-start | bytes 344072 | tf_op jit(solution)/shard_map/ppermute | solution.py:647
  119.2 7.4 %collective-permute-start.25 = (bf16[512,128]{1,0:T(8,128)(2,1)S(1)}, bf16[512,128]{1,0:T(8,128)(2,1)S(1)}, u32[]{:S(2)}, u32[]{:S(2)}) collective-permute-start(bf16[512,128]{1,0:T(8,128)(2,1)S(1)} %last.2), channel_id=1, source_target_pairs={{0,16},{4,20},{8,24},{12,28},{16,0},{20,4},{24,8},{28,12},{1,17},{... | collective-permute-start | bytes 393224 | tf_op jit(solution)/shard_map/ppermute | solution.py:647
  124.0 5.5 %collective-permute-start.26 = (bf16[672,128]{1,0:T(8,128)(2,1)S(1)}, bf16[672,128]{1,0:T(8,128)(2,1)S(1)}, u32[]{:S(2)}, u32[]{:S(2)}) collective-permute-start(bf16[672,128]{1,0:T(8,128)(2,1)S(1)} %bitcast.87), channel_id=1, source_target_pairs={{0,8},{4,12},{8,0},{12,4},{16,24},{20,28},{24,16},{28,20},{1,9},{5... | collective-permute-start | bytes 516104 | tf_op jit(solution)/shard_map/ppermute | solution.py:647
  130.0 6.9 %collective-permute-start.27 = (bf16[336,128]{1,0:T(8,128)(2,1)S(1)}, bf16[336,128]{1,0:T(8,128)(2,1)S(1)}, u32[]{:S(2)}, u32[]{:S(2)}) collective-permute-start(bf16[336,128]{1,0:T(8,128)(2,1)S(1)} %get-tuple-element.204), channel_id=1, source_target_pairs={{0,16},{4,20},{8,24},{12,28},{16,0},{20,4},{24,8},{28,12},{1,17},{... | collective-permute-start | bytes 258056 | tf_op jit(solution)/shard_map/ppermute | solution.py:647
  130.5 8.3 %collective-permute-start.28 = (bf16[1024,128]{1,0:T(8,128)(2,1)S(1)}, bf16[1024,128]{1,0:T(8,128)(2,1)S(1)}, u32[]{:S(2)}, u32[]{:S(2)}) collective-permute-start(bf16[1024,128]{1,0:T(8,128)(2,1)S(1)} %constant_dynamic-update-slice_fusion), channel_id=1, source_target_pairs={{0,8},{4,12},{8,0},{12,4},{16,24},{20,28},{24,16},{28,20},{1,9},{5... | collective-permute-start | bytes 786440 | tf_op jit(solution)/shard_map/ppermute | solution.py:647
  137.0 7.2 %collective-permute-start.29 = (bf16[272,128]{1,0:T(8,128)(2,1)S(1)}, bf16[272,128]{1,0:T(8,128)(2,1)S(1)}, u32[]{:S(2)}, u32[]{:S(2)}) collective-permute-start(bf16[272,128]{1,0:T(8,128)(2,1)S(1)} %get-tuple-element.212), channel_id=1, source_target_pairs={{0,16},{4,20},{8,24},{12,28},{16,0},{20,4},{24,8},{28,12},{1,17},{... | collective-permute-start | bytes 208904 | tf_op jit(solution)/shard_map/ppermute | solution.py:647
  138.8 14.5 %collective-permute-start.31 = (bf16[2048,128]{1,0:T(8,128)(2,1)S(1)}, bf16[2048,128]{1,0:T(8,128)(2,1)S(1)}, u32[]{:S(2)}, u32[]{:S(2)}) collective-permute-start(bf16[2048,128]{1,0:T(8,128)(2,1)S(1)} %constant_dynamic-update-slice_fusion.2), channel_id=1, source_target_pairs={{0,4},{4,0},{8,12},{12,8},{16,20},{20,16},{24,28},{28,24},{1,5},{5... | collective-permute-start | bytes 1572872 | tf_op jit(solution)/shard_map/ppermute | solution.py:647
  144.2 5.1 %collective-permute-start.30 = (bf16[544,128]{1,0:T(8,128)(2,1)S(1)}, bf16[544,128]{1,0:T(8,128)(2,1)S(1)}, u32[]{:S(2)}, u32[]{:S(2)}) collective-permute-start(bf16[544,128]{1,0:T(8,128)(2,1)S(1)} %constant_dynamic-update-slice_fusion.4), channel_id=1, source_target_pairs={{0,8},{4,12},{8,0},{12,4},{16,24},{20,28},{24,16},{28,20},{1,9},{5... | collective-permute-start | bytes 417800 | tf_op jit(solution)/shard_map/ppermute | solution.py:647
  149.3 8.0 %collective-permute-start.32 = (bf16[1088,128]{1,0:T(8,128)(2,1)S(1)}, bf16[1088,128]{1,0:T(8,128)(2,1)S(1)}, u32[]{:S(2)}, u32[]{:S(2)}) collective-permute-start(bf16[1088,128]{1,0:T(8,128)(2,1)S(1)} %constant_dynamic-update-slice_fusion.6), channel_id=1, source_target_pairs={{0,4},{4,0},{8,12},{12,8},{16,20},{20,16},{24,28},{28,24},{1,5},{5... | collective-permute-start | bytes 835592 | tf_op jit(solution)/shard_map/ppermute | solution.py:647
  (11 other events, 77.6 us)

commit v4 on v3

--- a/solution.py
+++ b/solution.py
@@ -79,15 +79,24 @@
 
 
 def block_rows(i, size=ROWS):
+    if isinstance(i, int):
+        return slice(i * size, (i + 1) * size)
     return pl.ds(pl.multiple_of(i * size, size), size)
 
 
-def each_block(rows, body):
-    def step(i, carry):
-        body(i)
+def each_block(rows, body, size=ROWS, parts=1):
+    each = rows // size // parts
+    if parts == 1:
+        for i in range(each):
+            body(i)
+        return
+
+    def step(n, carry):
+        for k in range(each):
+            body(n * each + k)
         return carry
 
-    lax.fori_loop(0, rows // ROWS, step, 0)
+    lax.fori_loop(0, parts, step, 0)
 
 
 def sums_kernel(x_ref, o_ref):
@@ -155,7 +164,8 @@
     hs = nsum_ref[...] * vec[G1 : G1 + 1, :D] + SPAN * vec[S1 : S1 + 1, :D]
     hi = hs.astype(BF16)
     lo = (hs - hi.astype(F32)).astype(BF16)
-    t = dot(hi, wqkv[:, D:]) + dot(lo, wqkv[:, D:]) + SPAN * vec[QB : QB + 1, D : 3 * D]
+    both = dot(jnp.concatenate([hi, lo], axis=0), wqkv[:, D:])
+    t = both[:nspan] + both[nspan:] + SPAN * vec[QB : QB + 1, D : 3 * D]
     tabs[...] = (t * INV_ROOT).astype(BF16)
     prompt = lax.div(sc[SC_LEN], SPAN)
     spans = ROWS // SPAN
@@ -195,11 +205,12 @@
                 peak = jnp.max(scores, axis=1, keepdims=True)
                 e = jnp.exp(scores - peak)
                 w = (e * (1.0 / jnp.sum(e, axis=1, keepdims=True))).astype(BF16)
-                p_ref[(i * spans + s) * PAIRS + p] = w
+                p_ref[(i * spans + s) * PAIRS + p, :SPAN] = w[:, :SPAN].T
+                p_ref[(i * spans + s) * PAIRS + p, SPAN:] = w[:, SPAN:].T
                 o2 = dot(w, vc)
                 att_ref[at, cq] = jnp.where(low, o2[:SPAN], o2[SPAN:]).astype(BF16)
 
-    each_block(x_ref.shape[0], body)
+    each_block(x_ref.shape[0], body, parts=2)
 
 
 def proj_kernel(x_ref, att_ref, wout, vec, r1_ref, h2_ref):
@@ -223,7 +234,7 @@
     nspan = nsum.shape[0]
     outs = [
         ((rows, 3 * D), BF16),
-        ((rows // SPAN * PAIRS, 2 * SPAN, SPAN + nspan), BF16),
+        ((rows // SPAN * PAIRS, SPAN + nspan, 2 * SPAN), BF16),
         ((rows, D), BF16),
         ((rows, D), BF16),
         ((D, 3 * D), BF16),
@@ -250,10 +261,11 @@
     for q in range(nf):
         at = pl.ds(pl.multiple_of((sc[SC_F] ^ q) * block, block), block)
         w_ref[at, :] = up_refs[q][...]
-    for j in range(nf):
-        cols = slice(j * width, (j + 1) * width)
-
-        def body(i):
+    rows = h2_ref.shape[0]
+
+    def body(j):
+        cols = pl.ds(pl.multiple_of(j * width, width), width)
+        for i in range(rows // ROWS):
             at = block_rows(i)
             u = dot(h2_ref[at, :], w_ref[:, cols]) + vec_ref[UB : UB + 1, cols]
             u2 = u * u
@@ -263,7 +275,7 @@
             slope = u * (k0 + (3 * k0 * 0.044715) * u2)
             gp_ref[at, cols] = (half + (0.5 - 0.5 * t * t) * slope).astype(BF16)
 
-        each_block(h2_ref.shape[0], body)
+    each_block(nf, body, 1, parts=2)
 
 
 def ffn_up(sc, h2, vec, up):
@@ -302,7 +314,7 @@
         dub_ref[:, cols] = jnp.zeros((1, width), F32)
 
         def body(i):
-            at = block_rows(i)
+            at = block_rows(i, 2 * ROWS)
             dg = dot_bt(c_ref[at, :], down_refs[s][...])
             du = (dg * gp_ref[at, cols].astype(F32)).astype(BF16)
             du_ref[at, :] = du
@@ -313,7 +325,7 @@
             else:
                 dh2_ref[at, :] += dh2
 
-        each_block(rows, body)
+        each_block(rows, body, 2 * ROWS)
         grad_ref[...] = dot_at(h2_ref[...], du_ref[...])
         for q in range(nf):
             ref = send_ref if q % 2 else keep_ref
@@ -413,13 +425,13 @@
                 vc = jnp.concatenate([packed_ref[at, cv], tabs[:, ck]], axis=0)
                 w = p_ref[(i * (ROWS // SPAN) + s) * PAIRS + p]
                 wf = w.astype(F32)
-                dp = dot_bt(do2, vc)
-                delta = jnp.sum(wf * dp, axis=1, keepdims=True)
+                dp = dot_bt(vc, do2)
+                delta = jnp.sum(wf * dp, axis=0, keepdims=True)
                 ds = (wf * (dp - delta)).astype(BF16)
-                dq2 = dot(ds, kc)
+                dq2 = dot_at(ds, kc)
                 dq = jnp.where(low, dq2[:SPAN], dq2[SPAN:]) * SCALE
-                dk = dot_at(ds, q2)
-                dv = dot_at(w, do2)
+                dk = dot(ds, q2)
+                dv = dot(w, do2)
                 acc_span[:, oq] += dk[SPAN:]
                 acc_span[:, ok] += dv[SPAN:]
                 dp_ref[to, oq] = dq.astype(BF16)
@@ -440,7 +452,7 @@
 
     blocks = dh1_ref.shape[0] // ROWS
     start = 0 if first else x_ref.shape[0] // ROWS - blocks
-    each_block(blocks * ROWS, lambda i: body(i + start))
+    each_block(blocks * ROWS, lambda i: body(i + start), parts=max(blocks // 2, 1))
     if not last:
         return
 
@@ -889,9 +901,8 @@
     up = gathered(up_weight, after(far_up, att), "fsdp")
     r1, h2 = proj(x, att, wout, vec)
     g, gp, wup = ffn_up(scalars, h2, vec, up)
-    down = gathered(down_weight, after(far_down, g), "fsdp")
     dsend, dkeep = down_gradient(scalars, g, c, nf)
-    gp = after(gp, dkeep)
+    down = gathered(down_weight, after(far_down, dkeep), "fsdp")
     dh2, dub, usend, ukeep = ffn_down(scalars, h2, c, gp, wup, down)
     bits = ctx_bits()
     near = [("fsdp", 1 << k) for k in range(1, nf.bit_length() - 1)]

time: 160 us -> 152 us (0.950)
  Pallas kernels: 84.3 us -> 71.1 us
  waiting for transfers between devices: 42.3 us -> 47.5 us
    pallas_call x24, Pallas kernels: 70.9 us -> 57.7 us  [resident(): pl.pallas_call(kernel, in_specs=[pl.BlockSpec(memory_space=pltpu.SMEM)] *...]
    ppermute x33, waiting for transfers between devices: 35.1 us -> 40.2 us  [swap(): return lax.ppermute(array, axis, [(k, k ^ bit) for k in range(n)])]
  transfers between devices with their start and end apart: 34 -> 34, of which waited for: 14 -> 16; matrix products, arithmetic and copies ran while one was open for 0% -> 0% of each run, Pallas kernels for 50% -> 44%
where the time goes in v4:
time: 152 us
  Pallas kernels  71.1 us (47%)
  waiting for transfers between devices  47.5 us (31%)
  starting transfers between devices  31.1 us (20%)
    pallas_call x24, Pallas kernels, resident(): pl.pallas_call(kernel, in_specs=[pl.BlockSpec(memory_space=pltpu.SMEM)] *...  57.7 us
    ppermute x33, waiting for transfers between devices, swap(): return lax.ppermute(array, axis, [(k, k ^ bit) for k in range(n)])  40.2 us
    ppermute x33, starting transfers between devices, swap(): return lax.ppermute(array, axis, [(k, k ^ bit) for k in range(n)])  25.3 us
    all_to_all x1, waiting for transfers between devices, local(): nsum = lax.all_to_all(sums, 'ctx', 0, 0, tiled=True).reshape(nc * spans, D)  7.26 us
    all_to_all x1, starting transfers between devices, local(): nsum = lax.all_to_all(sums, 'ctx', 0, 0, tiled=True).reshape(nc * spans, D)  5.81 us
    pallas_call x1, Pallas kernels, block_output(): pl.pallas_call(mixed_kernel, grid=(rows // ROWS,), in_specs=[pl.BlockSpec...  4.13 us
    pallas_call x2, Pallas kernels, finish(): pl.pallas_call(functools.partial(finish_kernel, heights=heights, plan=pla...  3.78 us
    pallas_call x1, Pallas kernels, first_back(): pl.pallas_call(first_kernel, grid=(rows // ROWS,), in_specs=in_vmem(7), o...  3.44 us
  transfers between devices with their start and end apart: 34, of which 16 were waited for; matrix products, arithmetic and copies ran while one was open for 0% of the time, Pallas kernels for 44%

profile of v4, /device:TPU:0, one launch (start us, length us, event | category | flops | bytes accessed | tf_op | source)
XLA Modules:
  0.0 151.6 jit_solution(5994579544501075198)
XLA Ops:
  0.7 2.1 %pack.1.refs_0_ = bf16[144,2048]{1,0:T(8,128)(2,1)} custom-call(bf16[128,1536]{1,0:T(8,128)(2,1)} %qkv_ref.1, bf16[128,512]{1,0:T(8,128)(2,1)} %out_ref.1, bf16[1,128]{1,0:T(2,128)(2,1)} %bitcast.111, bf16[1,128]{1,0:T(2,128)(2,1)} %bitcast.112, bf16[3,128]{1,0:T(4,128)(2,1)} %bitcast.109, bf16[1,128]{1,0:T(2,128)(2,1)} %bitcast.113, ...), custom_call_target="tpu_custom_call" | custom-call | flops 1000000000 | bytes 1000000 | tf_op jit(solution)/shard_map/pack/pallas_call | solution.py:134
  2.7 3.0 %collective-permute-start.1 = (bf16[144,2048]{1,0:T(8,128)(2,1)}, bf16[144,2048]{1,0:T(8,128)(2,1)S(1)}, u32[]{:S(2)}, u32[]{:S(2)}) collective-permute-start(bf16[144,2048]{1,0:T(8,128)(2,1)} %pack.1.refs_0_), channel_id=1, source_target_pairs={{0,2},{1,3},{2,0},{3,1},{4,6},{5,7},{6,4},{7,5},{8,10},{9,11},{10,... | collective-permute-start | bytes 1769480 | tf_op jit(solution)/shard_map/ppermute | solution.py:659
  7.1 5.8 %all-to-all-start = ((f32[8,8,512]{2,1,0:T(8,128)}), f32[8,8,512]{2,1,0:T(8,128)S(1)}, u32[]{:S(2)}, u32[]{:S(2)}) async-start(f32[8,8,512]{2,1,0:T(8,128)} %span_sums.1), calls=%async_computation | async-start | bytes 262144 | tf_op jit(solution)/shard_map/all_to_all | solution.py:890
  13.0 7.3 %all-to-all-done = f32[8,8,512]{2,1,0:T(8,128)S(1)} async-done(((f32[8,8,512]{2,1,0:T(8,128)}), f32[8,8,512]{2,1,0:T(8,128)S(1)}, u32[]{:S(2)}, u32[]{:S(2)}) %all-to-all-start) | async-done | bytes 131104 | tf_op jit(solution)/shard_map/all_to_all | solution.py:890
  22.3 8.3 %attend.1 = (bf16[1024,1536]{1,0:T(8,128)(2,1)S(1)}, bf16[32,192,256]{2,1,0:T(8,128)(2,1)S(1)}, bf16[1024,512]{1,0:T(8,128)(2,1)S(1)}, bf16[1024,512]{1,0:T(8,12...) custom-call(s32[76]{0:T(128)S(1)} %concatenate.21.sc.refs_0_, ...), custom_call_target="tpu_custom_call" | custom-call | flops 12000000000 | bytes 12000000 | tf_op jit(solution)/shard_map/attend/pallas_call | solution.py:69
  30.6 4.3 %collective-permute-done.4.refs_2_ = bf16[128,2048]{1,0:T(8,128)(2,1)S(1)} collective-permute-done((bf16[128,2048]{1,0:T(8,128)(2,1)}, bf16[128,2048]{1,0:T(8,128)(2,1)S(1)}, u32[]{:S(2)}, u32[]{:S(2)}) %collective-permute-start.4) | collective-permute-done | bytes 524320 | tf_op jit(solution)/shard_map/ppermute | solution.py:659
  37.0 6.9 %ffn_up.1 = (bf16[1024,2048]{1,0:T(8,128)(2,1)S(1)}, bf16[1024,2048]{1,0:T(8,128)(2,1)S(1)}, bf16[512,2048]{1,0:T(8,128)(2,1)S(1)}) custom-call(s32[76]{0:T(128)S(1)} %concatenate.21.sc.refs_0_, bf16[1024,512]{1,0:T(8,128)(2,1)S(1)} %get-tuple-element.125.h2_ref, f32[8,2048]{1,0:T(8,128)S(1)} %get-tuple-element.123.vec.vec_ref.refs_8_, ...), custom_call_target="tpu_custom_call" | custom-call | flops 8000000000 | bytes 8000000 | tf_op jit(solution)/shard_map/ffn_up/pallas_call | solution.py:69
  44.0 2.9 %down_grad.1 = (bf16[2,2048,128]{2,1,0:T(8,128)(2,1)S(1)}, bf16[2,2048,128]{2,1,0:T(8,128)(2,1)S(1)}) custom-call(s32[76]{0:T(128)S(1)} %concatenate.21.sc.refs_0_, bf16[1024,2048]{1,0:T(8,128)(2,1)S(1)} %get-tuple-element.131.g_ref, bf16[1024,512]{1,0:T(8,128)(2,1)S(1)} %bitcast.66), custom_call_target="tpu_custom_call" | custom-call | flops 4000000000 | bytes 4000000 | tf_op jit(solution)/shard_map/down_grad/pallas_call | solution.py:69
  46.9 2.4 %collective-permute-done.7.refs_2_ = bf16[512,512]{1,0:T(8,128)(2,1)S(1)} collective-permute-done((bf16[512,512]{1,0:T(8,128)(2,1)S(1)}, bf16[512,512]{1,0:T(8,128)(2,1)S(1)}, u32[]{:S(2)}, u32[]{:S(2)}) %collective-permute-start.7) | collective-permute-done | bytes 524320 | tf_op jit(solution)/shard_map/ppermute | solution.py:659
  51.2 7.8 %ffn_down.1 = (f32[1024,512]{1,0:T(8,128)S(1)}, f32[1,2048]{1,0:T(1,128)S(1)}, bf16[2,2048,128]{2,1,0:T(8,128)(2,1)S(1)}, bf16[2,2048,128]{2,1,0:T(8,128)(2,1)S(1)}) custom-call(s32[76]{0:T(128)S(1)} %concatenate.21.sc.refs_0_, bf16[1024,512]{1,0:T(8,128)(2,1)S(1)} %get-tuple-element.125.h2_ref, bf16[1024,512]{1,0:T(8,128)(2,1)S(1)} %bitcast.67, ...), custom_call_target="tpu_custom_call" | custom-call | flops 8000000000 | bytes 8000000 | tf_op jit(solution)/shard_map/ffn_down/pallas_call | solution.py:69
  60.8 2.6 %mid.1 = (f32[1024,512]{1,0:T(8,128)S(1)}, bf16[1024,512]{1,0:T(8,128)(2,1)S(1)}, f32[512,512]{1,0:T(8,128)S(1)}, f32[8,512]{1,0:T(8,128)S(1)}) custom-call(bf16[1024,512]{1,0:T(8,128)(2,1)S(1)} %bitcast.68, f32[1024,512]{1,0:T(8,128)S(1)} %get-tuple-element.138.dh2_ref, f32[1024,512]{1,0:T(8,128)S(1)} %get-tuple-element.187.r1_ref, ...), custom_call_target="tpu_custom_call" | custom-call | flops 5000000000 | bytes 5000000 | tf_op jit(solution)/shard_map/mid/pallas_call | solution.py:69
  65.7 8.8 %back_0.1 = (f32[1024,512]{1,0:T(8,128)S(1)}, f32[72,512]{1,0:T(8,128)S(1)}, bf16[128,128]{1,0:T(8,128)(2,1)S(1)}, bf16[128,128]{1,0:T(8,128)(2,1)S(1)}, bf16[2,...) custom-call(s32[76]{0:T(128)S(1)} %concatenate.21.sc.refs_0_, bf16[1024,512]{1,0:T(8,128)(2,1)S(1)} %bitcast.72, ...), custom_call_target="tpu_custom_call" | custom-call | flops 8999999488 | bytes 9000000 | tf_op jit(solution)/shard_map/back_0/pallas_call | solution.py:69
  79.2 1.9 %collective-permute-start.15 = (bf16[1,1024,128]{2,1,0:T(8,128)(2,1)S(1)}, bf16[1,1024,128]{2,1,0:T(8,128)(2,1)S(1)}, u32[]{:S(2)}, u32[]{:S(2)}) collective-permute-start(bf16[1,1024,128]{2,1,0:T(8,128)(2,1)S(1)} %get-tuple-element.160), channel_id=1, source_target_pairs={{0,2},{1,3},{2,0},{3,1},{4,6},{5,7},{6,4},{7,5},{8,10},{9,11},{10,... | collective-permute-start | bytes 786440 | tf_op jit(solution)/shard_map/ppermute | solution.py:659
  81.1 4.3 %back_1.2 = (f32[512,512]{1,0:T(8,128)S(1)}, f32[512,768]{1,0:T(8,128)S(1)}, f32[64,512]{1,0:T(8,128)S(1)}, f32[16,1536]{1,0:T(8,128)S(1)}) custom-call(s32[76]{0:T(128)S(1)} %concatenate.21.sc.refs_0_, bf16[1024,512]{1,0:T(8,128)(2,1)S(1)} %bitcast.73, bf16[1024,512]{1,0:T(8,128)(2,1)S(1)} %get-tuple-element.145.refs_2_, ...), custom_call_target="tpu_custom_call" | custom-call | flops 8999999488 | bytes 9000000 | tf_op jit(solution)/shard_map/back_1/pallas_call | solution.py:69
  87.2 1.9 %collective-permute-start.16 = (bf16[1024,128]{1,0:T(8,128)(2,1)S(1)}, bf16[1024,128]{1,0:T(8,128)(2,1)S(1)}, u32[]{:S(2)}, u32[]{:S(2)}) collective-permute-start(bf16[1024,128]{1,0:T(8,128)(2,1)S(1)} %bitcast.84), channel_id=1, source_target_pairs={{0,8},{4,12},{8,0},{12,4},{16,24},{20,28},{24,16},{28,20},{1,9},{5... | collective-permute-start | bytes 786440 | tf_op jit(solution)/shard_map/ppermute | solution.py:659
  89.1 5.4 %back_1.3 = (f32[512,512]{1,0:T(8,128)S(1)}, f32[72,512]{1,0:T(8,128)}, bf16[128,128]{1,0:T(8,128)(2,1)S(1)}, bf16[128,128]{1,0:T(8,128)(2,1)S(1)}, bf16[2,896,1...) custom-call(s32[76]{0:T(128)S(1)} %concatenate.21.sc.refs_0_, bf16[1024,512]{1,0:T(8,128)(2,1)S(1)} %bitcast.74, ...), custom_call_target="tpu_custom_call" | custom-call | flops 8999999488 | bytes 9000000 | tf_op jit(solution)/shard_map/back_1/pallas_call | solution.py:69
  94.5 1.6 %collective-permute-start.20 = (bf16[128,128]{1,0:T(8,128)(2,1)S(1)}, bf16[128,128]{1,0:T(8,128)(2,1)S(1)}, u32[]{:S(2)}, u32[]{:S(2)}) collective-permute-start(bf16[128,128]{1,0:T(8,128)(2,1)S(1)} %get-tuple-element.189), channel_id=1, source_target_pairs={{0,4},{4,0},{8,12},{12,8},{16,20},{20,16},{24,28},{28,24},{1,5},{5... | collective-permute-start | bytes 98312 | tf_op jit(solution)/shard_map/ppermute | solution.py:659
  96.7 2.7 %collective-permute-start.22 = (bf16[512,128]{1,0:T(8,128)(2,1)S(1)}, bf16[512,128]{1,0:T(8,128)(2,1)S(1)}, u32[]{:S(2)}, u32[]{:S(2)}) collective-permute-start(bf16[512,128]{1,0:T(8,128)(2,1)S(1)} %get-tuple-element.179), channel_id=1, source_target_pairs={{0,16},{4,20},{8,24},{12,28},{16,0},{20,4},{24,8},{28,12},{1,17},{... | collective-permute-start | bytes 393224 | tf_op jit(solution)/shard_map/ppermute | solution.py:659
  101.5 4.1 %block_output.1 = bf16[1024,512]{1,0:T(8,128)(2,1)} custom-call(s32[76]{0:T(128)S(1)} %concatenate.21.sc.refs_0_, f32[1024,512]{1,0:T(8,128)S(1)} %get-tuple-element.187.r1_ref, bf16[1024,2048]{1,0:T(8,128)(2,1)S(1)} %get-tuple-element.131.g_ref, f32[8,2048]{1,0:T(8,128)S(1)} %get-tuple-element.123.vec.vec_ref.refs_8_, bf16[512,512]{1,0:T(8,128)(2,1)S(1)} %copy-done.5, ...), custom_call_target="tpu_custom_call" | custom-call | flops 4000000000 | bytes 4000000 | tf_op jit(solution)/shard_map/block_output/pallas_call | solution.py:645
  105.7 2.7 %collective-permute-done.21 = bf16[1,896,128]{2,1,0:T(8,128)(2,1)S(1)} collective-permute-done((bf16[1,896,128]{2,1,0:T(8,128)(2,1)S(1)}, bf16[1,896,128]{2,1,0:T(8,128)(2,1)S(1)}, u32[]{:S(2)}, u32[]{:S(2)}) %collective-permute-start.21) | collective-permute-done | bytes 229408 | tf_op jit(solution)/shard_map/ppermute | solution.py:659
  109.0 1.7 %collective-permute-start.24 = (bf16[1,448,128]{2,1,0:T(8,128)(2,1)S(1)}, bf16[1,448,128]{2,1,0:T(8,128)(2,1)S(1)}, u32[]{:S(2)}, u32[]{:S(2)}) collective-permute-start(bf16[1,448,128]{2,1,0:T(8,128)(2,1)S(1)} %get-tuple-element.192), channel_id=1, source_target_pairs={{0,4},{4,0},{8,12},{12,8},{16,20},{20,16},{24,28},{28,24},{1,5},{5... | collective-permute-start | bytes 344072 | tf_op jit(solution)/shard_map/ppermute | solution.py:659
  111.1 2.7 %collective-permute-done.24 = bf16[1,448,128]{2,1,0:T(8,128)(2,1)S(1)} collective-permute-done((bf16[1,448,128]{2,1,0:T(8,128)(2,1)S(1)}, bf16[1,448,128]{2,1,0:T(8,128)(2,1)S(1)}, u32[]{:S(2)}, u32[]{:S(2)}) %collective-permute-start.24) | collective-permute-done | bytes 114720 | tf_op jit(solution)/shard_map/ppermute | solution.py:659
  115.0 3.3 %collective-permute-done.25 = bf16[512,128]{1,0:T(8,128)(2,1)S(1)} collective-permute-done((bf16[512,128]{1,0:T(8,128)(2,1)S(1)}, bf16[512,128]{1,0:T(8,128)(2,1)S(1)}, u32[]{:S(2)}, u32[]{:S(2)}) %collective-permute-start.25) | collective-permute-done | bytes 131104 | tf_op jit(solution)/shard_map/ppermute | solution.py:659
  118.4 2.2 %collective-permute-done.26.got_ref = bf16[672,128]{1,0:T(8,128)(2,1)S(1)} collective-permute-done((bf16[672,128]{1,0:T(8,128)(2,1)S(1)}, bf16[672,128]{1,0:T(8,128)(2,1)S(1)}, u32[]{:S(2)}, u32[]{:S(2)}) %collective-permute-start.26) | collective-permute-done | bytes 172064 | tf_op jit(solution)/shard_map/ppermute | solution.py:659
  121.7 5.5 %collective-permute-done.27.got_ref = bf16[336,128]{1,0:T(8,128)(2,1)S(1)} collective-permute-done((bf16[336,128]{1,0:T(8,128)(2,1)S(1)}, bf16[336,128]{1,0:T(8,128)(2,1)S(1)}, u32[]{:S(2)}, u32[]{:S(2)}) %collective-permute-start.27) | collective-permute-done | bytes 86048 | tf_op jit(solution)/shard_map/ppermute | solution.py:659
  127.7 3.0 %collective-permute-done.28 = bf16[1024,128]{1,0:T(8,128)(2,1)S(1)} collective-permute-done((bf16[1024,128]{1,0:T(8,128)(2,1)S(1)}, bf16[1024,128]{1,0:T(8,128)(2,1)S(1)}, u32[]{:S(2)}, u32[]{:S(2)}) %collective-permute-start.28) | collective-permute-done | bytes 262176 | tf_op jit(solution)/shard_map/ppermute | solution.py:659
  131.2 3.4 %first_back.1 = f32[1024,512]{1,0:T(8,128)} custom-call(bf16[1024,512]{1,0:T(8,128)(2,1)S(1)} %bitcast.75, f32[1024,512]{1,0:T(8,128)S(1)} %get-tuple-element.207.dr1_ref, f32[512,512]{1,0:T(8,128)S(1)} %get-tuple-element.208.upper_ref, f32[512,512]{1,0:T(8,128)S(1)} %get-tuple-element.176.lower_ref, bf16[64,128]{1,0:T(8,128)(2,1)S(1)} %get-tuple-element.209.own_ref, ...), custom_call_target="tpu_custom_call" | custom-call | flops 3000000000 | bytes 3000000 | tf_op jit(solution)/shard_map/first_back/pallas_call | solution.py:619
  135.0 4.8 %collective-permute-done.30 = bf16[544,128]{1,0:T(8,128)(2,1)S(1)} collective-permute-done((bf16[544,128]{1,0:T(8,128)(2,1)S(1)}, bf16[544,128]{1,0:T(8,128)(2,1)S(1)}, u32[]{:S(2)}, u32[]{:S(2)}) %collective-permute-start.30) | collective-permute-done | bytes 139296 | tf_op jit(solution)/shard_map/ppermute | solution.py:659
  139.8 1.7 %collective-permute-start.32 = (bf16[1088,128]{1,0:T(8,128)(2,1)S(1)}, bf16[1088,128]{1,0:T(8,128)(2,1)S(1)}, u32[]{:S(2)}, u32[]{:S(2)}) collective-permute-start(bf16[1088,128]{1,0:T(8,128)(2,1)S(1)} %constant_dynamic-update-slice_fusion.6), channel_id=1, source_target_pairs={{0,4},{4,0},{8,12},{12,8},{16,20},{20,16},{24,28},{28,24},{1,5},{5... | collective-permute-start | bytes 835592 | tf_op jit(solution)/shard_map/ppermute | solution.py:659
  141.6 4.2 %collective-permute-done.31 = bf16[2048,128]{1,0:T(8,128)(2,1)S(1)} collective-permute-done((bf16[2048,128]{1,0:T(8,128)(2,1)S(1)}, bf16[2048,128]{1,0:T(8,128)(2,1)S(1)}, u32[]{:S(2)}, u32[]{:S(2)}) %collective-permute-start.31) | collective-permute-done | bytes 524320 | tf_op jit(solution)/shard_map/ppermute | solution.py:659
  145.8 2.1 %finish.2 = (f32[512,512]{1,0:T(8,128)}, f32[128,2048]{1,0:T(8,128)}) custom-call(s32[76]{0:T(128)S(1)} %concatenate.21.sc.refs_0_, bf16[8,512,128]{2,1,0:T(8,128)(2,1)S(1)} %bitcast.59), custom_call_target="tpu_custom_call" | custom-call | flops 2000000000 | bytes 2000000 | tf_op jit(solution)/shard_map/finish/pallas_call | solution.py:855
  149.3 1.6 %finish.3 = (f32[128,1536]{1,0:T(8,128)}, f32[128,512]{1,0:T(8,128)}, f32[1,128]{1,0:T(1,128)}, f32[1,128]{1,0:T(1,128)}, f32[1,384]{1,0:T(1,128)S(1)}, /*index=...) custom-call(s32[76]{0:T(128)S(1)} %concatenate.21.sc.refs_0_, ...), custom_call_target="tpu_custom_call" | custom-call | flops 2000000000 | bytes 2000000 | tf_op jit(solution)/shard_map/finish/pallas_call | solution.py:855
  (91 shorter events, 27.4 us)
Async XLA Ops:
  2.7 17.5 %collective-permute-start.1 = (bf16[144,2048]{1,0:T(8,128)(2,1)}, bf16[144,2048]{1,0:T(8,128)(2,1)S(1)}, u32[]{:S(2)}, u32[]{:S(2)}) collective-permute-start(bf16[144,2048]{1,0:T(8,128)(2,1)} %pack.1.refs_0_), channel_id=1, source_target_pairs={{0,2},{1,3},{2,0},{3,1},{4,6},{5,7},{6,4},{7,5},{8,10},{9,11},{10,... | collective-permute-start | bytes 1769480 | tf_op jit(solution)/shard_map/ppermute | solution.py:659
  7.1 13.1 %all-to-all-start = ((f32[8,8,512]{2,1,0:T(8,128)}), f32[8,8,512]{2,1,0:T(8,128)S(1)}, u32[]{:S(2)}, u32[]{:S(2)}) async-start(f32[8,8,512]{2,1,0:T(8,128)} %span_sums.1), calls=%async_computation | async-start | bytes 262144 | tf_op jit(solution)/shard_map/all_to_all | solution.py:890
  12.9 8.4 %collective-permute-start = (bf16[144,2048]{1,0:T(8,128)(2,1)S(1)}, bf16[144,2048]{1,0:T(8,128)(2,1)S(1)}, u32[]{:S(2)}, u32[]{:S(2)}) collective-permute-start(bf16[144,2048]{1,0:T(8,128)(2,1)S(1)} %copy-done.3), channel_id=1, source_target_pairs={{0,1},{1,0},{2,3},{3,2},{4,5},{5,4},{6,7},{7,6},{8,9},{9,8},{10,11... | collective-permute-start | bytes 1769480 | tf_op jit(solution)/shard_map/ppermute | solution.py:659
  20.4 14.6 %collective-permute-start.4 = (bf16[128,2048]{1,0:T(8,128)(2,1)}, bf16[128,2048]{1,0:T(8,128)(2,1)S(1)}, u32[]{:S(2)}, u32[]{:S(2)}) collective-permute-start(bf16[128,2048]{1,0:T(8,128)(2,1)} %refs_0_), channel_id=1, source_target_pairs={{0,2},{1,3},{2,0},{3,1},{4,6},{5,7},{6,4},{7,5},{8,10},{9,11},{10,... | collective-permute-start | bytes 1572872 | tf_op jit(solution)/shard_map/ppermute | solution.py:659
  21.1 15.9 %collective-permute-start.3 = (bf16[128,2048]{1,0:T(8,128)(2,1)}, bf16[128,2048]{1,0:T(8,128)(2,1)S(1)}, u32[]{:S(2)}, u32[]{:S(2)}) collective-permute-start(bf16[128,2048]{1,0:T(8,128)(2,1)} %refs_0_), channel_id=1, source_target_pairs={{0,1},{1,0},{2,3},{3,2},{4,5},{5,4},{6,7},{7,6},{8,9},{9,8},{10,11... | collective-permute-start | bytes 1572872 | tf_op jit(solution)/shard_map/ppermute | solution.py:659
  34.9 2.1 %collective-permute-start.5 = (bf16[128,2048]{1,0:T(8,128)(2,1)S(1)}, bf16[128,2048]{1,0:T(8,128)(2,1)S(1)}, u32[]{:S(2)}, u32[]{:S(2)}) collective-permute-start(bf16[128,2048]{1,0:T(8,128)(2,1)S(1)} %collective-permute-done.4.refs_2_), channel_id=1, source_target_pairs={{0,1},{1,0},{2,3},{3,2},{4,5},{5,4},{6,7},{7,6},{8,9},{9,8},{10,11... | collective-permute-start | bytes 1572872 | tf_op jit(solution)/shard_map/ppermute | solution.py:659
  34.9 14.3 %collective-permute-start.7 = (bf16[512,512]{1,0:T(8,128)(2,1)S(1)}, bf16[512,512]{1,0:T(8,128)(2,1)S(1)}, u32[]{:S(2)}, u32[]{:S(2)}) collective-permute-start(bf16[512,512]{1,0:T(8,128)(2,1)S(1)} %copy-done.5), channel_id=1, source_target_pairs={{0,2},{1,3},{2,0},{3,1},{4,6},{5,7},{6,4},{7,5},{8,10},{9,11},{10,... | collective-permute-start | bytes 1572872 | tf_op jit(solution)/shard_map/ppermute | solution.py:659
  35.6 14.1 %collective-permute-start.6 = (bf16[512,512]{1,0:T(8,128)(2,1)S(1)}, bf16[512,512]{1,0:T(8,128)(2,1)S(1)}, u32[]{:S(2)}, u32[]{:S(2)}) collective-permute-start(bf16[512,512]{1,0:T(8,128)(2,1)S(1)} %copy-done.5), channel_id=1, source_target_pairs={{0,1},{1,0},{2,3},{3,2},{4,5},{5,4},{6,7},{7,6},{8,9},{9,8},{10,11... | collective-permute-start | bytes 1572872 | tf_op jit(solution)/shard_map/ppermute | solution.py:659
  49.2 9.9 %collective-permute-start.9 = (bf16[2,2048,128]{2,1,0:T(8,128)(2,1)S(1)}, bf16[2,2048,128]{2,1,0:T(8,128)(2,1)S(1)}, u32[]{:S(2)}, u32[]{:S(2)}) collective-permute-start(bf16[2,2048,128]{2,1,0:T(8,128)(2,1)S(1)} %get-tuple-element.135), channel_id=1, source_target_pairs={{0,1},{1,0},{2,3},{3,2},{4,5},{5,4},{6,7},{7,6},{8,9},{9,8},{10,11... | collective-permute-start | bytes 3145736 | tf_op jit(solution)/shard_map/ppermute | solution.py:659
  59.0 4.4 %collective-permute-start.10 = (bf16[2,2048,128]{2,1,0:T(8,128)(2,1)S(1)}, bf16[2,2048,128]{2,1,0:T(8,128)(2,1)S(1)}, u32[]{:S(2)}, u32[]{:S(2)}) collective-permute-start(bf16[2,2048,128]{2,1,0:T(8,128)(2,1)S(1)} %get-tuple-element.142), channel_id=1, source_target_pairs={{0,1},{1,0},{2,3},{3,2},{4,5},{5,4},{6,7},{7,6},{8,9},{9,8},{10,11... | collective-permute-start | bytes 3145736 | tf_op jit(solution)/shard_map/ppermute | solution.py:659
  60.0 14.6 %collective-permute-start.11 = (bf16[1,2048,128]{2,1,0:T(8,128)(2,1)S(1)}, bf16[1,2048,128]{2,1,0:T(8,128)(2,1)S(1)}, u32[]{:S(2)}, u32[]{:S(2)}) collective-permute-start(bf16[1,2048,128]{2,1,0:T(8,128)(2,1)S(1)} %get-tuple-element.137), channel_id=1, source_target_pairs={{0,2},{1,3},{2,0},{3,1},{4,6},{5,7},{6,4},{7,5},{8,10},{9,11},{10,... | collective-permute-start | bytes 1572872 | tf_op jit(solution)/shard_map/ppermute | solution.py:659
  64.2 14.3 %collective-permute-start.12 = (bf16[2,1024,128]{2,1,0:T(8,128)(2,1)S(1)}, bf16[2,1024,128]{2,1,0:T(8,128)(2,1)S(1)}, u32[]{:S(2)}, u32[]{:S(2)}) collective-permute-start(bf16[2,1024,128]{2,1,0:T(8,128)(2,1)S(1)} %get-tuple-element.144), channel_id=1, source_target_pairs={{0,4},{4,0},{8,12},{12,8},{16,20},{20,16},{24,28},{28,24},{1,5},{5... | collective-permute-start | bytes 1572872 | tf_op jit(solution)/shard_map/ppermute | solution.py:659
  75.3 11.1 %collective-permute-start.14 = (bf16[1,1024,128]{2,1,0:T(8,128)(2,1)S(1)}, bf16[1,1024,128]{2,1,0:T(8,128)(2,1)S(1)}, u32[]{:S(2)}, u32[]{:S(2)}) collective-permute-start(bf16[1,1024,128]{2,1,0:T(8,128)(2,1)S(1)} %get-tuple-element.157), channel_id=1, source_target_pairs={{0,4},{4,0},{8,12},{12,8},{16,20},{20,16},{24,28},{28,24},{1,5},{5... | collective-permute-start | bytes 786440 | tf_op jit(solution)/shard_map/ppermute | solution.py:659
  75.9 9.5 %collective-permute-start.13 = (bf16[2,1280,128]{2,1,0:T(8,128)(2,1)S(1)}, bf16[2,1280,128]{2,1,0:T(8,128)(2,1)S(1)}, u32[]{:S(2)}, u32[]{:S(2)}) collective-permute-start(bf16[2,1280,128]{2,1,0:T(8,128)(2,1)S(1)} %get-tuple-element.166), channel_id=1, source_target_pairs={{0,1},{1,0},{2,3},{3,2},{4,5},{5,4},{6,7},{7,6},{8,9},{9,8},{10,11... | collective-permute-start | bytes 1966088 | tf_op jit(solution)/shard_map/ppermute | solution.py:659
  75.9 29.8 %collective-permute-start.19 = (bf16[128,128]{1,0:T(8,128)(2,1)S(1)}, bf16[128,128]{1,0:T(8,128)(2,1)S(1)}, u32[]{:S(2)}, u32[]{:S(2)}) collective-permute-start(bf16[128,128]{1,0:T(8,128)(2,1)S(1)} %get-tuple-element.188), channel_id=1, source_target_pairs={{0,4},{4,0},{8,12},{12,8},{16,20},{20,16},{24,28},{28,24},{1,5},{5... | collective-permute-start | bytes 98312 | tf_op jit(solution)/shard_map/ppermute | solution.py:659
  79.2 7.3 %collective-permute-start.15 = (bf16[1,1024,128]{2,1,0:T(8,128)(2,1)S(1)}, bf16[1,1024,128]{2,1,0:T(8,128)(2,1)S(1)}, u32[]{:S(2)}, u32[]{:S(2)}) collective-permute-start(bf16[1,1024,128]{2,1,0:T(8,128)(2,1)S(1)} %get-tuple-element.160), channel_id=1, source_target_pairs={{0,2},{1,3},{2,0},{3,1},{4,6},{5,7},{6,4},{7,5},{8,10},{9,11},{10,... | collective-permute-start | bytes 786440 | tf_op jit(solution)/shard_map/ppermute | solution.py:659
  86.1 13.3 %collective-permute-start.17 = (bf16[1,1280,128]{2,1,0:T(8,128)(2,1)S(1)}, bf16[1,1280,128]{2,1,0:T(8,128)(2,1)S(1)}, u32[]{:S(2)}, u32[]{:S(2)}) collective-permute-start(bf16[1,1280,128]{2,1,0:T(8,128)(2,1)S(1)} %get-tuple-element.168), channel_id=1, source_target_pairs={{0,2},{1,3},{2,0},{3,1},{4,6},{5,7},{6,4},{7,5},{8,10},{9,11},{10,... | collective-permute-start | bytes 983048 | tf_op jit(solution)/shard_map/ppermute | solution.py:659
  87.2 8.9 %collective-permute-start.16 = (bf16[1024,128]{1,0:T(8,128)(2,1)S(1)}, bf16[1024,128]{1,0:T(8,128)(2,1)S(1)}, u32[]{:S(2)}, u32[]{:S(2)}) collective-permute-start(bf16[1024,128]{1,0:T(8,128)(2,1)S(1)} %bitcast.84), channel_id=1, source_target_pairs={{0,8},{4,12},{8,0},{12,4},{16,24},{20,28},{24,16},{28,20},{1,9},{5... | collective-permute-start | bytes 786440 | tf_op jit(solution)/shard_map/ppermute | solution.py:659
  94.5 6.0 %collective-permute-start.18 = (bf16[2,896,128]{2,1,0:T(8,128)(2,1)S(1)}, bf16[2,896,128]{2,1,0:T(8,128)(2,1)S(1)}, u32[]{:S(2)}, u32[]{:S(2)}) collective-permute-start(bf16[2,896,128]{2,1,0:T(8,128)(2,1)S(1)} %get-tuple-element.184), channel_id=1, source_target_pairs={{0,1},{1,0},{2,3},{3,2},{4,5},{5,4},{6,7},{7,6},{8,9},{9,8},{10,11... | collective-permute-start | bytes 1376264 | tf_op jit(solution)/shard_map/ppermute | solution.py:659
  94.5 11.2 %collective-permute-start.20 = (bf16[128,128]{1,0:T(8,128)(2,1)S(1)}, bf16[128,128]{1,0:T(8,128)(2,1)S(1)}, u32[]{:S(2)}, u32[]{:S(2)}) collective-permute-start(bf16[128,128]{1,0:T(8,128)(2,1)S(1)} %get-tuple-element.189), channel_id=1, source_target_pairs={{0,4},{4,0},{8,12},{12,8},{16,20},{20,16},{24,28},{28,24},{1,5},{5... | collective-permute-start | bytes 98312 | tf_op jit(solution)/shard_map/ppermute | solution.py:659
  96.7 14.0 %collective-permute-start.22 = (bf16[512,128]{1,0:T(8,128)(2,1)S(1)}, bf16[512,128]{1,0:T(8,128)(2,1)S(1)}, u32[]{:S(2)}, u32[]{:S(2)}) collective-permute-start(bf16[512,128]{1,0:T(8,128)(2,1)S(1)} %get-tuple-element.179), channel_id=1, source_target_pairs={{0,16},{4,20},{8,24},{12,28},{16,0},{20,4},{24,8},{28,12},{1,17},{... | collective-permute-start | bytes 393224 | tf_op jit(solution)/shard_map/ppermute | solution.py:659
  100.0 11.1 %collective-permute-start.23 = (bf16[1,640,128]{2,1,0:T(8,128)(2,1)S(1)}, bf16[1,640,128]{2,1,0:T(8,128)(2,1)S(1)}, u32[]{:S(2)}, u32[]{:S(2)}) collective-permute-start(bf16[1,640,128]{2,1,0:T(8,128)(2,1)S(1)} %get-tuple-element.182), channel_id=1, source_target_pairs={{0,4},{4,0},{8,12},{12,8},{16,20},{20,16},{24,28},{28,24},{1,5},{5... | collective-permute-start | bytes 491528 | tf_op jit(solution)/shard_map/ppermute | solution.py:659
  101.1 7.2 %collective-permute-start.21 = (bf16[1,896,128]{2,1,0:T(8,128)(2,1)S(1)}, bf16[1,896,128]{2,1,0:T(8,128)(2,1)S(1)}, u32[]{:S(2)}, u32[]{:S(2)}) collective-permute-start(bf16[1,896,128]{2,1,0:T(8,128)(2,1)S(1)} %get-tuple-element.186), channel_id=1, source_target_pairs={{0,2},{1,3},{2,0},{3,1},{4,6},{5,7},{6,4},{7,5},{8,10},{9,11},{10,... | collective-permute-start | bytes 688136 | tf_op jit(solution)/shard_map/ppermute | solution.py:659
  109.0 4.9 %collective-permute-start.24 = (bf16[1,448,128]{2,1,0:T(8,128)(2,1)S(1)}, bf16[1,448,128]{2,1,0:T(8,128)(2,1)S(1)}, u32[]{:S(2)}, u32[]{:S(2)}) collective-permute-start(bf16[1,448,128]{2,1,0:T(8,128)(2,1)S(1)} %get-tuple-element.192), channel_id=1, source_target_pairs={{0,4},{4,0},{8,12},{12,8},{16,20},{20,16},{24,28},{28,24},{1,5},{5... | collective-permute-start | bytes 344072 | tf_op jit(solution)/shard_map/ppermute | solution.py:659
  110.7 7.6 %collective-permute-start.25 = (bf16[512,128]{1,0:T(8,128)(2,1)S(1)}, bf16[512,128]{1,0:T(8,128)(2,1)S(1)}, u32[]{:S(2)}, u32[]{:S(2)}) collective-permute-start(bf16[512,128]{1,0:T(8,128)(2,1)S(1)} %last.2), channel_id=1, source_target_pairs={{0,16},{4,20},{8,24},{12,28},{16,0},{20,4},{24,8},{28,12},{1,17},{... | collective-permute-start | bytes 393224 | tf_op jit(solution)/shard_map/ppermute | solution.py:659
  114.5 6.1 %collective-permute-start.26 = (bf16[672,128]{1,0:T(8,128)(2,1)S(1)}, bf16[672,128]{1,0:T(8,128)(2,1)S(1)}, u32[]{:S(2)}, u32[]{:S(2)}) collective-permute-start(bf16[672,128]{1,0:T(8,128)(2,1)S(1)} %bitcast.87), channel_id=1, source_target_pairs={{0,8},{4,12},{8,0},{12,4},{16,24},{20,28},{24,16},{28,20},{1,9},{5... | collective-permute-start | bytes 516104 | tf_op jit(solution)/shard_map/ppermute | solution.py:659
  121.2 6.1 %collective-permute-start.27 = (bf16[336,128]{1,0:T(8,128)(2,1)S(1)}, bf16[336,128]{1,0:T(8,128)(2,1)S(1)}, u32[]{:S(2)}, u32[]{:S(2)}) collective-permute-start(bf16[336,128]{1,0:T(8,128)(2,1)S(1)} %get-tuple-element.202), channel_id=1, source_target_pairs={{0,16},{4,20},{8,24},{12,28},{16,0},{20,4},{24,8},{28,12},{1,17},{... | collective-permute-start | bytes 258056 | tf_op jit(solution)/shard_map/ppermute | solution.py:659
  121.3 9.5 %collective-permute-start.28 = (bf16[1024,128]{1,0:T(8,128)(2,1)S(1)}, bf16[1024,128]{1,0:T(8,128)(2,1)S(1)}, u32[]{:S(2)}, u32[]{:S(2)}) collective-permute-start(bf16[1024,128]{1,0:T(8,128)(2,1)S(1)} %constant_dynamic-update-slice_fusion), channel_id=1, source_target_pairs={{0,8},{4,12},{8,0},{12,4},{16,24},{20,28},{24,16},{28,20},{1,9},{5... | collective-permute-start | bytes 786440 | tf_op jit(solution)/shard_map/ppermute | solution.py:659
  127.3 7.4 %collective-permute-start.29 = (bf16[272,128]{1,0:T(8,128)(2,1)S(1)}, bf16[272,128]{1,0:T(8,128)(2,1)S(1)}, u32[]{:S(2)}, u32[]{:S(2)}) collective-permute-start(bf16[272,128]{1,0:T(8,128)(2,1)S(1)} %get-tuple-element.210), channel_id=1, source_target_pairs={{0,16},{4,20},{8,24},{12,28},{16,0},{20,4},{24,8},{28,12},{1,17},{... | collective-permute-start | bytes 208904 | tf_op jit(solution)/shard_map/ppermute | solution.py:659
  130.8 14.9 %collective-permute-start.31 = (bf16[2048,128]{1,0:T(8,128)(2,1)S(1)}, bf16[2048,128]{1,0:T(8,128)(2,1)S(1)}, u32[]{:S(2)}, u32[]{:S(2)}) collective-permute-start(bf16[2048,128]{1,0:T(8,128)(2,1)S(1)} %constant_dynamic-update-slice_fusion.2), channel_id=1, source_target_pairs={{0,4},{4,0},{8,12},{12,8},{16,20},{20,16},{24,28},{28,24},{1,5},{5... | collective-permute-start | bytes 1572872 | tf_op jit(solution)/shard_map/ppermute | solution.py:659
  134.7 5.1 %collective-permute-start.30 = (bf16[544,128]{1,0:T(8,128)(2,1)S(1)}, bf16[544,128]{1,0:T(8,128)(2,1)S(1)}, u32[]{:S(2)}, u32[]{:S(2)}) collective-permute-start(bf16[544,128]{1,0:T(8,128)(2,1)S(1)} %constant_dynamic-update-slice_fusion.4), channel_id=1, source_target_pairs={{0,8},{4,12},{8,0},{12,4},{16,24},{20,28},{24,16},{28,20},{1,9},{5... | collective-permute-start | bytes 417800 | tf_op jit(solution)/shard_map/ppermute | solution.py:659
  139.8 9.4 %collective-permute-start.32 = (bf16[1088,128]{1,0:T(8,128)(2,1)S(1)}, bf16[1088,128]{1,0:T(8,128)(2,1)S(1)}, u32[]{:S(2)}, u32[]{:S(2)}) collective-permute-start(bf16[1088,128]{1,0:T(8,128)(2,1)S(1)} %constant_dynamic-update-slice_fusion.6), channel_id=1, source_target_pairs={{0,4},{4,0},{8,12},{12,8},{16,20},{20,16},{24,28},{28,24},{1,5},{5... | collective-permute-start | bytes 835592 | tf_op jit(solution)/shard_map/ppermute | solution.py:659
  (9 other events, 68.0 us)

commit v5 on v4

--- a/solution.py
+++ b/solution.py
@@ -17,7 +17,7 @@
 EPSILON = 1e-05
 MASKED = -1e30
 SCALE = HEAD**-0.5
-FILL = 4
+FILL = 6
 INV_ROOT = SPAN**-0.5
 F32 = jnp.float32
 BF16 = jnp.bfloat16
@@ -679,42 +679,81 @@
     return [held[r] for r in range(n)]
 
 
-def fold_kernel(sc, *refs, bit):
+def total_of(values):
+    total = values[0].astype(F32)
+    for value in values[1:]:
+        total = total + value.astype(F32)
+    return total.astype(BF16)
+
+
+def fold_kernel(sc, *refs, bit, counts):
     own = lax.div(sc[SC_C], bit) & 1 if bit else 0
     arrays, (send_ref, own_ref) = refs[:-2], refs[-2:]
     at = 0
-    for keep_ref, got_ref in zip(arrays[0::2], arrays[1::2]):
-        a, _, h, _ = keep_ref.shape
+    for count in counts:
+        group, arrays = arrays[:count], arrays[count:]
+        a, _, h, _ = group[0].shape
         for ref, half in ((send_ref, 1 - own), (own_ref, own)):
             for k in range(a):
-                total = keep_ref[k, half].astype(F32) + got_ref[k, half].astype(F32)
-                ref[k, at : at + h, :] = total.astype(BF16)
+                ref[k, at : at + h, :] = total_of([g[k, half] for g in group])
         at += h
 
 
-def fold(sc, bit, *pairs, micros=1):
-    a = pairs[0][0].shape[0]
-    h = sum(keep.shape[2] for keep, _ in pairs)
-    arrays = [array for pair in pairs for array in pair]
-    kernel = functools.partial(fold_kernel, bit=bit)
+def fold(sc, bit, *groups, micros=1):
+    a = groups[0][0].shape[0]
+    h = sum(group[0].shape[2] for group in groups)
+    arrays = [array for group in groups for array in group]
+    counts = tuple(len(group) for group in groups)
+    kernel = functools.partial(fold_kernel, bit=bit, counts=counts)
     return resident(kernel, "fold", micros, 8, (sc,), arrays, [((a, h, LANE), BF16)] * 2)
 
 
-def refold_kernel(sc, keep_ref, got_ref, send_ref, own_ref, *, bit, sizes):
+def quad_kernel(sc, keep_ref, got_ref, *refs, bit):
+    along, (own_ref, ctx_ref, near_ref, both_ref) = refs[:-4], refs[-4:]
+    own = lax.div(sc[SC_C], bit) & 1
+    for ref, x in ((own_ref, own), (ctx_ref, 1 - own)):
+        at = keep_ref.shape[2]
+        ref[:at, :] = total_of((keep_ref[0, x], got_ref[0, x]))
+        for array in along[0::2] if ref is own_ref else along[1::2]:
+            ref[at : at + array.shape[0], :] = array[...]
+            at += array.shape[0]
+    near_ref[...] = total_of((keep_ref[1, own], got_ref[1, own]))
+    both_ref[...] = total_of((keep_ref[1, 1 - own], got_ref[1, 1 - own]))
+
+
+def quad(sc, bit, keep, got, along):
+    kernel = functools.partial(quad_kernel, bit=bit)
+    arrays = (keep, got, *(a for pair in along for a in pair))
+    h = keep.shape[2]
+    rows = h + sum(kept.shape[0] for kept, _ in along)
+    outs = [((n, LANE), BF16) for n in (rows, rows, h, h)]
+    return resident(kernel, "quad", 1, 8, (sc,), arrays, outs)
+
+
+def swap_both(array, ctx_bit, near_bit):
+    n, nf = lax.axis_size("ctx"), lax.axis_size("fsdp")
+    pairs = [
+        (a * nf + b, (a ^ ctx_bit) * nf + (b ^ near_bit)) for a in range(n) for b in range(nf)
+    ]
+    return lax.ppermute(array, ("ctx", "fsdp"), pairs)
+
+
+def refold_kernel(sc, *refs, bit, sizes, whole):
+    arrays, (send_ref, own_ref) = refs[:-2], refs[-2:]
     own = lax.div(sc[SC_C], bit) & 1
     at = 0
-    for h in sizes:
+    for n, h in enumerate(sizes):
+        group = arrays if n == 0 else arrays[:whole]
         for ref, half in ((send_ref, 1 - own), (own_ref, own)):
             rows = pl.ds(pl.multiple_of(2 * at + half * h, 16), h)
-            total = keep_ref[rows, :].astype(F32) + got_ref[rows, :].astype(F32)
-            ref[at : at + h, :] = total.astype(BF16)
+            ref[at : at + h, :] = total_of([g[rows, :] for g in group])
         at += h
 
 
-def refold(sc, bit, keep, got, sizes, micros=1):
+def refold(sc, bit, arrays, sizes, micros=1, whole=2):
     outs = [((sum(sizes), LANE), BF16)] * 2
-    kernel = functools.partial(refold_kernel, bit=bit, sizes=sizes)
-    return resident(kernel, "fold", micros, 8, (sc,), (keep, got), outs)
+    kernel = functools.partial(refold_kernel, bit=bit, sizes=sizes, whole=whole)
+    return resident(kernel, "fold", micros, 8, (sc,), arrays, outs)
 
 
 def last_kernel(keep_ref, got_ref, o_ref, *rest):
@@ -752,7 +791,7 @@
         self.move("fsdp", 1)
 
     def move(self, axis, bit):
-        self.got = swap(self.send, axis, bit)
+        self.gots = (swap(self.send, axis, bit),)
 
     def view(self, axis):
         if axis == "fsdp":
@@ -763,13 +802,16 @@
 
     def pair(self, axis):
         view = self.view(axis)
-        return self.keep.reshape(view), self.got.reshape(view)
-
-    def step(self, axis, bit, micros=1):
+        return tuple(a.reshape(view) for a in (self.keep, *self.gots))
+
+    def split(self, axis, bit, micros=1):
         keep, got = self.pair(axis)
         pair = (self.seq.next(keep), got)
         self.send, self.keep = fold(self.sc, bit if axis == "ctx" else 0, pair, micros=micros)
         self.seq.made(self.keep, self.send)
+
+    def step(self, axis, bit, micros=1):
+        self.split(axis, bit, micros)
         self.move(axis, bit)
 
 
@@ -778,18 +820,19 @@
     return [1 << k for k in range(n.bit_length() - 1)]
 
 
+def united(sc, seq, parts):
+    groups = [part.pair("ctx") for part in parts]
+    groups[0] = (seq.next(groups[0][0]), *groups[0][1:])
+    sizes = [group[0].shape[2] for group in groups]
+    return Union(sc, seq, [a[0] for a in fold(sc, ctx_bits()[1], *groups)], sizes, len(sizes))
+
+
 class Union:
-    def __init__(self, sc, seq, parts, extra=()):
-        self.sc, self.seq = sc, seq
+    def __init__(self, sc, seq, halves, sizes, few):
+        self.sc, self.seq, self.sizes = sc, seq, sizes
         self.bits = ctx_bits()
-        pairs = [part.pair("ctx") for part in parts]
-        for keep, got in extra:
-            view = (1, 2, keep.shape[0] // 2, LANE)
-            pairs.append((keep.reshape(view), got.reshape(view)))
-        self.sizes = [keep.shape[2] for keep, _ in pairs]
-        self.used = sum(self.sizes[: len(parts)]) * 2 // self.bits[-1]
-        pairs[0] = (self.seq.next(pairs[0][0]), pairs[0][1])
-        self.received(self.bits[1], *(a[0] for a in fold(sc, self.bits[1], *pairs)))
+        self.used = sum(sizes[:few]) * 2 // self.bits[-1]
+        self.received(self.bits[1], *halves)
         self.at = 2
 
     def received(self, bit, send, keep):
@@ -805,7 +848,7 @@
         self.at += 1
         self.sizes = [size // 2 for size in self.sizes]
         keep = self.seq.next(self.keep)
-        self.received(bit, *refold(self.sc, bit, keep, self.got, self.sizes, micros))
+        self.received(bit, *refold(self.sc, bit, (keep, self.got), self.sizes, micros))
 
     def end(self):
         own, *rest = last_sum(self.seq.next(self.keep), self.got, self.used)
@@ -925,30 +968,40 @@
     upper, *old = back(scalars, fixed, (dub, gvec, dh1, sums), 1, nf, nc, last=False)
     seq.made(old[0])
     first.step(*near[0])
-    feed = Union(scalars, seq, [from_down, from_up])
+    feed = united(scalars, seq, [from_down, from_up])
     old[0] = seq.next(old[0])
     lower, _, fsend1, fkeep1, send, keep = back(
         scalars, fixed, (dub, gvec, dh1, sums), 1, nf, nc, old=old
     )
     seq.made(lower)
     second = Part(scalars, seq, keep, send)
-    far = [(k, swap(t, "ctx", bits[0])) for k, t in ((fkeep0, fsend0), (fkeep1, fsend1))]
     while feed.more():
         feed.step(FILL)
-    first.step("ctx", bits[0], FILL)
-    second.step(*near[0])
+    first.split("ctx", bits[0], FILL)
+    along = ((first.keep[0], first.send[0]), (fkeep0, fsend0), (fkeep1, fsend1))
+    view = (2, 2, second.rows // 2, LANE)
+    keep, got = (a.reshape(view) for a in (second.keep, *second.gots))
+    own, to_ctx, to_near, to_both = quad(scalars, bits[0], seq.next(keep), got, along)
+    seq.made(own)
+    arrays = (
+        own,
+        swap(to_ctx, "ctx", bits[0]),
+        swap(to_near, *near[0]),
+        swap_both(to_both, bits[0], near[0][1]),
+    )
     mixed = block_output(scalars, seq.next(r1), g, vec, down)
-    seq.made(mixed, *(got for _, got in far))
-    second.step("ctx", bits[0])
+    seq.made(mixed)
     feed.end()
-    rest = Union(scalars, seq, [first, second], far)
-    feed.join()
+    sizes = [second.total // 4] + [kept.shape[0] // 2 for kept, _ in along]
+    arrays = (seq.next(arrays[0]), *arrays[1:])
+    rest = Union(scalars, seq, refold(scalars, bits[1], arrays, sizes), sizes, 2)
+    while feed.at > 1:
+        feed.join()
     while rest.more():
         rest.step()
-    while feed.at > 1:
-        feed.join()
+    feed.join()
     own_span = rest.end()
-    feed.join()
+    rest.join()
     tokens_grad = first_back(seq.next(x), dr1, upper, lower, own_span, wqkv, vec)
     seq.made(tokens_grad)
     while rest.gathering():
@@ -970,20 +1023,20 @@
     half = PAIRS // 2
     plan = [
         [
-            p // half * first.total + block * (t * half + p % half)
+            (second.total if p < half else 0) + block * (t * half + p % half)
             for t in range(3)
             for p in range(PAIRS)
         ],
-        [block * (3 * half + j) for j in range(D // LANE)],
+        [second.total + block * (3 * half + j) for j in range(D // LANE)],
     ]
     shapes = [(block, 3 * D), (block, D)]
-    at = first.total + 3 * half * block
+    at = 3 * half * block
     for wide in (block, block, 3 * block, block, block, block, 4 * block, block):
         shapes.append((1, wide))
         plan.append([at + j for j in range(wide // LANE)])
         at += wide // LANE
     grad_qkv, grad_out, *vectors = finish(
-        scalars, rest.rows(), (first.total, second.total), shapes, plan
+        scalars, rest.rows(), (second.total, first.total), shapes, plan
     )
     g1, s1, qb, ob, g2, s2, ub, db = (v.reshape(-1) for v in vectors)
     return (

time: 152 us -> 149 us (0.980)
    ppermute x33 -> x30, waiting for transfers between devices: 40.2 us -> 34.5 us  [swap(): return lax.ppermute(array, axis, [(k, k ^ bit) for k in range(n)])]
    ppermute x0 -> x1, waiting for transfers between devices: none -> 4.36 us  [swap_both(): return lax.ppermute(array, ('ctx', 'fsdp'), pairs)]
    ppermute x33 -> x30, starting transfers between devices: 25.3 us -> 22.6 us  [swap(): return lax.ppermute(array, axis, [(k, k ^ bit) for k in range(n)])]
    pallas_call x24 -> x23, Pallas kernels: 57.7 us -> 57.1 us  [resident(): pl.pallas_call(kernel, in_specs=[pl.BlockSpec(memory_space=pltpu.SMEM)] *...]
  transfers between devices with their start and end apart: 34 -> 32, of which waited for: 16 -> 14; matrix products, arithmetic and copies ran while one was open for 0% -> 0% of each run, Pallas kernels for 44% -> 45%
where the time goes in v5:
time: 149 us; the launch traced here: 148 us
  Pallas kernels  70.6 us (47%)
  waiting for transfers between devices  46.2 us (31%)
  starting transfers between devices  29.6 us (20%)
    pallas_call x23, Pallas kernels, resident(): pl.pallas_call(kernel, in_specs=[pl.BlockSpec(memory_space=pltpu.SMEM)] *...  57.1 us
    ppermute x30, waiting for transfers between devices, swap(): return lax.ppermute(array, axis, [(k, k ^ bit) for k in range(n)])  34.5 us
    ppermute x30, starting transfers between devices, swap(): return lax.ppermute(array, axis, [(k, k ^ bit) for k in range(n)])  22.6 us
    all_to_all x1, waiting for transfers between devices, local(): nsum = lax.all_to_all(sums, 'ctx', 0, 0, tiled=True).reshape(nc * spans, D)  7.26 us
    all_to_all x1, starting transfers between devices, local(): nsum = lax.all_to_all(sums, 'ctx', 0, 0, tiled=True).reshape(nc * spans, D)  5.81 us
    ppermute x1, waiting for transfers between devices, swap_both(): return lax.ppermute(array, ('ctx', 'fsdp'), pairs)  4.36 us
    pallas_call x1, Pallas kernels, block_output(): pl.pallas_call(mixed_kernel, grid=(rows // ROWS,), in_specs=[pl.BlockSpec...  4.13 us
    pallas_call x2, Pallas kernels, finish(): pl.pallas_call(functools.partial(finish_kernel, heights=heights, plan=pla...  3.78 us
  transfers between devices with their start and end apart: 32, of which 14 were waited for; matrix products, arithmetic and copies ran while one was open for 0% of the time, Pallas kernels for 45%

profile of v5, /device:TPU:0, one launch (start us, length us, event | category | flops | bytes accessed | tf_op | source)
XLA Modules:
  0.0 148.3 jit_solution(6073007761583229918)
XLA Ops:
  0.7 2.1 %pack.1.refs_0_ = bf16[144,2048]{1,0:T(8,128)(2,1)} custom-call(bf16[128,1536]{1,0:T(8,128)(2,1)} %qkv_ref.1, bf16[128,512]{1,0:T(8,128)(2,1)} %out_ref.1, bf16[1,128]{1,0:T(2,128)(2,1)} %bitcast.91, bf16[1,128]{1,0:T(2,128)(2,1)} %bitcast.92, bf16[3,128]{1,0:T(4,128)(2,1)} %bitcast.89, bf16[1,128]{1,0:T(2,128)(2,1)} %bitcast.93, bf16[1,128]{1,0:T(2,128)(2,1)} %bitcast.94, ...), custom_call_target="tpu_custom_call" | custom-call | flops 1000000000 | bytes 1000000 | tf_op jit(solution)/shard_map/pack/pallas_call | solution.py:134
  2.7 3.0 %collective-permute-start.1 = (bf16[144,2048]{1,0:T(8,128)(2,1)}, bf16[144,2048]{1,0:T(8,128)(2,1)S(1)}, u32[]{:S(2)}, u32[]{:S(2)}) collective-permute-start(bf16[144,2048]{1,0:T(8,128)(2,1)} %pack.1.refs_0_), channel_id=1, source_target_pairs={{0,2},{1,3},{2,0},{3,1},{4,6},{5,7},{6,4},{7,5},{8,10},{9,11},{10,... | collective-permute-start | bytes 1769480 | tf_op jit(solution)/shard_map/ppermute | solution.py:659
  7.1 5.8 %all-to-all-start = ((f32[8,8,512]{2,1,0:T(8,128)}), f32[8,8,512]{2,1,0:T(8,128)S(1)}, u32[]{:S(2)}, u32[]{:S(2)}) async-start(f32[8,8,512]{2,1,0:T(8,128)} %span_sums.1), calls=%async_computation | async-start | bytes 262144 | tf_op jit(solution)/shard_map/all_to_all | solution.py:933
  13.0 7.3 %all-to-all-done = f32[8,8,512]{2,1,0:T(8,128)S(1)} async-done(((f32[8,8,512]{2,1,0:T(8,128)}), f32[8,8,512]{2,1,0:T(8,128)S(1)}, u32[]{:S(2)}, u32[]{:S(2)}) %all-to-all-start) | async-done | bytes 131104 | tf_op jit(solution)/shard_map/all_to_all | solution.py:933
  22.3 8.3 %attend.1 = (bf16[1024,1536]{1,0:T(8,128)(2,1)S(1)}, bf16[32,192,256]{2,1,0:T(8,128)(2,1)S(1)}, bf16[1024,512]{1,0:T(8,128)(2,1)S(1)}, bf16[1024,512]{1,0:T(8,12...) custom-call(s32[76]{0:T(128)S(1)} %concatenate.21.sc.refs_0_, ...), custom_call_target="tpu_custom_call" | custom-call | flops 12000000000 | bytes 12000000 | tf_op jit(solution)/shard_map/attend/pallas_call | solution.py:69
  30.6 4.3 %collective-permute-done.4.refs_2_ = bf16[128,2048]{1,0:T(8,128)(2,1)S(1)} collective-permute-done((bf16[128,2048]{1,0:T(8,128)(2,1)}, bf16[128,2048]{1,0:T(8,128)(2,1)S(1)}, u32[]{:S(2)}, u32[]{:S(2)}) %collective-permute-start.4) | collective-permute-done | bytes 524320 | tf_op jit(solution)/shard_map/ppermute | solution.py:659
  37.0 6.9 %ffn_up.1 = (bf16[1024,2048]{1,0:T(8,128)(2,1)S(1)}, bf16[1024,2048]{1,0:T(8,128)(2,1)S(1)}, bf16[512,2048]{1,0:T(8,128)(2,1)S(1)}) custom-call(s32[76]{0:T(128)S(1)} %concatenate.21.sc.refs_0_, bf16[1024,512]{1,0:T(8,128)(2,1)S(1)} %get-tuple-element.124.h2_ref, f32[8,2048]{1,0:T(8,128)S(1)} %get-tuple-element.122.vec.vec_ref.refs_8_, ...), custom_call_target="tpu_custom_call" | custom-call | flops 8000000000 | bytes 8000000 | tf_op jit(solution)/shard_map/ffn_up/pallas_call | solution.py:69
  44.0 2.9 %down_grad.1 = (bf16[2,2048,128]{2,1,0:T(8,128)(2,1)S(1)}, bf16[2,2048,128]{2,1,0:T(8,128)(2,1)S(1)}) custom-call(s32[76]{0:T(128)S(1)} %concatenate.21.sc.refs_0_, bf16[1024,2048]{1,0:T(8,128)(2,1)S(1)} %get-tuple-element.130.g_ref, bf16[1024,512]{1,0:T(8,128)(2,1)S(1)} %bitcast.56), custom_call_target="tpu_custom_call" | custom-call | flops 4000000000 | bytes 4000000 | tf_op jit(solution)/shard_map/down_grad/pallas_call | solution.py:69
  46.9 2.4 %collective-permute-done.7.refs_2_ = bf16[512,512]{1,0:T(8,128)(2,1)S(1)} collective-permute-done((bf16[512,512]{1,0:T(8,128)(2,1)S(1)}, bf16[512,512]{1,0:T(8,128)(2,1)S(1)}, u32[]{:S(2)}, u32[]{:S(2)}) %collective-permute-start.7) | collective-permute-done | bytes 524320 | tf_op jit(solution)/shard_map/ppermute | solution.py:659
  51.2 7.8 %ffn_down.1 = (f32[1024,512]{1,0:T(8,128)S(1)}, f32[1,2048]{1,0:T(1,128)S(1)}, bf16[2,2048,128]{2,1,0:T(8,128)(2,1)S(1)}, bf16[2,2048,128]{2,1,0:T(8,128)(2,1)S(1)}) custom-call(s32[76]{0:T(128)S(1)} %concatenate.21.sc.refs_0_, bf16[1024,512]{1,0:T(8,128)(2,1)S(1)} %get-tuple-element.124.h2_ref, bf16[1024,512]{1,0:T(8,128)(2,1)S(1)} %bitcast.57, ...), custom_call_target="tpu_custom_call" | custom-call | flops 8000000000 | bytes 8000000 | tf_op jit(solution)/shard_map/ffn_down/pallas_call | solution.py:69
  60.8 2.6 %mid.1 = (f32[1024,512]{1,0:T(8,128)S(1)}, bf16[1024,512]{1,0:T(8,128)(2,1)S(1)}, f32[512,512]{1,0:T(8,128)S(1)}, f32[8,512]{1,0:T(8,128)S(1)}) custom-call(bf16[1024,512]{1,0:T(8,128)(2,1)S(1)} %bitcast.58, f32[1024,512]{1,0:T(8,128)S(1)} %get-tuple-element.137.dh2_ref, f32[1024,512]{1,0:T(8,128)S(1)} %get-tuple-element.189.r1_ref, ...), custom_call_target="tpu_custom_call" | custom-call | flops 5000000000 | bytes 5000000 | tf_op jit(solution)/shard_map/mid/pallas_call | solution.py:69
  65.7 8.8 %back_0.1 = (f32[1024,512]{1,0:T(8,128)S(1)}, f32[72,512]{1,0:T(8,128)S(1)}, bf16[128,128]{1,0:T(8,128)(2,1)S(1)}, bf16[128,128]{1,0:T(8,128)(2,1)S(1)}, bf16[2,...) custom-call(s32[76]{0:T(128)S(1)} %concatenate.21.sc.refs_0_, bf16[1024,512]{1,0:T(8,128)(2,1)S(1)} %bitcast.62, ...), custom_call_target="tpu_custom_call" | custom-call | flops 8999999488 | bytes 9000000 | tf_op jit(solution)/shard_map/back_0/pallas_call | solution.py:69
  75.9 2.7 %collective-permute-done.12 = bf16[2,1024,128]{2,1,0:T(8,128)(2,1)S(1)} collective-permute-done((bf16[2,1024,128]{2,1,0:T(8,128)(2,1)S(1)}, bf16[2,1024,128]{2,1,0:T(8,128)(2,1)S(1)}, u32[]{:S(2)}, u32[]{:S(2)}) %collective-permute-start.12) | collective-permute-done | bytes 524320 | tf_op jit(solution)/shard_map/ppermute | solution.py:659
  79.2 1.9 %collective-permute-start.15 = (bf16[1,1024,128]{2,1,0:T(8,128)(2,1)S(1)}, bf16[1,1024,128]{2,1,0:T(8,128)(2,1)S(1)}, u32[]{:S(2)}, u32[]{:S(2)}) collective-permute-start(bf16[1,1024,128]{2,1,0:T(8,128)(2,1)S(1)} %get-tuple-element.159), channel_id=1, source_target_pairs={{0,2},{1,3},{2,0},{3,1},{4,6},{5,7},{6,4},{7,5},{8,10},{9,11},{10,... | collective-permute-start | bytes 786440 | tf_op jit(solution)/shard_map/ppermute | solution.py:659
  81.1 4.3 %back_1.2 = (f32[512,512]{1,0:T(8,128)S(1)}, f32[512,768]{1,0:T(8,128)S(1)}, f32[64,512]{1,0:T(8,128)S(1)}, f32[16,1536]{1,0:T(8,128)S(1)}) custom-call(s32[76]{0:T(128)S(1)} %concatenate.21.sc.refs_0_, bf16[1024,512]{1,0:T(8,128)(2,1)S(1)} %bitcast.63, bf16[1024,512]{1,0:T(8,128)(2,1)S(1)} %get-tuple-element.144.refs_2_, ...), custom_call_target="tpu_custom_call" | custom-call | flops 8999999488 | bytes 9000000 | tf_op jit(solution)/shard_map/back_1/pallas_call | solution.py:69
  87.1 1.8 %collective-permute-start.16 = (bf16[1024,128]{1,0:T(8,128)(2,1)S(1)}, bf16[1024,128]{1,0:T(8,128)(2,1)S(1)}, u32[]{:S(2)}, u32[]{:S(2)}) collective-permute-start(bf16[1024,128]{1,0:T(8,128)(2,1)S(1)} %bitcast.75), channel_id=1, source_target_pairs={{0,8},{4,12},{8,0},{12,4},{16,24},{20,28},{24,16},{28,20},{1,9},{5... | collective-permute-start | bytes 786440 | tf_op jit(solution)/shard_map/ppermute | solution.py:659
  88.9 5.4 %back_1.3 = (f32[512,512]{1,0:T(8,128)S(1)}, f32[72,512]{1,0:T(8,128)}, bf16[128,128]{1,0:T(8,128)(2,1)S(1)}, bf16[128,128]{1,0:T(8,128)(2,1)S(1)}, bf16[2,896,1...) custom-call(s32[76]{0:T(128)S(1)} %concatenate.21.sc.refs_0_, bf16[1024,512]{1,0:T(8,128)(2,1)S(1)} %bitcast.64, ...), custom_call_target="tpu_custom_call" | custom-call | flops 8999999488 | bytes 9000000 | tf_op jit(solution)/shard_map/back_1/pallas_call | solution.py:69
  94.9 2.7 %collective-permute-start.19 = (bf16[512,128]{1,0:T(8,128)(2,1)S(1)}, bf16[512,128]{1,0:T(8,128)(2,1)S(1)}, u32[]{:S(2)}, u32[]{:S(2)}) collective-permute-start(bf16[512,128]{1,0:T(8,128)(2,1)S(1)} %get-tuple-element.178), channel_id=1, source_target_pairs={{0,16},{4,20},{8,24},{12,28},{16,0},{20,4},{24,8},{28,12},{1,17},{... | collective-permute-start | bytes 393224 | tf_op jit(solution)/shard_map/ppermute | solution.py:659
  98.9 1.9 %collective-permute-start.20 = (bf16[1344,128]{1,0:T(8,128)(2,1)S(1)}, bf16[1344,128]{1,0:T(8,128)(2,1)S(1)}, u32[]{:S(2)}, u32[]{:S(2)}) collective-permute-start(bf16[1344,128]{1,0:T(8,128)(2,1)S(1)} %get-tuple-element.192), channel_id=1, source_target_pairs={{0,4},{4,0},{8,12},{12,8},{16,20},{20,16},{24,28},{28,24},{1,5},{5... | collective-permute-start | bytes 1032200 | tf_op jit(solution)/shard_map/ppermute | solution.py:659
  102.5 4.1 %block_output.1 = bf16[1024,512]{1,0:T(8,128)(2,1)} custom-call(s32[76]{0:T(128)S(1)} %concatenate.21.sc.refs_0_, f32[1024,512]{1,0:T(8,128)S(1)} %get-tuple-element.189.r1_ref, bf16[1024,2048]{1,0:T(8,128)(2,1)S(1)} %get-tuple-element.130.g_ref, f32[8,2048]{1,0:T(8,128)S(1)} %get-tuple-element.122.vec.vec_ref.refs_8_, bf16[512,512]{1,0:T(8,128)(2,1)S(1)} %copy-done.5, ...), custom_call_target="tpu_custom_call" | custom-call | flops 4000000000 | bytes 4000000 | tf_op jit(solution)/shard_map/block_output/pallas_call | solution.py:645
  107.2 4.4 %collective-permute-done.22.refs_3_ = bf16[448,128]{1,0:T(8,128)(2,1)S(1)} collective-permute-done((bf16[448,128]{1,0:T(8,128)(2,1)S(1)}, bf16[448,128]{1,0:T(8,128)(2,1)S(1)}, u32[]{:S(2)}, u32[]{:S(2)}) %collective-permute-start.22) | collective-permute-done | bytes 114720 | tf_op jit(solution)/shard_map/ppermute | solution.py:738
  112.7 2.6 %collective-permute-done.23 = bf16[512,128]{1,0:T(8,128)(2,1)S(1)} collective-permute-done((bf16[512,128]{1,0:T(8,128)(2,1)S(1)}, bf16[512,128]{1,0:T(8,128)(2,1)S(1)}, u32[]{:S(2)}, u32[]{:S(2)}) %collective-permute-start.23) | collective-permute-done | bytes 131104 | tf_op jit(solution)/shard_map/ppermute | solution.py:659
  115.4 4.2 %collective-permute-done.24.refs_1_ = bf16[672,128]{1,0:T(8,128)(2,1)S(1)} collective-permute-done((bf16[672,128]{1,0:T(8,128)(2,1)S(1)}, bf16[672,128]{1,0:T(8,128)(2,1)S(1)}, u32[]{:S(2)}, u32[]{:S(2)}) %collective-permute-start.24) | collective-permute-done | bytes 172064 | tf_op jit(solution)/shard_map/ppermute | solution.py:659
  120.3 6.1 %collective-permute-done.25 = bf16[1024,128]{1,0:T(8,128)(2,1)S(1)} collective-permute-done((bf16[1024,128]{1,0:T(8,128)(2,1)S(1)}, bf16[1024,128]{1,0:T(8,128)(2,1)S(1)}, u32[]{:S(2)}, u32[]{:S(2)}) %collective-permute-start.25) | collective-permute-done | bytes 262176 | tf_op jit(solution)/shard_map/ppermute | solution.py:659
  128.6 3.2 %collective-permute-done.27 = bf16[272,128]{1,0:T(8,128)(2,1)S(1)} collective-permute-done((bf16[272,128]{1,0:T(8,128)(2,1)S(1)}, bf16[272,128]{1,0:T(8,128)(2,1)S(1)}, u32[]{:S(2)}, u32[]{:S(2)}) %collective-permute-start.27) | collective-permute-done | bytes 69664 | tf_op jit(solution)/shard_map/ppermute | solution.py:659
  131.8 3.5 %first_back.1 = f32[1024,512]{1,0:T(8,128)} custom-call(bf16[1024,512]{1,0:T(8,128)(2,1)S(1)} %bitcast.65, f32[1024,512]{1,0:T(8,128)S(1)} %get-tuple-element.206.dr1_ref, f32[512,512]{1,0:T(8,128)S(1)} %get-tuple-element.207.upper_ref, f32[512,512]{1,0:T(8,128)S(1)} %get-tuple-element.175.lower_ref, bf16[64,128]{1,0:T(8,128)(2,1)S(1)} %get-tuple-element.208.own_ref, ...), custom_call_target="tpu_custom_call" | custom-call | flops 3000000000 | bytes 3000000 | tf_op jit(solution)/shard_map/first_back/pallas_call | solution.py:619
  135.3 1.6 %collective-permute-done.28 = bf16[544,128]{1,0:T(8,128)(2,1)S(1)} collective-permute-done((bf16[544,128]{1,0:T(8,128)(2,1)S(1)}, bf16[544,128]{1,0:T(8,128)(2,1)S(1)}, u32[]{:S(2)}, u32[]{:S(2)}) %collective-permute-start.28) | collective-permute-done | bytes 139296 | tf_op jit(solution)/shard_map/ppermute | solution.py:659
  136.9 1.7 %collective-permute-start.30 = (bf16[1088,128]{1,0:T(8,128)(2,1)S(1)}, bf16[1088,128]{1,0:T(8,128)(2,1)S(1)}, u32[]{:S(2)}, u32[]{:S(2)}) collective-permute-start(bf16[1088,128]{1,0:T(8,128)(2,1)S(1)} %constant_dynamic-update-slice_fusion.6), channel_id=1, source_target_pairs={{0,4},{4,0},{8,12},{12,8},{16,20},{20,16},{24,28},{28,24},{1,5},{5... | collective-permute-start | bytes 835592 | tf_op jit(solution)/shard_map/ppermute | solution.py:659
  138.6 3.2 %collective-permute-done.29 = bf16[2048,128]{1,0:T(8,128)(2,1)S(1)} collective-permute-done((bf16[2048,128]{1,0:T(8,128)(2,1)S(1)}, bf16[2048,128]{1,0:T(8,128)(2,1)S(1)}, u32[]{:S(2)}, u32[]{:S(2)}) %collective-permute-start.29) | collective-permute-done | bytes 524320 | tf_op jit(solution)/shard_map/ppermute | solution.py:659
  141.9 2.1 %finish.2 = (f32[512,512]{1,0:T(8,128)}, f32[128,2048]{1,0:T(8,128)}) custom-call(s32[76]{0:T(128)S(1)} %concatenate.21.sc.refs_0_, bf16[8,512,128]{2,1,0:T(8,128)(2,1)S(1)} %bitcast.49), custom_call_target="tpu_custom_call" | custom-call | flops 2000000000 | bytes 2000000 | tf_op jit(solution)/shard_map/finish/pallas_call | solution.py:898
  144.1 1.9 %collective-permute-done.30 = bf16[1088,128]{1,0:T(8,128)(2,1)S(1)} collective-permute-done((bf16[1088,128]{1,0:T(8,128)(2,1)S(1)}, bf16[1088,128]{1,0:T(8,128)(2,1)S(1)}, u32[]{:S(2)}, u32[]{:S(2)}) %collective-permute-start.30) | collective-permute-done | bytes 278560 | tf_op jit(solution)/shard_map/ppermute | solution.py:659
  146.1 1.6 %finish.3 = (f32[128,1536]{1,0:T(8,128)}, f32[128,512]{1,0:T(8,128)}, f32[1,128]{1,0:T(1,128)}, f32[1,128]{1,0:T(1,128)}, f32[1,384]{1,0:T(1,128)S(1)}, /*index=...) custom-call(s32[76]{0:T(128)S(1)} %concatenate.21.sc.refs_0_, ...), custom_call_target="tpu_custom_call" | custom-call | flops 2000000000 | bytes 2000000 | tf_op jit(solution)/shard_map/finish/pallas_call | solution.py:898
  (86 shorter events, 24.3 us)
Async XLA Ops:
  2.7 17.5 %collective-permute-start.1 = (bf16[144,2048]{1,0:T(8,128)(2,1)}, bf16[144,2048]{1,0:T(8,128)(2,1)S(1)}, u32[]{:S(2)}, u32[]{:S(2)}) collective-permute-start(bf16[144,2048]{1,0:T(8,128)(2,1)} %pack.1.refs_0_), channel_id=1, source_target_pairs={{0,2},{1,3},{2,0},{3,1},{4,6},{5,7},{6,4},{7,5},{8,10},{9,11},{10,... | collective-permute-start | bytes 1769480 | tf_op jit(solution)/shard_map/ppermute | solution.py:659
  7.1 13.1 %all-to-all-start = ((f32[8,8,512]{2,1,0:T(8,128)}), f32[8,8,512]{2,1,0:T(8,128)S(1)}, u32[]{:S(2)}, u32[]{:S(2)}) async-start(f32[8,8,512]{2,1,0:T(8,128)} %span_sums.1), calls=%async_computation | async-start | bytes 262144 | tf_op jit(solution)/shard_map/all_to_all | solution.py:933
  12.9 8.4 %collective-permute-start = (bf16[144,2048]{1,0:T(8,128)(2,1)S(1)}, bf16[144,2048]{1,0:T(8,128)(2,1)S(1)}, u32[]{:S(2)}, u32[]{:S(2)}) collective-permute-start(bf16[144,2048]{1,0:T(8,128)(2,1)S(1)} %copy-done.3), channel_id=1, source_target_pairs={{0,1},{1,0},{2,3},{3,2},{4,5},{5,4},{6,7},{7,6},{8,9},{9,8},{10,11... | collective-permute-start | bytes 1769480 | tf_op jit(solution)/shard_map/ppermute | solution.py:659
  20.3 2.0 %collective-permute-start.2 = (bf16[144,2048]{1,0:T(8,128)(2,1)S(1)}, bf16[144,2048]{1,0:T(8,128)(2,1)S(1)}, u32[]{:S(2)}, u32[]{:S(2)}) collective-permute-start(bf16[144,2048]{1,0:T(8,128)(2,1)S(1)} %collective-permute-done.1.refs_2_), channel_id=1, source_target_pairs={{0,1},{1,0},{2,3},{3,2},{4,5},{5,4},{6,7},{7,6},{8,9},{9,8},{10,11... | collective-permute-start | bytes 1769480 | tf_op jit(solution)/shard_map/ppermute | solution.py:659
  20.4 14.6 %collective-permute-start.4 = (bf16[128,2048]{1,0:T(8,128)(2,1)}, bf16[128,2048]{1,0:T(8,128)(2,1)S(1)}, u32[]{:S(2)}, u32[]{:S(2)}) collective-permute-start(bf16[128,2048]{1,0:T(8,128)(2,1)} %refs_0_), channel_id=1, source_target_pairs={{0,2},{1,3},{2,0},{3,1},{4,6},{5,7},{6,4},{7,5},{8,10},{9,11},{10,... | collective-permute-start | bytes 1572872 | tf_op jit(solution)/shard_map/ppermute | solution.py:659
  21.1 15.9 %collective-permute-start.3 = (bf16[128,2048]{1,0:T(8,128)(2,1)}, bf16[128,2048]{1,0:T(8,128)(2,1)S(1)}, u32[]{:S(2)}, u32[]{:S(2)}) collective-permute-start(bf16[128,2048]{1,0:T(8,128)(2,1)} %refs_0_), channel_id=1, source_target_pairs={{0,1},{1,0},{2,3},{3,2},{4,5},{5,4},{6,7},{7,6},{8,9},{9,8},{10,11... | collective-permute-start | bytes 1572872 | tf_op jit(solution)/shard_map/ppermute | solution.py:659
  34.9 2.1 %collective-permute-start.5 = (bf16[128,2048]{1,0:T(8,128)(2,1)S(1)}, bf16[128,2048]{1,0:T(8,128)(2,1)S(1)}, u32[]{:S(2)}, u32[]{:S(2)}) collective-permute-start(bf16[128,2048]{1,0:T(8,128)(2,1)S(1)} %collective-permute-done.4.refs_2_), channel_id=1, source_target_pairs={{0,1},{1,0},{2,3},{3,2},{4,5},{5,4},{6,7},{7,6},{8,9},{9,8},{10,11... | collective-permute-start | bytes 1572872 | tf_op jit(solution)/shard_map/ppermute | solution.py:659
  34.9 14.3 %collective-permute-start.7 = (bf16[512,512]{1,0:T(8,128)(2,1)S(1)}, bf16[512,512]{1,0:T(8,128)(2,1)S(1)}, u32[]{:S(2)}, u32[]{:S(2)}) collective-permute-start(bf16[512,512]{1,0:T(8,128)(2,1)S(1)} %copy-done.5), channel_id=1, source_target_pairs={{0,2},{1,3},{2,0},{3,1},{4,6},{5,7},{6,4},{7,5},{8,10},{9,11},{10,... | collective-permute-start | bytes 1572872 | tf_op jit(solution)/shard_map/ppermute | solution.py:659
  35.6 14.1 %collective-permute-start.6 = (bf16[512,512]{1,0:T(8,128)(2,1)S(1)}, bf16[512,512]{1,0:T(8,128)(2,1)S(1)}, u32[]{:S(2)}, u32[]{:S(2)}) collective-permute-start(bf16[512,512]{1,0:T(8,128)(2,1)S(1)} %copy-done.5), channel_id=1, source_target_pairs={{0,1},{1,0},{2,3},{3,2},{4,5},{5,4},{6,7},{7,6},{8,9},{9,8},{10,11... | collective-permute-start | bytes 1572872 | tf_op jit(solution)/shard_map/ppermute | solution.py:659
  49.2 1.9 %collective-permute-start.8 = (bf16[512,512]{1,0:T(8,128)(2,1)S(1)}, bf16[512,512]{1,0:T(8,128)(2,1)S(1)}, u32[]{:S(2)}, u32[]{:S(2)}) collective-permute-start(bf16[512,512]{1,0:T(8,128)(2,1)S(1)} %collective-permute-done.7.refs_2_), channel_id=1, source_target_pairs={{0,1},{1,0},{2,3},{3,2},{4,5},{5,4},{6,7},{7,6},{8,9},{9,8},{10,11... | collective-permute-start | bytes 1572872 | tf_op jit(solution)/shard_map/ppermute | solution.py:659
  49.2 9.9 %collective-permute-start.9 = (bf16[2,2048,128]{2,1,0:T(8,128)(2,1)S(1)}, bf16[2,2048,128]{2,1,0:T(8,128)(2,1)S(1)}, u32[]{:S(2)}, u32[]{:S(2)}) collective-permute-start(bf16[2,2048,128]{2,1,0:T(8,128)(2,1)S(1)} %get-tuple-element.134), channel_id=1, source_target_pairs={{0,1},{1,0},{2,3},{3,2},{4,5},{5,4},{6,7},{7,6},{8,9},{9,8},{10,11... | collective-permute-start | bytes 3145736 | tf_op jit(solution)/shard_map/ppermute | solution.py:659
  59.0 4.4 %collective-permute-start.10 = (bf16[2,2048,128]{2,1,0:T(8,128)(2,1)S(1)}, bf16[2,2048,128]{2,1,0:T(8,128)(2,1)S(1)}, u32[]{:S(2)}, u32[]{:S(2)}) collective-permute-start(bf16[2,2048,128]{2,1,0:T(8,128)(2,1)S(1)} %get-tuple-element.141), channel_id=1, source_target_pairs={{0,1},{1,0},{2,3},{3,2},{4,5},{5,4},{6,7},{7,6},{8,9},{9,8},{10,11... | collective-permute-start | bytes 3145736 | tf_op jit(solution)/shard_map/ppermute | solution.py:659
  60.0 14.6 %collective-permute-start.11 = (bf16[1,2048,128]{2,1,0:T(8,128)(2,1)S(1)}, bf16[1,2048,128]{2,1,0:T(8,128)(2,1)S(1)}, u32[]{:S(2)}, u32[]{:S(2)}) collective-permute-start(bf16[1,2048,128]{2,1,0:T(8,128)(2,1)S(1)} %get-tuple-element.136), channel_id=1, source_target_pairs={{0,2},{1,3},{2,0},{3,1},{4,6},{5,7},{6,4},{7,5},{8,10},{9,11},{10,... | collective-permute-start | bytes 1572872 | tf_op jit(solution)/shard_map/ppermute | solution.py:659
  64.2 14.3 %collective-permute-start.12 = (bf16[2,1024,128]{2,1,0:T(8,128)(2,1)S(1)}, bf16[2,1024,128]{2,1,0:T(8,128)(2,1)S(1)}, u32[]{:S(2)}, u32[]{:S(2)}) collective-permute-start(bf16[2,1024,128]{2,1,0:T(8,128)(2,1)S(1)} %get-tuple-element.143), channel_id=1, source_target_pairs={{0,4},{4,0},{8,12},{12,8},{16,20},{20,16},{24,28},{28,24},{1,5},{5... | collective-permute-start | bytes 1572872 | tf_op jit(solution)/shard_map/ppermute | solution.py:659
  75.3 11.1 %collective-permute-start.14 = (bf16[1,1024,128]{2,1,0:T(8,128)(2,1)S(1)}, bf16[1,1024,128]{2,1,0:T(8,128)(2,1)S(1)}, u32[]{:S(2)}, u32[]{:S(2)}) collective-permute-start(bf16[1,1024,128]{2,1,0:T(8,128)(2,1)S(1)} %get-tuple-element.156), channel_id=1, source_target_pairs={{0,4},{4,0},{8,12},{12,8},{16,20},{20,16},{24,28},{28,24},{1,5},{5... | collective-permute-start | bytes 786440 | tf_op jit(solution)/shard_map/ppermute | solution.py:659
  75.9 9.5 %collective-permute-start.13 = (bf16[2,1280,128]{2,1,0:T(8,128)(2,1)S(1)}, bf16[2,1280,128]{2,1,0:T(8,128)(2,1)S(1)}, u32[]{:S(2)}, u32[]{:S(2)}) collective-permute-start(bf16[2,1280,128]{2,1,0:T(8,128)(2,1)S(1)} %get-tuple-element.165), channel_id=1, source_target_pairs={{0,1},{1,0},{2,3},{3,2},{4,5},{5,4},{6,7},{7,6},{8,9},{9,8},{10,11... | collective-permute-start | bytes 1966088 | tf_op jit(solution)/shard_map/ppermute | solution.py:659
  79.2 7.2 %collective-permute-start.15 = (bf16[1,1024,128]{2,1,0:T(8,128)(2,1)S(1)}, bf16[1,1024,128]{2,1,0:T(8,128)(2,1)S(1)}, u32[]{:S(2)}, u32[]{:S(2)}) collective-permute-start(bf16[1,1024,128]{2,1,0:T(8,128)(2,1)S(1)} %get-tuple-element.159), channel_id=1, source_target_pairs={{0,2},{1,3},{2,0},{3,1},{4,6},{5,7},{6,4},{7,5},{8,10},{9,11},{10,... | collective-permute-start | bytes 786440 | tf_op jit(solution)/shard_map/ppermute | solution.py:659
  86.1 11.5 %collective-permute-start.17 = (bf16[1,1280,128]{2,1,0:T(8,128)(2,1)S(1)}, bf16[1,1280,128]{2,1,0:T(8,128)(2,1)S(1)}, u32[]{:S(2)}, u32[]{:S(2)}) collective-permute-start(bf16[1,1280,128]{2,1,0:T(8,128)(2,1)S(1)} %get-tuple-element.167), channel_id=1, source_target_pairs={{0,2},{1,3},{2,0},{3,1},{4,6},{5,7},{6,4},{7,5},{8,10},{9,11},{10,... | collective-permute-start | bytes 983048 | tf_op jit(solution)/shard_map/ppermute | solution.py:659
  87.1 7.2 %collective-permute-start.16 = (bf16[1024,128]{1,0:T(8,128)(2,1)S(1)}, bf16[1024,128]{1,0:T(8,128)(2,1)S(1)}, u32[]{:S(2)}, u32[]{:S(2)}) collective-permute-start(bf16[1024,128]{1,0:T(8,128)(2,1)S(1)} %bitcast.75), channel_id=1, source_target_pairs={{0,8},{4,12},{8,0},{12,4},{16,24},{20,28},{24,16},{28,20},{1,9},{5... | collective-permute-start | bytes 786440 | tf_op jit(solution)/shard_map/ppermute | solution.py:659
  94.3 3.9 %collective-permute-start.18 = (bf16[2,896,128]{2,1,0:T(8,128)(2,1)S(1)}, bf16[2,896,128]{2,1,0:T(8,128)(2,1)S(1)}, u32[]{:S(2)}, u32[]{:S(2)}) collective-permute-start(bf16[2,896,128]{2,1,0:T(8,128)(2,1)S(1)} %get-tuple-element.183), channel_id=1, source_target_pairs={{0,1},{1,0},{2,3},{3,2},{4,5},{5,4},{6,7},{7,6},{8,9},{9,8},{10,11... | collective-permute-start | bytes 1376264 | tf_op jit(solution)/shard_map/ppermute | solution.py:659
  94.9 11.7 %collective-permute-start.19 = (bf16[512,128]{1,0:T(8,128)(2,1)S(1)}, bf16[512,128]{1,0:T(8,128)(2,1)S(1)}, u32[]{:S(2)}, u32[]{:S(2)}) collective-permute-start(bf16[512,128]{1,0:T(8,128)(2,1)S(1)} %get-tuple-element.178), channel_id=1, source_target_pairs={{0,16},{4,20},{8,24},{12,28},{16,0},{20,4},{24,8},{28,12},{1,17},{... | collective-permute-start | bytes 393224 | tf_op jit(solution)/shard_map/ppermute | solution.py:659
  98.9 12.6 %collective-permute-start.20 = (bf16[1344,128]{1,0:T(8,128)(2,1)S(1)}, bf16[1344,128]{1,0:T(8,128)(2,1)S(1)}, u32[]{:S(2)}, u32[]{:S(2)}) collective-permute-start(bf16[1344,128]{1,0:T(8,128)(2,1)S(1)} %get-tuple-element.192), channel_id=1, source_target_pairs={{0,4},{4,0},{8,12},{12,8},{16,20},{20,16},{24,28},{28,24},{1,5},{5... | collective-permute-start | bytes 1032200 | tf_op jit(solution)/shard_map/ppermute | solution.py:659
  100.8 6.4 %collective-permute-start.21 = (bf16[448,128]{1,0:T(8,128)(2,1)S(1)}, bf16[448,128]{1,0:T(8,128)(2,1)S(1)}, u32[]{:S(2)}, u32[]{:S(2)}) collective-permute-start(bf16[448,128]{1,0:T(8,128)(2,1)S(1)} %get-tuple-element.193), channel_id=1, source_target_pairs={{0,2},{1,3},{2,0},{3,1},{4,6},{5,7},{6,4},{7,5},{8,10},{9,11},{10,... | collective-permute-start | bytes 344072 | tf_op jit(solution)/shard_map/ppermute | solution.py:659
  101.2 10.3 %collective-permute-start.22 = (bf16[448,128]{1,0:T(8,128)(2,1)S(1)}, bf16[448,128]{1,0:T(8,128)(2,1)S(1)}, u32[]{:S(2)}, u32[]{:S(2)}) collective-permute-start(bf16[448,128]{1,0:T(8,128)(2,1)S(1)} %get-tuple-element.194), channel_id=1, source_target_pairs={{0,6},{1,7},{2,4},{3,5},{4,2},{5,3},{6,0},{7,1},{8,14},{9,15},{10,... | collective-permute-start | bytes 344072 | tf_op jit(solution)/shard_map/ppermute | solution.py:738
  106.6 8.7 %collective-permute-start.23 = (bf16[512,128]{1,0:T(8,128)(2,1)S(1)}, bf16[512,128]{1,0:T(8,128)(2,1)S(1)}, u32[]{:S(2)}, u32[]{:S(2)}) collective-permute-start(bf16[512,128]{1,0:T(8,128)(2,1)S(1)} %last.2), channel_id=1, source_target_pairs={{0,16},{4,20},{8,24},{12,28},{16,0},{20,4},{24,8},{28,12},{1,17},{... | collective-permute-start | bytes 393224 | tf_op jit(solution)/shard_map/ppermute | solution.py:659
  112.2 7.4 %collective-permute-start.24 = (bf16[672,128]{1,0:T(8,128)(2,1)S(1)}, bf16[672,128]{1,0:T(8,128)(2,1)S(1)}, u32[]{:S(2)}, u32[]{:S(2)}) collective-permute-start(bf16[672,128]{1,0:T(8,128)(2,1)S(1)} %get-tuple-element.196), channel_id=1, source_target_pairs={{0,8},{4,12},{8,0},{12,4},{16,24},{20,28},{24,16},{28,20},{1,9},{5... | collective-permute-start | bytes 516104 | tf_op jit(solution)/shard_map/ppermute | solution.py:659
  115.3 11.0 %collective-permute-start.25 = (bf16[1024,128]{1,0:T(8,128)(2,1)S(1)}, bf16[1024,128]{1,0:T(8,128)(2,1)S(1)}, u32[]{:S(2)}, u32[]{:S(2)}) collective-permute-start(bf16[1024,128]{1,0:T(8,128)(2,1)S(1)} %constant_dynamic-update-slice_fusion), channel_id=1, source_target_pairs={{0,8},{4,12},{8,0},{12,4},{16,24},{20,28},{24,16},{28,20},{1,9},{5... | collective-permute-start | bytes 786440 | tf_op jit(solution)/shard_map/ppermute | solution.py:659
  120.2 6.3 %collective-permute-start.26 = (bf16[336,128]{1,0:T(8,128)(2,1)S(1)}, bf16[336,128]{1,0:T(8,128)(2,1)S(1)}, u32[]{:S(2)}, u32[]{:S(2)}) collective-permute-start(bf16[336,128]{1,0:T(8,128)(2,1)S(1)} %get-tuple-element.200), channel_id=1, source_target_pairs={{0,16},{4,20},{8,24},{12,28},{16,0},{20,4},{24,8},{28,12},{1,17},{... | collective-permute-start | bytes 258056 | tf_op jit(solution)/shard_map/ppermute | solution.py:659
  126.5 5.3 %collective-permute-start.27 = (bf16[272,128]{1,0:T(8,128)(2,1)S(1)}, bf16[272,128]{1,0:T(8,128)(2,1)S(1)}, u32[]{:S(2)}, u32[]{:S(2)}) collective-permute-start(bf16[272,128]{1,0:T(8,128)(2,1)S(1)} %get-tuple-element.204), channel_id=1, source_target_pairs={{0,16},{4,20},{8,24},{12,28},{16,0},{20,4},{24,8},{28,12},{1,17},{... | collective-permute-start | bytes 208904 | tf_op jit(solution)/shard_map/ppermute | solution.py:659
  127.0 14.9 %collective-permute-start.29 = (bf16[2048,128]{1,0:T(8,128)(2,1)S(1)}, bf16[2048,128]{1,0:T(8,128)(2,1)S(1)}, u32[]{:S(2)}, u32[]{:S(2)}) collective-permute-start(bf16[2048,128]{1,0:T(8,128)(2,1)S(1)} %constant_dynamic-update-slice_fusion.2), channel_id=1, source_target_pairs={{0,4},{4,0},{8,12},{12,8},{16,20},{20,16},{24,28},{28,24},{1,5},{5... | collective-permute-start | bytes 1572872 | tf_op jit(solution)/shard_map/ppermute | solution.py:659
  131.8 5.1 %collective-permute-start.28 = (bf16[544,128]{1,0:T(8,128)(2,1)S(1)}, bf16[544,128]{1,0:T(8,128)(2,1)S(1)}, u32[]{:S(2)}, u32[]{:S(2)}) collective-permute-start(bf16[544,128]{1,0:T(8,128)(2,1)S(1)} %constant_dynamic-update-slice_fusion.4), channel_id=1, source_target_pairs={{0,8},{4,12},{8,0},{12,4},{16,24},{20,28},{24,16},{28,20},{1,9},{5... | collective-permute-start | bytes 417800 | tf_op jit(solution)/shard_map/ppermute | solution.py:659
  136.9 9.1 %collective-permute-start.30 = (bf16[1088,128]{1,0:T(8,128)(2,1)S(1)}, bf16[1088,128]{1,0:T(8,128)(2,1)S(1)}, u32[]{:S(2)}, u32[]{:S(2)}) collective-permute-start(bf16[1088,128]{1,0:T(8,128)(2,1)S(1)} %constant_dynamic-update-slice_fusion.6), channel_id=1, source_target_pairs={{0,4},{4,0},{8,12},{12,8},{16,20},{20,16},{24,28},{28,24},{1,5},{5... | collective-permute-start | bytes 835592 | tf_op jit(solution)/shard_map/ppermute | solution.py:659
  (7 other events, 64.0 us)

commit v6 on v5

--- a/solution.py
+++ b/solution.py
@@ -17,7 +17,7 @@
 EPSILON = 1e-05
 MASKED = -1e30
 SCALE = HEAD**-0.5
-FILL = 6
+FILL = 3
 INV_ROOT = SPAN**-0.5
 F32 = jnp.float32
 BF16 = jnp.bfloat16
@@ -708,25 +708,31 @@
     return resident(kernel, "fold", micros, 8, (sc,), arrays, [((a, h, LANE), BF16)] * 2)
 
 
-def quad_kernel(sc, keep_ref, got_ref, *refs, bit):
-    along, (own_ref, ctx_ref, near_ref, both_ref) = refs[:-4], refs[-4:]
+def quad_kernel(sc, keep_ref, got_ref, *refs, bit, beside):
+    pairs, (own_ref, ctx_ref, near_ref, both_ref) = refs[:-4], refs[-4:]
     own = lax.div(sc[SC_C], bit) & 1
-    for ref, x in ((own_ref, own), (ctx_ref, 1 - own)):
-        at = keep_ref.shape[2]
-        ref[:at, :] = total_of((keep_ref[0, x], got_ref[0, x]))
-        for array in along[0::2] if ref is own_ref else along[1::2]:
-            ref[at : at + array.shape[0], :] = array[...]
-            at += array.shape[0]
-    near_ref[...] = total_of((keep_ref[1, own], got_ref[1, own]))
+    at = keep_ref.shape[2]
+    own_ref[:at, :] = total_of((keep_ref[0, own], got_ref[0, own]))
+    ctx_ref[:at, :] = total_of((keep_ref[0, 1 - own], got_ref[0, 1 - own]))
+    near_ref[:at, :] = total_of((keep_ref[1, own], got_ref[1, own]))
     both_ref[...] = total_of((keep_ref[1, 1 - own], got_ref[1, 1 - own]))
-
-
-def quad(sc, bit, keep, got, along):
-    kernel = functools.partial(quad_kernel, bit=bit)
-    arrays = (keep, got, *(a for pair in along for a in pair))
+    ends = {True: at, False: at}
+    for n, (kept, sent) in enumerate(zip(pairs[0::2], pairs[1::2])):
+        rows = kept.shape[0]
+        own_ref[at : at + rows, :] = kept[...]
+        at += rows
+        ref, end = (near_ref if n < beside else ctx_ref), ends[n < beside]
+        ref[end : end + rows, :] = sent[...]
+        ends[n < beside] += rows
+
+
+def quad(sc, bit, keep, got, with_near, with_ctx):
+    kernel = functools.partial(quad_kernel, bit=bit, beside=len(with_near))
+    arrays = (keep, got, *(a for pair in (*with_near, *with_ctx) for a in pair))
     h = keep.shape[2]
-    rows = h + sum(kept.shape[0] for kept, _ in along)
-    outs = [((n, LANE), BF16) for n in (rows, rows, h, h)]
+    near = h + sum(kept.shape[0] for kept, _ in with_near)
+    ctx = h + sum(kept.shape[0] for kept, _ in with_ctx)
+    outs = [((n, LANE), BF16) for n in (near + ctx - h, ctx, near, h)]
     return resident(kernel, "quad", 1, 8, (sc,), arrays, outs)
 
 
@@ -738,21 +744,25 @@
     return lax.ppermute(array, ("ctx", "fsdp"), pairs)
 
 
-def refold_kernel(sc, *refs, bit, sizes, whole):
+def refold_kernel(sc, *refs, bit, sizes, sources):
     arrays, (send_ref, own_ref) = refs[:-2], refs[-2:]
     own = lax.div(sc[SC_C], bit) & 1
     at = 0
-    for n, h in enumerate(sizes):
-        group = arrays if n == 0 else arrays[:whole]
+    for h, source in zip(sizes, sources):
         for ref, half in ((send_ref, 1 - own), (own_ref, own)):
-            rows = pl.ds(pl.multiple_of(2 * at + half * h, 16), h)
-            ref[at : at + h, :] = total_of([g[rows, :] for g in group])
+            values = [
+                arrays[k][pl.ds(pl.multiple_of(base + half * h, 16), h), :] for k, base in source
+            ]
+            ref[at : at + h, :] = total_of(values)
         at += h
 
 
-def refold(sc, bit, arrays, sizes, micros=1, whole=2):
+def refold(sc, bit, arrays, sizes, micros=1, sources=None):
+    if sources is None:
+        starts = [2 * sum(sizes[:n]) for n in range(len(sizes))]
+        sources = [[(k, start) for k in range(len(arrays))] for start in starts]
     outs = [((sum(sizes), LANE), BF16)] * 2
-    kernel = functools.partial(refold_kernel, bit=bit, sizes=sizes, whole=whole)
+    kernel = functools.partial(refold_kernel, bit=bit, sizes=sizes, sources=sources)
     return resident(kernel, "fold", micros, 8, (sc,), arrays, outs)
 
 
@@ -889,6 +899,10 @@
             rows[pl.ds(to, h), :] = got_ref[k, at : at + h, :].astype(F32)
             at, base = at + h, base + height
     for ref, places in zip(outs, plan):
+        if len(ref.shape) == 1:
+            for j, place in enumerate(places):
+                ref[j * LANE : (j + 1) * LANE] = rows[place, :]
+            continue
         height = ref.shape[0]
         for j, place in enumerate(places):
             ref[:, j * LANE : (j + 1) * LANE] = rows[place : place + height, :]
@@ -967,7 +981,7 @@
     dh1 = seq.next(dh1)
     upper, *old = back(scalars, fixed, (dub, gvec, dh1, sums), 1, nf, nc, last=False)
     seq.made(old[0])
-    first.step(*near[0])
+    first.step("ctx", bits[0])
     feed = united(scalars, seq, [from_down, from_up])
     old[0] = seq.next(old[0])
     lower, _, fsend1, fkeep1, send, keep = back(
@@ -977,11 +991,14 @@
     second = Part(scalars, seq, keep, send)
     while feed.more():
         feed.step(FILL)
-    first.split("ctx", bits[0], FILL)
-    along = ((first.keep[0], first.send[0]), (fkeep0, fsend0), (fkeep1, fsend1))
+    first.split(*near[0], FILL)
+    with_near = ((first.keep[0], first.send[0]),)
+    with_ctx = ((fkeep0, fsend0), (fkeep1, fsend1))
     view = (2, 2, second.rows // 2, LANE)
     keep, got = (a.reshape(view) for a in (second.keep, *second.gots))
-    own, to_ctx, to_near, to_both = quad(scalars, bits[0], seq.next(keep), got, along)
+    own, to_ctx, to_near, to_both = quad(
+        scalars, bits[0], seq.next(keep), got, with_near, with_ctx
+    )
     seq.made(own)
     arrays = (
         own,
@@ -989,12 +1006,20 @@
         swap(to_near, *near[0]),
         swap_both(to_both, bits[0], near[0][1]),
     )
+    feed.end()
+    heights = [second.total // 2] + [kept.shape[0] for kept, _ in (*with_near, *with_ctx)]
+    sources, at, ends = [[(k, 0) for k in range(4)]], heights[0], {1: heights[0], 2: heights[0]}
+    for n, rows in enumerate(heights[1:]):
+        where = 2 if n < len(with_near) else 1
+        sources.append([(0, at), (where, ends[where])])
+        at += rows
+        ends[where] += rows
+    sizes = [rows // 2 for rows in heights]
+    arrays = (seq.next(arrays[0]), *arrays[1:])
+    halves = refold(scalars, bits[1], arrays, sizes, sources=sources)
+    rest = Union(scalars, seq, halves, sizes, 2)
     mixed = block_output(scalars, seq.next(r1), g, vec, down)
     seq.made(mixed)
-    feed.end()
-    sizes = [second.total // 4] + [kept.shape[0] // 2 for kept, _ in along]
-    arrays = (seq.next(arrays[0]), *arrays[1:])
-    rest = Union(scalars, seq, refold(scalars, bits[1], arrays, sizes), sizes, 2)
     while feed.at > 1:
         feed.join()
     while rest.more():
@@ -1032,13 +1057,13 @@
     shapes = [(block, 3 * D), (block, D)]
     at = 3 * half * block
     for wide in (block, block, 3 * block, block, block, block, 4 * block, block):
-        shapes.append((1, wide))
+        shapes.append((wide,))
         plan.append([at + j for j in range(wide // LANE)])
         at += wide // LANE
     grad_qkv, grad_out, *vectors = finish(
         scalars, rest.rows(), (second.total, first.total), shapes, plan
     )
-    g1, s1, qb, ob, g2, s2, ub, db = (v.reshape(-1) for v in vectors)
+    g1, s1, qb, ob, g2, s2, ub, db = vectors
     return (
         mixed[None], tokens_grad[None], g1, s1, grad_qkv, qb, grad_out, ob, g2, s2,
         grad_up, ub, grad_down, db,

time: 149 us -> 147 us (0.987)
  waiting for transfers between devices: 46.2 us -> 43 us
  starting transfers between devices: 29.6 us -> 31.7 us
    ppermute x1, waiting for transfers between devices: 4.36 us -> 1.92 us  [swap_both(): return lax.ppermute(array, ('ctx', 'fsdp'), pairs)]
    ppermute x30, starting transfers between devices: 22.6 us -> 24 us  [swap(): return lax.ppermute(array, axis, [(k, k ^ bit) for k in range(n)])]
  transfers between devices with their start and end apart: 32 -> 32, of which waited for: 14 -> 16; matrix products, arithmetic and copies ran while one was open for 0% -> 0% of each run, Pallas kernels for 45% -> 45%
where the time goes in v6:
time: 147 us
  Pallas kernels  70.8 us (48%)
  waiting for transfers between devices  43 us (29%)
  starting transfers between devices  31.7 us (22%)
    pallas_call x23, Pallas kernels, resident(): pl.pallas_call(kernel, in_specs=[pl.BlockSpec(memory_space=pltpu.SMEM)] *...  57.4 us
    ppermute x30, waiting for transfers between devices, swap(): return lax.ppermute(array, axis, [(k, k ^ bit) for k in range(n)])  33.8 us
    ppermute x30, starting transfers between devices, swap(): return lax.ppermute(array, axis, [(k, k ^ bit) for k in range(n)])  24 us
    all_to_all x1, waiting for transfers between devices, local(): nsum = lax.all_to_all(sums, 'ctx', 0, 0, tiled=True).reshape(nc * spans, D)  7.26 us
    all_to_all x1, starting transfers between devices, local(): nsum = lax.all_to_all(sums, 'ctx', 0, 0, tiled=True).reshape(nc * spans, D)  5.81 us
    pallas_call x1, Pallas kernels, block_output(): pl.pallas_call(mixed_kernel, grid=(rows // ROWS,), in_specs=[pl.BlockSpec...  4.13 us
    pallas_call x2, Pallas kernels, finish(): pl.pallas_call(functools.partial(finish_kernel, heights=heights, plan=pla...  3.78 us
    pallas_call x1, Pallas kernels, first_back(): pl.pallas_call(first_kernel, grid=(rows // ROWS,), in_specs=in_vmem(7), o...  3.44 us
  transfers between devices with their start and end apart: 32, of which 16 were waited for; matrix products, arithmetic and copies ran while one was open for 0% of the time, Pallas kernels for 45%

profile of v6, /device:TPU:0, one launch (start us, length us, event | category | flops | bytes accessed | tf_op | source)
XLA Modules:
  0.0 147.0 jit_solution(11980450965651096113)
XLA Ops:
  0.7 2.1 %pack.1.refs_0_ = bf16[144,2048]{1,0:T(8,128)(2,1)} custom-call(bf16[128,1536]{1,0:T(8,128)(2,1)} %qkv_ref.1, bf16[128,512]{1,0:T(8,128)(2,1)} %out_ref.1, bf16[1,128]{1,0:T(2,128)(2,1)} %bitcast.84, bf16[1,128]{1,0:T(2,128)(2,1)} %bitcast.85, bf16[3,128]{1,0:T(4,128)(2,1)} %bitcast.82, bf16[1,128]{1,0:T(2,128)(2,1)} %bitcast.86, bf16[1,128]{1,0:T(2,128)(2,1)} %bitcast.87, ...), custom_call_target="tpu_custom_call" | custom-call | flops 1000000000 | bytes 1000000 | tf_op jit(solution)/shard_map/pack/pallas_call | solution.py:134
  2.7 3.0 %collective-permute-start.1 = (bf16[144,2048]{1,0:T(8,128)(2,1)}, bf16[144,2048]{1,0:T(8,128)(2,1)S(1)}, u32[]{:S(2)}, u32[]{:S(2)}) collective-permute-start(bf16[144,2048]{1,0:T(8,128)(2,1)} %pack.1.refs_0_), channel_id=1, source_target_pairs={{0,2},{1,3},{2,0},{3,1},{4,6},{5,7},{6,4},{7,5},{8,10},{9,11},{10,... | collective-permute-start | bytes 1769480 | tf_op jit(solution)/shard_map/ppermute | solution.py:659
  5.7 1.4 span_sums.1
  7.1 5.8 %all-to-all-start = ((f32[8,8,512]{2,1,0:T(8,128)}), f32[8,8,512]{2,1,0:T(8,128)S(1)}, u32[]{:S(2)}, u32[]{:S(2)}) async-start(f32[8,8,512]{2,1,0:T(8,128)} %span_sums.1), calls=%async_computation | async-start | bytes 262144 | tf_op jit(solution)/shard_map/all_to_all | solution.py:947
  13.0 7.3 %all-to-all-done = f32[8,8,512]{2,1,0:T(8,128)S(1)} async-done(((f32[8,8,512]{2,1,0:T(8,128)}), f32[8,8,512]{2,1,0:T(8,128)S(1)}, u32[]{:S(2)}, u32[]{:S(2)}) %all-to-all-start) | async-done | bytes 131104 | tf_op jit(solution)/shard_map/all_to_all | solution.py:947
  22.3 8.3 %attend.1 = (bf16[1024,1536]{1,0:T(8,128)(2,1)S(1)}, bf16[32,192,256]{2,1,0:T(8,128)(2,1)S(1)}, bf16[1024,512]{1,0:T(8,128)(2,1)S(1)}, bf16[1024,512]{1,0:T(8,12...) custom-call(s32[76]{0:T(128)S(1)} %concatenate.21.sc.refs_0_, ...), custom_call_target="tpu_custom_call" | custom-call | flops 12000000000 | bytes 12000000 | tf_op jit(solution)/shard_map/attend/pallas_call | solution.py:69
  30.6 4.3 %collective-permute-done.4.refs_2_ = bf16[128,2048]{1,0:T(8,128)(2,1)S(1)} collective-permute-done((bf16[128,2048]{1,0:T(8,128)(2,1)}, bf16[128,2048]{1,0:T(8,128)(2,1)S(1)}, u32[]{:S(2)}, u32[]{:S(2)}) %collective-permute-start.4) | collective-permute-done | bytes 524320 | tf_op jit(solution)/shard_map/ppermute | solution.py:659
  37.0 6.9 %ffn_up.1 = (bf16[1024,2048]{1,0:T(8,128)(2,1)S(1)}, bf16[1024,2048]{1,0:T(8,128)(2,1)S(1)}, bf16[512,2048]{1,0:T(8,128)(2,1)S(1)}) custom-call(s32[76]{0:T(128)S(1)} %concatenate.21.sc.refs_0_, bf16[1024,512]{1,0:T(8,128)(2,1)S(1)} %get-tuple-element.124.h2_ref, f32[8,2048]{1,0:T(8,128)S(1)} %get-tuple-element.122.vec.vec_ref.refs_8_, ...), custom_call_target="tpu_custom_call" | custom-call | flops 8000000000 | bytes 8000000 | tf_op jit(solution)/shard_map/ffn_up/pallas_call | solution.py:69
  44.0 2.9 %down_grad.1 = (bf16[2,2048,128]{2,1,0:T(8,128)(2,1)S(1)}, bf16[2,2048,128]{2,1,0:T(8,128)(2,1)S(1)}) custom-call(s32[76]{0:T(128)S(1)} %concatenate.21.sc.refs_0_, bf16[1024,2048]{1,0:T(8,128)(2,1)S(1)} %get-tuple-element.130.g_ref, bf16[1024,512]{1,0:T(8,128)(2,1)S(1)} %bitcast.49), custom_call_target="tpu_custom_call" | custom-call | flops 4000000000 | bytes 4000000 | tf_op jit(solution)/shard_map/down_grad/pallas_call | solution.py:69
  46.9 2.4 %collective-permute-done.7.refs_2_ = bf16[512,512]{1,0:T(8,128)(2,1)S(1)} collective-permute-done((bf16[512,512]{1,0:T(8,128)(2,1)S(1)}, bf16[512,512]{1,0:T(8,128)(2,1)S(1)}, u32[]{:S(2)}, u32[]{:S(2)}) %collective-permute-start.7) | collective-permute-done | bytes 524320 | tf_op jit(solution)/shard_map/ppermute | solution.py:659
  51.2 7.8 %ffn_down.1 = (f32[1024,512]{1,0:T(8,128)S(1)}, f32[1,2048]{1,0:T(1,128)S(1)}, bf16[2,2048,128]{2,1,0:T(8,128)(2,1)S(1)}, bf16[2,2048,128]{2,1,0:T(8,128)(2,1)S(1)}) custom-call(s32[76]{0:T(128)S(1)} %concatenate.21.sc.refs_0_, bf16[1024,512]{1,0:T(8,128)(2,1)S(1)} %get-tuple-element.124.h2_ref, bf16[1024,512]{1,0:T(8,128)(2,1)S(1)} %bitcast.50, ...), custom_call_target="tpu_custom_call" | custom-call | flops 8000000000 | bytes 8000000 | tf_op jit(solution)/shard_map/ffn_down/pallas_call | solution.py:69
  60.7 2.6 %mid.1 = (f32[1024,512]{1,0:T(8,128)S(1)}, bf16[1024,512]{1,0:T(8,128)(2,1)S(1)}, f32[512,512]{1,0:T(8,128)S(1)}, f32[8,512]{1,0:T(8,128)S(1)}) custom-call(bf16[1024,512]{1,0:T(8,128)(2,1)S(1)} %bitcast.51, f32[1024,512]{1,0:T(8,128)S(1)} %get-tuple-element.137.dh2_ref, f32[1024,512]{1,0:T(8,128)S(1)} %get-tuple-element.196.r1_ref, ...), custom_call_target="tpu_custom_call" | custom-call | flops 5000000000 | bytes 5000000 | tf_op jit(solution)/shard_map/mid/pallas_call | solution.py:69
  64.2 1.6 %collective-permute-start.12 = (bf16[2,1024,128]{2,1,0:T(8,128)(2,1)S(1)}, bf16[2,1024,128]{2,1,0:T(8,128)(2,1)S(1)}, u32[]{:S(2)}, u32[]{:S(2)}) collective-permute-start(bf16[2,1024,128]{2,1,0:T(8,128)(2,1)S(1)} %get-tuple-element.143), channel_id=1, source_target_pairs={{0,4},{4,0},{8,12},{12,8},{16,20},{20,16},{24,28},{28,24},{1,5},{5... | collective-permute-start | bytes 1572872 | tf_op jit(solution)/shard_map/ppermute | solution.py:659
  65.7 8.8 %back_0.1 = (f32[1024,512]{1,0:T(8,128)S(1)}, f32[72,512]{1,0:T(8,128)S(1)}, bf16[128,128]{1,0:T(8,128)(2,1)S(1)}, bf16[128,128]{1,0:T(8,128)(2,1)S(1)}, bf16[2,...) custom-call(s32[76]{0:T(128)S(1)} %concatenate.21.sc.refs_0_, bf16[1024,512]{1,0:T(8,128)(2,1)S(1)} %bitcast.55, ...), custom_call_target="tpu_custom_call" | custom-call | flops 8999999488 | bytes 9000000 | tf_op jit(solution)/shard_map/back_0/pallas_call | solution.py:69
  75.9 2.6 %collective-permute-done.12 = bf16[2,1024,128]{2,1,0:T(8,128)(2,1)S(1)} collective-permute-done((bf16[2,1024,128]{2,1,0:T(8,128)(2,1)S(1)}, bf16[2,1024,128]{2,1,0:T(8,128)(2,1)S(1)}, u32[]{:S(2)}, u32[]{:S(2)}) %collective-permute-start.12) | collective-permute-done | bytes 524320 | tf_op jit(solution)/shard_map/ppermute | solution.py:659
  79.2 1.9 %collective-permute-start.15 = (bf16[1,1024,128]{2,1,0:T(8,128)(2,1)S(1)}, bf16[1,1024,128]{2,1,0:T(8,128)(2,1)S(1)}, u32[]{:S(2)}, u32[]{:S(2)}) collective-permute-start(bf16[1,1024,128]{2,1,0:T(8,128)(2,1)S(1)} %get-tuple-element.159), channel_id=1, source_target_pairs={{0,2},{1,3},{2,0},{3,1},{4,6},{5,7},{6,4},{7,5},{8,10},{9,11},{10,... | collective-permute-start | bytes 786440 | tf_op jit(solution)/shard_map/ppermute | solution.py:659
  81.1 4.3 %back_1.2 = (f32[512,512]{1,0:T(8,128)S(1)}, f32[512,768]{1,0:T(8,128)S(1)}, f32[64,512]{1,0:T(8,128)S(1)}, f32[16,1536]{1,0:T(8,128)S(1)}) custom-call(s32[76]{0:T(128)S(1)} %concatenate.21.sc.refs_0_, bf16[1024,512]{1,0:T(8,128)(2,1)S(1)} %bitcast.56, bf16[1024,512]{1,0:T(8,128)(2,1)S(1)} %get-tuple-element.144.refs_2_, ...), custom_call_target="tpu_custom_call" | custom-call | flops 8999999488 | bytes 9000000 | tf_op jit(solution)/shard_map/back_1/pallas_call | solution.py:69
  87.2 1.9 %collective-permute-start.16 = (bf16[1024,128]{1,0:T(8,128)(2,1)S(1)}, bf16[1024,128]{1,0:T(8,128)(2,1)S(1)}, u32[]{:S(2)}, u32[]{:S(2)}) collective-permute-start(bf16[1024,128]{1,0:T(8,128)(2,1)S(1)} %bitcast.68), channel_id=1, source_target_pairs={{0,8},{4,12},{8,0},{12,4},{16,24},{20,28},{24,16},{28,20},{1,9},{5... | collective-permute-start | bytes 786440 | tf_op jit(solution)/shard_map/ppermute | solution.py:659
  89.1 5.7 %back_1.3 = (f32[512,512]{1,0:T(8,128)S(1)}, f32[72,512]{1,0:T(8,128)}, bf16[128,128]{1,0:T(8,128)(2,1)S(1)}, bf16[128,128]{1,0:T(8,128)(2,1)S(1)}, bf16[2,896,1...) custom-call(s32[76]{0:T(128)S(1)} %concatenate.21.sc.refs_0_, bf16[1024,512]{1,0:T(8,128)(2,1)S(1)} %bitcast.57, ...), custom_call_target="tpu_custom_call" | custom-call | flops 8999999488 | bytes 9000000 | tf_op jit(solution)/shard_map/back_1/pallas_call | solution.py:69
  97.2 1.7 %collective-permute-start.21 = (bf16[1088,128]{1,0:T(8,128)(2,1)S(1)}, bf16[1088,128]{1,0:T(8,128)(2,1)S(1)}, u32[]{:S(2)}, u32[]{:S(2)}) collective-permute-start(bf16[1088,128]{1,0:T(8,128)(2,1)S(1)} %get-tuple-element.192), channel_id=1, source_target_pairs={{0,2},{1,3},{2,0},{3,1},{4,6},{5,7},{6,4},{7,5},{8,10},{9,11},{10,... | collective-permute-start | bytes 835592 | tf_op jit(solution)/shard_map/ppermute | solution.py:659
  98.9 2.6 %collective-permute-start.19 = (bf16[512,128]{1,0:T(8,128)(2,1)S(1)}, bf16[512,128]{1,0:T(8,128)(2,1)S(1)}, u32[]{:S(2)}, u32[]{:S(2)}) collective-permute-start(bf16[512,128]{1,0:T(8,128)(2,1)S(1)} %get-tuple-element.178), channel_id=1, source_target_pairs={{0,16},{4,20},{8,24},{12,28},{16,0},{20,4},{24,8},{28,12},{1,17},{... | collective-permute-start | bytes 393224 | tf_op jit(solution)/shard_map/ppermute | solution.py:659
  101.6 1.8 %collective-permute-start.22 = (bf16[448,128]{1,0:T(8,128)(2,1)S(1)}, bf16[448,128]{1,0:T(8,128)(2,1)S(1)}, u32[]{:S(2)}, u32[]{:S(2)}) collective-permute-start(bf16[448,128]{1,0:T(8,128)(2,1)S(1)} %get-tuple-element.193), channel_id=1, source_target_pairs={{0,6},{1,7},{2,4},{3,5},{4,2},{5,3},{6,0},{7,1},{8,14},{9,15},{10,... | collective-permute-start | bytes 344072 | tf_op jit(solution)/shard_map/ppermute | solution.py:744
  103.4 4.4 %collective-permute-done.19.got_ref = bf16[512,128]{1,0:T(8,128)(2,1)S(1)} collective-permute-done((bf16[512,128]{1,0:T(8,128)(2,1)S(1)}, bf16[512,128]{1,0:T(8,128)(2,1)S(1)}, u32[]{:S(2)}, u32[]{:S(2)}) %collective-permute-start.19) | collective-permute-done | bytes 131104 | tf_op jit(solution)/shard_map/ppermute | solution.py:659
  107.9 1.9 %collective-permute-done.22.refs_3_ = bf16[448,128]{1,0:T(8,128)(2,1)S(1)} collective-permute-done((bf16[448,128]{1,0:T(8,128)(2,1)S(1)}, bf16[448,128]{1,0:T(8,128)(2,1)S(1)}, u32[]{:S(2)}, u32[]{:S(2)}) %collective-permute-start.22) | collective-permute-done | bytes 114720 | tf_op jit(solution)/shard_map/ppermute | solution.py:744
  111.8 4.1 %block_output.1 = bf16[1024,512]{1,0:T(8,128)(2,1)} custom-call(s32[76]{0:T(128)S(1)} %concatenate.21.sc.refs_0_, f32[1024,512]{1,0:T(8,128)S(1)} %get-tuple-element.196.r1_ref, bf16[1024,2048]{1,0:T(8,128)(2,1)S(1)} %get-tuple-element.130.g_ref, f32[8,2048]{1,0:T(8,128)S(1)} %get-tuple-element.122.vec.vec_ref.refs_8_, bf16[512,512]{1,0:T(8,128)(2,1)S(1)} %copy-done.5, ...), custom_call_target="tpu_custom_call" | custom-call | flops 4000000000 | bytes 4000000 | tf_op jit(solution)/shard_map/block_output/pallas_call | solution.py:645
  119.7 6.3 %collective-permute-done.25 = bf16[1024,128]{1,0:T(8,128)(2,1)S(1)} collective-permute-done((bf16[1024,128]{1,0:T(8,128)(2,1)S(1)}, bf16[1024,128]{1,0:T(8,128)(2,1)S(1)}, u32[]{:S(2)}, u32[]{:S(2)}) %collective-permute-start.25) | collective-permute-done | bytes 262176 | tf_op jit(solution)/shard_map/ppermute | solution.py:659
  127.3 4.1 %collective-permute-done.27 = bf16[272,128]{1,0:T(8,128)(2,1)S(1)} collective-permute-done((bf16[272,128]{1,0:T(8,128)(2,1)S(1)}, bf16[272,128]{1,0:T(8,128)(2,1)S(1)}, u32[]{:S(2)}, u32[]{:S(2)}) %collective-permute-start.27) | collective-permute-done | bytes 69664 | tf_op jit(solution)/shard_map/ppermute | solution.py:659
  132.7 3.4 %first_back.1 = f32[1024,512]{1,0:T(8,128)} custom-call(bf16[1024,512]{1,0:T(8,128)(2,1)S(1)} %bitcast.58, f32[1024,512]{1,0:T(8,128)S(1)} %get-tuple-element.206.dr1_ref, f32[512,512]{1,0:T(8,128)S(1)} %get-tuple-element.207.upper_ref, f32[512,512]{1,0:T(8,128)S(1)} %get-tuple-element.175.lower_ref, bf16[64,128]{1,0:T(8,128)(2,1)S(1)} %get-tuple-element.208.own_ref, ...), custom_call_target="tpu_custom_call" | custom-call | flops 3000000000 | bytes 3000000 | tf_op jit(solution)/shard_map/first_back/pallas_call | solution.py:619
  137.7 3.8 %collective-permute-done.29 = bf16[2048,128]{1,0:T(8,128)(2,1)S(1)} collective-permute-done((bf16[2048,128]{1,0:T(8,128)(2,1)S(1)}, bf16[2048,128]{1,0:T(8,128)(2,1)S(1)}, u32[]{:S(2)}, u32[]{:S(2)}) %collective-permute-start.29) | collective-permute-done | bytes 524320 | tf_op jit(solution)/shard_map/ppermute | solution.py:659
  141.6 2.1 %finish.2 = (f32[512,512]{1,0:T(8,128)}, f32[128,2048]{1,0:T(8,128)}) custom-call(s32[76]{0:T(128)S(1)} %concatenate.21.sc.refs_0_, bf16[8,512,128]{2,1,0:T(8,128)(2,1)S(1)} %bitcast.42), custom_call_target="tpu_custom_call" | custom-call | flops 2000000000 | bytes 2000000 | tf_op jit(solution)/shard_map/finish/pallas_call | solution.py:912
  143.7 1.4 collective-permute-done.30
  145.2 1.6 %finish.3 = (f32[128,1536]{1,0:T(8,128)}, f32[128,512]{1,0:T(8,128)}, f32[128]{0:T(128)}, f32[128]{0:T(128)}, f32[384]{0:T(512)}, /*index=5*/f32[128]{0:T(128)},...) custom-call(s32[76]{0:T(128)S(1)} %concatenate.21.sc.refs_0_, bf16[8,272,128]{2,1,0:T(8,128)(2,1)S(1)} %bitcast.43), custom_call_target="tpu_custom_call" | custom-call | flops 2000000000 | bytes 2000000 | tf_op jit(solution)/shard_map/finish/pallas_call | solution.py:912
  (85 shorter events, 24.9 us)
Async XLA Ops:
  2.7 17.5 %collective-permute-start.1 = (bf16[144,2048]{1,0:T(8,128)(2,1)}, bf16[144,2048]{1,0:T(8,128)(2,1)S(1)}, u32[]{:S(2)}, u32[]{:S(2)}) collective-permute-start(bf16[144,2048]{1,0:T(8,128)(2,1)} %pack.1.refs_0_), channel_id=1, source_target_pairs={{0,2},{1,3},{2,0},{3,1},{4,6},{5,7},{6,4},{7,5},{8,10},{9,11},{10,... | collective-permute-start | bytes 1769480 | tf_op jit(solution)/shard_map/ppermute | solution.py:659
  7.1 13.1 %all-to-all-start = ((f32[8,8,512]{2,1,0:T(8,128)}), f32[8,8,512]{2,1,0:T(8,128)S(1)}, u32[]{:S(2)}, u32[]{:S(2)}) async-start(f32[8,8,512]{2,1,0:T(8,128)} %span_sums.1), calls=%async_computation | async-start | bytes 262144 | tf_op jit(solution)/shard_map/all_to_all | solution.py:947
  12.9 8.4 %collective-permute-start = (bf16[144,2048]{1,0:T(8,128)(2,1)S(1)}, bf16[144,2048]{1,0:T(8,128)(2,1)S(1)}, u32[]{:S(2)}, u32[]{:S(2)}) collective-permute-start(bf16[144,2048]{1,0:T(8,128)(2,1)S(1)} %copy-done.3), channel_id=1, source_target_pairs={{0,1},{1,0},{2,3},{3,2},{4,5},{5,4},{6,7},{7,6},{8,9},{9,8},{10,11... | collective-permute-start | bytes 1769480 | tf_op jit(solution)/shard_map/ppermute | solution.py:659
  20.3 2.0 %collective-permute-start.2 = (bf16[144,2048]{1,0:T(8,128)(2,1)S(1)}, bf16[144,2048]{1,0:T(8,128)(2,1)S(1)}, u32[]{:S(2)}, u32[]{:S(2)}) collective-permute-start(bf16[144,2048]{1,0:T(8,128)(2,1)S(1)} %collective-permute-done.1.refs_2_), channel_id=1, source_target_pairs={{0,1},{1,0},{2,3},{3,2},{4,5},{5,4},{6,7},{7,6},{8,9},{9,8},{10,11... | collective-permute-start | bytes 1769480 | tf_op jit(solution)/shard_map/ppermute | solution.py:659
  20.4 14.6 %collective-permute-start.4 = (bf16[128,2048]{1,0:T(8,128)(2,1)}, bf16[128,2048]{1,0:T(8,128)(2,1)S(1)}, u32[]{:S(2)}, u32[]{:S(2)}) collective-permute-start(bf16[128,2048]{1,0:T(8,128)(2,1)} %refs_0_), channel_id=1, source_target_pairs={{0,2},{1,3},{2,0},{3,1},{4,6},{5,7},{6,4},{7,5},{8,10},{9,11},{10,... | collective-permute-start | bytes 1572872 | tf_op jit(solution)/shard_map/ppermute | solution.py:659
  21.1 15.9 %collective-permute-start.3 = (bf16[128,2048]{1,0:T(8,128)(2,1)}, bf16[128,2048]{1,0:T(8,128)(2,1)S(1)}, u32[]{:S(2)}, u32[]{:S(2)}) collective-permute-start(bf16[128,2048]{1,0:T(8,128)(2,1)} %refs_0_), channel_id=1, source_target_pairs={{0,1},{1,0},{2,3},{3,2},{4,5},{5,4},{6,7},{7,6},{8,9},{9,8},{10,11... | collective-permute-start | bytes 1572872 | tf_op jit(solution)/shard_map/ppermute | solution.py:659
  34.9 2.1 %collective-permute-start.5 = (bf16[128,2048]{1,0:T(8,128)(2,1)S(1)}, bf16[128,2048]{1,0:T(8,128)(2,1)S(1)}, u32[]{:S(2)}, u32[]{:S(2)}) collective-permute-start(bf16[128,2048]{1,0:T(8,128)(2,1)S(1)} %collective-permute-done.4.refs_2_), channel_id=1, source_target_pairs={{0,1},{1,0},{2,3},{3,2},{4,5},{5,4},{6,7},{7,6},{8,9},{9,8},{10,11... | collective-permute-start | bytes 1572872 | tf_op jit(solution)/shard_map/ppermute | solution.py:659
  34.9 14.3 %collective-permute-start.7 = (bf16[512,512]{1,0:T(8,128)(2,1)S(1)}, bf16[512,512]{1,0:T(8,128)(2,1)S(1)}, u32[]{:S(2)}, u32[]{:S(2)}) collective-permute-start(bf16[512,512]{1,0:T(8,128)(2,1)S(1)} %copy-done.5), channel_id=1, source_target_pairs={{0,2},{1,3},{2,0},{3,1},{4,6},{5,7},{6,4},{7,5},{8,10},{9,11},{10,... | collective-permute-start | bytes 1572872 | tf_op jit(solution)/shard_map/ppermute | solution.py:659
  35.6 14.1 %collective-permute-start.6 = (bf16[512,512]{1,0:T(8,128)(2,1)S(1)}, bf16[512,512]{1,0:T(8,128)(2,1)S(1)}, u32[]{:S(2)}, u32[]{:S(2)}) collective-permute-start(bf16[512,512]{1,0:T(8,128)(2,1)S(1)} %copy-done.5), channel_id=1, source_target_pairs={{0,1},{1,0},{2,3},{3,2},{4,5},{5,4},{6,7},{7,6},{8,9},{9,8},{10,11... | collective-permute-start | bytes 1572872 | tf_op jit(solution)/shard_map/ppermute | solution.py:659
  49.2 1.9 %collective-permute-start.8 = (bf16[512,512]{1,0:T(8,128)(2,1)S(1)}, bf16[512,512]{1,0:T(8,128)(2,1)S(1)}, u32[]{:S(2)}, u32[]{:S(2)}) collective-permute-start(bf16[512,512]{1,0:T(8,128)(2,1)S(1)} %collective-permute-done.7.refs_2_), channel_id=1, source_target_pairs={{0,1},{1,0},{2,3},{3,2},{4,5},{5,4},{6,7},{7,6},{8,9},{9,8},{10,11... | collective-permute-start | bytes 1572872 | tf_op jit(solution)/shard_map/ppermute | solution.py:659
  49.3 9.9 %collective-permute-start.9 = (bf16[2,2048,128]{2,1,0:T(8,128)(2,1)S(1)}, bf16[2,2048,128]{2,1,0:T(8,128)(2,1)S(1)}, u32[]{:S(2)}, u32[]{:S(2)}) collective-permute-start(bf16[2,2048,128]{2,1,0:T(8,128)(2,1)S(1)} %get-tuple-element.134), channel_id=1, source_target_pairs={{0,1},{1,0},{2,3},{3,2},{4,5},{5,4},{6,7},{7,6},{8,9},{9,8},{10,11... | collective-permute-start | bytes 3145736 | tf_op jit(solution)/shard_map/ppermute | solution.py:659
  59.0 4.4 %collective-permute-start.10 = (bf16[2,2048,128]{2,1,0:T(8,128)(2,1)S(1)}, bf16[2,2048,128]{2,1,0:T(8,128)(2,1)S(1)}, u32[]{:S(2)}, u32[]{:S(2)}) collective-permute-start(bf16[2,2048,128]{2,1,0:T(8,128)(2,1)S(1)} %get-tuple-element.141), channel_id=1, source_target_pairs={{0,1},{1,0},{2,3},{3,2},{4,5},{5,4},{6,7},{7,6},{8,9},{9,8},{10,11... | collective-permute-start | bytes 3145736 | tf_op jit(solution)/shard_map/ppermute | solution.py:659
  60.0 14.6 %collective-permute-start.11 = (bf16[1,2048,128]{2,1,0:T(8,128)(2,1)S(1)}, bf16[1,2048,128]{2,1,0:T(8,128)(2,1)S(1)}, u32[]{:S(2)}, u32[]{:S(2)}) collective-permute-start(bf16[1,2048,128]{2,1,0:T(8,128)(2,1)S(1)} %get-tuple-element.136), channel_id=1, source_target_pairs={{0,2},{1,3},{2,0},{3,1},{4,6},{5,7},{6,4},{7,5},{8,10},{9,11},{10,... | collective-permute-start | bytes 1572872 | tf_op jit(solution)/shard_map/ppermute | solution.py:659
  64.2 14.3 %collective-permute-start.12 = (bf16[2,1024,128]{2,1,0:T(8,128)(2,1)S(1)}, bf16[2,1024,128]{2,1,0:T(8,128)(2,1)S(1)}, u32[]{:S(2)}, u32[]{:S(2)}) collective-permute-start(bf16[2,1024,128]{2,1,0:T(8,128)(2,1)S(1)} %get-tuple-element.143), channel_id=1, source_target_pairs={{0,4},{4,0},{8,12},{12,8},{16,20},{20,16},{24,28},{28,24},{1,5},{5... | collective-permute-start | bytes 1572872 | tf_op jit(solution)/shard_map/ppermute | solution.py:659
  75.3 11.2 %collective-permute-start.14 = (bf16[1,1024,128]{2,1,0:T(8,128)(2,1)S(1)}, bf16[1,1024,128]{2,1,0:T(8,128)(2,1)S(1)}, u32[]{:S(2)}, u32[]{:S(2)}) collective-permute-start(bf16[1,1024,128]{2,1,0:T(8,128)(2,1)S(1)} %get-tuple-element.156), channel_id=1, source_target_pairs={{0,4},{4,0},{8,12},{12,8},{16,20},{20,16},{24,28},{28,24},{1,5},{5... | collective-permute-start | bytes 786440 | tf_op jit(solution)/shard_map/ppermute | solution.py:659
  75.9 9.5 %collective-permute-start.13 = (bf16[2,1280,128]{2,1,0:T(8,128)(2,1)S(1)}, bf16[2,1280,128]{2,1,0:T(8,128)(2,1)S(1)}, u32[]{:S(2)}, u32[]{:S(2)}) collective-permute-start(bf16[2,1280,128]{2,1,0:T(8,128)(2,1)S(1)} %get-tuple-element.165), channel_id=1, source_target_pairs={{0,1},{1,0},{2,3},{3,2},{4,5},{5,4},{6,7},{7,6},{8,9},{9,8},{10,11... | collective-permute-start | bytes 1966088 | tf_op jit(solution)/shard_map/ppermute | solution.py:659
  79.2 7.3 %collective-permute-start.15 = (bf16[1,1024,128]{2,1,0:T(8,128)(2,1)S(1)}, bf16[1,1024,128]{2,1,0:T(8,128)(2,1)S(1)}, u32[]{:S(2)}, u32[]{:S(2)}) collective-permute-start(bf16[1,1024,128]{2,1,0:T(8,128)(2,1)S(1)} %get-tuple-element.159), channel_id=1, source_target_pairs={{0,2},{1,3},{2,0},{3,1},{4,6},{5,7},{6,4},{7,5},{8,10},{9,11},{10,... | collective-permute-start | bytes 786440 | tf_op jit(solution)/shard_map/ppermute | solution.py:659
  86.1 9.3 %collective-permute-start.17 = (bf16[2,640,128]{2,1,0:T(8,128)(2,1)S(1)}, bf16[2,640,128]{2,1,0:T(8,128)(2,1)S(1)}, u32[]{:S(2)}, u32[]{:S(2)}) collective-permute-start(bf16[2,640,128]{2,1,0:T(8,128)(2,1)S(1)} %get-tuple-element.167), channel_id=1, source_target_pairs={{0,4},{4,0},{8,12},{12,8},{16,20},{20,16},{24,28},{28,24},{1,5},{5... | collective-permute-start | bytes 983048 | tf_op jit(solution)/shard_map/ppermute | solution.py:659
  87.2 7.6 %collective-permute-start.16 = (bf16[1024,128]{1,0:T(8,128)(2,1)S(1)}, bf16[1024,128]{1,0:T(8,128)(2,1)S(1)}, u32[]{:S(2)}, u32[]{:S(2)}) collective-permute-start(bf16[1024,128]{1,0:T(8,128)(2,1)S(1)} %bitcast.68), channel_id=1, source_target_pairs={{0,8},{4,12},{8,0},{12,4},{16,24},{20,28},{24,16},{28,20},{1,9},{5... | collective-permute-start | bytes 786440 | tf_op jit(solution)/shard_map/ppermute | solution.py:659
  94.8 1.8 %collective-permute-start.18 = (bf16[2,896,128]{2,1,0:T(8,128)(2,1)S(1)}, bf16[2,896,128]{2,1,0:T(8,128)(2,1)S(1)}, u32[]{:S(2)}, u32[]{:S(2)}) collective-permute-start(bf16[2,896,128]{2,1,0:T(8,128)(2,1)S(1)} %get-tuple-element.183), channel_id=1, source_target_pairs={{0,1},{1,0},{2,3},{3,2},{4,5},{5,4},{6,7},{7,6},{8,9},{9,8},{10,11... | collective-permute-start | bytes 1376264 | tf_op jit(solution)/shard_map/ppermute | solution.py:659
  97.2 12.6 %collective-permute-start.21 = (bf16[1088,128]{1,0:T(8,128)(2,1)S(1)}, bf16[1088,128]{1,0:T(8,128)(2,1)S(1)}, u32[]{:S(2)}, u32[]{:S(2)}) collective-permute-start(bf16[1088,128]{1,0:T(8,128)(2,1)S(1)} %get-tuple-element.192), channel_id=1, source_target_pairs={{0,2},{1,3},{2,0},{3,1},{4,6},{5,7},{6,4},{7,5},{8,10},{9,11},{10,... | collective-permute-start | bytes 835592 | tf_op jit(solution)/shard_map/ppermute | solution.py:659
  98.9 8.9 %collective-permute-start.19 = (bf16[512,128]{1,0:T(8,128)(2,1)S(1)}, bf16[512,128]{1,0:T(8,128)(2,1)S(1)}, u32[]{:S(2)}, u32[]{:S(2)}) collective-permute-start(bf16[512,128]{1,0:T(8,128)(2,1)S(1)} %get-tuple-element.178), channel_id=1, source_target_pairs={{0,16},{4,20},{8,24},{12,28},{16,0},{20,4},{24,8},{28,12},{1,17},{... | collective-permute-start | bytes 393224 | tf_op jit(solution)/shard_map/ppermute | solution.py:659
  101.5 8.3 %collective-permute-start.20 = (bf16[704,128]{1,0:T(8,128)(2,1)S(1)}, bf16[704,128]{1,0:T(8,128)(2,1)S(1)}, u32[]{:S(2)}, u32[]{:S(2)}) collective-permute-start(bf16[704,128]{1,0:T(8,128)(2,1)S(1)} %get-tuple-element.191), channel_id=1, source_target_pairs={{0,4},{4,0},{8,12},{12,8},{16,20},{20,16},{24,28},{28,24},{1,5},{5... | collective-permute-start | bytes 540680 | tf_op jit(solution)/shard_map/ppermute | solution.py:659
  101.6 8.3 %collective-permute-start.22 = (bf16[448,128]{1,0:T(8,128)(2,1)S(1)}, bf16[448,128]{1,0:T(8,128)(2,1)S(1)}, u32[]{:S(2)}, u32[]{:S(2)}) collective-permute-start(bf16[448,128]{1,0:T(8,128)(2,1)S(1)} %get-tuple-element.193), channel_id=1, source_target_pairs={{0,6},{1,7},{2,4},{3,5},{4,2},{5,3},{6,0},{7,1},{8,14},{9,15},{10,... | collective-permute-start | bytes 344072 | tf_op jit(solution)/shard_map/ppermute | solution.py:744
  107.8 8.2 %collective-permute-start.23 = (bf16[512,128]{1,0:T(8,128)(2,1)S(1)}, bf16[512,128]{1,0:T(8,128)(2,1)S(1)}, u32[]{:S(2)}, u32[]{:S(2)}) collective-permute-start(bf16[512,128]{1,0:T(8,128)(2,1)S(1)} %last.2), channel_id=1, source_target_pairs={{0,16},{4,20},{8,24},{12,28},{16,0},{20,4},{24,8},{28,12},{1,17},{... | collective-permute-start | bytes 393224 | tf_op jit(solution)/shard_map/ppermute | solution.py:659
  110.5 7.5 %collective-permute-start.24 = (bf16[672,128]{1,0:T(8,128)(2,1)S(1)}, bf16[672,128]{1,0:T(8,128)(2,1)S(1)}, u32[]{:S(2)}, u32[]{:S(2)}) collective-permute-start(bf16[672,128]{1,0:T(8,128)(2,1)S(1)} %get-tuple-element.195), channel_id=1, source_target_pairs={{0,8},{4,12},{8,0},{12,4},{16,24},{20,28},{24,16},{28,20},{1,9},{5... | collective-permute-start | bytes 516104 | tf_op jit(solution)/shard_map/ppermute | solution.py:659
  116.1 9.9 %collective-permute-start.25 = (bf16[1024,128]{1,0:T(8,128)(2,1)S(1)}, bf16[1024,128]{1,0:T(8,128)(2,1)S(1)}, u32[]{:S(2)}, u32[]{:S(2)}) collective-permute-start(bf16[1024,128]{1,0:T(8,128)(2,1)S(1)} %constant_dynamic-update-slice_fusion), channel_id=1, source_target_pairs={{0,8},{4,12},{8,0},{12,4},{16,24},{20,28},{24,16},{28,20},{1,9},{5... | collective-permute-start | bytes 786440 | tf_op jit(solution)/shard_map/ppermute | solution.py:659
  118.6 7.4 %collective-permute-start.26 = (bf16[336,128]{1,0:T(8,128)(2,1)S(1)}, bf16[336,128]{1,0:T(8,128)(2,1)S(1)}, u32[]{:S(2)}, u32[]{:S(2)}) collective-permute-start(bf16[336,128]{1,0:T(8,128)(2,1)S(1)} %get-tuple-element.200), channel_id=1, source_target_pairs={{0,16},{4,20},{8,24},{12,28},{16,0},{20,4},{24,8},{28,12},{1,17},{... | collective-permute-start | bytes 258056 | tf_op jit(solution)/shard_map/ppermute | solution.py:659
  126.1 5.3 %collective-permute-start.27 = (bf16[272,128]{1,0:T(8,128)(2,1)S(1)}, bf16[272,128]{1,0:T(8,128)(2,1)S(1)}, u32[]{:S(2)}, u32[]{:S(2)}) collective-permute-start(bf16[272,128]{1,0:T(8,128)(2,1)S(1)} %get-tuple-element.204), channel_id=1, source_target_pairs={{0,16},{4,20},{8,24},{12,28},{16,0},{20,4},{24,8},{28,12},{1,17},{... | collective-permute-start | bytes 208904 | tf_op jit(solution)/shard_map/ppermute | solution.py:659
  127.2 14.2 %collective-permute-start.29 = (bf16[2048,128]{1,0:T(8,128)(2,1)S(1)}, bf16[2048,128]{1,0:T(8,128)(2,1)S(1)}, u32[]{:S(2)}, u32[]{:S(2)}) collective-permute-start(bf16[2048,128]{1,0:T(8,128)(2,1)S(1)} %constant_dynamic-update-slice_fusion.2), channel_id=1, source_target_pairs={{0,4},{4,0},{8,12},{12,8},{16,20},{20,16},{24,28},{28,24},{1,5},{5... | collective-permute-start | bytes 1572872 | tf_op jit(solution)/shard_map/ppermute | solution.py:659
  131.4 5.1 %collective-permute-start.28 = (bf16[544,128]{1,0:T(8,128)(2,1)S(1)}, bf16[544,128]{1,0:T(8,128)(2,1)S(1)}, u32[]{:S(2)}, u32[]{:S(2)}) collective-permute-start(bf16[544,128]{1,0:T(8,128)(2,1)S(1)} %constant_dynamic-update-slice_fusion.4), channel_id=1, source_target_pairs={{0,8},{4,12},{8,0},{12,4},{16,24},{20,28},{24,16},{28,20},{1,9},{5... | collective-permute-start | bytes 417800 | tf_op jit(solution)/shard_map/ppermute | solution.py:659
  136.5 8.6 %collective-permute-start.30 = (bf16[1088,128]{1,0:T(8,128)(2,1)S(1)}, bf16[1088,128]{1,0:T(8,128)(2,1)S(1)}, u32[]{:S(2)}, u32[]{:S(2)}) collective-permute-start(bf16[1088,128]{1,0:T(8,128)(2,1)S(1)} %constant_dynamic-update-slice_fusion.6), channel_id=1, source_target_pairs={{0,4},{4,0},{8,12},{12,8},{16,20},{20,16},{24,28},{28,24},{1,5},{5... | collective-permute-start | bytes 835592 | tf_op jit(solution)/shard_map/ppermute | solution.py:659
  (7 other events, 64.1 us)

commit v7 on v6

--- a/solution.py
+++ b/solution.py
@@ -379,6 +379,34 @@
     return resident(mid_kernel, "mid", 5, 12, (), (c, dh2, r1, att, wout, vec), outs)
 
 
+def tiles_kernel(packed_ref, tabs, q2_ref, kc_ref, vc_ref):
+    low = lax.broadcasted_iota(jnp.int32, (SPAN, LANE), 1) < HEAD
+
+    def body(i):
+        at = block_rows(i, SPAN)
+        for p in range(PAIRS):
+            cq, ck, cv = (slice(t * D + p * LANE, t * D + (p + 1) * LANE) for t in range(3))
+            n = i * PAIRS + p
+            q = packed_ref[at, cq] * SCALE
+            zero = jnp.zeros_like(q)
+            q2_ref[n, :SPAN] = jnp.where(low, q, zero)
+            q2_ref[n, SPAN:] = jnp.where(low, zero, q)
+            kc_ref[n, :SPAN] = packed_ref[at, ck]
+            kc_ref[n, SPAN:] = tabs[:, cq]
+            vc_ref[n, :SPAN] = packed_ref[at, cv]
+            vc_ref[n, SPAN:] = tabs[:, ck]
+
+    spans = packed_ref.shape[0] // SPAN
+    each_block(spans, body, 1, parts=spans // 2)
+
+
+def tiles(packed, tabs):
+    n = packed.shape[0] // SPAN * PAIRS
+    keys = SPAN + tabs.shape[0]
+    outs = [((n, 2 * SPAN, LANE), BF16)] + [((n, keys, LANE), BF16)] * 2
+    return resident(tiles_kernel, "tiles", 1, 8, (), (packed, tabs), outs)
+
+
 def piece_rows(used, parts):
     return -(-used // (16 * parts)) * 16 * parts
 
@@ -388,7 +416,7 @@
     return [slice(t * D + half * wide, t * D + (half + 1) * wide) for t in range(3)]
 
 
-def back_kernel(sc, x_ref, da_ref, h1_ref, packed_ref, p_ref, tabs, wqkv, vec, nsum_ref, *refs, nf, copies, half, first, last):
+def back_kernel(sc, x_ref, da_ref, h1_ref, q2_ref, kc_ref, vc_ref, p_ref, wqkv, vec, nsum_ref, *refs, nf, copies, half, first, last):
     if half:
         (dub_ref, gvec_ref, before_ref, sums_ref), refs = refs[:4], refs[4:]
     else:
@@ -416,14 +444,11 @@
                 p = half * (PAIRS // 2) + k
                 cq, ck, cv = (slice(t * D + p * LANE, t * D + (p + 1) * LANE) for t in range(3))
                 oq, ok, ov = (slice(t * wide + k * LANE, t * wide + (k + 1) * LANE) for t in range(3))
-                q = packed_ref[at, cq] * SCALE
+                n = (i * (ROWS // SPAN) + s) * PAIRS + p
                 do = da_ref[at, cq]
-                zero = jnp.zeros_like(q)
-                q2 = jnp.concatenate([jnp.where(low, q, zero), jnp.where(low, zero, q)], axis=0)
+                zero = jnp.zeros_like(do)
                 do2 = jnp.concatenate([jnp.where(low, do, zero), jnp.where(low, zero, do)], axis=0)
-                kc = jnp.concatenate([packed_ref[at, ck], tabs[:, cq]], axis=0)
-                vc = jnp.concatenate([packed_ref[at, cv], tabs[:, ck]], axis=0)
-                w = p_ref[(i * (ROWS // SPAN) + s) * PAIRS + p]
+                q2, kc, vc, w = q2_ref[n], kc_ref[n], vc_ref[n], p_ref[n]
                 wf = w.astype(F32)
                 dp = dot_bt(vc, do2)
                 delta = jnp.sum(wf * dp, axis=0, keepdims=True)
@@ -960,6 +985,8 @@
     g, gp, wup = ffn_up(scalars, h2, vec, up)
     dsend, dkeep = down_gradient(scalars, g, c, nf)
     down = gathered(down_weight, after(far_down, dkeep), "fsdp")
+    queries, keys, values = tiles(after(packed, dkeep), tabs)
+    gp = after(gp, queries)
     dh2, dub, usend, ukeep = ffn_down(scalars, h2, c, gp, wup, down)
     bits = ctx_bits()
     near = [("fsdp", 1 << k) for k in range(1, nf.bit_length() - 1)]
@@ -972,7 +999,7 @@
     from_up = Part(scalars, seq, ukeep, usend)
     from_up.step("ctx", bits[0])
     da = seq.next(da)
-    fixed = (x, da, h1, packed, p, tabs, wqkv, vec, nsum)
+    fixed = (x, da, h1, queries, keys, values, p, wqkv, vec, nsum)
     dh1, sums, fsend0, fkeep0, send, keep = back(scalars, fixed, (gout,), 0, nf, nc)
     seq.made(dh1)
     first = Part(scalars, seq, keep, send)

time: 147 us -> 147 us (level)
    pallas_call x23 -> x24, Pallas kernels: 57.4 us -> 57.4 us  [resident(): pl.pallas_call(kernel, in_specs=[pl.BlockSpec(memory_space=pltpu.SMEM)] *...]
where the time goes in v7:
time: 147 us; the launch traced here: 146 us
  Pallas kernels  70.9 us (48%)
  waiting for transfers between devices  42.5 us (29%)
  starting transfers between devices  31.5 us (21%)
    pallas_call x24, Pallas kernels, resident(): pl.pallas_call(kernel, in_specs=[pl.BlockSpec(memory_space=pltpu.SMEM)] *...  57.4 us
    ppermute x30, waiting for transfers between devices, swap(): return lax.ppermute(array, axis, [(k, k ^ bit) for k in range(n)])  33.3 us
    ppermute x30, starting transfers between devices, swap(): return lax.ppermute(array, axis, [(k, k ^ bit) for k in range(n)])  24 us
    all_to_all x1, waiting for transfers between devices, local(): nsum = lax.all_to_all(sums, 'ctx', 0, 0, tiled=True).reshape(nc * spans, D)  7.26 us
    all_to_all x1, starting transfers between devices, local(): nsum = lax.all_to_all(sums, 'ctx', 0, 0, tiled=True).reshape(nc * spans, D)  5.81 us
    pallas_call x1, Pallas kernels, block_output(): pl.pallas_call(mixed_kernel, grid=(rows // ROWS,), in_specs=[pl.BlockSpec...  4.13 us
    pallas_call x2, Pallas kernels, finish(): pl.pallas_call(functools.partial(finish_kernel, heights=heights, plan=pla...  3.78 us
    pallas_call x1, Pallas kernels, first_back(): pl.pallas_call(first_kernel, grid=(rows // ROWS,), in_specs=in_vmem(7), o...  3.44 us
  transfers between devices with their start and end apart: 32, of which 16 were waited for; matrix products, arithmetic and copies ran while one was open for 0% of the time, Pallas kernels for 45%

profile of v7, /device:TPU:0, one launch (start us, length us, event | category | flops | bytes accessed | tf_op | source)
XLA Modules:
  0.0 146.4 jit_solution(18199027191206320642)
XLA Ops:
  0.7 2.1 %pack.1.refs_0_ = bf16[144,2048]{1,0:T(8,128)(2,1)} custom-call(bf16[128,1536]{1,0:T(8,128)(2,1)} %qkv_ref.1, bf16[128,512]{1,0:T(8,128)(2,1)} %out_ref.1, bf16[1,128]{1,0:T(2,128)(2,1)} %bitcast.84, bf16[1,128]{1,0:T(2,128)(2,1)} %bitcast.85, bf16[3,128]{1,0:T(4,128)(2,1)} %bitcast.82, bf16[1,128]{1,0:T(2,128)(2,1)} %bitcast.86, bf16[1,128]{1,0:T(2,128)(2,1)} %bitcast.87, ...), custom_call_target="tpu_custom_call" | custom-call | flops 1000000000 | bytes 1000000 | tf_op jit(solution)/shard_map/pack/pallas_call | solution.py:134
  2.7 3.0 %collective-permute-start.1 = (bf16[144,2048]{1,0:T(8,128)(2,1)}, bf16[144,2048]{1,0:T(8,128)(2,1)S(1)}, u32[]{:S(2)}, u32[]{:S(2)}) collective-permute-start(bf16[144,2048]{1,0:T(8,128)(2,1)} %pack.1.refs_0_), channel_id=1, source_target_pairs={{0,2},{1,3},{2,0},{3,1},{4,6},{5,7},{6,4},{7,5},{8,10},{9,11},{10,... | collective-permute-start | bytes 1769480 | tf_op jit(solution)/shard_map/ppermute | solution.py:684
  5.7 1.4 span_sums.1
  7.1 5.8 %all-to-all-start = ((f32[8,8,512]{2,1,0:T(8,128)}), f32[8,8,512]{2,1,0:T(8,128)S(1)}, u32[]{:S(2)}, u32[]{:S(2)}) async-start(f32[8,8,512]{2,1,0:T(8,128)} %span_sums.1), calls=%async_computation | async-start | bytes 262144 | tf_op jit(solution)/shard_map/all_to_all | solution.py:972
  13.0 7.3 %all-to-all-done = f32[8,8,512]{2,1,0:T(8,128)S(1)} async-done(((f32[8,8,512]{2,1,0:T(8,128)}), f32[8,8,512]{2,1,0:T(8,128)S(1)}, u32[]{:S(2)}, u32[]{:S(2)}) %all-to-all-start) | async-done | bytes 131104 | tf_op jit(solution)/shard_map/all_to_all | solution.py:972
  22.3 8.1 %attend.1 = (bf16[1024,1536]{1,0:T(8,128)(2,1)S(1)}, bf16[32,192,256]{2,1,0:T(8,128)(2,1)S(1)}, bf16[1024,512]{1,0:T(8,128)(2,1)S(1)}, bf16[1024,512]{1,0:T(8,12...) custom-call(s32[76]{0:T(128)S(1)} %concatenate.21.sc.refs_0_, ...), custom_call_target="tpu_custom_call" | custom-call | flops 12000000000 | bytes 12000000 | tf_op jit(solution)/shard_map/attend/pallas_call | solution.py:69
  30.4 4.5 %collective-permute-done.4.refs_2_ = bf16[128,2048]{1,0:T(8,128)(2,1)S(1)} collective-permute-done((bf16[128,2048]{1,0:T(8,128)(2,1)}, bf16[128,2048]{1,0:T(8,128)(2,1)S(1)}, u32[]{:S(2)}, u32[]{:S(2)}) %collective-permute-start.4) | collective-permute-done | bytes 524320 | tf_op jit(solution)/shard_map/ppermute | solution.py:684
  37.0 6.7 %ffn_up.1 = (bf16[1024,2048]{1,0:T(8,128)(2,1)S(1)}, bf16[1024,2048]{1,0:T(8,128)(2,1)S(1)}, bf16[512,2048]{1,0:T(8,128)(2,1)S(1)}) custom-call(s32[76]{0:T(128)S(1)} %concatenate.21.sc.refs_0_, bf16[1024,512]{1,0:T(8,128)(2,1)S(1)} %get-tuple-element.129.h2_ref, f32[8,2048]{1,0:T(8,128)S(1)} %get-tuple-element.127.vec.vec_ref.refs_9_, ...), custom_call_target="tpu_custom_call" | custom-call | flops 8000000000 | bytes 8000000 | tf_op jit(solution)/shard_map/ffn_up/pallas_call | solution.py:69
  43.7 2.9 %down_grad.1 = (bf16[2,2048,128]{2,1,0:T(8,128)(2,1)S(1)}, bf16[2,2048,128]{2,1,0:T(8,128)(2,1)S(1)}) custom-call(s32[76]{0:T(128)S(1)} %concatenate.21.sc.refs_0_, bf16[1024,2048]{1,0:T(8,128)(2,1)S(1)} %get-tuple-element.134.g_ref, bf16[1024,512]{1,0:T(8,128)(2,1)S(1)} %bitcast.49), custom_call_target="tpu_custom_call" | custom-call | flops 4000000000 | bytes 4000000 | tf_op jit(solution)/shard_map/down_grad/pallas_call | solution.py:69
  46.6 2.6 %collective-permute-done.7.refs_2_ = bf16[512,512]{1,0:T(8,128)(2,1)S(1)} collective-permute-done((bf16[512,512]{1,0:T(8,128)(2,1)S(1)}, bf16[512,512]{1,0:T(8,128)(2,1)S(1)}, u32[]{:S(2)}, u32[]{:S(2)}) %collective-permute-start.7) | collective-permute-done | bytes 524320 | tf_op jit(solution)/shard_map/ppermute | solution.py:684
  51.2 7.7 %ffn_down.1 = (f32[1024,512]{1,0:T(8,128)S(1)}, f32[1,2048]{1,0:T(1,128)S(1)}, bf16[2,2048,128]{2,1,0:T(8,128)(2,1)S(1)}, bf16[2,2048,128]{2,1,0:T(8,128)(2,1)S(1)}) custom-call(s32[76]{0:T(128)S(1)} %concatenate.21.sc.refs_0_, bf16[1024,512]{1,0:T(8,128)(2,1)S(1)} %get-tuple-element.129.h2_ref, bf16[1024,512]{1,0:T(8,128)(2,1)S(1)} %bitcast.50, ...), custom_call_target="tpu_custom_call" | custom-call | flops 8000000000 | bytes 8000000 | tf_op jit(solution)/shard_map/ffn_down/pallas_call | solution.py:69
  60.6 2.5 %mid.1 = (f32[1024,512]{1,0:T(8,128)S(1)}, bf16[1024,512]{1,0:T(8,128)(2,1)S(1)}, f32[512,512]{1,0:T(8,128)S(1)}, f32[8,512]{1,0:T(8,128)S(1)}) custom-call(bf16[1024,512]{1,0:T(8,128)(2,1)S(1)} %bitcast.51, f32[1024,512]{1,0:T(8,128)S(1)} %get-tuple-element.147.dh2_ref, f32[1024,512]{1,0:T(8,128)S(1)} %get-tuple-element.206.r1_ref, ...), custom_call_target="tpu_custom_call" | custom-call | flops 5000000000 | bytes 5000000 | tf_op jit(solution)/shard_map/mid/pallas_call | solution.py:69
  64.0 1.5 %collective-permute-start.12 = (bf16[2,1024,128]{2,1,0:T(8,128)(2,1)S(1)}, bf16[2,1024,128]{2,1,0:T(8,128)(2,1)S(1)}, u32[]{:S(2)}, u32[]{:S(2)}) collective-permute-start(bf16[2,1024,128]{2,1,0:T(8,128)(2,1)S(1)} %get-tuple-element.153), channel_id=1, source_target_pairs={{0,4},{4,0},{8,12},{12,8},{16,20},{20,16},{24,28},{28,24},{1,5},{5... | collective-permute-start | bytes 1572872 | tf_op jit(solution)/shard_map/ppermute | solution.py:684
  65.5 8.8 %back_0.1 = (f32[1024,512]{1,0:T(8,128)S(1)}, f32[72,512]{1,0:T(8,128)S(1)}, bf16[128,128]{1,0:T(8,128)(2,1)S(1)}, bf16[128,128]{1,0:T(8,128)(2,1)S(1)}, bf16[2,...) custom-call(s32[76]{0:T(128)S(1)} %concatenate.21.sc.refs_0_, bf16[1024,512]{1,0:T(8,128)(2,1)S(1)} %bitcast.55, ...), custom_call_target="tpu_custom_call" | custom-call | flops 8999999488 | bytes 9000000 | tf_op jit(solution)/shard_map/back_0/pallas_call | solution.py:69
  75.6 2.8 %collective-permute-done.12 = bf16[2,1024,128]{2,1,0:T(8,128)(2,1)S(1)} collective-permute-done((bf16[2,1024,128]{2,1,0:T(8,128)(2,1)S(1)}, bf16[2,1024,128]{2,1,0:T(8,128)(2,1)S(1)}, u32[]{:S(2)}, u32[]{:S(2)}) %collective-permute-start.12) | collective-permute-done | bytes 524320 | tf_op jit(solution)/shard_map/ppermute | solution.py:684
  79.1 1.8 %collective-permute-start.15 = (bf16[1,1024,128]{2,1,0:T(8,128)(2,1)S(1)}, bf16[1,1024,128]{2,1,0:T(8,128)(2,1)S(1)}, u32[]{:S(2)}, u32[]{:S(2)}) collective-permute-start(bf16[1,1024,128]{2,1,0:T(8,128)(2,1)S(1)} %get-tuple-element.169), channel_id=1, source_target_pairs={{0,2},{1,3},{2,0},{3,1},{4,6},{5,7},{6,4},{7,5},{8,10},{9,11},{10,... | collective-permute-start | bytes 786440 | tf_op jit(solution)/shard_map/ppermute | solution.py:684
  80.9 4.3 %back_1.2 = (f32[512,512]{1,0:T(8,128)S(1)}, f32[512,768]{1,0:T(8,128)S(1)}, f32[64,512]{1,0:T(8,128)S(1)}, f32[16,1536]{1,0:T(8,128)S(1)}) custom-call(s32[76]{0:T(128)S(1)} %concatenate.21.sc.refs_0_, bf16[1024,512]{1,0:T(8,128)(2,1)S(1)} %bitcast.56, bf16[1024,512]{1,0:T(8,128)(2,1)S(1)} %get-tuple-element.154.refs_2_, ...), custom_call_target="tpu_custom_call" | custom-call | flops 8999999488 | bytes 9000000 | tf_op jit(solution)/shard_map/back_1/pallas_call | solution.py:69
  87.0 1.7 %collective-permute-start.16 = (bf16[1024,128]{1,0:T(8,128)(2,1)S(1)}, bf16[1024,128]{1,0:T(8,128)(2,1)S(1)}, u32[]{:S(2)}, u32[]{:S(2)}) collective-permute-start(bf16[1024,128]{1,0:T(8,128)(2,1)S(1)} %bitcast.67), channel_id=1, source_target_pairs={{0,8},{4,12},{8,0},{12,4},{16,24},{20,28},{24,16},{28,20},{1,9},{5... | collective-permute-start | bytes 786440 | tf_op jit(solution)/shard_map/ppermute | solution.py:684
  88.7 5.4 %back_1.3 = (f32[512,512]{1,0:T(8,128)S(1)}, f32[72,512]{1,0:T(8,128)}, bf16[128,128]{1,0:T(8,128)(2,1)S(1)}, bf16[128,128]{1,0:T(8,128)(2,1)S(1)}, bf16[2,896,1...) custom-call(s32[76]{0:T(128)S(1)} %concatenate.21.sc.refs_0_, bf16[1024,512]{1,0:T(8,128)(2,1)S(1)} %bitcast.57, ...), custom_call_target="tpu_custom_call" | custom-call | flops 8999999488 | bytes 9000000 | tf_op jit(solution)/shard_map/back_1/pallas_call | solution.py:69
  96.6 1.8 %collective-permute-start.21 = (bf16[1088,128]{1,0:T(8,128)(2,1)S(1)}, bf16[1088,128]{1,0:T(8,128)(2,1)S(1)}, u32[]{:S(2)}, u32[]{:S(2)}) collective-permute-start(bf16[1088,128]{1,0:T(8,128)(2,1)S(1)} %get-tuple-element.202), channel_id=1, source_target_pairs={{0,2},{1,3},{2,0},{3,1},{4,6},{5,7},{6,4},{7,5},{8,10},{9,11},{10,... | collective-permute-start | bytes 835592 | tf_op jit(solution)/shard_map/ppermute | solution.py:684
  98.4 2.6 %collective-permute-start.19 = (bf16[512,128]{1,0:T(8,128)(2,1)S(1)}, bf16[512,128]{1,0:T(8,128)(2,1)S(1)}, u32[]{:S(2)}, u32[]{:S(2)}) collective-permute-start(bf16[512,128]{1,0:T(8,128)(2,1)S(1)} %get-tuple-element.188), channel_id=1, source_target_pairs={{0,16},{4,20},{8,24},{12,28},{16,0},{20,4},{24,8},{28,12},{1,17},{... | collective-permute-start | bytes 393224 | tf_op jit(solution)/shard_map/ppermute | solution.py:684
  101.1 1.7 %collective-permute-start.22 = (bf16[448,128]{1,0:T(8,128)(2,1)S(1)}, bf16[448,128]{1,0:T(8,128)(2,1)S(1)}, u32[]{:S(2)}, u32[]{:S(2)}) collective-permute-start(bf16[448,128]{1,0:T(8,128)(2,1)S(1)} %get-tuple-element.203), channel_id=1, source_target_pairs={{0,6},{1,7},{2,4},{3,5},{4,2},{5,3},{6,0},{7,1},{8,14},{9,15},{10,... | collective-permute-start | bytes 344072 | tf_op jit(solution)/shard_map/ppermute | solution.py:769
  102.7 4.5 %collective-permute-done.19.got_ref = bf16[512,128]{1,0:T(8,128)(2,1)S(1)} collective-permute-done((bf16[512,128]{1,0:T(8,128)(2,1)S(1)}, bf16[512,128]{1,0:T(8,128)(2,1)S(1)}, u32[]{:S(2)}, u32[]{:S(2)}) %collective-permute-start.19) | collective-permute-done | bytes 131104 | tf_op jit(solution)/shard_map/ppermute | solution.py:684
  107.3 1.9 %collective-permute-done.22.refs_3_ = bf16[448,128]{1,0:T(8,128)(2,1)S(1)} collective-permute-done((bf16[448,128]{1,0:T(8,128)(2,1)S(1)}, bf16[448,128]{1,0:T(8,128)(2,1)S(1)}, u32[]{:S(2)}, u32[]{:S(2)}) %collective-permute-start.22) | collective-permute-done | bytes 114720 | tf_op jit(solution)/shard_map/ppermute | solution.py:769
  111.2 4.1 %block_output.1 = bf16[1024,512]{1,0:T(8,128)(2,1)} custom-call(s32[76]{0:T(128)S(1)} %concatenate.21.sc.refs_0_, f32[1024,512]{1,0:T(8,128)S(1)} %get-tuple-element.206.r1_ref, bf16[1024,2048]{1,0:T(8,128)(2,1)S(1)} %get-tuple-element.134.g_ref, f32[8,2048]{1,0:T(8,128)S(1)} %get-tuple-element.127.vec.vec_ref.refs_9_, bf16[512,512]{1,0:T(8,128)(2,1)S(1)} %copy-done.5, ...), custom_call_target="tpu_custom_call" | custom-call | flops 4000000000 | bytes 4000000 | tf_op jit(solution)/shard_map/block_output/pallas_call | solution.py:670
  119.1 6.3 %collective-permute-done.25 = bf16[1024,128]{1,0:T(8,128)(2,1)S(1)} collective-permute-done((bf16[1024,128]{1,0:T(8,128)(2,1)S(1)}, bf16[1024,128]{1,0:T(8,128)(2,1)S(1)}, u32[]{:S(2)}, u32[]{:S(2)}) %collective-permute-start.25) | collective-permute-done | bytes 262176 | tf_op jit(solution)/shard_map/ppermute | solution.py:684
  126.7 4.0 %collective-permute-done.27 = bf16[272,128]{1,0:T(8,128)(2,1)S(1)} collective-permute-done((bf16[272,128]{1,0:T(8,128)(2,1)S(1)}, bf16[272,128]{1,0:T(8,128)(2,1)S(1)}, u32[]{:S(2)}, u32[]{:S(2)}) %collective-permute-start.27) | collective-permute-done | bytes 69664 | tf_op jit(solution)/shard_map/ppermute | solution.py:684
  132.1 3.4 %first_back.1 = f32[1024,512]{1,0:T(8,128)} custom-call(bf16[1024,512]{1,0:T(8,128)(2,1)S(1)} %bitcast.58, f32[1024,512]{1,0:T(8,128)S(1)} %get-tuple-element.216.dr1_ref, f32[512,512]{1,0:T(8,128)S(1)} %get-tuple-element.217.upper_ref, f32[512,512]{1,0:T(8,128)S(1)} %get-tuple-element.185.lower_ref, bf16[64,128]{1,0:T(8,128)(2,1)S(1)} %get-tuple-element.218.own_ref, ...), custom_call_target="tpu_custom_call" | custom-call | flops 3000000000 | bytes 3000000 | tf_op jit(solution)/shard_map/first_back/pallas_call | solution.py:644
  137.2 3.7 %collective-permute-done.29 = bf16[2048,128]{1,0:T(8,128)(2,1)S(1)} collective-permute-done((bf16[2048,128]{1,0:T(8,128)(2,1)S(1)}, bf16[2048,128]{1,0:T(8,128)(2,1)S(1)}, u32[]{:S(2)}, u32[]{:S(2)}) %collective-permute-start.29) | collective-permute-done | bytes 524320 | tf_op jit(solution)/shard_map/ppermute | solution.py:684
  141.0 2.1 %finish.2 = (f32[512,512]{1,0:T(8,128)}, f32[128,2048]{1,0:T(8,128)}) custom-call(s32[76]{0:T(128)S(1)} %concatenate.21.sc.refs_0_, bf16[8,512,128]{2,1,0:T(8,128)(2,1)S(1)} %bitcast.42), custom_call_target="tpu_custom_call" | custom-call | flops 2000000000 | bytes 2000000 | tf_op jit(solution)/shard_map/finish/pallas_call | solution.py:937
  143.1 1.4 collective-permute-done.30
  144.6 1.6 %finish.3 = (f32[128,1536]{1,0:T(8,128)}, f32[128,512]{1,0:T(8,128)}, f32[128]{0:T(128)}, f32[128]{0:T(128)}, f32[384]{0:T(512)}, /*index=5*/f32[128]{0:T(128)},...) custom-call(s32[76]{0:T(128)S(1)} %concatenate.21.sc.refs_0_, bf16[8,272,128]{2,1,0:T(8,128)(2,1)S(1)} %bitcast.43), custom_call_target="tpu_custom_call" | custom-call | flops 2000000000 | bytes 2000000 | tf_op jit(solution)/shard_map/finish/pallas_call | solution.py:937
  (90 shorter events, 25.1 us)
Async XLA Ops:
  2.7 17.5 %collective-permute-start.1 = (bf16[144,2048]{1,0:T(8,128)(2,1)}, bf16[144,2048]{1,0:T(8,128)(2,1)S(1)}, u32[]{:S(2)}, u32[]{:S(2)}) collective-permute-start(bf16[144,2048]{1,0:T(8,128)(2,1)} %pack.1.refs_0_), channel_id=1, source_target_pairs={{0,2},{1,3},{2,0},{3,1},{4,6},{5,7},{6,4},{7,5},{8,10},{9,11},{10,... | collective-permute-start | bytes 1769480 | tf_op jit(solution)/shard_map/ppermute | solution.py:684
  7.1 13.1 %all-to-all-start = ((f32[8,8,512]{2,1,0:T(8,128)}), f32[8,8,512]{2,1,0:T(8,128)S(1)}, u32[]{:S(2)}, u32[]{:S(2)}) async-start(f32[8,8,512]{2,1,0:T(8,128)} %span_sums.1), calls=%async_computation | async-start | bytes 262144 | tf_op jit(solution)/shard_map/all_to_all | solution.py:972
  12.9 8.4 %collective-permute-start = (bf16[144,2048]{1,0:T(8,128)(2,1)S(1)}, bf16[144,2048]{1,0:T(8,128)(2,1)S(1)}, u32[]{:S(2)}, u32[]{:S(2)}) collective-permute-start(bf16[144,2048]{1,0:T(8,128)(2,1)S(1)} %copy-done.3), channel_id=1, source_target_pairs={{0,1},{1,0},{2,3},{3,2},{4,5},{5,4},{6,7},{7,6},{8,9},{9,8},{10,11... | collective-permute-start | bytes 1769480 | tf_op jit(solution)/shard_map/ppermute | solution.py:684
  20.3 2.0 %collective-permute-start.2 = (bf16[144,2048]{1,0:T(8,128)(2,1)S(1)}, bf16[144,2048]{1,0:T(8,128)(2,1)S(1)}, u32[]{:S(2)}, u32[]{:S(2)}) collective-permute-start(bf16[144,2048]{1,0:T(8,128)(2,1)S(1)} %collective-permute-done.1.refs_2_), channel_id=1, source_target_pairs={{0,1},{1,0},{2,3},{3,2},{4,5},{5,4},{6,7},{7,6},{8,9},{9,8},{10,11... | collective-permute-start | bytes 1769480 | tf_op jit(solution)/shard_map/ppermute | solution.py:684
  20.4 14.6 %collective-permute-start.4 = (bf16[128,2048]{1,0:T(8,128)(2,1)}, bf16[128,2048]{1,0:T(8,128)(2,1)S(1)}, u32[]{:S(2)}, u32[]{:S(2)}) collective-permute-start(bf16[128,2048]{1,0:T(8,128)(2,1)} %refs_0_), channel_id=1, source_target_pairs={{0,2},{1,3},{2,0},{3,1},{4,6},{5,7},{6,4},{7,5},{8,10},{9,11},{10,... | collective-permute-start | bytes 1572872 | tf_op jit(solution)/shard_map/ppermute | solution.py:684
  21.1 15.9 %collective-permute-start.3 = (bf16[128,2048]{1,0:T(8,128)(2,1)}, bf16[128,2048]{1,0:T(8,128)(2,1)S(1)}, u32[]{:S(2)}, u32[]{:S(2)}) collective-permute-start(bf16[128,2048]{1,0:T(8,128)(2,1)} %refs_0_), channel_id=1, source_target_pairs={{0,1},{1,0},{2,3},{3,2},{4,5},{5,4},{6,7},{7,6},{8,9},{9,8},{10,11... | collective-permute-start | bytes 1572872 | tf_op jit(solution)/shard_map/ppermute | solution.py:684
  34.9 2.1 %collective-permute-start.5 = (bf16[128,2048]{1,0:T(8,128)(2,1)S(1)}, bf16[128,2048]{1,0:T(8,128)(2,1)S(1)}, u32[]{:S(2)}, u32[]{:S(2)}) collective-permute-start(bf16[128,2048]{1,0:T(8,128)(2,1)S(1)} %collective-permute-done.4.refs_2_), channel_id=1, source_target_pairs={{0,1},{1,0},{2,3},{3,2},{4,5},{5,4},{6,7},{7,6},{8,9},{9,8},{10,11... | collective-permute-start | bytes 1572872 | tf_op jit(solution)/shard_map/ppermute | solution.py:684
  34.9 14.3 %collective-permute-start.7 = (bf16[512,512]{1,0:T(8,128)(2,1)S(1)}, bf16[512,512]{1,0:T(8,128)(2,1)S(1)}, u32[]{:S(2)}, u32[]{:S(2)}) collective-permute-start(bf16[512,512]{1,0:T(8,128)(2,1)S(1)} %copy-done.5), channel_id=1, source_target_pairs={{0,2},{1,3},{2,0},{3,1},{4,6},{5,7},{6,4},{7,5},{8,10},{9,11},{10,... | collective-permute-start | bytes 1572872 | tf_op jit(solution)/shard_map/ppermute | solution.py:684
  35.6 15.3 %collective-permute-start.6 = (bf16[512,512]{1,0:T(8,128)(2,1)S(1)}, bf16[512,512]{1,0:T(8,128)(2,1)S(1)}, u32[]{:S(2)}, u32[]{:S(2)}) collective-permute-start(bf16[512,512]{1,0:T(8,128)(2,1)S(1)} %copy-done.5), channel_id=1, source_target_pairs={{0,1},{1,0},{2,3},{3,2},{4,5},{5,4},{6,7},{7,6},{8,9},{9,8},{10,11... | collective-permute-start | bytes 1572872 | tf_op jit(solution)/shard_map/ppermute | solution.py:684
  49.2 1.9 %collective-permute-start.8 = (bf16[512,512]{1,0:T(8,128)(2,1)S(1)}, bf16[512,512]{1,0:T(8,128)(2,1)S(1)}, u32[]{:S(2)}, u32[]{:S(2)}) collective-permute-start(bf16[512,512]{1,0:T(8,128)(2,1)S(1)} %collective-permute-done.7.refs_2_), channel_id=1, source_target_pairs={{0,1},{1,0},{2,3},{3,2},{4,5},{5,4},{6,7},{7,6},{8,9},{9,8},{10,11... | collective-permute-start | bytes 1572872 | tf_op jit(solution)/shard_map/ppermute | solution.py:684
  49.2 9.8 %collective-permute-start.9 = (bf16[2,2048,128]{2,1,0:T(8,128)(2,1)S(1)}, bf16[2,2048,128]{2,1,0:T(8,128)(2,1)S(1)}, u32[]{:S(2)}, u32[]{:S(2)}) collective-permute-start(bf16[2,2048,128]{2,1,0:T(8,128)(2,1)S(1)} %get-tuple-element.144), channel_id=1, source_target_pairs={{0,1},{1,0},{2,3},{3,2},{4,5},{5,4},{6,7},{7,6},{8,9},{9,8},{10,11... | collective-permute-start | bytes 3145736 | tf_op jit(solution)/shard_map/ppermute | solution.py:684
  58.8 4.3 %collective-permute-start.10 = (bf16[2,2048,128]{2,1,0:T(8,128)(2,1)S(1)}, bf16[2,2048,128]{2,1,0:T(8,128)(2,1)S(1)}, u32[]{:S(2)}, u32[]{:S(2)}) collective-permute-start(bf16[2,2048,128]{2,1,0:T(8,128)(2,1)S(1)} %get-tuple-element.151), channel_id=1, source_target_pairs={{0,1},{1,0},{2,3},{3,2},{4,5},{5,4},{6,7},{7,6},{8,9},{9,8},{10,11... | collective-permute-start | bytes 3145736 | tf_op jit(solution)/shard_map/ppermute | solution.py:684
  59.8 14.4 %collective-permute-start.11 = (bf16[1,2048,128]{2,1,0:T(8,128)(2,1)S(1)}, bf16[1,2048,128]{2,1,0:T(8,128)(2,1)S(1)}, u32[]{:S(2)}, u32[]{:S(2)}) collective-permute-start(bf16[1,2048,128]{2,1,0:T(8,128)(2,1)S(1)} %get-tuple-element.146), channel_id=1, source_target_pairs={{0,2},{1,3},{2,0},{3,1},{4,6},{5,7},{6,4},{7,5},{8,10},{9,11},{10,... | collective-permute-start | bytes 1572872 | tf_op jit(solution)/shard_map/ppermute | solution.py:684
  64.0 14.4 %collective-permute-start.12 = (bf16[2,1024,128]{2,1,0:T(8,128)(2,1)S(1)}, bf16[2,1024,128]{2,1,0:T(8,128)(2,1)S(1)}, u32[]{:S(2)}, u32[]{:S(2)}) collective-permute-start(bf16[2,1024,128]{2,1,0:T(8,128)(2,1)S(1)} %get-tuple-element.153), channel_id=1, source_target_pairs={{0,4},{4,0},{8,12},{12,8},{16,20},{20,16},{24,28},{28,24},{1,5},{5... | collective-permute-start | bytes 1572872 | tf_op jit(solution)/shard_map/ppermute | solution.py:684
  75.0 11.3 %collective-permute-start.14 = (bf16[1,1024,128]{2,1,0:T(8,128)(2,1)S(1)}, bf16[1,1024,128]{2,1,0:T(8,128)(2,1)S(1)}, u32[]{:S(2)}, u32[]{:S(2)}) collective-permute-start(bf16[1,1024,128]{2,1,0:T(8,128)(2,1)S(1)} %get-tuple-element.166), channel_id=1, source_target_pairs={{0,4},{4,0},{8,12},{12,8},{16,20},{20,16},{24,28},{28,24},{1,5},{5... | collective-permute-start | bytes 786440 | tf_op jit(solution)/shard_map/ppermute | solution.py:684
  75.6 9.6 %collective-permute-start.13 = (bf16[2,1280,128]{2,1,0:T(8,128)(2,1)S(1)}, bf16[2,1280,128]{2,1,0:T(8,128)(2,1)S(1)}, u32[]{:S(2)}, u32[]{:S(2)}) collective-permute-start(bf16[2,1280,128]{2,1,0:T(8,128)(2,1)S(1)} %get-tuple-element.175), channel_id=1, source_target_pairs={{0,1},{1,0},{2,3},{3,2},{4,5},{5,4},{6,7},{7,6},{8,9},{9,8},{10,11... | collective-permute-start | bytes 1966088 | tf_op jit(solution)/shard_map/ppermute | solution.py:684
  79.1 7.2 %collective-permute-start.15 = (bf16[1,1024,128]{2,1,0:T(8,128)(2,1)S(1)}, bf16[1,1024,128]{2,1,0:T(8,128)(2,1)S(1)}, u32[]{:S(2)}, u32[]{:S(2)}) collective-permute-start(bf16[1,1024,128]{2,1,0:T(8,128)(2,1)S(1)} %get-tuple-element.169), channel_id=1, source_target_pairs={{0,2},{1,3},{2,0},{3,1},{4,6},{5,7},{6,4},{7,5},{8,10},{9,11},{10,... | collective-permute-start | bytes 786440 | tf_op jit(solution)/shard_map/ppermute | solution.py:684
  85.9 8.9 %collective-permute-start.17 = (bf16[2,640,128]{2,1,0:T(8,128)(2,1)S(1)}, bf16[2,640,128]{2,1,0:T(8,128)(2,1)S(1)}, u32[]{:S(2)}, u32[]{:S(2)}) collective-permute-start(bf16[2,640,128]{2,1,0:T(8,128)(2,1)S(1)} %get-tuple-element.177), channel_id=1, source_target_pairs={{0,4},{4,0},{8,12},{12,8},{16,20},{20,16},{24,28},{28,24},{1,5},{5... | collective-permute-start | bytes 983048 | tf_op jit(solution)/shard_map/ppermute | solution.py:684
  87.0 7.1 %collective-permute-start.16 = (bf16[1024,128]{1,0:T(8,128)(2,1)S(1)}, bf16[1024,128]{1,0:T(8,128)(2,1)S(1)}, u32[]{:S(2)}, u32[]{:S(2)}) collective-permute-start(bf16[1024,128]{1,0:T(8,128)(2,1)S(1)} %bitcast.67), channel_id=1, source_target_pairs={{0,8},{4,12},{8,0},{12,4},{16,24},{20,28},{24,16},{28,20},{1,9},{5... | collective-permute-start | bytes 786440 | tf_op jit(solution)/shard_map/ppermute | solution.py:684
  94.1 1.8 %collective-permute-start.18 = (bf16[2,896,128]{2,1,0:T(8,128)(2,1)S(1)}, bf16[2,896,128]{2,1,0:T(8,128)(2,1)S(1)}, u32[]{:S(2)}, u32[]{:S(2)}) collective-permute-start(bf16[2,896,128]{2,1,0:T(8,128)(2,1)S(1)} %get-tuple-element.193), channel_id=1, source_target_pairs={{0,1},{1,0},{2,3},{3,2},{4,5},{5,4},{6,7},{7,6},{8,9},{9,8},{10,11... | collective-permute-start | bytes 1376264 | tf_op jit(solution)/shard_map/ppermute | solution.py:684
  96.6 12.7 %collective-permute-start.21 = (bf16[1088,128]{1,0:T(8,128)(2,1)S(1)}, bf16[1088,128]{1,0:T(8,128)(2,1)S(1)}, u32[]{:S(2)}, u32[]{:S(2)}) collective-permute-start(bf16[1088,128]{1,0:T(8,128)(2,1)S(1)} %get-tuple-element.202), channel_id=1, source_target_pairs={{0,2},{1,3},{2,0},{3,1},{4,6},{5,7},{6,4},{7,5},{8,10},{9,11},{10,... | collective-permute-start | bytes 835592 | tf_op jit(solution)/shard_map/ppermute | solution.py:684
  98.4 8.9 %collective-permute-start.19 = (bf16[512,128]{1,0:T(8,128)(2,1)S(1)}, bf16[512,128]{1,0:T(8,128)(2,1)S(1)}, u32[]{:S(2)}, u32[]{:S(2)}) collective-permute-start(bf16[512,128]{1,0:T(8,128)(2,1)S(1)} %get-tuple-element.188), channel_id=1, source_target_pairs={{0,16},{4,20},{8,24},{12,28},{16,0},{20,4},{24,8},{28,12},{1,17},{... | collective-permute-start | bytes 393224 | tf_op jit(solution)/shard_map/ppermute | solution.py:684
  100.9 8.3 %collective-permute-start.20 = (bf16[704,128]{1,0:T(8,128)(2,1)S(1)}, bf16[704,128]{1,0:T(8,128)(2,1)S(1)}, u32[]{:S(2)}, u32[]{:S(2)}) collective-permute-start(bf16[704,128]{1,0:T(8,128)(2,1)S(1)} %get-tuple-element.201), channel_id=1, source_target_pairs={{0,4},{4,0},{8,12},{12,8},{16,20},{20,16},{24,28},{28,24},{1,5},{5... | collective-permute-start | bytes 540680 | tf_op jit(solution)/shard_map/ppermute | solution.py:684
  101.1 8.2 %collective-permute-start.22 = (bf16[448,128]{1,0:T(8,128)(2,1)S(1)}, bf16[448,128]{1,0:T(8,128)(2,1)S(1)}, u32[]{:S(2)}, u32[]{:S(2)}) collective-permute-start(bf16[448,128]{1,0:T(8,128)(2,1)S(1)} %get-tuple-element.203), channel_id=1, source_target_pairs={{0,6},{1,7},{2,4},{3,5},{4,2},{5,3},{6,0},{7,1},{8,14},{9,15},{10,... | collective-permute-start | bytes 344072 | tf_op jit(solution)/shard_map/ppermute | solution.py:769
  107.2 8.2 %collective-permute-start.23 = (bf16[512,128]{1,0:T(8,128)(2,1)S(1)}, bf16[512,128]{1,0:T(8,128)(2,1)S(1)}, u32[]{:S(2)}, u32[]{:S(2)}) collective-permute-start(bf16[512,128]{1,0:T(8,128)(2,1)S(1)} %last.2), channel_id=1, source_target_pairs={{0,16},{4,20},{8,24},{12,28},{16,0},{20,4},{24,8},{28,12},{1,17},{... | collective-permute-start | bytes 393224 | tf_op jit(solution)/shard_map/ppermute | solution.py:684
  109.9 7.6 %collective-permute-start.24 = (bf16[672,128]{1,0:T(8,128)(2,1)S(1)}, bf16[672,128]{1,0:T(8,128)(2,1)S(1)}, u32[]{:S(2)}, u32[]{:S(2)}) collective-permute-start(bf16[672,128]{1,0:T(8,128)(2,1)S(1)} %get-tuple-element.205), channel_id=1, source_target_pairs={{0,8},{4,12},{8,0},{12,4},{16,24},{20,28},{24,16},{28,20},{1,9},{5... | collective-permute-start | bytes 516104 | tf_op jit(solution)/shard_map/ppermute | solution.py:684
  115.5 9.9 %collective-permute-start.25 = (bf16[1024,128]{1,0:T(8,128)(2,1)S(1)}, bf16[1024,128]{1,0:T(8,128)(2,1)S(1)}, u32[]{:S(2)}, u32[]{:S(2)}) collective-permute-start(bf16[1024,128]{1,0:T(8,128)(2,1)S(1)} %constant_dynamic-update-slice_fusion), channel_id=1, source_target_pairs={{0,8},{4,12},{8,0},{12,4},{16,24},{20,28},{24,16},{28,20},{1,9},{5... | collective-permute-start | bytes 786440 | tf_op jit(solution)/shard_map/ppermute | solution.py:684
  118.1 7.4 %collective-permute-start.26 = (bf16[336,128]{1,0:T(8,128)(2,1)S(1)}, bf16[336,128]{1,0:T(8,128)(2,1)S(1)}, u32[]{:S(2)}, u32[]{:S(2)}) collective-permute-start(bf16[336,128]{1,0:T(8,128)(2,1)S(1)} %get-tuple-element.210), channel_id=1, source_target_pairs={{0,16},{4,20},{8,24},{12,28},{16,0},{20,4},{24,8},{28,12},{1,17},{... | collective-permute-start | bytes 258056 | tf_op jit(solution)/shard_map/ppermute | solution.py:684
  125.5 5.3 %collective-permute-start.27 = (bf16[272,128]{1,0:T(8,128)(2,1)S(1)}, bf16[272,128]{1,0:T(8,128)(2,1)S(1)}, u32[]{:S(2)}, u32[]{:S(2)}) collective-permute-start(bf16[272,128]{1,0:T(8,128)(2,1)S(1)} %get-tuple-element.214), channel_id=1, source_target_pairs={{0,16},{4,20},{8,24},{12,28},{16,0},{20,4},{24,8},{28,12},{1,17},{... | collective-permute-start | bytes 208904 | tf_op jit(solution)/shard_map/ppermute | solution.py:684
  126.7 14.2 %collective-permute-start.29 = (bf16[2048,128]{1,0:T(8,128)(2,1)S(1)}, bf16[2048,128]{1,0:T(8,128)(2,1)S(1)}, u32[]{:S(2)}, u32[]{:S(2)}) collective-permute-start(bf16[2048,128]{1,0:T(8,128)(2,1)S(1)} %constant_dynamic-update-slice_fusion.2), channel_id=1, source_target_pairs={{0,4},{4,0},{8,12},{12,8},{16,20},{20,16},{24,28},{28,24},{1,5},{5... | collective-permute-start | bytes 1572872 | tf_op jit(solution)/shard_map/ppermute | solution.py:684
  130.8 5.1 %collective-permute-start.28 = (bf16[544,128]{1,0:T(8,128)(2,1)S(1)}, bf16[544,128]{1,0:T(8,128)(2,1)S(1)}, u32[]{:S(2)}, u32[]{:S(2)}) collective-permute-start(bf16[544,128]{1,0:T(8,128)(2,1)S(1)} %constant_dynamic-update-slice_fusion.4), channel_id=1, source_target_pairs={{0,8},{4,12},{8,0},{12,4},{16,24},{20,28},{24,16},{28,20},{1,9},{5... | collective-permute-start | bytes 417800 | tf_op jit(solution)/shard_map/ppermute | solution.py:684
  135.9 8.6 %collective-permute-start.30 = (bf16[1088,128]{1,0:T(8,128)(2,1)S(1)}, bf16[1088,128]{1,0:T(8,128)(2,1)S(1)}, u32[]{:S(2)}, u32[]{:S(2)}) collective-permute-start(bf16[1088,128]{1,0:T(8,128)(2,1)S(1)} %constant_dynamic-update-slice_fusion.6), channel_id=1, source_target_pairs={{0,4},{4,0},{8,12},{12,8},{16,20},{20,16},{24,28},{28,24},{1,5},{5... | collective-permute-start | bytes 835592 | tf_op jit(solution)/shard_map/ppermute | solution.py:684
  (9 other events, 117.2 us)

commit v8 on v7

--- a/solution.py
+++ b/solution.py
@@ -133,6 +133,7 @@
     arrays = [qkv, out] + vectors
     return pl.pallas_call(
         pack_kernel,
+        out_specs=pl.BlockSpec(memory_space=pltpu.VMEM),
         out_shape=jax.ShapeDtypeStruct(shape, BF16),
         compiler_params=params(58),
         name="pack",

time: 147 us -> 147 us (level)
  no operation moved by 1% of the time
where the time goes in v8:
time: 147 us; the launch traced here: 146 us
  Pallas kernels  70.9 us (48%)
  waiting for transfers between devices  42.5 us (29%)
  starting transfers between devices  31.5 us (21%)
    pallas_call x24, Pallas kernels, resident(): pl.pallas_call(kernel, in_specs=[pl.BlockSpec(memory_space=pltpu.SMEM)] *...  57.4 us
    ppermute x30, waiting for transfers between devices, swap(): return lax.ppermute(array, axis, [(k, k ^ bit) for k in range(n)])  33.3 us
    ppermute x30, starting transfers between devices, swap(): return lax.ppermute(array, axis, [(k, k ^ bit) for k in range(n)])  24 us
    all_to_all x1, waiting for transfers between devices, local(): nsum = lax.all_to_all(sums, 'ctx', 0, 0, tiled=True).reshape(nc * spans, D)  7.26 us
    all_to_all x1, starting transfers between devices, local(): nsum = lax.all_to_all(sums, 'ctx', 0, 0, tiled=True).reshape(nc * spans, D)  5.81 us
    pallas_call x1, Pallas kernels, block_output(): pl.pallas_call(mixed_kernel, grid=(rows // ROWS,), in_specs=[pl.BlockSpec...  4.13 us
    pallas_call x2, Pallas kernels, finish(): pl.pallas_call(functools.partial(finish_kernel, heights=heights, plan=pla...  3.78 us
    pallas_call x1, Pallas kernels, first_back(): pl.pallas_call(first_kernel, grid=(rows // ROWS,), in_specs=in_vmem(7), o...  3.44 us
  transfers between devices with their start and end apart: 32, of which 16 were waited for; matrix products, arithmetic and copies ran while one was open for 0% of the time, Pallas kernels for 45%

profile of v8, /device:TPU:0, one launch (start us, length us, event | category | flops | bytes accessed | tf_op | source)
XLA Modules:
  0.0 146.4 jit_solution(18199027191206320642)
XLA Ops:
  0.7 2.1 %pack.1.refs_0_ = bf16[144,2048]{1,0:T(8,128)(2,1)} custom-call(bf16[128,1536]{1,0:T(8,128)(2,1)} %qkv_ref.1, bf16[128,512]{1,0:T(8,128)(2,1)} %out_ref.1, bf16[1,128]{1,0:T(2,128)(2,1)} %bitcast.84, bf16[1,128]{1,0:T(2,128)(2,1)} %bitcast.85, bf16[3,128]{1,0:T(4,128)(2,1)} %bitcast.82, bf16[1,128]{1,0:T(2,128)(2,1)} %bitcast.86, bf16[1,128]{1,0:T(2,128)(2,1)} %bitcast.87, ...), custom_call_target="tpu_custom_call" | custom-call | flops 1000000000 | bytes 1000000 | tf_op jit(solution)/shard_map/pack/pallas_call | solution.py:134
  2.7 3.0 %collective-permute-start.1 = (bf16[144,2048]{1,0:T(8,128)(2,1)}, bf16[144,2048]{1,0:T(8,128)(2,1)S(1)}, u32[]{:S(2)}, u32[]{:S(2)}) collective-permute-start(bf16[144,2048]{1,0:T(8,128)(2,1)} %pack.1.refs_0_), channel_id=1, source_target_pairs={{0,2},{1,3},{2,0},{3,1},{4,6},{5,7},{6,4},{7,5},{8,10},{9,11},{10,... | collective-permute-start | bytes 1769480 | tf_op jit(solution)/shard_map/ppermute | solution.py:685
  5.7 1.4 span_sums.1
  7.1 5.8 %all-to-all-start = ((f32[8,8,512]{2,1,0:T(8,128)}), f32[8,8,512]{2,1,0:T(8,128)S(1)}, u32[]{:S(2)}, u32[]{:S(2)}) async-start(f32[8,8,512]{2,1,0:T(8,128)} %span_sums.1), calls=%async_computation | async-start | bytes 262144 | tf_op jit(solution)/shard_map/all_to_all | solution.py:973
  13.0 7.3 %all-to-all-done = f32[8,8,512]{2,1,0:T(8,128)S(1)} async-done(((f32[8,8,512]{2,1,0:T(8,128)}), f32[8,8,512]{2,1,0:T(8,128)S(1)}, u32[]{:S(2)}, u32[]{:S(2)}) %all-to-all-start) | async-done | bytes 131104 | tf_op jit(solution)/shard_map/all_to_all | solution.py:973
  22.3 8.1 %attend.1 = (bf16[1024,1536]{1,0:T(8,128)(2,1)S(1)}, bf16[32,192,256]{2,1,0:T(8,128)(2,1)S(1)}, bf16[1024,512]{1,0:T(8,128)(2,1)S(1)}, bf16[1024,512]{1,0:T(8,12...) custom-call(s32[76]{0:T(128)S(1)} %concatenate.21.sc.refs_0_, ...), custom_call_target="tpu_custom_call" | custom-call | flops 12000000000 | bytes 12000000 | tf_op jit(solution)/shard_map/attend/pallas_call | solution.py:69
  30.4 4.5 %collective-permute-done.4.refs_2_ = bf16[128,2048]{1,0:T(8,128)(2,1)S(1)} collective-permute-done((bf16[128,2048]{1,0:T(8,128)(2,1)}, bf16[128,2048]{1,0:T(8,128)(2,1)S(1)}, u32[]{:S(2)}, u32[]{:S(2)}) %collective-permute-start.4) | collective-permute-done | bytes 524320 | tf_op jit(solution)/shard_map/ppermute | solution.py:685
  37.0 6.7 %ffn_up.1 = (bf16[1024,2048]{1,0:T(8,128)(2,1)S(1)}, bf16[1024,2048]{1,0:T(8,128)(2,1)S(1)}, bf16[512,2048]{1,0:T(8,128)(2,1)S(1)}) custom-call(s32[76]{0:T(128)S(1)} %concatenate.21.sc.refs_0_, bf16[1024,512]{1,0:T(8,128)(2,1)S(1)} %get-tuple-element.129.h2_ref, f32[8,2048]{1,0:T(8,128)S(1)} %get-tuple-element.127.vec.vec_ref.refs_9_, ...), custom_call_target="tpu_custom_call" | custom-call | flops 8000000000 | bytes 8000000 | tf_op jit(solution)/shard_map/ffn_up/pallas_call | solution.py:69
  43.7 2.9 %down_grad.1 = (bf16[2,2048,128]{2,1,0:T(8,128)(2,1)S(1)}, bf16[2,2048,128]{2,1,0:T(8,128)(2,1)S(1)}) custom-call(s32[76]{0:T(128)S(1)} %concatenate.21.sc.refs_0_, bf16[1024,2048]{1,0:T(8,128)(2,1)S(1)} %get-tuple-element.134.g_ref, bf16[1024,512]{1,0:T(8,128)(2,1)S(1)} %bitcast.49), custom_call_target="tpu_custom_call" | custom-call | flops 4000000000 | bytes 4000000 | tf_op jit(solution)/shard_map/down_grad/pallas_call | solution.py:69
  46.6 2.6 %collective-permute-done.7.refs_2_ = bf16[512,512]{1,0:T(8,128)(2,1)S(1)} collective-permute-done((bf16[512,512]{1,0:T(8,128)(2,1)S(1)}, bf16[512,512]{1,0:T(8,128)(2,1)S(1)}, u32[]{:S(2)}, u32[]{:S(2)}) %collective-permute-start.7) | collective-permute-done | bytes 524320 | tf_op jit(solution)/shard_map/ppermute | solution.py:685
  51.2 7.7 %ffn_down.1 = (f32[1024,512]{1,0:T(8,128)S(1)}, f32[1,2048]{1,0:T(1,128)S(1)}, bf16[2,2048,128]{2,1,0:T(8,128)(2,1)S(1)}, bf16[2,2048,128]{2,1,0:T(8,128)(2,1)S(1)}) custom-call(s32[76]{0:T(128)S(1)} %concatenate.21.sc.refs_0_, bf16[1024,512]{1,0:T(8,128)(2,1)S(1)} %get-tuple-element.129.h2_ref, bf16[1024,512]{1,0:T(8,128)(2,1)S(1)} %bitcast.50, ...), custom_call_target="tpu_custom_call" | custom-call | flops 8000000000 | bytes 8000000 | tf_op jit(solution)/shard_map/ffn_down/pallas_call | solution.py:69
  60.6 2.5 %mid.1 = (f32[1024,512]{1,0:T(8,128)S(1)}, bf16[1024,512]{1,0:T(8,128)(2,1)S(1)}, f32[512,512]{1,0:T(8,128)S(1)}, f32[8,512]{1,0:T(8,128)S(1)}) custom-call(bf16[1024,512]{1,0:T(8,128)(2,1)S(1)} %bitcast.51, f32[1024,512]{1,0:T(8,128)S(1)} %get-tuple-element.147.dh2_ref, f32[1024,512]{1,0:T(8,128)S(1)} %get-tuple-element.206.r1_ref, ...), custom_call_target="tpu_custom_call" | custom-call | flops 5000000000 | bytes 5000000 | tf_op jit(solution)/shard_map/mid/pallas_call | solution.py:69
  64.0 1.5 %collective-permute-start.12 = (bf16[2,1024,128]{2,1,0:T(8,128)(2,1)S(1)}, bf16[2,1024,128]{2,1,0:T(8,128)(2,1)S(1)}, u32[]{:S(2)}, u32[]{:S(2)}) collective-permute-start(bf16[2,1024,128]{2,1,0:T(8,128)(2,1)S(1)} %get-tuple-element.153), channel_id=1, source_target_pairs={{0,4},{4,0},{8,12},{12,8},{16,20},{20,16},{24,28},{28,24},{1,5},{5... | collective-permute-start | bytes 1572872 | tf_op jit(solution)/shard_map/ppermute | solution.py:685
  65.5 8.8 %back_0.1 = (f32[1024,512]{1,0:T(8,128)S(1)}, f32[72,512]{1,0:T(8,128)S(1)}, bf16[128,128]{1,0:T(8,128)(2,1)S(1)}, bf16[128,128]{1,0:T(8,128)(2,1)S(1)}, bf16[2,...) custom-call(s32[76]{0:T(128)S(1)} %concatenate.21.sc.refs_0_, bf16[1024,512]{1,0:T(8,128)(2,1)S(1)} %bitcast.55, ...), custom_call_target="tpu_custom_call" | custom-call | flops 8999999488 | bytes 9000000 | tf_op jit(solution)/shard_map/back_0/pallas_call | solution.py:69
  75.6 2.8 %collective-permute-done.12 = bf16[2,1024,128]{2,1,0:T(8,128)(2,1)S(1)} collective-permute-done((bf16[2,1024,128]{2,1,0:T(8,128)(2,1)S(1)}, bf16[2,1024,128]{2,1,0:T(8,128)(2,1)S(1)}, u32[]{:S(2)}, u32[]{:S(2)}) %collective-permute-start.12) | collective-permute-done | bytes 524320 | tf_op jit(solution)/shard_map/ppermute | solution.py:685
  79.1 1.8 %collective-permute-start.15 = (bf16[1,1024,128]{2,1,0:T(8,128)(2,1)S(1)}, bf16[1,1024,128]{2,1,0:T(8,128)(2,1)S(1)}, u32[]{:S(2)}, u32[]{:S(2)}) collective-permute-start(bf16[1,1024,128]{2,1,0:T(8,128)(2,1)S(1)} %get-tuple-element.169), channel_id=1, source_target_pairs={{0,2},{1,3},{2,0},{3,1},{4,6},{5,7},{6,4},{7,5},{8,10},{9,11},{10,... | collective-permute-start | bytes 786440 | tf_op jit(solution)/shard_map/ppermute | solution.py:685
  80.9 4.3 %back_1.2 = (f32[512,512]{1,0:T(8,128)S(1)}, f32[512,768]{1,0:T(8,128)S(1)}, f32[64,512]{1,0:T(8,128)S(1)}, f32[16,1536]{1,0:T(8,128)S(1)}) custom-call(s32[76]{0:T(128)S(1)} %concatenate.21.sc.refs_0_, bf16[1024,512]{1,0:T(8,128)(2,1)S(1)} %bitcast.56, bf16[1024,512]{1,0:T(8,128)(2,1)S(1)} %get-tuple-element.154.refs_2_, ...), custom_call_target="tpu_custom_call" | custom-call | flops 8999999488 | bytes 9000000 | tf_op jit(solution)/shard_map/back_1/pallas_call | solution.py:69
  87.0 1.7 %collective-permute-start.16 = (bf16[1024,128]{1,0:T(8,128)(2,1)S(1)}, bf16[1024,128]{1,0:T(8,128)(2,1)S(1)}, u32[]{:S(2)}, u32[]{:S(2)}) collective-permute-start(bf16[1024,128]{1,0:T(8,128)(2,1)S(1)} %bitcast.67), channel_id=1, source_target_pairs={{0,8},{4,12},{8,0},{12,4},{16,24},{20,28},{24,16},{28,20},{1,9},{5... | collective-permute-start | bytes 786440 | tf_op jit(solution)/shard_map/ppermute | solution.py:685
  88.7 5.4 %back_1.3 = (f32[512,512]{1,0:T(8,128)S(1)}, f32[72,512]{1,0:T(8,128)}, bf16[128,128]{1,0:T(8,128)(2,1)S(1)}, bf16[128,128]{1,0:T(8,128)(2,1)S(1)}, bf16[2,896,1...) custom-call(s32[76]{0:T(128)S(1)} %concatenate.21.sc.refs_0_, bf16[1024,512]{1,0:T(8,128)(2,1)S(1)} %bitcast.57, ...), custom_call_target="tpu_custom_call" | custom-call | flops 8999999488 | bytes 9000000 | tf_op jit(solution)/shard_map/back_1/pallas_call | solution.py:69
  96.6 1.8 %collective-permute-start.21 = (bf16[1088,128]{1,0:T(8,128)(2,1)S(1)}, bf16[1088,128]{1,0:T(8,128)(2,1)S(1)}, u32[]{:S(2)}, u32[]{:S(2)}) collective-permute-start(bf16[1088,128]{1,0:T(8,128)(2,1)S(1)} %get-tuple-element.202), channel_id=1, source_target_pairs={{0,2},{1,3},{2,0},{3,1},{4,6},{5,7},{6,4},{7,5},{8,10},{9,11},{10,... | collective-permute-start | bytes 835592 | tf_op jit(solution)/shard_map/ppermute | solution.py:685
  98.4 2.6 %collective-permute-start.19 = (bf16[512,128]{1,0:T(8,128)(2,1)S(1)}, bf16[512,128]{1,0:T(8,128)(2,1)S(1)}, u32[]{:S(2)}, u32[]{:S(2)}) collective-permute-start(bf16[512,128]{1,0:T(8,128)(2,1)S(1)} %get-tuple-element.188), channel_id=1, source_target_pairs={{0,16},{4,20},{8,24},{12,28},{16,0},{20,4},{24,8},{28,12},{1,17},{... | collective-permute-start | bytes 393224 | tf_op jit(solution)/shard_map/ppermute | solution.py:685
  101.1 1.7 %collective-permute-start.22 = (bf16[448,128]{1,0:T(8,128)(2,1)S(1)}, bf16[448,128]{1,0:T(8,128)(2,1)S(1)}, u32[]{:S(2)}, u32[]{:S(2)}) collective-permute-start(bf16[448,128]{1,0:T(8,128)(2,1)S(1)} %get-tuple-element.203), channel_id=1, source_target_pairs={{0,6},{1,7},{2,4},{3,5},{4,2},{5,3},{6,0},{7,1},{8,14},{9,15},{10,... | collective-permute-start | bytes 344072 | tf_op jit(solution)/shard_map/ppermute | solution.py:770
  102.7 4.5 %collective-permute-done.19.got_ref = bf16[512,128]{1,0:T(8,128)(2,1)S(1)} collective-permute-done((bf16[512,128]{1,0:T(8,128)(2,1)S(1)}, bf16[512,128]{1,0:T(8,128)(2,1)S(1)}, u32[]{:S(2)}, u32[]{:S(2)}) %collective-permute-start.19) | collective-permute-done | bytes 131104 | tf_op jit(solution)/shard_map/ppermute | solution.py:685
  107.3 1.9 %collective-permute-done.22.refs_3_ = bf16[448,128]{1,0:T(8,128)(2,1)S(1)} collective-permute-done((bf16[448,128]{1,0:T(8,128)(2,1)S(1)}, bf16[448,128]{1,0:T(8,128)(2,1)S(1)}, u32[]{:S(2)}, u32[]{:S(2)}) %collective-permute-start.22) | collective-permute-done | bytes 114720 | tf_op jit(solution)/shard_map/ppermute | solution.py:770
  111.2 4.1 %block_output.1 = bf16[1024,512]{1,0:T(8,128)(2,1)} custom-call(s32[76]{0:T(128)S(1)} %concatenate.21.sc.refs_0_, f32[1024,512]{1,0:T(8,128)S(1)} %get-tuple-element.206.r1_ref, bf16[1024,2048]{1,0:T(8,128)(2,1)S(1)} %get-tuple-element.134.g_ref, f32[8,2048]{1,0:T(8,128)S(1)} %get-tuple-element.127.vec.vec_ref.refs_9_, bf16[512,512]{1,0:T(8,128)(2,1)S(1)} %copy-done.5, ...), custom_call_target="tpu_custom_call" | custom-call | flops 4000000000 | bytes 4000000 | tf_op jit(solution)/shard_map/block_output/pallas_call | solution.py:671
  119.1 6.3 %collective-permute-done.25 = bf16[1024,128]{1,0:T(8,128)(2,1)S(1)} collective-permute-done((bf16[1024,128]{1,0:T(8,128)(2,1)S(1)}, bf16[1024,128]{1,0:T(8,128)(2,1)S(1)}, u32[]{:S(2)}, u32[]{:S(2)}) %collective-permute-start.25) | collective-permute-done | bytes 262176 | tf_op jit(solution)/shard_map/ppermute | solution.py:685
  126.7 4.0 %collective-permute-done.27 = bf16[272,128]{1,0:T(8,128)(2,1)S(1)} collective-permute-done((bf16[272,128]{1,0:T(8,128)(2,1)S(1)}, bf16[272,128]{1,0:T(8,128)(2,1)S(1)}, u32[]{:S(2)}, u32[]{:S(2)}) %collective-permute-start.27) | collective-permute-done | bytes 69664 | tf_op jit(solution)/shard_map/ppermute | solution.py:685
  132.1 3.4 %first_back.1 = f32[1024,512]{1,0:T(8,128)} custom-call(bf16[1024,512]{1,0:T(8,128)(2,1)S(1)} %bitcast.58, f32[1024,512]{1,0:T(8,128)S(1)} %get-tuple-element.216.dr1_ref, f32[512,512]{1,0:T(8,128)S(1)} %get-tuple-element.217.upper_ref, f32[512,512]{1,0:T(8,128)S(1)} %get-tuple-element.185.lower_ref, bf16[64,128]{1,0:T(8,128)(2,1)S(1)} %get-tuple-element.218.own_ref, ...), custom_call_target="tpu_custom_call" | custom-call | flops 3000000000 | bytes 3000000 | tf_op jit(solution)/shard_map/first_back/pallas_call | solution.py:645
  137.2 3.7 %collective-permute-done.29 = bf16[2048,128]{1,0:T(8,128)(2,1)S(1)} collective-permute-done((bf16[2048,128]{1,0:T(8,128)(2,1)S(1)}, bf16[2048,128]{1,0:T(8,128)(2,1)S(1)}, u32[]{:S(2)}, u32[]{:S(2)}) %collective-permute-start.29) | collective-permute-done | bytes 524320 | tf_op jit(solution)/shard_map/ppermute | solution.py:685
  141.0 2.1 %finish.2 = (f32[512,512]{1,0:T(8,128)}, f32[128,2048]{1,0:T(8,128)}) custom-call(s32[76]{0:T(128)S(1)} %concatenate.21.sc.refs_0_, bf16[8,512,128]{2,1,0:T(8,128)(2,1)S(1)} %bitcast.42), custom_call_target="tpu_custom_call" | custom-call | flops 2000000000 | bytes 2000000 | tf_op jit(solution)/shard_map/finish/pallas_call | solution.py:938
  143.1 1.4 collective-permute-done.30
  144.6 1.6 %finish.3 = (f32[128,1536]{1,0:T(8,128)}, f32[128,512]{1,0:T(8,128)}, f32[128]{0:T(128)}, f32[128]{0:T(128)}, f32[384]{0:T(512)}, /*index=5*/f32[128]{0:T(128)},...) custom-call(s32[76]{0:T(128)S(1)} %concatenate.21.sc.refs_0_, bf16[8,272,128]{2,1,0:T(8,128)(2,1)S(1)} %bitcast.43), custom_call_target="tpu_custom_call" | custom-call | flops 2000000000 | bytes 2000000 | tf_op jit(solution)/shard_map/finish/pallas_call | solution.py:938
  (90 shorter events, 25.1 us)
Async XLA Ops:
  2.7 17.5 %collective-permute-start.1 = (bf16[144,2048]{1,0:T(8,128)(2,1)}, bf16[144,2048]{1,0:T(8,128)(2,1)S(1)}, u32[]{:S(2)}, u32[]{:S(2)}) collective-permute-start(bf16[144,2048]{1,0:T(8,128)(2,1)} %pack.1.refs_0_), channel_id=1, source_target_pairs={{0,2},{1,3},{2,0},{3,1},{4,6},{5,7},{6,4},{7,5},{8,10},{9,11},{10,... | collective-permute-start | bytes 1769480 | tf_op jit(solution)/shard_map/ppermute | solution.py:685
  7.1 13.1 %all-to-all-start = ((f32[8,8,512]{2,1,0:T(8,128)}), f32[8,8,512]{2,1,0:T(8,128)S(1)}, u32[]{:S(2)}, u32[]{:S(2)}) async-start(f32[8,8,512]{2,1,0:T(8,128)} %span_sums.1), calls=%async_computation | async-start | bytes 262144 | tf_op jit(solution)/shard_map/all_to_all | solution.py:973
  12.9 8.4 %collective-permute-start = (bf16[144,2048]{1,0:T(8,128)(2,1)S(1)}, bf16[144,2048]{1,0:T(8,128)(2,1)S(1)}, u32[]{:S(2)}, u32[]{:S(2)}) collective-permute-start(bf16[144,2048]{1,0:T(8,128)(2,1)S(1)} %copy-done.3), channel_id=1, source_target_pairs={{0,1},{1,0},{2,3},{3,2},{4,5},{5,4},{6,7},{7,6},{8,9},{9,8},{10,11... | collective-permute-start | bytes 1769480 | tf_op jit(solution)/shard_map/ppermute | solution.py:685
  20.3 2.0 %collective-permute-start.2 = (bf16[144,2048]{1,0:T(8,128)(2,1)S(1)}, bf16[144,2048]{1,0:T(8,128)(2,1)S(1)}, u32[]{:S(2)}, u32[]{:S(2)}) collective-permute-start(bf16[144,2048]{1,0:T(8,128)(2,1)S(1)} %collective-permute-done.1.refs_2_), channel_id=1, source_target_pairs={{0,1},{1,0},{2,3},{3,2},{4,5},{5,4},{6,7},{7,6},{8,9},{9,8},{10,11... | collective-permute-start | bytes 1769480 | tf_op jit(solution)/shard_map/ppermute | solution.py:685
  20.4 14.6 %collective-permute-start.4 = (bf16[128,2048]{1,0:T(8,128)(2,1)}, bf16[128,2048]{1,0:T(8,128)(2,1)S(1)}, u32[]{:S(2)}, u32[]{:S(2)}) collective-permute-start(bf16[128,2048]{1,0:T(8,128)(2,1)} %refs_0_), channel_id=1, source_target_pairs={{0,2},{1,3},{2,0},{3,1},{4,6},{5,7},{6,4},{7,5},{8,10},{9,11},{10,... | collective-permute-start | bytes 1572872 | tf_op jit(solution)/shard_map/ppermute | solution.py:685
  21.1 15.9 %collective-permute-start.3 = (bf16[128,2048]{1,0:T(8,128)(2,1)}, bf16[128,2048]{1,0:T(8,128)(2,1)S(1)}, u32[]{:S(2)}, u32[]{:S(2)}) collective-permute-start(bf16[128,2048]{1,0:T(8,128)(2,1)} %refs_0_), channel_id=1, source_target_pairs={{0,1},{1,0},{2,3},{3,2},{4,5},{5,4},{6,7},{7,6},{8,9},{9,8},{10,11... | collective-permute-start | bytes 1572872 | tf_op jit(solution)/shard_map/ppermute | solution.py:685
  34.9 2.1 %collective-permute-start.5 = (bf16[128,2048]{1,0:T(8,128)(2,1)S(1)}, bf16[128,2048]{1,0:T(8,128)(2,1)S(1)}, u32[]{:S(2)}, u32[]{:S(2)}) collective-permute-start(bf16[128,2048]{1,0:T(8,128)(2,1)S(1)} %collective-permute-done.4.refs_2_), channel_id=1, source_target_pairs={{0,1},{1,0},{2,3},{3,2},{4,5},{5,4},{6,7},{7,6},{8,9},{9,8},{10,11... | collective-permute-start | bytes 1572872 | tf_op jit(solution)/shard_map/ppermute | solution.py:685
  34.9 14.3 %collective-permute-start.7 = (bf16[512,512]{1,0:T(8,128)(2,1)S(1)}, bf16[512,512]{1,0:T(8,128)(2,1)S(1)}, u32[]{:S(2)}, u32[]{:S(2)}) collective-permute-start(bf16[512,512]{1,0:T(8,128)(2,1)S(1)} %copy-done.5), channel_id=1, source_target_pairs={{0,2},{1,3},{2,0},{3,1},{4,6},{5,7},{6,4},{7,5},{8,10},{9,11},{10,... | collective-permute-start | bytes 1572872 | tf_op jit(solution)/shard_map/ppermute | solution.py:685
  35.6 15.3 %collective-permute-start.6 = (bf16[512,512]{1,0:T(8,128)(2,1)S(1)}, bf16[512,512]{1,0:T(8,128)(2,1)S(1)}, u32[]{:S(2)}, u32[]{:S(2)}) collective-permute-start(bf16[512,512]{1,0:T(8,128)(2,1)S(1)} %copy-done.5), channel_id=1, source_target_pairs={{0,1},{1,0},{2,3},{3,2},{4,5},{5,4},{6,7},{7,6},{8,9},{9,8},{10,11... | collective-permute-start | bytes 1572872 | tf_op jit(solution)/shard_map/ppermute | solution.py:685
  49.2 1.9 %collective-permute-start.8 = (bf16[512,512]{1,0:T(8,128)(2,1)S(1)}, bf16[512,512]{1,0:T(8,128)(2,1)S(1)}, u32[]{:S(2)}, u32[]{:S(2)}) collective-permute-start(bf16[512,512]{1,0:T(8,128)(2,1)S(1)} %collective-permute-done.7.refs_2_), channel_id=1, source_target_pairs={{0,1},{1,0},{2,3},{3,2},{4,5},{5,4},{6,7},{7,6},{8,9},{9,8},{10,11... | collective-permute-start | bytes 1572872 | tf_op jit(solution)/shard_map/ppermute | solution.py:685
  49.2 9.8 %collective-permute-start.9 = (bf16[2,2048,128]{2,1,0:T(8,128)(2,1)S(1)}, bf16[2,2048,128]{2,1,0:T(8,128)(2,1)S(1)}, u32[]{:S(2)}, u32[]{:S(2)}) collective-permute-start(bf16[2,2048,128]{2,1,0:T(8,128)(2,1)S(1)} %get-tuple-element.144), channel_id=1, source_target_pairs={{0,1},{1,0},{2,3},{3,2},{4,5},{5,4},{6,7},{7,6},{8,9},{9,8},{10,11... | collective-permute-start | bytes 3145736 | tf_op jit(solution)/shard_map/ppermute | solution.py:685
  58.8 4.3 %collective-permute-start.10 = (bf16[2,2048,128]{2,1,0:T(8,128)(2,1)S(1)}, bf16[2,2048,128]{2,1,0:T(8,128)(2,1)S(1)}, u32[]{:S(2)}, u32[]{:S(2)}) collective-permute-start(bf16[2,2048,128]{2,1,0:T(8,128)(2,1)S(1)} %get-tuple-element.151), channel_id=1, source_target_pairs={{0,1},{1,0},{2,3},{3,2},{4,5},{5,4},{6,7},{7,6},{8,9},{9,8},{10,11... | collective-permute-start | bytes 3145736 | tf_op jit(solution)/shard_map/ppermute | solution.py:685
  59.8 14.4 %collective-permute-start.11 = (bf16[1,2048,128]{2,1,0:T(8,128)(2,1)S(1)}, bf16[1,2048,128]{2,1,0:T(8,128)(2,1)S(1)}, u32[]{:S(2)}, u32[]{:S(2)}) collective-permute-start(bf16[1,2048,128]{2,1,0:T(8,128)(2,1)S(1)} %get-tuple-element.146), channel_id=1, source_target_pairs={{0,2},{1,3},{2,0},{3,1},{4,6},{5,7},{6,4},{7,5},{8,10},{9,11},{10,... | collective-permute-start | bytes 1572872 | tf_op jit(solution)/shard_map/ppermute | solution.py:685
  64.0 14.4 %collective-permute-start.12 = (bf16[2,1024,128]{2,1,0:T(8,128)(2,1)S(1)}, bf16[2,1024,128]{2,1,0:T(8,128)(2,1)S(1)}, u32[]{:S(2)}, u32[]{:S(2)}) collective-permute-start(bf16[2,1024,128]{2,1,0:T(8,128)(2,1)S(1)} %get-tuple-element.153), channel_id=1, source_target_pairs={{0,4},{4,0},{8,12},{12,8},{16,20},{20,16},{24,28},{28,24},{1,5},{5... | collective-permute-start | bytes 1572872 | tf_op jit(solution)/shard_map/ppermute | solution.py:685
  75.0 11.3 %collective-permute-start.14 = (bf16[1,1024,128]{2,1,0:T(8,128)(2,1)S(1)}, bf16[1,1024,128]{2,1,0:T(8,128)(2,1)S(1)}, u32[]{:S(2)}, u32[]{:S(2)}) collective-permute-start(bf16[1,1024,128]{2,1,0:T(8,128)(2,1)S(1)} %get-tuple-element.166), channel_id=1, source_target_pairs={{0,4},{4,0},{8,12},{12,8},{16,20},{20,16},{24,28},{28,24},{1,5},{5... | collective-permute-start | bytes 786440 | tf_op jit(solution)/shard_map/ppermute | solution.py:685
  75.6 9.6 %collective-permute-start.13 = (bf16[2,1280,128]{2,1,0:T(8,128)(2,1)S(1)}, bf16[2,1280,128]{2,1,0:T(8,128)(2,1)S(1)}, u32[]{:S(2)}, u32[]{:S(2)}) collective-permute-start(bf16[2,1280,128]{2,1,0:T(8,128)(2,1)S(1)} %get-tuple-element.175), channel_id=1, source_target_pairs={{0,1},{1,0},{2,3},{3,2},{4,5},{5,4},{6,7},{7,6},{8,9},{9,8},{10,11... | collective-permute-start | bytes 1966088 | tf_op jit(solution)/shard_map/ppermute | solution.py:685
  79.1 7.2 %collective-permute-start.15 = (bf16[1,1024,128]{2,1,0:T(8,128)(2,1)S(1)}, bf16[1,1024,128]{2,1,0:T(8,128)(2,1)S(1)}, u32[]{:S(2)}, u32[]{:S(2)}) collective-permute-start(bf16[1,1024,128]{2,1,0:T(8,128)(2,1)S(1)} %get-tuple-element.169), channel_id=1, source_target_pairs={{0,2},{1,3},{2,0},{3,1},{4,6},{5,7},{6,4},{7,5},{8,10},{9,11},{10,... | collective-permute-start | bytes 786440 | tf_op jit(solution)/shard_map/ppermute | solution.py:685
  85.9 8.9 %collective-permute-start.17 = (bf16[2,640,128]{2,1,0:T(8,128)(2,1)S(1)}, bf16[2,640,128]{2,1,0:T(8,128)(2,1)S(1)}, u32[]{:S(2)}, u32[]{:S(2)}) collective-permute-start(bf16[2,640,128]{2,1,0:T(8,128)(2,1)S(1)} %get-tuple-element.177), channel_id=1, source_target_pairs={{0,4},{4,0},{8,12},{12,8},{16,20},{20,16},{24,28},{28,24},{1,5},{5... | collective-permute-start | bytes 983048 | tf_op jit(solution)/shard_map/ppermute | solution.py:685
  87.0 7.1 %collective-permute-start.16 = (bf16[1024,128]{1,0:T(8,128)(2,1)S(1)}, bf16[1024,128]{1,0:T(8,128)(2,1)S(1)}, u32[]{:S(2)}, u32[]{:S(2)}) collective-permute-start(bf16[1024,128]{1,0:T(8,128)(2,1)S(1)} %bitcast.67), channel_id=1, source_target_pairs={{0,8},{4,12},{8,0},{12,4},{16,24},{20,28},{24,16},{28,20},{1,9},{5... | collective-permute-start | bytes 786440 | tf_op jit(solution)/shard_map/ppermute | solution.py:685
  94.1 1.8 %collective-permute-start.18 = (bf16[2,896,128]{2,1,0:T(8,128)(2,1)S(1)}, bf16[2,896,128]{2,1,0:T(8,128)(2,1)S(1)}, u32[]{:S(2)}, u32[]{:S(2)}) collective-permute-start(bf16[2,896,128]{2,1,0:T(8,128)(2,1)S(1)} %get-tuple-element.193), channel_id=1, source_target_pairs={{0,1},{1,0},{2,3},{3,2},{4,5},{5,4},{6,7},{7,6},{8,9},{9,8},{10,11... | collective-permute-start | bytes 1376264 | tf_op jit(solution)/shard_map/ppermute | solution.py:685
  96.6 12.7 %collective-permute-start.21 = (bf16[1088,128]{1,0:T(8,128)(2,1)S(1)}, bf16[1088,128]{1,0:T(8,128)(2,1)S(1)}, u32[]{:S(2)}, u32[]{:S(2)}) collective-permute-start(bf16[1088,128]{1,0:T(8,128)(2,1)S(1)} %get-tuple-element.202), channel_id=1, source_target_pairs={{0,2},{1,3},{2,0},{3,1},{4,6},{5,7},{6,4},{7,5},{8,10},{9,11},{10,... | collective-permute-start | bytes 835592 | tf_op jit(solution)/shard_map/ppermute | solution.py:685
  98.4 8.9 %collective-permute-start.19 = (bf16[512,128]{1,0:T(8,128)(2,1)S(1)}, bf16[512,128]{1,0:T(8,128)(2,1)S(1)}, u32[]{:S(2)}, u32[]{:S(2)}) collective-permute-start(bf16[512,128]{1,0:T(8,128)(2,1)S(1)} %get-tuple-element.188), channel_id=1, source_target_pairs={{0,16},{4,20},{8,24},{12,28},{16,0},{20,4},{24,8},{28,12},{1,17},{... | collective-permute-start | bytes 393224 | tf_op jit(solution)/shard_map/ppermute | solution.py:685
  100.9 8.3 %collective-permute-start.20 = (bf16[704,128]{1,0:T(8,128)(2,1)S(1)}, bf16[704,128]{1,0:T(8,128)(2,1)S(1)}, u32[]{:S(2)}, u32[]{:S(2)}) collective-permute-start(bf16[704,128]{1,0:T(8,128)(2,1)S(1)} %get-tuple-element.201), channel_id=1, source_target_pairs={{0,4},{4,0},{8,12},{12,8},{16,20},{20,16},{24,28},{28,24},{1,5},{5... | collective-permute-start | bytes 540680 | tf_op jit(solution)/shard_map/ppermute | solution.py:685
  101.1 8.2 %collective-permute-start.22 = (bf16[448,128]{1,0:T(8,128)(2,1)S(1)}, bf16[448,128]{1,0:T(8,128)(2,1)S(1)}, u32[]{:S(2)}, u32[]{:S(2)}) collective-permute-start(bf16[448,128]{1,0:T(8,128)(2,1)S(1)} %get-tuple-element.203), channel_id=1, source_target_pairs={{0,6},{1,7},{2,4},{3,5},{4,2},{5,3},{6,0},{7,1},{8,14},{9,15},{10,... | collective-permute-start | bytes 344072 | tf_op jit(solution)/shard_map/ppermute | solution.py:770
  107.2 8.2 %collective-permute-start.23 = (bf16[512,128]{1,0:T(8,128)(2,1)S(1)}, bf16[512,128]{1,0:T(8,128)(2,1)S(1)}, u32[]{:S(2)}, u32[]{:S(2)}) collective-permute-start(bf16[512,128]{1,0:T(8,128)(2,1)S(1)} %last.2), channel_id=1, source_target_pairs={{0,16},{4,20},{8,24},{12,28},{16,0},{20,4},{24,8},{28,12},{1,17},{... | collective-permute-start | bytes 393224 | tf_op jit(solution)/shard_map/ppermute | solution.py:685
  109.9 7.6 %collective-permute-start.24 = (bf16[672,128]{1,0:T(8,128)(2,1)S(1)}, bf16[672,128]{1,0:T(8,128)(2,1)S(1)}, u32[]{:S(2)}, u32[]{:S(2)}) collective-permute-start(bf16[672,128]{1,0:T(8,128)(2,1)S(1)} %get-tuple-element.205), channel_id=1, source_target_pairs={{0,8},{4,12},{8,0},{12,4},{16,24},{20,28},{24,16},{28,20},{1,9},{5... | collective-permute-start | bytes 516104 | tf_op jit(solution)/shard_map/ppermute | solution.py:685
  115.5 9.9 %collective-permute-start.25 = (bf16[1024,128]{1,0:T(8,128)(2,1)S(1)}, bf16[1024,128]{1,0:T(8,128)(2,1)S(1)}, u32[]{:S(2)}, u32[]{:S(2)}) collective-permute-start(bf16[1024,128]{1,0:T(8,128)(2,1)S(1)} %constant_dynamic-update-slice_fusion), channel_id=1, source_target_pairs={{0,8},{4,12},{8,0},{12,4},{16,24},{20,28},{24,16},{28,20},{1,9},{5... | collective-permute-start | bytes 786440 | tf_op jit(solution)/shard_map/ppermute | solution.py:685
  118.1 7.4 %collective-permute-start.26 = (bf16[336,128]{1,0:T(8,128)(2,1)S(1)}, bf16[336,128]{1,0:T(8,128)(2,1)S(1)}, u32[]{:S(2)}, u32[]{:S(2)}) collective-permute-start(bf16[336,128]{1,0:T(8,128)(2,1)S(1)} %get-tuple-element.210), channel_id=1, source_target_pairs={{0,16},{4,20},{8,24},{12,28},{16,0},{20,4},{24,8},{28,12},{1,17},{... | collective-permute-start | bytes 258056 | tf_op jit(solution)/shard_map/ppermute | solution.py:685
  125.5 5.3 %collective-permute-start.27 = (bf16[272,128]{1,0:T(8,128)(2,1)S(1)}, bf16[272,128]{1,0:T(8,128)(2,1)S(1)}, u32[]{:S(2)}, u32[]{:S(2)}) collective-permute-start(bf16[272,128]{1,0:T(8,128)(2,1)S(1)} %get-tuple-element.214), channel_id=1, source_target_pairs={{0,16},{4,20},{8,24},{12,28},{16,0},{20,4},{24,8},{28,12},{1,17},{... | collective-permute-start | bytes 208904 | tf_op jit(solution)/shard_map/ppermute | solution.py:685
  126.7 14.2 %collective-permute-start.29 = (bf16[2048,128]{1,0:T(8,128)(2,1)S(1)}, bf16[2048,128]{1,0:T(8,128)(2,1)S(1)}, u32[]{:S(2)}, u32[]{:S(2)}) collective-permute-start(bf16[2048,128]{1,0:T(8,128)(2,1)S(1)} %constant_dynamic-update-slice_fusion.2), channel_id=1, source_target_pairs={{0,4},{4,0},{8,12},{12,8},{16,20},{20,16},{24,28},{28,24},{1,5},{5... | collective-permute-start | bytes 1572872 | tf_op jit(solution)/shard_map/ppermute | solution.py:685
  130.8 5.1 %collective-permute-start.28 = (bf16[544,128]{1,0:T(8,128)(2,1)S(1)}, bf16[544,128]{1,0:T(8,128)(2,1)S(1)}, u32[]{:S(2)}, u32[]{:S(2)}) collective-permute-start(bf16[544,128]{1,0:T(8,128)(2,1)S(1)} %constant_dynamic-update-slice_fusion.4), channel_id=1, source_target_pairs={{0,8},{4,12},{8,0},{12,4},{16,24},{20,28},{24,16},{28,20},{1,9},{5... | collective-permute-start | bytes 417800 | tf_op jit(solution)/shard_map/ppermute | solution.py:685
  135.9 8.6 %collective-permute-start.30 = (bf16[1088,128]{1,0:T(8,128)(2,1)S(1)}, bf16[1088,128]{1,0:T(8,128)(2,1)S(1)}, u32[]{:S(2)}, u32[]{:S(2)}) collective-permute-start(bf16[1088,128]{1,0:T(8,128)(2,1)S(1)} %constant_dynamic-update-slice_fusion.6), channel_id=1, source_target_pairs={{0,4},{4,0},{8,12},{12,8},{16,20},{20,16},{24,28},{28,24},{1,5},{5... | collective-permute-start | bytes 835592 | tf_op jit(solution)/shard_map/ppermute | solution.py:685
  (9 other events, 117.2 us)
